TPU v7x, 32 devices: a whole 2x2x4 slice. The times are simulated.
32 devices in a mesh: dp: 4 (over z), ctx: 4 (over x, core), expert: 2 (over y).
Axes of the slice: x: 2, y: 2, z: 4, core: 2. Of those that a mesh axis runs over, the one named last changes fastest.
Arguments:
- x_prompt: bfloat16 [8, 1024, 1536], P(('dp', 'expert'), 'ctx'), may hold values from -6 to 6
- x_cont: bfloat16 [8, 4, 256, 1536], P(('dp', 'expert'), 'ctx'), may hold values from -6 to 6
- norm1_gain: bfloat16 [1536], replicated, may hold values from 0.099609375 to 1.8984375
- w_query: bfloat16 [1536, 1536], replicated, may hold values from -0.625 to 0.625
- key_weight: bfloat16 [1536, 512], replicated, may hold values from -0.625 to 0.625
- value_weight: bfloat16 [1536, 512], replicated, may hold values from -0.15625 to 0.15625
- w_out: bfloat16 [1536, 1536], replicated, may hold values from -3 to 3
- norm2_gain: bfloat16 [1536], replicated, may hold values from 0.099609375 to 1.8984375
- w_router: bfloat16 [1536, 40], replicated, may hold values from -0.078125 to 0.078125
- w_gate_up: bfloat16 [40, 1536, 1024], P('expert'), may hold values from -0.15625 to 0.15625
- w_down: bfloat16 [40, 512, 1536], P('expert'), may hold values from -6 to 6
- routes_prompt: int32 [8, 1024, 8], P(('dp', 'expert'), 'ctx'), may hold values from 0 to 39, all different within a row
- routes_cont: int32 [8, 4, 256, 8], P(('dp', 'expert'), 'ctx'), may hold values from 0 to 39, all different within a row
- slot_order: int32 [8, 4, 512], P(('dp', 'expert'), 'ctx'), may hold values from 0 to 511, each once within a row
- dy_prompt: bfloat16 [8, 1024, 1536], P(('dp', 'expert'), 'ctx'), may hold values from -6 to 6
- dy_cont: bfloat16 [8, 4, 256, 1536], P(('dp', 'expert'), 'ctx'), may hold values from -6 to 6
Outputs:
- y_prompt: bfloat16 [8, 1024, 1536], P(('dp', 'expert'), 'ctx')
- y_cont: bfloat16 [8, 4, 256, 1536], P(('dp', 'expert'), 'ctx')
- dx_prompt: float32 [8, 1024, 1536], P(('dp', 'expert'), 'ctx')
- dx_cont: float32 [8, 4, 256, 1536], P(('dp', 'expert'), 'ctx')
- grad_norm1: float32 [1536], P(('dp', 'ctx'))
- grad_query: float32 [1536, 1536], P(('dp', 'ctx'))
- grad_key: float32 [1536, 512], P(('dp', 'ctx'))
- grad_value: float32 [1536, 512], P(('dp', 'ctx'))
- grad_out: float32 [1536, 1536], P(('dp', 'ctx'))
- grad_norm2: float32 [1536], P(('dp', 'ctx'))
- grad_router: float32 [1536, 40], P(('dp', 'ctx'))
- grad_gate_up: float32 [40, 1536, 1024], P('expert', ('dp', 'ctx'))
- grad_down: float32 [40, 512, 1536], P('expert', ('dp', 'ctx'))
Inputs may be any that keep to these rules, and one draw needn't show every extreme that they name: `routes_prompt`: each token names 8 different experts. `routes_cont`: each token names 8 different experts. slot_order[s, c] lists each of the block's 512 tokens once.
All inputs are finite; a program needn't handle non-finite values.
Results may differ from a plain program's by a relative error of at most 0.025.
Values may be sent and summed in bfloat16 or wider, within the bound.
No kernel may reach another device: no remote copies, remote signals or barrier semaphores. Data moves between devices by JAX's collectives and lax.ppermute only.
A program may use at most 448 MiB of HBM per device.

v0:
```python
from functools import partial

import jax
import jax.numpy as jnp
from jax import lax
from jax.sharding import PartitionSpec as P

QUERY_HEADS = 24
KEY_VALUE_HEADS = 8
HEAD_SIZE = 64


EPS = 1e-06
RESID = 0.22
ATT_SCALE = 0.015625
THETA = 10000.0
NEG = -1e30


def rope_tables(positions, head_dim):
    half_dim = head_dim // 2
    frequency = THETA ** (-(jnp.arange(half_dim, dtype=jnp.float32) * 2.0 / head_dim))
    angles = positions[:, None] * frequency[None, :]
    cosine_lookup = jnp.concatenate([jnp.cos(angles), jnp.cos(angles)], axis=-1)
    sine_lookup = jnp.concatenate([jnp.sin(angles), jnp.sin(angles)], axis=-1)
    return (cosine_lookup, sine_lookup)


def apply_rotary(values, cosine_lookup, sine_lookup, sign):
    half_dim = values.shape[-1] // 2
    turned = jnp.concatenate([-values[..., half_dim:], values[..., :half_dim]], axis=-1)
    return values * cosine_lookup[:, None, :] + sign * turned * sine_lookup[:, None, :]


def rms_forward(values, norm_gain):
    inverse = lax.rsqrt(jnp.mean(values * values, axis=-1, keepdims=True) + EPS)
    return (values * inverse * norm_gain, inverse)


def rms_backward(values, inverse, norm_gain, upstream):
    normed = values * inverse
    weighted = upstream * norm_gain
    projected = jnp.mean(weighted * normed, axis=-1, keepdims=True)
    return (inverse * (weighted - normed * projected), jnp.sum(upstream * normed, axis=0))


def slot_tables(routes, visit_order, experts, capacity):
    count_of_tokens, top_count = routes.shape
    ordered = routes[visit_order]
    hit_table = (ordered[:, :, None] == jnp.arange(experts, dtype=jnp.int32)[None, None, :]).astype(
        jnp.int32
    )
    counts = jnp.sum(hit_table, axis=1, dtype=jnp.int32)
    before = jnp.cumsum(counts, axis=0, dtype=jnp.int32) - counts
    slot_rank = jnp.sum(hit_table * before[:, None, :], axis=2, dtype=jnp.int32)
    slot_total = experts * capacity
    flat_ordered = jnp.where(slot_rank < capacity, ordered * capacity + slot_rank, slot_total)
    flat = jnp.zeros((count_of_tokens, top_count), jnp.int32).at[visit_order].set(flat_ordered)
    owners = jnp.repeat(visit_order, top_count)
    token_slot = (
        jnp.full((slot_total + 1,), count_of_tokens, jnp.int32)
        .at[flat_ordered.reshape(-1)]
        .set(owners)[:slot_total]
    )
    return (flat, token_slot)


def attend_forward(allowed, pieces):
    query_row_block, key_row_block, value_row_block = pieces
    scores = (
        jnp.einsum(
            "trd,kd->trk", query_row_block, key_row_block, preferred_element_type=jnp.float32
        )
        * ATT_SCALE
    )
    scores = jnp.where(allowed[:, None, :], scores, NEG)
    highest = jnp.max(scores, axis=-1, keepdims=True)
    lifted = jnp.exp(scores - highest)
    summed = jnp.sum(lifted, axis=-1, keepdims=True)
    weights = (lifted / summed).astype(jnp.bfloat16)
    result = jnp.einsum("trk,kd->trd", weights, value_row_block, preferred_element_type=jnp.float32)
    return (result, highest[..., 0] + jnp.log(summed[..., 0]))


def attend_backward(allowed, pieces):
    query_row_block, key_row_block, value_row_block, d_out, out_rows, log_total = pieces
    scores = (
        jnp.einsum(
            "trd,kd->trk", query_row_block, key_row_block, preferred_element_type=jnp.float32
        )
        * ATT_SCALE
    )
    scores = jnp.where(allowed[:, None, :], scores, NEG)
    weights = jnp.exp(scores - log_total[..., None])
    d_weights = jnp.einsum(
        "trd,kd->trk", d_out, value_row_block, preferred_element_type=jnp.float32
    )
    centre = jnp.sum(d_out.astype(jnp.float32) * out_rows, axis=-1, keepdims=True)
    d_scores = (weights * (d_weights - centre)).astype(jnp.bfloat16)
    d_query = (
        jnp.einsum("trk,kd->trd", d_scores, key_row_block, preferred_element_type=jnp.float32)
        * ATT_SCALE
    )
    d_key = (
        jnp.einsum("trk,trd->kd", d_scores, query_row_block, preferred_element_type=jnp.float32)
        * ATT_SCALE
    )
    d_value = jnp.einsum(
        "trk,trd->kd", weights.astype(jnp.bfloat16), d_out, preferred_element_type=jnp.float32
    )
    return (d_query, d_key, d_value)


def per_device(
    x_prompt,
    x_cont,
    norm1_gain,
    w_query,
    key_weight,
    value_weight,
    w_out,
    norm2_gain,
    w_router,
    w_gate_up,
    w_down,
    routes_prompt,
    routes_cont,
    slot_order,
    dy_prompt,
    dy_cont,
):
    model_width = x_prompt.shape[2]
    prompt_rows = x_prompt.shape[1]
    cont_count = x_cont.shape[1]
    cont_len = x_cont.shape[2]
    cont_rows = cont_count * cont_len
    count_of_tokens = prompt_rows + cont_rows
    queries_per_group = QUERY_HEADS // KEY_VALUE_HEADS
    key_value_width = KEY_VALUE_HEADS * HEAD_SIZE
    local_experts = w_gate_up.shape[0]
    expert_groups = lax.axis_size("expert")
    expert_total = local_experts * expert_groups
    top_count = routes_prompt.shape[2]
    capacity = (count_of_tokens * top_count + expert_total - 1) // expert_total
    hidden_units = w_down.shape[1]
    prompt_total = prompt_rows * lax.axis_size("ctx")
    count_of_keys = prompt_total + cont_rows
    gain_one = norm1_gain.astype(jnp.float32)
    gain_two = norm2_gain.astype(jnp.float32)
    tokens = jnp.concatenate(
        [x_prompt[0], x_cont[0].reshape(cont_rows, model_width)], axis=0
    ).astype(jnp.float32)
    normed_one, scale_one = rms_forward(tokens, gain_one)
    h1_low = normed_one.astype(jnp.bfloat16)
    q_lin = jnp.dot(h1_low, w_query, preferred_element_type=jnp.float32)
    key_linear = jnp.dot(h1_low, key_weight, preferred_element_type=jnp.float32)
    value_linear = jnp.dot(h1_low, value_weight, preferred_element_type=jnp.float32)
    row_index = jnp.arange(count_of_tokens, dtype=jnp.int32)
    in_cont = row_index >= prompt_rows
    cont_offset = row_index - prompt_rows
    ctx_index = lax.axis_index("ctx")
    query_pos = jnp.where(
        in_cont, prompt_total + cont_offset % cont_len, ctx_index * prompt_rows + row_index
    )
    query_cont = jnp.where(in_cont, cont_offset // cont_len, -1)
    cosine_lookup, sine_lookup = rope_tables(query_pos.astype(jnp.float32), HEAD_SIZE)
    query_row_block = apply_rotary(
        q_lin.reshape(count_of_tokens, QUERY_HEADS, HEAD_SIZE), cosine_lookup, sine_lookup, 1.0
    ).astype(jnp.bfloat16)
    key_row_block = (
        apply_rotary(
            key_linear.reshape(count_of_tokens, KEY_VALUE_HEADS, HEAD_SIZE),
            cosine_lookup,
            sine_lookup,
            1.0,
        )
        .astype(jnp.bfloat16)
        .reshape(count_of_tokens, key_value_width)
    )
    value_row_block = value_linear.astype(jnp.bfloat16)
    prompt_kv = lax.all_gather(
        jnp.stack([key_row_block[:prompt_rows], value_row_block[:prompt_rows]]),
        "ctx",
        axis=1,
        tiled=True,
    )
    every_key_row = jnp.concatenate([prompt_kv[0], key_row_block[prompt_rows:]], axis=0)
    every_value_row = jnp.concatenate([prompt_kv[1], value_row_block[prompt_rows:]], axis=0)
    key_index = jnp.arange(count_of_keys, dtype=jnp.int32)
    key_in_cont = key_index >= prompt_total
    key_offset = key_index - prompt_total
    key_pos = jnp.where(key_in_cont, prompt_total + key_offset % cont_len, key_index)
    key_cont = jnp.where(key_in_cont, key_offset // cont_len, -1)
    seen = key_pos[None, :] <= query_pos[:, None]
    allowed = (key_cont[None, :] < 0) & ((query_cont[:, None] >= 0) | seen) | (
        key_cont[None, :] >= 0
    ) & (key_cont[None, :] == query_cont[:, None]) & seen
    grouped_query = query_row_block.reshape(
        count_of_tokens, KEY_VALUE_HEADS, queries_per_group, HEAD_SIZE
    ).transpose(1, 0, 2, 3)
    grouped_key = every_key_row.reshape(count_of_keys, KEY_VALUE_HEADS, HEAD_SIZE).transpose(
        1, 0, 2
    )
    grouped_value = every_value_row.reshape(count_of_keys, KEY_VALUE_HEADS, HEAD_SIZE).transpose(
        1, 0, 2
    )
    attended, log_total = lax.map(
        partial(attend_forward, allowed), (grouped_query, grouped_key, grouped_value)
    )
    merged_low = (
        attended.transpose(1, 0, 2, 3)
        .reshape(count_of_tokens, QUERY_HEADS * HEAD_SIZE)
        .astype(jnp.bfloat16)
    )
    branch = jnp.dot(merged_low, w_out, preferred_element_type=jnp.float32)
    resid = tokens + RESID * branch
    normed_two, scale_two = rms_forward(resid, gain_two)
    h2_low = normed_two.astype(jnp.bfloat16)
    logits = jnp.dot(h2_low, w_router, preferred_element_type=jnp.float32)
    routes = jnp.concatenate(
        [routes_prompt[0], routes_cont[0].reshape(cont_rows, top_count)], axis=0
    )
    hit_table = routes[:, :, None] == jnp.arange(expert_total, dtype=jnp.int32)[None, None, :]
    chosen = jnp.sum(jnp.where(hit_table, logits[:, None, :], 0.0), axis=-1)
    gates = jax.nn.softmax(chosen, axis=-1)
    flat, token_slot = slot_tables(routes, slot_order[0, 0], expert_total, capacity)
    slot_total = expert_total * capacity
    kept = flat < slot_total
    combine = jnp.where(kept, gates, 0.0)
    padded = jnp.concatenate([h2_low, jnp.zeros((1, model_width), jnp.bfloat16)], axis=0)
    outgoing = padded[token_slot].reshape(expert_groups, local_experts, capacity, model_width)
    incoming = lax.all_to_all(outgoing, "expert", split_axis=0, concat_axis=0, tiled=True)
    both = jnp.einsum("slcd,ldf->slcf", incoming, w_gate_up, preferred_element_type=jnp.float32)
    gate_part = both[..., :hidden_units]
    up_part = both[..., hidden_units:]
    hidden = (jax.nn.silu(gate_part) * up_part).astype(jnp.bfloat16)
    expert_out = jnp.einsum(
        "slcf,lfd->slcd", hidden, w_down, preferred_element_type=jnp.float32
    ).astype(jnp.bfloat16)
    returned = lax.all_to_all(
        expert_out, "expert", split_axis=0, concat_axis=0, tiled=True
    ).reshape(slot_total, model_width)
    returned = jnp.concatenate([returned, jnp.zeros((1, model_width), jnp.bfloat16)], axis=0)
    pairs = returned[flat]
    mixed = jnp.einsum("tkd,tk->td", pairs, combine, preferred_element_type=jnp.float32)
    output = resid + RESID * mixed
    y_prompt = output[:prompt_rows].astype(jnp.bfloat16)[None]
    y_cont = output[prompt_rows:].reshape(1, cont_count, cont_len, model_width).astype(jnp.bfloat16)
    upstream = jnp.concatenate(
        [dy_prompt[0], dy_cont[0].reshape(cont_rows, model_width)], axis=0
    ).astype(jnp.float32)
    d_mixed = RESID * upstream
    d_gates = jnp.where(
        kept, jnp.einsum("td,tkd->tk", d_mixed, pairs, preferred_element_type=jnp.float32), 0.0
    )
    d_chosen = gates * (d_gates - jnp.sum(gates * d_gates, axis=-1, keepdims=True))
    d_logits = jnp.sum(jnp.where(hit_table, d_chosen[:, :, None], 0.0), axis=1).astype(jnp.bfloat16)
    grad_router = jnp.einsum("td,te->de", h2_low, d_logits, preferred_element_type=jnp.float32)
    d_normed_two = jnp.einsum("te,de->td", d_logits, w_router, preferred_element_type=jnp.float32)
    slot_weight = (
        jnp.zeros((slot_total + 1,), jnp.float32)
        .at[flat.reshape(-1)]
        .set(combine.reshape(-1))[:slot_total]
    )
    d_padded = jnp.concatenate([d_mixed, jnp.zeros((1, model_width), jnp.float32)], axis=0)
    d_outgoing = (
        (d_padded[token_slot] * slot_weight[:, None])
        .astype(jnp.bfloat16)
        .reshape(expert_groups, local_experts, capacity, model_width)
    )
    d_incoming, expert_in = (
        lax.all_to_all(d_outgoing, "expert", split_axis=0, concat_axis=0, tiled=True),
        lax.all_to_all(outgoing, "expert", split_axis=0, concat_axis=0, tiled=True),
    )
    both_again = jnp.einsum(
        "slcd,ldf->slcf", expert_in, w_gate_up, preferred_element_type=jnp.float32
    )
    gate_again = both_again[..., :hidden_units]
    up_again = both_again[..., hidden_units:]
    hidden_again = (jax.nn.silu(gate_again) * up_again).astype(jnp.bfloat16)
    d_hidden = jnp.einsum("slcd,lfd->slcf", d_incoming, w_down, preferred_element_type=jnp.float32)
    logistic = jax.nn.sigmoid(gate_again)
    d_gate = d_hidden * up_again * logistic * (1.0 + gate_again * (1.0 - logistic))
    d_up = d_hidden * gate_again * logistic
    d_both = jnp.concatenate([d_gate, d_up], axis=-1).astype(jnp.bfloat16)
    grad_down = jnp.einsum(
        "slcf,slcd->lfd", hidden_again, d_incoming, preferred_element_type=jnp.float32
    )
    grad_gate_up = jnp.einsum(
        "slcd,slcf->ldf", expert_in, d_both, preferred_element_type=jnp.float32
    )
    d_slots = jnp.einsum(
        "slcf,ldf->slcd", d_both, w_gate_up, preferred_element_type=jnp.float32
    ).astype(jnp.bfloat16)
    d_returned = lax.all_to_all(d_slots, "expert", split_axis=0, concat_axis=0, tiled=True).reshape(
        slot_total, model_width
    )
    d_returned = jnp.concatenate([d_returned, jnp.zeros((1, model_width), jnp.bfloat16)], axis=0)
    d_normed_two = d_normed_two + jnp.sum(d_returned[flat].astype(jnp.float32), axis=1)
    d_resid_norm, grad_norm2 = rms_backward(resid, scale_two, gain_two, d_normed_two)
    d_resid = upstream + d_resid_norm
    d_branch = (RESID * d_resid).astype(jnp.bfloat16)
    grad_out = jnp.einsum("tq,td->qd", merged_low, d_branch, preferred_element_type=jnp.float32)
    merged_gradient = jnp.einsum(
        "td,qd->tq", d_branch, w_out, preferred_element_type=jnp.float32
    ).astype(jnp.bfloat16)
    grouped_output_gradient = merged_gradient.reshape(
        count_of_tokens, KEY_VALUE_HEADS, queries_per_group, HEAD_SIZE
    ).transpose(1, 0, 2, 3)
    d_q, d_k, d_v = lax.map(
        partial(attend_backward, allowed),
        (grouped_query, grouped_key, grouped_value, grouped_output_gradient, attended, log_total),
    )
    d_query = d_q.transpose(1, 0, 2, 3).reshape(count_of_tokens, QUERY_HEADS, HEAD_SIZE)
    d_key_all = d_k.transpose(1, 0, 2).reshape(count_of_keys, key_value_width)
    d_value_all = d_v.transpose(1, 0, 2).reshape(count_of_keys, key_value_width)
    summed = lax.psum_scatter(
        jnp.stack([d_key_all[:prompt_total], d_value_all[:prompt_total]]).astype(jnp.bfloat16),
        "ctx",
        scatter_dimension=1,
        tiled=True,
    ).astype(jnp.float32)
    d_key = jnp.concatenate([summed[0], d_key_all[prompt_total:]], axis=0).reshape(
        count_of_tokens, KEY_VALUE_HEADS, HEAD_SIZE
    )
    d_value_low = jnp.concatenate([summed[1], d_value_all[prompt_total:]], axis=0).astype(
        jnp.bfloat16
    )
    d_query_low = (
        apply_rotary(d_query, cosine_lookup, sine_lookup, -1.0)
        .reshape(count_of_tokens, QUERY_HEADS * HEAD_SIZE)
        .astype(jnp.bfloat16)
    )
    d_key_low = (
        apply_rotary(d_key, cosine_lookup, sine_lookup, -1.0)
        .reshape(count_of_tokens, key_value_width)
        .astype(jnp.bfloat16)
    )
    grad_query = jnp.einsum("td,tq->dq", h1_low, d_query_low, preferred_element_type=jnp.float32)
    grad_key = jnp.einsum("td,tq->dq", h1_low, d_key_low, preferred_element_type=jnp.float32)
    grad_value = jnp.einsum("td,tq->dq", h1_low, d_value_low, preferred_element_type=jnp.float32)
    d_normed_one = jnp.einsum("tq,dq->td", d_query_low, w_query, preferred_element_type=jnp.float32)
    d_normed_one = d_normed_one + jnp.einsum(
        "tq,dq->td", d_key_low, key_weight, preferred_element_type=jnp.float32
    )
    d_normed_one = d_normed_one + jnp.einsum(
        "tq,dq->td", d_value_low, value_weight, preferred_element_type=jnp.float32
    )
    d_tokens_norm, grad_norm1 = rms_backward(tokens, scale_one, gain_one, d_normed_one)
    d_tokens = d_resid + d_tokens_norm
    dx_prompt = d_tokens[:prompt_rows][None]
    dx_cont = d_tokens[prompt_rows:].reshape(1, cont_count, cont_len, model_width)
    reduced = (
        lax.psum_scatter(
            grad_norm1.astype(jnp.bfloat16), ("dp", "ctx"), scatter_dimension=0, tiled=True
        ).astype(jnp.float32),
        lax.psum_scatter(
            grad_query.astype(jnp.bfloat16), ("dp", "ctx"), scatter_dimension=0, tiled=True
        ).astype(jnp.float32),
        lax.psum_scatter(
            grad_key.astype(jnp.bfloat16), ("dp", "ctx"), scatter_dimension=0, tiled=True
        ).astype(jnp.float32),
        lax.psum_scatter(
            grad_value.astype(jnp.bfloat16), ("dp", "ctx"), scatter_dimension=0, tiled=True
        ).astype(jnp.float32),
        lax.psum_scatter(
            grad_out.astype(jnp.bfloat16), ("dp", "ctx"), scatter_dimension=0, tiled=True
        ).astype(jnp.float32),
        lax.psum_scatter(
            grad_norm2.astype(jnp.bfloat16), ("dp", "ctx"), scatter_dimension=0, tiled=True
        ).astype(jnp.float32),
        lax.psum_scatter(
            grad_router.astype(jnp.bfloat16), ("dp", "ctx"), scatter_dimension=0, tiled=True
        ).astype(jnp.float32),
        lax.psum_scatter(
            grad_gate_up.astype(jnp.bfloat16), ("dp", "ctx"), scatter_dimension=1, tiled=True
        ).astype(jnp.float32),
        lax.psum_scatter(
            grad_down.astype(jnp.bfloat16), ("dp", "ctx"), scatter_dimension=1, tiled=True
        ).astype(jnp.float32),
    )
    dense = (
        lax.psum(reduced[0].astype(jnp.bfloat16), "expert").astype(jnp.float32),
        lax.psum(reduced[1].astype(jnp.bfloat16), "expert").astype(jnp.float32),
        lax.psum(reduced[2].astype(jnp.bfloat16), "expert").astype(jnp.float32),
        lax.psum(reduced[3].astype(jnp.bfloat16), "expert").astype(jnp.float32),
        lax.psum(reduced[4].astype(jnp.bfloat16), "expert").astype(jnp.float32),
        lax.psum(reduced[5].astype(jnp.bfloat16), "expert").astype(jnp.float32),
        lax.psum(reduced[6].astype(jnp.bfloat16), "expert").astype(jnp.float32),
    )
    return (
        y_prompt,
        y_cont,
        dx_prompt,
        dx_cont,
        dense[0],
        dense[1],
        dense[2],
        dense[3],
        dense[4],
        dense[5],
        dense[6],
        reduced[7],
        reduced[8],
    )


def solution(mesh):
    return jax.shard_map(
        per_device,
        mesh=mesh,
        in_specs=(
            P(("dp", "expert"), "ctx", None),
            P(("dp", "expert"), "ctx", None, None),
            P(),
            P(),
            P(),
            P(),
            P(),
            P(),
            P(),
            P("expert", None, None),
            P("expert", None, None),
            P(("dp", "expert"), "ctx", None),
            P(("dp", "expert"), "ctx", None, None),
            P(("dp", "expert"), "ctx", None),
            P(("dp", "expert"), "ctx", None),
            P(("dp", "expert"), "ctx", None, None),
        ),
        out_specs=(
            P(("dp", "expert"), "ctx", None),
            P(("dp", "expert"), "ctx", None, None),
            P(("dp", "expert"), "ctx", None),
            P(("dp", "expert"), "ctx", None, None),
            P(("dp", "ctx")),
            P(("dp", "ctx"), None),
            P(("dp", "ctx"), None),
            P(("dp", "ctx"), None),
            P(("dp", "ctx"), None),
            P(("dp", "ctx")),
            P(("dp", "ctx"), None),
            P("expert", ("dp", "ctx"), None),
            P("expert", ("dp", "ctx"), None),
        ),
        check_vma=False,
    )
```

profile of v0, /device:TPU:9, one launch (start us, length us, event | category | flops | bytes accessed | tf_op | source)
XLA Modules:
  0.0 2513.2 jit_solution(7363210047782785154)
XLA Ops:
  22.3 16.0 scatter_custom_fusion
  51.1 87.4 %while.28 = (s32[]{:T(128)}, f32[8,512,3,64]{1,3,2,0:T(8,128)}, f32[8,512,3]{1,2,0:T(4,128)}, bf16[8,512,3,64]{1,3,2,0:T(8,128)(2,1)S(1)}, bf16[8,1280,64]{1,2,0...) while((s32[]{:T(128)}, f32[8,512,3,64]{1,3,2,0:T(8,128)}, ...), condition=%wide.region_4.5_spmd.clone, body=%wide.region_1.4_spmd.clone.sunk | while | flops 531495424 | bytes 27202704 | solution.py:207
  150.1 15.1 gather_fusion.1
  165.1 12.6 reshape.402
  177.8 153.8 %all_to_all.21 = bf16[2,20,103,1536]{3,2,1,0:T(8,128)(2,1)} all-to-all(bf16[2,20,103,1536]{3,2,1,0:T(8,128)(2,1)} %reshape.402), channel_id=1, replica_groups=mesh['dp'=4,'ctx'=4,'expert'=2] {'expert'}, dimensions={0} | all-to-all | bytes 25313280 | tf_op jit(solution)/shard_map/all_to_all | solution.py:232
  331.6 32.8 %fusion.95 = f32[2,20,103,1024]{3,2,0,1:T(8,128)} fusion(bf16[20,1536,1024]{2,1,0:T(8,128)(2,1)} %param.29, bf16[2,20,103,1536]{3,2,1,0:T(8,128)(2,1)} %all_to_all.21), kind=kOutput, calls=%fused_computation.111 | convolution fusion | flops 12960399360 | bytes 92446720 | tf_op jit(solution)/shard_map/slcd,ldf->slcf/dot_general | solution.py:233
  371.8 24.0 fusion.86
  395.8 10.7 copy.113
  421.5 27.7 %gather_fusion.3 = f32[4120,1536]{1,0:T(8,128)} fusion(f32[513,1536]{1,0:T(8,128)} %concatenate.95, s32[5120]{0:T(1024)S(1)} %pad_clamp_fusion), kind=kCustom, calls=%fused_computation.3 | custom fusion | bytes 50643040 | tf_op jit(solution)/shard_map/gather | solution.py:267
  449.2 26.6 %gather.21 = f32[2,20,103,1536]{3,2,1,0:T(8,128)} reshape(f32[4120,1536]{1,0:T(8,128)} %gather_fusion.3) | data formatting | bytes 50626560 | tf_op jit(solution)/shard_map/gather | solution.py:267
  481.8 71.2 %all-to-all-done.1 = bf16[2,20,103,1536]{3,2,1,0:T(8,128)(2,1)} async-done(((bf16[2,20,103,1536]{3,2,1,0:T(8,128)(2,1)}), bf16[2,20,103,1536]{3,2,1,0:T(8,128)(2,1)}, u32[]{:S(2)}, u32[]{:S(2)}) %all-to-all-start.1) | async-done | bytes 12656672 | tf_op jit(solution)/shard_map/all_to_all | solution.py:240
  553.0 12.6 reshape.403
  576.2 31.7 %gather_fusion.2 = bf16[4096,1536]{1,0:T(8,128)(2,1)} fusion(bf16[4121,1536]{1,0:T(8,128)(2,1)} %concatenate.93, s32[4096]{0:T(1024)S(1)} %broadcast_clamp_fusion), kind=kCustom, calls=%fused_computation.2 | custom fusion | bytes 25182208 | tf_op jit(solution)/shard_map/gather | solution.py:244
  617.9 15.7 scatter_custom_fusion.2
  643.2 142.3 %all_to_all.22 = bf16[2,20,103,1536]{3,2,1,0:T(8,128)(2,1)} all-to-all(bf16[2,20,103,1536]{3,2,1,0:T(8,128)(2,1)S(1)} %multiply_convert_fusion.1), channel_id=1, replica_groups=mesh['dp'=4,'ctx'=4,'expert'=2] {'expert'}, dimensions={0} | all-to-all | bytes 25313280 | tf_op jit(solution)/shard_map/all_to_all | solution.py:272
  785.5 25.3 %fusion.91 = (bf16[2,20,103,512]{3,2,0,1:T(8,128)(2,1)}, bf16[2,20,103,512]{3,2,0,1:T(8,128)(2,1)}) fusion(f32[2,20,103,1024]{3,2,0,1:T(8,128)} %fusion.95, bf16[20,512,1536]{2,1,0:T(8,128)(2,1)} %param.30, bf16[2,20,103,1536]{3,2,1,0:T(8,128)(2,1)} %all_to_all.22), kind=kOutput, calls=%fused_computation.105 | convolution fusion | flops 6507622400 | bytes 69427200 | tf_op jit(solution)/shard_map/slcd,lfd->slcf/dot_general | solution.py:281
  810.7 33.2 %fusion.83 = bf16[2,20,103,1536]{3,2,0,1:T(8,128)(2,1)} fusion(bf16[20,1536,1024]{2,1,0:T(8,128)(2,1)} %param.29, bf16[2,20,103,512]{3,2,0,1:T(8,128)(2,1)} %get-tuple-element.271, bf16[2,20,103,512]{3,2,0,1:T(8,128)(2,1)} %get-tuple-element.270), kind=kOutput, calls=%fused_computation.98 | convolution fusion | flops 12983603200 | bytes 84008960 | tf_op jit(solution)/shard_map/slcf,ldf->slcd/dot_general | solution.py:292
  870.9 128.3 %all-to-all-done.3 = bf16[2,20,103,1536]{3,2,1,0:T(8,128)(2,1)} async-done(((bf16[2,20,103,1536]{3,2,1,0:T(8,128)(2,1)}), bf16[2,20,103,1536]{3,2,1,0:T(8,128)(2,1)}, u32[]{:S(2)}, u32[]{:S(2)}) %all-to-all-start.3) | async-done | bytes 12656672 | tf_op jit(solution)/shard_map/all_to_all | solution.py:295
  999.2 12.6 reshape.406
  1011.8 10.7 concatenate.97
  1022.5 31.5 %gather_fusion.4 = bf16[4096,1536]{1,0:T(8,128)(2,1)} fusion(bf16[4121,1536]{1,0:T(8,128)(2,1)} %concatenate.97, s32[4096]{0:T(1024)S(1)} %broadcast_clamp_fusion), kind=kCustom, calls=%fused_computation.4 | custom fusion | bytes 25182208 | tf_op jit(solution)/shard_map/gather | solution.py:299
  1080.2 139.8 %while.29 = (s32[]{:T(128)}, f32[8,512,3,64]{1,3,2,0:T(8,128)}, f32[8,1280,64]{1,2,0:T(8,128)}, bf16[8,1280,64]{1,2,0:T(8,128)(2,1)}, bf16[8,512,3,64]{1,3,2,0:T...) while((s32[]{:T(128)}, f32[8,512,3,64]{1,3,2,0:T(8,128)}, ...), condition=%wide.region_22.23_spmd.clone, body=%wide.region_20.22_spmd.clone.sunk | while | flops 1283013120 | bytes 40337588 | solution.py:310
  1225.7 33.6 %reduce-scatter.11.cloned.1.call-done = bf16[2,256,512]{1,2,0:T(8,128)(2,1)} async-done(((bf16[2,1024,512]{1,2,0:T(8,128)(2,1)}), bf16[2,256,512]{1,2,0:T(8,128)(2,1)}) %reduce-scatter.11.cloned.1.call-update) | async-done | bytes 524304 | tf_op jit(solution)/shard_map/reduce_scatter | solution.py:317
  1291.6 31.2 %reduce-scatter.15.cloned.1.call-done = bf16[96,512]{1,0:T(8,128)(2,1)} async-done(((bf16[1536,512]{1,0:T(8,128)(2,1)}), bf16[96,512]{1,0:T(8,128)(2,1)}) %reduce-scatter.15.cloned.1.call-update) | async-done | bytes 98320 | tf_op jit(solution)/shard_map/reduce_scatter | solution.py:360
  1322.9 62.1 %reduce-scatter.17.cloned.1.call-done = bf16[96,512]{1,0:T(8,128)(2,1)} async-done(((bf16[1536,512]{1,0:T(8,128)(2,1)}), bf16[96,512]{1,0:T(8,128)(2,1)}) %reduce-scatter.17.cloned.1.call-update) | async-done | bytes 98320 | tf_op jit(solution)/shard_map/reduce_scatter | solution.py:363
  1385.0 78.8 %reduce-scatter.13.cloned.1.call-done = bf16[96,1536]{1,0:T(8,128)(2,1)} async-done(((bf16[1536,1536]{1,0:T(8,128)(2,1)}), bf16[96,1536]{1,0:T(8,128)(2,1)}) %reduce-scatter.13.cloned.1.call-update) | async-done | bytes 294928 | tf_op jit(solution)/shard_map/reduce_scatter | solution.py:357
  1463.8 78.5 %reduce-scatter.19.cloned.1.call-done = bf16[96,1536]{1,0:T(8,128)(2,1)} async-done(((bf16[1536,1536]{1,0:T(8,128)(2,1)}), bf16[96,1536]{1,0:T(8,128)(2,1)}) %reduce-scatter.19.cloned.1.call-update) | async-done | bytes 294928 | tf_op jit(solution)/shard_map/reduce_scatter | solution.py:366
  1542.4 20.5 bitcast_convert_fusion.1
  1562.9 32.2 %bitcast_convert_fusion = bf16[20,1536,1024]{2,1,0:T(8,128)(2,1)} fusion(bf16[2,20,103,1536]{3,2,1,0:T(8,128)(2,1)} %all_to_all.21, bf16[2,20,103,512]{3,2,0,1:T(8,128)(2,1)} %get-tuple-element.271, bf16[2,20,103,512]{3,2,0,1:T(8,128)(2,1)} %get-tuple-element.270), kind=kOutput, calls=%fused_computation.77 | convolution fusion | flops 13008732160 | bytes 84008960 | tf_op jit(solution)/shard_map/slcd,slcf->ldf/dot_general | solution.py:289
  1614.2 25.0 all-reduce.6
  1659.5 273.7 %reduce-scatter.23.cloned.1.call-done = bf16[20,32,1536]{2,1,0:T(8,128)(2,1)} async-done(((bf16[20,512,1536]{2,1,0:T(8,128)(2,1)}), bf16[20,32,1536]{2,1,0:T(8,128)(2,1)}) %reduce-scatter.23.cloned.1.call-update) | async-done | bytes 1966096 | tf_op jit(solution)/shard_map/reduce_scatter | solution.py:378
  1937.2 562.7 %reduce-scatter.21.cloned.1.call-done = bf16[20,96,1024]{2,1,0:T(8,128)(2,1)} async-done(((bf16[20,1536,1024]{2,1,0:T(8,128)(2,1)}), bf16[20,96,1024]{2,1,0:T(8,128)(2,1)}) %reduce-scatter.21.cloned.1.call-update) | async-done | bytes 3932176 | tf_op jit(solution)/shard_map/reduce_scatter | solution.py:375
  (421 shorter events, 463.6 us)
Async XLA Ops:
  7.2 37.7 %all-gather.2.cloned.1.call-start = ((), (), s32[]{:S(2)}) async-start(), calls=%async_computation.12 | async-start | bytes 2621440 | tf_op jit(solution)/shard_map/all_gather | solution.py:181
  8.1 30.3 %copy-start.67 = (f32[1536]{0:T(1024)}, f32[1536]{0:T(1024)S(1)}, u32[]{:S(2)}) copy-start(f32[1536]{0:T(1024)S(1)} %convert_element_type.175) | copy-start | bytes 18436
  9.8 28.6 %copy-start.71 = (f32[512]{0:T(512)}, f32[512]{0:T(512)S(1)}, u32[]{:S(2)}) copy-start(f32[512]{0:T(512)S(1)} %add_rsqrt_fusion.1) | copy-start | bytes 6148
  10.9 33.1 %copy-start.16 = (f32[512,64]{0,1:T(8,128)}, f32[512,64]{0,1:T(8,128)S(1)}, u32[]{:S(2)}) copy-start(f32[512,64]{0,1:T(8,128)S(1)} %pad_maximum_fusion.9) | copy-start | bytes 393220
  18.1 128.8 %copy-start.59 = (f32[1536]{0:T(1024)}, f32[1536]{0:T(1024)S(1)}, u32[]{:S(2)}) copy-start(f32[1536]{0:T(1024)S(1)} %convert_element_type.184) | copy-start | bytes 18436
  21.8 21.6 copy-start.36
  138.5 8.3 copy-start.53
  138.5 8.3 copy-start.55
  138.5 8.3 copy-start.57
  138.5 8.3 copy-start.63
  371.8 24.1 copy-start.1
  406.6 12.6 copy-start.11
  406.6 12.6 copy-start.13
  406.6 146.5 %all-to-all-start.1 = ((bf16[2,20,103,1536]{3,2,1,0:T(8,128)(2,1)}), bf16[2,20,103,1536]{3,2,1,0:T(8,128)(2,1)}, u32[]{:S(2)}, u32[]{:S(2)}) async-start(bf16[2,20,103,1536]{3,2,1,0:T(8,128)(2,1)} %copy.113), calls=%async_computation.1 | async-start | bytes 25559040 | tf_op jit(solution)/shard_map/all_to_all | solution.py:240
  576.2 31.7 %copy-start.30 = (bf16[512,1536,1]{1,0,2:T(8,128)(2,1)S(1)}, bf16[512,1536,1]{1,0,2:T(8,128)(2,1)}, u32[]{:S(2)}) copy-start(bf16[512,1536,1]{1,0,2:T(8,128)(2,1)} %fusion.131) | copy-start | bytes 4718596
  607.8 9.7 copy-start.62
  854.6 144.6 %all-to-all-start.3 = ((bf16[2,20,103,1536]{3,2,1,0:T(8,128)(2,1)}), bf16[2,20,103,1536]{3,2,1,0:T(8,128)(2,1)}, u32[]{:S(2)}, u32[]{:S(2)}) async-start(bf16[2,20,103,1536]{3,2,1,0:T(8,128)(2,1)} %copy.118), calls=%async_computation.3 | async-start | bytes 25559040 | tf_op jit(solution)/shard_map/all_to_all | solution.py:295
  863.0 396.4 %reduce-scatter.11.cloned.1.call-start = ((), (), s32[]{:S(2)}) async-start(), calls=%async_computation.13 | async-start | bytes 2621440 | tf_op jit(solution)/shard_map/reduce_scatter | solution.py:317
  1054.0 10.7 copy-start.4
  1054.0 10.7 copy-start.44
  1054.0 10.7 copy-start.60
  1054.0 10.7 copy-start.66
  1224.6 36.7 %copy-start.35 = (f32[512,64]{0,1:T(8,128)S(1)}, f32[512,64]{0,1:T(8,128)}, u32[]{:S(2)}) copy-start(f32[512,64]{0,1:T(8,128)} %get-tuple-element.293) | copy-start | bytes 393220
  1224.6 98.3 %reduce-scatter.15.cloned.1.call-start = ((), (), s32[]{:S(2)}) async-start(), calls=%async_computation.15 | async-start | bytes 1671168 | tf_op jit(solution)/shard_map/reduce_scatter | solution.py:360
  1225.7 35.7 %copy-start.17 = (f32[512,64]{0,1:T(8,128)S(1)}, f32[512,64]{0,1:T(8,128)}, u32[]{:S(2)}) copy-start(f32[512,64]{0,1:T(8,128)} %copy-done.16) | copy-start | bytes 393220
  1265.1 119.8 %reduce-scatter.17.cloned.1.call-start = ((), (), s32[]{:S(2)}) async-start(), calls=%async_computation.16 | async-start | bytes 1671168 | tf_op jit(solution)/shard_map/reduce_scatter | solution.py:363
  1269.8 194.0 %reduce-scatter.13.cloned.1.call-start = ((), (), s32[]{:S(2)}) async-start(), calls=%async_computation.14 | async-start | bytes 5013504 | tf_op jit(solution)/shard_map/reduce_scatter | solution.py:357
  1281.3 261.0 %reduce-scatter.19.cloned.1.call-start = ((), (), s32[]{:S(2)}) async-start(), calls=%async_computation.17 | async-start | bytes 5013504 | tf_op jit(solution)/shard_map/reduce_scatter | solution.py:366
  1288.9 312.8 %reduce-scatter.25.cloned.1.call-start = ((), (), s32[]{:S(2)}) async-start(), calls=%async_computation.20 | async-start | bytes 417792
  1291.6 360.9 %all-reduce.11.cloned.1.call-start = ((), (), s32[]{:S(2)}) async-start(), calls=%async_computation.21 | async-start | bytes 1572864 | tf_op jit(solution)/shard_map/psum | solution.py:384
  1542.3 390.9 %reduce-scatter.23.cloned.1.call-start = ((), (), s32[]{:S(2)}) async-start(), calls=%async_computation.19 | async-start | bytes 33423360 | tf_op jit(solution)/shard_map/reduce_scatter | solution.py:378
  1562.9 937.0 %reduce-scatter.21.cloned.1.call-start = ((), (), s32[]{:S(2)}) async-start(), calls=%async_computation.18 | async-start | bytes 66846720 | tf_op jit(solution)/shard_map/reduce_scatter | solution.py:375
  (60 other events, 196.9 us)
Sparse Core Ops, SparseCore 0:
  18.2 24.3 all-gather.1
  1224.7 34.6 reduce-scatter.10
  1265.2 57.5 reduce-scatter.14
  1326.4 58.5 reduce-scatter.16
  1389.2 74.4 reduce-scatter.12
  1467.5 74.7 reduce-scatter.18
  1546.4 55.2 reduce-scatter.24
  1604.1 35.4 all-reduce.10
  1643.7 289.4 reduce-scatter.22
  1937.3 562.5 reduce-scatter.20
where the time goes:
time: 2530 us; the launch traced here: 2510 us
  waiting for transfers between devices  1320 us (52%)
  matrix products  403 us (16%)
  blocking collectives  327 us (13%)
  local copies, waits for them, and re-layouts  294 us (12%)
  other arithmetic  130 us (5%)
    reduce_scatter x1, waiting for transfers between devices, per_device(): lax.psum_scatter(grad_gate_up.astype(jnp.bfloat16), ('dp', 'ctx'), scatte...  563 us
    reduce_scatter x1, waiting for transfers between devices, per_device(): lax.psum_scatter(grad_down.astype(jnp.bfloat16), ('dp', 'ctx'), scatter_d...  274 us
    all_to_all x1, blocking collectives, per_device(): lax.all_to_all(outgoing, 'expert', split_axis=0, concat_axis=0, tiled=True)  154 us
    all_to_all x1, blocking collectives, per_device(): lax.all_to_all(d_outgoing, 'expert', split_axis=0, concat_axis=0, tiled=T...  142 us
    all_to_all x1, waiting for transfers between devices, per_device(): lax.all_to_all(d_slots, 'expert', split_axis=0, concat_axis=0, tiled=True)  128 us
    reduce_scatter x1, waiting for transfers between devices, per_device(): lax.psum_scatter(grad_query.astype(jnp.bfloat16), ('dp', 'ctx'), scatter_...  78.8 us
    reduce_scatter x1, waiting for transfers between devices, per_device(): lax.psum_scatter(grad_out.astype(jnp.bfloat16), ('dp', 'ctx'), scatter_di...  78.5 us
    all_to_all x1, waiting for transfers between devices, per_device(): lax.all_to_all(expert_out, 'expert', split_axis=0, concat_axis=0, tiled=T...  71.2 us
  transfers between devices with their start and end apart: 12, of which 10 were waited for; matrix products, arithmetic and copies ran while one was open for 8% of the time, Pallas kernels for 0%

commit v1 on v0

--- a/solution.py
+++ b/solution.py
@@ -3,6 +3,8 @@
 import jax
 import jax.numpy as jnp
 from jax import lax
+from jax.experimental import pallas as pl
+from jax.experimental.pallas import tpu as pltpu
 from jax.sharding import PartitionSpec as P
 
 QUERY_HEADS = 24
@@ -44,25 +46,85 @@
     return (inverse * (weighted - normed * projected), jnp.sum(upstream * normed, axis=0))
 
 
-def slot_tables(routes, visit_order, experts, capacity):
-    count_of_tokens, top_count = routes.shape
-    ordered = routes[visit_order]
-    hit_table = (ordered[:, :, None] == jnp.arange(experts, dtype=jnp.int32)[None, None, :]).astype(
-        jnp.int32
-    )
-    counts = jnp.sum(hit_table, axis=1, dtype=jnp.int32)
-    before = jnp.cumsum(counts, axis=0, dtype=jnp.int32) - counts
-    slot_rank = jnp.sum(hit_table * before[:, None, :], axis=2, dtype=jnp.int32)
-    slot_total = experts * capacity
-    flat_ordered = jnp.where(slot_rank < capacity, ordered * capacity + slot_rank, slot_total)
-    flat = jnp.zeros((count_of_tokens, top_count), jnp.int32).at[visit_order].set(flat_ordered)
-    owners = jnp.repeat(visit_order, top_count)
-    token_slot = (
-        jnp.full((slot_total + 1,), count_of_tokens, jnp.int32)
-        .at[flat_ordered.reshape(-1)]
-        .set(owners)[:slot_total]
-    )
-    return (flat, token_slot)
+def slot_codes(routes, visit_order, experts, capacity):
+    count = routes.shape[0]
+    ids = jnp.arange(count, dtype=jnp.int32)
+    visit = jnp.arange(count, dtype=jnp.float32)
+    place = (visit_order[:, None] == ids[None, :]).astype(jnp.float32)
+    place_row = jnp.sum(place * visit[:, None], axis=0)
+    place_col = jnp.sum((visit_order[None, :] == ids[:, None]).astype(jnp.float32) * visit[None, :], axis=1)
+    earlier = (place_col[:, None] < place_row[None, :]).astype(jnp.bfloat16)
+    named = jnp.any(
+        routes.T[None, :, :] == jnp.arange(experts, dtype=jnp.int32)[:, None, None], axis=1
+    )
+    rank = jnp.dot(named.astype(jnp.bfloat16), earlier, preferred_element_type=jnp.float32)
+    return jnp.where(named, jnp.where(rank < capacity, rank, -1.0), -2.0)
+
+
+def selection(codes, own, slots):
+    tokens = codes.shape[-1]
+    slot_index = lax.broadcasted_iota(jnp.int32, (slots, tokens), 0).astype(jnp.float32)
+    picks = [
+        jnp.where(codes[e : e + 1, :] == slot_index, 1.0, 0.0).astype(jnp.bfloat16)
+        for e in range(own)
+    ]
+    return jnp.concatenate(picks, axis=0)
+
+
+def dispatch_body(own, slots, codes_ref, rows_ref, out_ref):
+    pick = selection(codes_ref[0], own, slots)
+    moved = jnp.dot(pick, rows_ref[0], preferred_element_type=jnp.float32).astype(jnp.bfloat16)
+    for e in range(own):
+        out_ref[e] = moved[e * slots : (e + 1) * slots]
+
+
+def dispatch(codes, rows, own, slots):
+    blocks, tokens, width = rows.shape
+    return pl.pallas_call(
+        partial(dispatch_body, own, slots),
+        grid=(blocks,),
+        in_specs=[
+            pl.BlockSpec((1, codes.shape[1], tokens), lambda b: (b, 0, 0)),
+            pl.BlockSpec((1, tokens, width), lambda b: (b, 0, 0)),
+        ],
+        out_specs=pl.BlockSpec((own, slots, width), lambda b: (0, b, 0)),
+        out_shape=jax.ShapeDtypeStruct((own, blocks * slots, width), jnp.bfloat16),
+        cost_estimate=pl.CostEstimate(
+            flops=2 * blocks * own * slots * tokens * width,
+            transcendentals=0,
+            bytes_accessed=2 * blocks * (tokens + own * slots) * width,
+        ),
+        name="dispatch",
+    )(codes, rows)
+
+
+def combine_body(own, slots, codes_ref, rows_ref, out_ref):
+    pick = selection(codes_ref[0], own, slots)
+    rows = rows_ref[...].reshape(own * slots, rows_ref.shape[-1])
+    out_ref[0] = lax.dot_general(
+        pick, rows, (((0,), (0,)), ((), ())), preferred_element_type=jnp.float32
+    ).astype(out_ref.dtype)
+
+
+def combine(codes, rows, own, slots):
+    blocks, tokens = codes.shape[0], codes.shape[2]
+    width = rows.shape[-1]
+    return pl.pallas_call(
+        partial(combine_body, own, slots),
+        grid=(blocks,),
+        in_specs=[
+            pl.BlockSpec((1, codes.shape[1], tokens), lambda b: (b, 0, 0)),
+            pl.BlockSpec((own, slots, width), lambda b: (0, b, 0)),
+        ],
+        out_specs=pl.BlockSpec((1, tokens, width), lambda b: (b, 0, 0)),
+        out_shape=jax.ShapeDtypeStruct((blocks, tokens, width), jnp.bfloat16),
+        cost_estimate=pl.CostEstimate(
+            flops=2 * blocks * own * slots * tokens * width,
+            transcendentals=0,
+            bytes_accessed=2 * blocks * (tokens + own * slots) * width,
+        ),
+        name="combine",
+    )(codes, rows)
 
 
 def attend_forward(allowed, pieces):
@@ -109,6 +171,15 @@
         "trk,trd->kd", weights.astype(jnp.bfloat16), d_out, preferred_element_type=jnp.float32
     )
     return (d_query, d_key, d_value)
+
+
+def reduce_experts(grad, split):
+    if split == 1:
+        return lax.psum_scatter(
+            grad, ("dp", "ctx"), scatter_dimension=1, tiled=True
+        ).astype(jnp.float32)
+    part = lax.psum_scatter(grad, "dp", scatter_dimension=1, tiled=True)
+    return lax.all_to_all(part, "ctx", split_axis=1, concat_axis=0, tiled=True).astype(jnp.float32)
 
 
 def per_device(
@@ -145,6 +216,32 @@
     hidden_units = w_down.shape[1]
     prompt_total = prompt_rows * lax.axis_size("ctx")
     count_of_keys = prompt_total + cont_rows
+    split = lax.axis_size("ctx") if local_experts % lax.axis_size("ctx") == 0 else 1
+    own = local_experts // split
+    blocks = split * expert_groups
+    slots = -(-capacity // 8) * 8
+    group = ("ctx", "expert") if split > 1 else ("expert",)
+    block_index = lax.axis_index(group)
+    own_offset = lax.axis_index("ctx") * own if split > 1 else 0
+    first_expert = lax.axis_index("expert") * local_experts + own_offset
+    gate_up_own = w_gate_up
+    down_own = w_down
+    if split > 1:
+        gate_up_own = lax.dynamic_slice_in_dim(w_gate_up, own_offset, own, axis=0)
+        down_own = lax.dynamic_slice_in_dim(w_down, own_offset, own, axis=0)
+    routes = jnp.concatenate(
+        [routes_prompt[0], routes_cont[0].reshape(cont_rows, top_count)], axis=0
+    )
+    codes_all = lax.all_gather(
+        slot_codes(routes, slot_order[0, 0], expert_total, capacity), group, axis=0, tiled=False
+    )
+    own_codes = lax.dynamic_slice_in_dim(codes_all, first_expert, own, axis=1)
+    own_codes = jnp.pad(own_codes, ((0, 0), (0, -own % 8), (0, 0)), constant_values=-2.0)
+    upstream_low = jnp.concatenate([dy_prompt[0], dy_cont[0].reshape(cont_rows, model_width)], axis=0)
+    upstream = upstream_low.astype(jnp.float32)
+    upstream_all = lax.all_gather(upstream_low, group, axis=0, tiled=False)
+    d_slot_rows = dispatch(own_codes, upstream_all, own, slots)
+    d_plain = jnp.einsum("ecd,efd->ecf", d_slot_rows, down_own, preferred_element_type=jnp.float32)
     gain_one = norm1_gain.astype(jnp.float32)
     gain_two = norm2_gain.astype(jnp.float32)
     tokens = jnp.concatenate(
@@ -216,87 +313,77 @@
     resid = tokens + RESID * branch
     normed_two, scale_two = rms_forward(resid, gain_two)
     h2_low = normed_two.astype(jnp.bfloat16)
-    logits = jnp.dot(h2_low, w_router, preferred_element_type=jnp.float32)
-    routes = jnp.concatenate(
-        [routes_prompt[0], routes_cont[0].reshape(cont_rows, top_count)], axis=0
-    )
-    hit_table = routes[:, :, None] == jnp.arange(expert_total, dtype=jnp.int32)[None, None, :]
-    chosen = jnp.sum(jnp.where(hit_table, logits[:, None, :], 0.0), axis=-1)
-    gates = jax.nn.softmax(chosen, axis=-1)
-    flat, token_slot = slot_tables(routes, slot_order[0, 0], expert_total, capacity)
-    slot_total = expert_total * capacity
-    kept = flat < slot_total
-    combine = jnp.where(kept, gates, 0.0)
-    padded = jnp.concatenate([h2_low, jnp.zeros((1, model_width), jnp.bfloat16)], axis=0)
-    outgoing = padded[token_slot].reshape(expert_groups, local_experts, capacity, model_width)
-    incoming = lax.all_to_all(outgoing, "expert", split_axis=0, concat_axis=0, tiled=True)
-    both = jnp.einsum("slcd,ldf->slcf", incoming, w_gate_up, preferred_element_type=jnp.float32)
+    rows_all = lax.all_gather(h2_low, group, axis=0, tiled=False)
+    slot_rows = dispatch(own_codes, rows_all, own, slots)
+    logits = jnp.einsum("btd,de->bet", rows_all, w_router, preferred_element_type=jnp.float32)
+    named = codes_all > -1.5
+    logits = jnp.where(named, logits, NEG)
+    lifted = jnp.where(named, jnp.exp(logits - jnp.max(logits, axis=1, keepdims=True)), 0.0)
+    gates_all = lifted / jnp.sum(lifted, axis=1, keepdims=True)
+    own_gates = lax.dynamic_slice_in_dim(gates_all, first_expert, own, axis=1)
+    gates = lax.dynamic_index_in_dim(gates_all, block_index, 0, keepdims=False)
+    slot_index = jnp.arange(slots, dtype=jnp.int32).astype(jnp.float32)
+    picked = own_codes[:, :own, None, :] == slot_index[None, None, :, None]
+    slot_gate = jnp.sum(jnp.where(picked, own_gates[:, :, None, :], 0.0), axis=-1)
+    slot_gate = slot_gate.transpose(1, 0, 2).reshape(own, blocks * slots)
+    both = jnp.einsum("ecd,edf->ecf", slot_rows, gate_up_own, preferred_element_type=jnp.float32)
     gate_part = both[..., :hidden_units]
     up_part = both[..., hidden_units:]
-    hidden = (jax.nn.silu(gate_part) * up_part).astype(jnp.bfloat16)
+    weight = RESID * slot_gate[:, :, None]
+    logistic = jax.nn.sigmoid(gate_part)
+    silu = gate_part * logistic
+    hidden = silu * up_part
+    d_slot_gate = RESID * jnp.sum(hidden * d_plain, axis=-1)
+    weighted = (weight * hidden).astype(jnp.bfloat16)
+    d_hidden = weight * d_plain
+    d_gate = d_hidden * up_part * logistic * (1.0 + gate_part * (1.0 - logistic))
+    d_both = jnp.concatenate([d_gate, d_hidden * silu], axis=-1).astype(jnp.bfloat16)
+    d_slots = jnp.einsum(
+        "ecf,edf->ecd", d_both, gate_up_own, preferred_element_type=jnp.float32
+    ).astype(jnp.bfloat16)
+    d_rows = lax.psum_scatter(combine(own_codes, d_slots, own, slots), group, scatter_dimension=0)
+    d_gates_own = jnp.sum(
+        jnp.where(
+            picked,
+            d_slot_gate.reshape(own, blocks, slots).transpose(1, 0, 2)[..., None],
+            0.0,
+        ),
+        axis=2,
+    )
+    d_gates = lax.psum_scatter(
+        lax.dynamic_update_slice_in_dim(
+            jnp.zeros((blocks, expert_total, count_of_tokens), jnp.float32),
+            d_gates_own,
+            first_expert,
+            axis=1,
+        ),
+        group,
+        scatter_dimension=0,
+    )
+    d_logits = (
+        gates * (d_gates - jnp.sum(gates * d_gates, axis=0, keepdims=True))
+    ).astype(jnp.bfloat16)
+    grad_router = jnp.einsum("td,et->de", h2_low, d_logits, preferred_element_type=jnp.float32)
+    d_normed_two = d_rows.astype(jnp.float32) + jnp.einsum(
+        "et,de->td", d_logits, w_router, preferred_element_type=jnp.float32
+    )
+    grad_down = jnp.einsum(
+        "ecf,ecd->efd", weighted, d_slot_rows, preferred_element_type=jnp.float32
+    ).astype(jnp.bfloat16)
+    grad_gate_up = jnp.einsum(
+        "ecd,ecf->edf", slot_rows, d_both, preferred_element_type=jnp.float32
+    ).astype(jnp.bfloat16)
+    grad_down = reduce_experts(grad_down, split)
+    grad_gate_up = reduce_experts(grad_gate_up, split)
     expert_out = jnp.einsum(
-        "slcf,lfd->slcd", hidden, w_down, preferred_element_type=jnp.float32
-    ).astype(jnp.bfloat16)
-    returned = lax.all_to_all(
-        expert_out, "expert", split_axis=0, concat_axis=0, tiled=True
-    ).reshape(slot_total, model_width)
-    returned = jnp.concatenate([returned, jnp.zeros((1, model_width), jnp.bfloat16)], axis=0)
-    pairs = returned[flat]
-    mixed = jnp.einsum("tkd,tk->td", pairs, combine, preferred_element_type=jnp.float32)
-    output = resid + RESID * mixed
+        "ecf,efd->ecd", weighted, down_own, preferred_element_type=jnp.float32
+    ).astype(jnp.bfloat16)
+    mixed = lax.psum_scatter(
+        combine(own_codes, expert_out, own, slots), group, scatter_dimension=0
+    ).astype(jnp.float32)
+    output = resid + mixed
     y_prompt = output[:prompt_rows].astype(jnp.bfloat16)[None]
     y_cont = output[prompt_rows:].reshape(1, cont_count, cont_len, model_width).astype(jnp.bfloat16)
-    upstream = jnp.concatenate(
-        [dy_prompt[0], dy_cont[0].reshape(cont_rows, model_width)], axis=0
-    ).astype(jnp.float32)
-    d_mixed = RESID * upstream
-    d_gates = jnp.where(
-        kept, jnp.einsum("td,tkd->tk", d_mixed, pairs, preferred_element_type=jnp.float32), 0.0
-    )
-    d_chosen = gates * (d_gates - jnp.sum(gates * d_gates, axis=-1, keepdims=True))
-    d_logits = jnp.sum(jnp.where(hit_table, d_chosen[:, :, None], 0.0), axis=1).astype(jnp.bfloat16)
-    grad_router = jnp.einsum("td,te->de", h2_low, d_logits, preferred_element_type=jnp.float32)
-    d_normed_two = jnp.einsum("te,de->td", d_logits, w_router, preferred_element_type=jnp.float32)
-    slot_weight = (
-        jnp.zeros((slot_total + 1,), jnp.float32)
-        .at[flat.reshape(-1)]
-        .set(combine.reshape(-1))[:slot_total]
-    )
-    d_padded = jnp.concatenate([d_mixed, jnp.zeros((1, model_width), jnp.float32)], axis=0)
-    d_outgoing = (
-        (d_padded[token_slot] * slot_weight[:, None])
-        .astype(jnp.bfloat16)
-        .reshape(expert_groups, local_experts, capacity, model_width)
-    )
-    d_incoming, expert_in = (
-        lax.all_to_all(d_outgoing, "expert", split_axis=0, concat_axis=0, tiled=True),
-        lax.all_to_all(outgoing, "expert", split_axis=0, concat_axis=0, tiled=True),
-    )
-    both_again = jnp.einsum(
-        "slcd,ldf->slcf", expert_in, w_gate_up, preferred_element_type=jnp.float32
-    )
-    gate_again = both_again[..., :hidden_units]
-    up_again = both_again[..., hidden_units:]
-    hidden_again = (jax.nn.silu(gate_again) * up_again).astype(jnp.bfloat16)
-    d_hidden = jnp.einsum("slcd,lfd->slcf", d_incoming, w_down, preferred_element_type=jnp.float32)
-    logistic = jax.nn.sigmoid(gate_again)
-    d_gate = d_hidden * up_again * logistic * (1.0 + gate_again * (1.0 - logistic))
-    d_up = d_hidden * gate_again * logistic
-    d_both = jnp.concatenate([d_gate, d_up], axis=-1).astype(jnp.bfloat16)
-    grad_down = jnp.einsum(
-        "slcf,slcd->lfd", hidden_again, d_incoming, preferred_element_type=jnp.float32
-    )
-    grad_gate_up = jnp.einsum(
-        "slcd,slcf->ldf", expert_in, d_both, preferred_element_type=jnp.float32
-    )
-    d_slots = jnp.einsum(
-        "slcf,ldf->slcd", d_both, w_gate_up, preferred_element_type=jnp.float32
-    ).astype(jnp.bfloat16)
-    d_returned = lax.all_to_all(d_slots, "expert", split_axis=0, concat_axis=0, tiled=True).reshape(
-        slot_total, model_width
-    )
-    d_returned = jnp.concatenate([d_returned, jnp.zeros((1, model_width), jnp.bfloat16)], axis=0)
-    d_normed_two = d_normed_two + jnp.sum(d_returned[flat].astype(jnp.float32), axis=1)
     d_resid_norm, grad_norm2 = rms_backward(resid, scale_two, gain_two, d_normed_two)
     d_resid = upstream + d_resid_norm
     d_branch = (RESID * d_resid).astype(jnp.bfloat16)
@@ -350,58 +437,29 @@
     d_tokens = d_resid + d_tokens_norm
     dx_prompt = d_tokens[:prompt_rows][None]
     dx_cont = d_tokens[prompt_rows:].reshape(1, cont_count, cont_len, model_width)
-    reduced = (
-        lax.psum_scatter(
-            grad_norm1.astype(jnp.bfloat16), ("dp", "ctx"), scatter_dimension=0, tiled=True
-        ).astype(jnp.float32),
-        lax.psum_scatter(
-            grad_query.astype(jnp.bfloat16), ("dp", "ctx"), scatter_dimension=0, tiled=True
-        ).astype(jnp.float32),
-        lax.psum_scatter(
-            grad_key.astype(jnp.bfloat16), ("dp", "ctx"), scatter_dimension=0, tiled=True
-        ).astype(jnp.float32),
-        lax.psum_scatter(
-            grad_value.astype(jnp.bfloat16), ("dp", "ctx"), scatter_dimension=0, tiled=True
-        ).astype(jnp.float32),
-        lax.psum_scatter(
-            grad_out.astype(jnp.bfloat16), ("dp", "ctx"), scatter_dimension=0, tiled=True
-        ).astype(jnp.float32),
-        lax.psum_scatter(
-            grad_norm2.astype(jnp.bfloat16), ("dp", "ctx"), scatter_dimension=0, tiled=True
-        ).astype(jnp.float32),
-        lax.psum_scatter(
-            grad_router.astype(jnp.bfloat16), ("dp", "ctx"), scatter_dimension=0, tiled=True
-        ).astype(jnp.float32),
-        lax.psum_scatter(
-            grad_gate_up.astype(jnp.bfloat16), ("dp", "ctx"), scatter_dimension=1, tiled=True
-        ).astype(jnp.float32),
-        lax.psum_scatter(
-            grad_down.astype(jnp.bfloat16), ("dp", "ctx"), scatter_dimension=1, tiled=True
-        ).astype(jnp.float32),
-    )
-    dense = (
-        lax.psum(reduced[0].astype(jnp.bfloat16), "expert").astype(jnp.float32),
-        lax.psum(reduced[1].astype(jnp.bfloat16), "expert").astype(jnp.float32),
-        lax.psum(reduced[2].astype(jnp.bfloat16), "expert").astype(jnp.float32),
-        lax.psum(reduced[3].astype(jnp.bfloat16), "expert").astype(jnp.float32),
-        lax.psum(reduced[4].astype(jnp.bfloat16), "expert").astype(jnp.float32),
-        lax.psum(reduced[5].astype(jnp.bfloat16), "expert").astype(jnp.float32),
-        lax.psum(reduced[6].astype(jnp.bfloat16), "expert").astype(jnp.float32),
-    )
+    wide = jnp.concatenate([grad_query, grad_key, grad_value, grad_out], axis=1)
+    small = jnp.concatenate([grad_router, grad_norm1[:, None], grad_norm2[:, None]], axis=1)
+    small = jnp.pad(small, ((0, 0), (0, -small.shape[1] % 128)))
+    dense = jnp.concatenate([wide, small], axis=1).astype(jnp.bfloat16)
+    dense = lax.psum_scatter(dense, ("dp", "ctx"), scatter_dimension=0, tiled=True)
+    dense = lax.psum(dense, "expert").astype(jnp.float32)
+    heads_width = QUERY_HEADS * HEAD_SIZE
+    edge = heads_width + 2 * key_value_width
+    tail = edge + w_out.shape[1]
     return (
         y_prompt,
         y_cont,
         dx_prompt,
         dx_cont,
-        dense[0],
-        dense[1],
-        dense[2],
-        dense[3],
-        dense[4],
-        dense[5],
-        dense[6],
-        reduced[7],
-        reduced[8],
+        dense[:, tail + expert_total],
+        dense[:, :heads_width],
+        dense[:, heads_width : heads_width + key_value_width],
+        dense[:, heads_width + key_value_width : edge],
+        dense[:, edge:tail],
+        dense[:, tail + expert_total + 1],
+        dense[:, tail : tail + expert_total],
+        grad_gate_up,
+        grad_down,
     )
 
 

time: 2530 us -> 1370 us (0.54)
  waiting for transfers between devices: 1320 us -> 686 us
  blocking collectives: 327 us -> 22.6 us
  local copies, waits for them, and re-layouts: 294 us -> 91.1 us
  Pallas kernels: 0 us -> 61 us
  matrix products: 403 us -> 355 us
    reduce_scatter x6 -> x5, waiting for transfers between devices: 1090 us -> 482 us  [the longest x2 334 us: reduce_experts(): part = lax.psum_scatter(grad, 'dp', scatter_dimension=1, tiled=True)]
    all_to_all x2 -> x0, blocking collectives: 296 us -> none  [the longest x1 154 us: per_device(): lax.all_to_all(outgoing, 'expert', split_axis=0, concat_axis=0, tiled=True)]
    all_to_all x2, waiting for transfers between devices: 200 us -> 0.01 us  [reduce_experts(): lax.all_to_all(part, 'ctx', split_axis=1, concat_axis=0, tiled=True)]
    gather x7 -> x0, local copies, waits for them, and re-layouts: 134 us -> none  [the longest x2 54.3 us: per_device(): d_padded[token_slot] * slot_weight[:, None]]
    unnamed x11 -> x12, waiting for transfers between devices: 4.73 us -> 133 us
    pallas_call x0 -> x4, Pallas kernels: none -> 61 us  [the longest x2 32.7 us: combine(): pl.pallas_call(partial(combine_body, own, slots), grid=(blocks,), in_spec...]
    dot_general x11 -> x9, matrix products: 188 us -> 131 us  [the longest x1 24.9 us: per_device(): jnp.einsum('ecf,edf->ecd', d_both, gate_up_own, preferred_element_type=jn...]
    reshape x7 -> x0, local copies, waits for them, and re-layouts: 38.9 us -> none  [the longest x1 12.6 us: per_device(): padded[token_slot]]
  transfers between devices with their start and end apart: 12 -> 13, of which waited for: 10 -> 8; matrix products, arithmetic and copies ran while one was open for 8% -> 23% of each run, Pallas kernels for 0% -> 3%
where the time goes in v1:
time: 1370 us; the launch traced here: 1360 us
  waiting for transfers between devices  686 us (50%)
  matrix products  355 us (26%)
  other arithmetic  117 us (9%)
  local copies, waits for them, and re-layouts  91.1 us (7%)
  Pallas kernels  61 us (4%)
  blocking collectives  22.6 us (2%)
  between operations  15 us (1%)
    reduce_scatter x2, waiting for transfers between devices, reduce_experts(): part = lax.psum_scatter(grad, 'dp', scatter_dimension=1, tiled=True)  334 us
    unnamed x12, waiting for transfers between devices  133 us
    reduce_scatter x1, waiting for transfers between devices, per_device(): lax.psum_scatter(combine(own_codes, expert_out, own, slots), group, scatt...  90.5 us
    reduce_scatter x1, waiting for transfers between devices, per_device(): lax.psum_scatter(combine(own_codes, d_slots, own, slots), group, scatter_...  57.4 us
    unnamed x124, local copies, waits for them, and re-layouts  38.3 us
    all_gather x1, waiting for transfers between devices, per_device(): rows_all = lax.all_gather(h2_low, group, axis=0, tiled=False)  36.5 us
    dot_general x8, matrix products, attend_forward(): jnp.einsum('trk,kd->trd', weights, value_row_block, preferred_element_typ...  33.4 us
    pallas_call x2, Pallas kernels, combine(): pl.pallas_call(partial(combine_body, own, slots), grid=(blocks,), in_spec...  32.7 us
  transfers between devices with their start and end apart: 13, of which 8 were waited for; matrix products, arithmetic and copies ran while one was open for 23% of the time, Pallas kernels for 3%

profile of v1, /device:TPU:9, one launch (start us, length us, event | category | flops | bytes accessed | tf_op | source)
XLA Modules:
  0.0 1360.8 jit_solution(3068759652363653597)
XLA Ops:
  23.2 5.2 fusion.169
  35.9 10.1 all-gather.7.cloned.1.call-done
  52.1 87.3 %while.28 = (s32[]{:T(128)}, f32[8,512,3,64]{1,3,2,0:T(8,128)}, f32[8,512,3]{1,2,0:T(4,128)}, bf16[8,512,3,64]{1,3,2,0:T(8,128)(2,1)S(1)}, bf16[8,1280,64]{1,2,0...) while((s32[]{:T(128)}, f32[8,512,3,64]{1,3,2,0:T(8,128)}, ...), condition=%wide.region_4.5_spmd.clone, body=%wide.region_1.4_spmd.clone.sunk | while | flops 531495424 | bytes 27203204 | solution.py:304
  142.3 5.3 multiply_reduce_fusion.3
  152.0 22.6 %all-gather = f32[320,512]{1,0:T(8,128)S(1)} all-gather(f32[40,512]{1,0:T(8,128)S(1)} %fusion.122), channel_id=2, replica_groups=mesh['dp'=4,'ctx'=4,'expert'=2] {'ctx','expert'}, dimensions={0}, use_global_device_ids=true | all-gather | bytes 737280 | tf_op jit(solution)/shard_map/all_gather | solution.py:235
  176.0 14.1 %dispatch.3 = bf16[5,832,1536]{2,1,0:T(8,128)(2,1)} custom-call(f32[8,8,512]{2,1,0:T(8,128)} %pad.9.codes_ref, bf16[8,512,1536]{2,1,0:T(8,128)(2,1)} %bitcast.263), custom_call_target="tpu_custom_call" | custom-call | flops 6543114240 | bytes 25362432 | tf_op jit(solution)/shard_map/dispatch/pallas_call | solution.py:83
  190.1 36.5 %all-gather.9.cloned.1.call-done = bf16[4096,1536]{1,0:T(8,128)(2,1)} async-done(((bf16[512,1536]{1,0:T(8,128)(2,1)}), bf16[4096,1536]{1,0:T(8,128)(2,1)}) %all-gather.9.cloned.1.call-update) | async-done | bytes 12582928 | tf_op jit(solution)/shard_map/all_gather | solution.py:316
  226.6 14.1 %dispatch.2 = bf16[5,832,1536]{2,1,0:T(8,128)(2,1)} custom-call(f32[8,8,512]{2,1,0:T(8,128)} %pad.9.codes_ref, bf16[8,512,1536]{2,1,0:T(8,128)(2,1)} %bitcast.260), custom_call_target="tpu_custom_call" | custom-call | flops 6543114240 | bytes 25362432 | tf_op jit(solution)/shard_map/dispatch/pallas_call | solution.py:83
  240.7 23.1 %fusion.65 = f32[5,832,1024]{2,1,0:T(8,128)} fusion(bf16[5,832,1536]{2,1,0:T(8,128)(2,1)} %dispatch.2, bf16[20,1536,1024]{2,1,0:T(8,128)(2,1)} %param.29, s32[]{:T(128)S(6)} %select_n.157), kind=kOutput, calls=%fused_computation.72 | convolution fusion | flops 13086228480 | bytes 45547524 | tf_op jit(solution)/shard_map/ecd,edf->ecf/dot_general | solution.py:329
  263.8 22.3 %multiply_reduce_fusion = (f32[5,832]{1,0:T(8,128)S(1)}, f32[5,832,512]{2,1,0:T(8,128)}) fusion(f32[5,832,1024]{2,1,0:T(8,128)} %fusion.65, bf16[5,832,1536]{2,1,0:T(8,128)(2,1)} %dispatch.3, bf16[20,512,1536]{2,1,0:T(8,128)(2,1)} %param.30, s32[]{:T(128)S(6)} %select_n.157), kind=kOutput, calls=%fused_computation.83 | convolution fusion | flops 6558019584 | bytes 46219524 | tf_op jit(solution)/shard_map/ecd,efd->ecf/dot_general | solution.py:244
  286.8 9.0 fusion.176
  301.6 15.8 %multiply_convert_fusion.2 = (bf16[5,832,512]{2,1,0:T(8,128)(2,1)}, bf16[5,832,512]{2,1,0:T(8,128)(2,1)}, bf16[5,832,512]{2,1,0:T(8,128)(2,1)}) fusion(f32[5,832,1024]{2,1,0:T(8,128)} %fusion.65, f32[5,832,512]{2,1,0:T(8,128)} %get-tuple-element.365, f32[5,832]{1,0:T(8,128)S(1)} %mul.355), kind=kLoop, calls=%fused_computation.85 | loop fusion | flops 36208640 | bytes 38355200 | tf_op jit(solution)/shard_map/convert.32
  317.4 24.9 %fusion.67.rows_ref = bf16[5,832,1536]{2,1,0:T(8,128)(2,1)} fusion(bf16[20,1536,1024]{2,1,0:T(8,128)(2,1)} %param.29, s32[]{:T(128)S(6)} %select_n.157, bf16[5,832,512]{2,1,0:T(8,128)(2,1)} %get-tuple-element.329, bf16[5,832,512]{2,1,0:T(8,128)(2,1)} %get-tuple-element.328), kind=kOutput, calls=%fused_computation.77 | convolution fusion | flops 13109657600 | bytes 37027844 | tf_op jit(solution)/shard_map/ecf,edf->ecd/dot_general | solution.py:341
  342.4 16.1 %combine.3 = bf16[8,512,1536]{2,1,0:T(8,128)(2,1)} custom-call(f32[8,8,512]{2,1,0:T(8,128)} %pad.9.codes_ref, bf16[5,832,1536]{2,1,0:T(8,128)(2,1)} %fusion.67.rows_ref), custom_call_target="tpu_custom_call" | custom-call | flops 6543114240 | bytes 25362432 | tf_op jit(solution)/shard_map/combine/pallas_call | solution.py:112
  358.5 14.9 %convolution_convert_fusion.1.rows_ref = bf16[5,832,1536]{2,1,0:T(8,128)(2,1)} fusion(bf16[5,832,512]{2,1,0:T(8,128)(2,1)} %get-tuple-element.330, bf16[20,512,1536]{2,1,0:T(8,128)(2,1)} %param.30, s32[]{:T(128)S(6)} %select_n.157), kind=kOutput, calls=%fused_computation.76 | convolution fusion | flops 6549504000 | bytes 24903684 | tf_op jit(solution)/shard_map/ecf,efd->ecd/dot_general | solution.py:378
  373.4 16.7 %combine.2 = bf16[8,512,1536]{2,1,0:T(8,128)(2,1)} custom-call(f32[8,8,512]{2,1,0:T(8,128)} %pad.9.codes_ref, bf16[5,832,1536]{2,1,0:T(8,128)(2,1)} %convolution_convert_fusion.1.rows_ref), custom_call_target="tpu_custom_call" | custom-call | flops 6543114240 | bytes 25362432 | tf_op jit(solution)/shard_map/combine/pallas_call | solution.py:112
  392.8 57.4 %reduce-scatter.12.cloned.1.call-done = bf16[1,512,1536]{2,1,0:T(8,128)(2,1)} async-done(((bf16[8,512,1536]{2,1,0:T(8,128)(2,1)}), bf16[1,512,1536]{2,1,0:T(8,128)(2,1)}) %reduce-scatter.12.cloned.1.call-update) | async-done | bytes 1572880 | tf_op jit(solution)/shard_map/reduce_scatter | solution.py:344
  455.4 90.5 %reduce-scatter.10.cloned.1.call-done = bf16[1,512,1536]{2,1,0:T(8,128)(2,1)} async-done(((bf16[8,512,1536]{2,1,0:T(8,128)(2,1)}), bf16[1,512,1536]{2,1,0:T(8,128)(2,1)}) %reduce-scatter.10.cloned.1.call-update) | async-done | bytes 1572880 | tf_op jit(solution)/shard_map/reduce_scatter | solution.py:381
  545.9 5.4 multiply_add_fusion
  553.0 6.1 convolution_convert_fusion.7
  562.9 139.6 %while.29 = (s32[]{:T(128)}, f32[8,512,3,64]{1,3,2,0:T(8,128)}, f32[8,1280,64]{1,2,0:T(8,128)}, bf16[8,1280,64]{1,2,0:T(8,128)(2,1)}, bf16[8,512,3,64]{1,3,2,0:T...) while((s32[]{:T(128)}, f32[8,512,3,64]{1,3,2,0:T(8,128)}, ...), condition=%wide.region_21.22_spmd.clone, body=%wide.region_19.21_spmd.clone.sunk | while | flops 1283013120 | bytes 40337580 | solution.py:397
  707.6 15.8 %convolution_convert_fusion.4 = bf16[5,512,1536]{2,1,0:T(8,128)(2,1)} fusion(bf16[5,832,512]{2,1,0:T(8,128)(2,1)} %get-tuple-element.330, bf16[5,832,1536]{2,1,0:T(8,128)(2,1)} %dispatch.3), kind=kOutput, calls=%fused_computation.98 | convolution fusion | flops 6547046400 | bytes 24903680 | tf_op jit(solution)/shard_map/ecf,ecd->efd/dot_general | solution.py:370
  723.4 24.3 %convolution_convert_fusion = bf16[5,1536,1024]{2,1,0:T(8,128)(2,1)} fusion(bf16[5,832,1536]{2,1,0:T(8,128)(2,1)} %dispatch.2, bf16[5,832,512]{2,1,0:T(8,128)(2,1)} %get-tuple-element.329, bf16[5,832,512]{2,1,0:T(8,128)(2,1)} %get-tuple-element.328), kind=kOutput, calls=%fused_computation.74 | convolution fusion | flops 13111132160 | bytes 37027840 | tf_op jit(solution)/shard_map/ecd,ecf->edf/dot_general | solution.py:373
  783.2 16.6 %copy.87 = bf16[1536,4224]{1,0:T(8,128)(2,1)} copy(bf16[1536,4224]{0,1:T(8,128)(2,1)} %fusion.119) | data formatting | bytes 25952256
  799.7 78.0 %reduce-scatter.20.cloned.1.call-done = bf16[5,128,1536]{2,1,0:T(8,128)(2,1)} async-done(((bf16[5,512,1536]{2,1,0:T(8,128)(2,1)}), bf16[5,128,1536]{2,1,0:T(8,128)(2,1)}) %reduce-scatter.20.cloned.1.call-update) | async-done | bytes 1966096 | tf_op jit(solution)/shard_map/reduce_scatter | solution.py:181
  882.1 5.4 all-to-all-start.1
  887.5 255.8 %reduce-scatter.18.cloned.1.call-done = bf16[5,384,1024]{2,1,0:T(8,128)(2,1)} async-done(((bf16[5,1536,1024]{2,1,0:T(8,128)(2,1)}), bf16[5,384,1024]{2,1,0:T(8,128)(2,1)}) %reduce-scatter.18.cloned.1.call-update) | async-done | bytes 3932176 | tf_op jit(solution)/shard_map/reduce_scatter | solution.py:181
  1143.3 7.3 copy.78
  1150.6 6.0 all-to-all-start
  1169.5 132.4 %reduce-scatter.22.cloned.1.call-done = bf16[96,4224]{1,0:T(8,128)(2,1)} async-done(((bf16[1536,4224]{1,0:T(8,128)(2,1)}), bf16[96,4224]{1,0:T(8,128)(2,1)}) %reduce-scatter.22.cloned.1.call-update) | async-done | bytes 811024
  1312.8 7.8 copy.79
  1320.6 24.9 %all-reduce.4.cloned.1.call-done = bf16[96,4224]{0,1:T(8,128)(2,1)} async-done(((bf16[96,4224]{0,1:T(8,128)(2,1)}), bf16[96,4224]{0,1:T(8,128)(2,1)}) %all-reduce.4.cloned.1.call-update) | async-done | bytes 811024 | tf_op jit(solution)/shard_map/psum | solution.py:445
  (347 shorter events, 361.2 us)
Async XLA Ops:
  7.2 10.1 copy-start
  7.2 38.7 %all-gather.7.cloned.1.call-start = ((), (), s32[]{:S(2)}) async-start(), calls=%async_computation.9 | async-start | bytes 2621440 | tf_op jit(solution)/shard_map/all_gather | solution.py:278
  9.1 14.0 %copy-start.51 = (f32[512]{0:T(512)}, f32[512]{0:T(512)S(1)}, u32[]{:S(2)}) copy-start(f32[512]{0:T(512)S(1)} %add_rsqrt_fusion.1) | copy-start | bytes 6148
  9.8 13.3 copy-start.49
  15.0 17.1 %copy-start.11 = (f32[512,64]{0,1:T(8,128)}, f32[512,64]{0,1:T(8,128)S(1)}, u32[]{:S(2)}) copy-start(f32[512,64]{0,1:T(8,128)S(1)} %get-tuple-element.372) | copy-start | bytes 393220
  21.4 154.6 %all-gather.11.cloned.1.call-start = ((), (), s32[]{:S(2)}) async-start(), calls=%async_computation.18 | async-start | bytes 14155776 | tf_op jit(solution)/shard_map/all_gather | solution.py:242
  22.7 203.9 %all-gather.9.cloned.1.call-start = ((), (), s32[]{:S(2)}) async-start(), calls=%async_computation.17 | async-start | bytes 14155776 | tf_op jit(solution)/shard_map/all_gather | solution.py:316
  35.9 11.8 copy-start.31
  139.4 8.2 copy-start.9
  139.4 8.2 copy-start.33
  139.4 8.3 copy-start.35
  139.4 8.3 copy-start.39
  139.4 8.3 copy-start.41
  139.4 8.3 copy-start.43
  139.4 8.3 copy-start.45
  139.5 8.3 copy-start.47
  142.2 5.6 copy-start.27
  150.9 239.5 %reduce-scatter.14.cloned.1.call-start = ((), (), s32[]{:S(2)}) async-start(), calls=%async_computation.12 | async-start | bytes 737280 | tf_op jit(solution)/shard_map/reduce_scatter | solution.py:353
  263.8 23.0 %copy-start.37 = (bf16[1536,40]{0,1:T(8,128)(2,1)S(1)}, bf16[1536,40]{0,1:T(8,128)(2,1)}, u32[]{:S(2)}) copy-start(bf16[1536,40]{0,1:T(8,128)(2,1)} %param.28) | copy-start | bytes 368644
  301.4 148.9 %reduce-scatter.12.cloned.1.call-start = ((), (), s32[]{:S(2)}) async-start(), calls=%async_computation.11 | async-start | bytes 14155776 | tf_op jit(solution)/shard_map/reduce_scatter | solution.py:344
  358.5 187.5 %reduce-scatter.10.cloned.1.call-start = ((), (), s32[]{:S(2)}) async-start(), calls=%async_computation.10 | async-start | bytes 14155776 | tf_op jit(solution)/shard_map/reduce_scatter | solution.py:381
  390.1 374.7 %reduce-scatter.16.cloned.1.call-start = ((), (), s32[]{:S(2)}) async-start(), calls=%async_computation.13 | async-start | bytes 2621440 | tf_op jit(solution)/shard_map/reduce_scatter | solution.py:404
  392.8 153.1 %copy-start.14 = (bf16[1,1,256,1536]{3,2,1,0:T(8,128)(2,1)S(1)}, bf16[1,1,256,1536]{3,2,1,0:T(8,128)(2,1)}, u32[]{:S(2)}) copy-start(bf16[1,1,256,1536]{3,2,1,0:T(8,128)(2,1)} %param.35) | copy-start | bytes 2359300
  392.8 153.1 %copy-start.16 = (bf16[1,256,1536]{2,1,0:T(8,128)(2,1)S(1)}, bf16[1,256,1536]{2,1,0:T(8,128)(2,1)}, u32[]{:S(2)}) copy-start(bf16[1,256,1536]{2,1,0:T(8,128)(2,1)} %param.34) | copy-start | bytes 2359300
  707.1 170.6 %reduce-scatter.20.cloned.1.call-start = ((), (), s32[]{:S(2)}) async-start(), calls=%async_computation.16 | async-start | bytes 9830400 | tf_op jit(solution)/shard_map/reduce_scatter | solution.py:181
  723.4 419.9 %reduce-scatter.18.cloned.1.call-start = ((), (), s32[]{:S(2)}) async-start(), calls=%async_computation.15 | async-start | bytes 19660800 | tf_op jit(solution)/shard_map/reduce_scatter | solution.py:181
  747.8 554.1 %reduce-scatter.22.cloned.1.call-start = ((), (), s32[]{:S(2)}) async-start(), calls=%async_computation.19 | async-start | bytes 13787136
  754.3 6.2 slice-start
  882.1 268.5 %all-to-all-start.1 = ((bf16[5,128,1536]{2,0,1:T(8,128)(2,1)}), bf16[5,128,1536]{2,0,1:T(8,128)(2,1)}, u32[]{:S(2)}, u32[]{:S(2)}) async-start(bf16[5,128,1536]{2,0,1:T(8,128)(2,1)} %copy.80), calls=%async_computation.7 | async-start | bytes 6291456 | tf_op jit(solution)/shard_map/all_to_all | solution.py:182
  1150.6 157.7 %all-to-all-start = ((bf16[5,384,1024]{2,0,1:T(8,128)(2,1)}), bf16[5,384,1024]{2,0,1:T(8,128)(2,1)}, u32[]{:S(2)}, u32[]{:S(2)}) async-start(bf16[5,384,1024]{2,0,1:T(8,128)(2,1)} %copy.78), calls=%async_computation.5 | async-start | bytes 12582912 | tf_op jit(solution)/shard_map/all_to_all | solution.py:182
  1156.5 189.0 %all-reduce.4.cloned.1.call-start = ((), (), s32[]{:S(2)}) async-start(), calls=%async_computation.14 | async-start | bytes 2162688 | tf_op jit(solution)/shard_map/psum | solution.py:445
  1159.8 5.6 copy-start.22
  (40 other events, 95.6 us)
Sparse Core Ops, SparseCore 0:
  21.5 24.3 all-gather.6
  47.8 71.9 all-gather.10
  151.0 75.5 all-gather.8
  301.5 33.5 reduce-scatter.13
  358.6 91.6 reduce-scatter.11
  453.6 92.2 reduce-scatter.9
  707.2 31.1 reduce-scatter.15
  741.3 136.3 reduce-scatter.19
  880.1 263.1 reduce-scatter.17
  1147.2 154.6 reduce-scatter.21
  1304.6 40.8 all-reduce.3

commit v2 on v1

--- a/solution.py
+++ b/solution.py
@@ -28,10 +28,12 @@
     return (cosine_lookup, sine_lookup)
 
 
-def apply_rotary(values, cosine_lookup, sine_lookup, sign):
-    half_dim = values.shape[-1] // 2
-    turned = jnp.concatenate([-values[..., half_dim:], values[..., :half_dim]], axis=-1)
-    return values * cosine_lookup[:, None, :] + sign * turned * sine_lookup[:, None, :]
+def signed_tables(positions, width):
+    cosine_lookup, sine_lookup = rope_tables(positions, HEAD_SIZE)
+    half_dim = HEAD_SIZE // 2
+    sine_lookup = jnp.concatenate([-sine_lookup[:, :half_dim], sine_lookup[:, half_dim:]], axis=-1)
+    copies = width // HEAD_SIZE
+    return (jnp.tile(cosine_lookup, (1, copies)), jnp.tile(sine_lookup, (1, copies)))
 
 
 def rms_forward(values, norm_gain):
@@ -98,7 +100,7 @@
     )(codes, rows)
 
 
-def combine_body(own, slots, codes_ref, rows_ref, out_ref):
+def combine_body(own, slots, at_ref, codes_ref, rows_ref, out_ref):
     pick = selection(codes_ref[0], own, slots)
     rows = rows_ref[...].reshape(own * slots, rows_ref.shape[-1])
     out_ref[0] = lax.dot_general(
@@ -106,71 +108,345 @@
     ).astype(out_ref.dtype)
 
 
-def combine(codes, rows, own, slots):
-    blocks, tokens = codes.shape[0], codes.shape[2]
+def combine(at, codes, rows, own, slots):
+    count, tokens = at.shape[0], codes.shape[2]
     width = rows.shape[-1]
     return pl.pallas_call(
         partial(combine_body, own, slots),
-        grid=(blocks,),
-        in_specs=[
-            pl.BlockSpec((1, codes.shape[1], tokens), lambda b: (b, 0, 0)),
-            pl.BlockSpec((own, slots, width), lambda b: (0, b, 0)),
+        grid_spec=pltpu.PrefetchScalarGridSpec(
+            num_scalar_prefetch=1,
+            grid=(count,),
+            in_specs=[
+                pl.BlockSpec((1, codes.shape[1], tokens), lambda b, at: (at[b], 0, 0)),
+                pl.BlockSpec((own, slots, width), lambda b, at: (0, at[b], 0)),
+            ],
+            out_specs=pl.BlockSpec((1, tokens, width), lambda b, at: (b, 0, 0)),
+        ),
+        out_shape=jax.ShapeDtypeStruct((count, tokens, width), jnp.bfloat16),
+        cost_estimate=pl.CostEstimate(
+            flops=2 * count * own * slots * tokens * width,
+            transcendentals=0,
+            bytes_accessed=2 * count * (tokens + own * slots) * width,
+        ),
+        name="combine",
+    )(at, codes, rows)
+
+
+def swap(values, axis, bit):
+    size = lax.axis_size(axis)
+    return lax.ppermute(values, axis, [(i, i ^ bit) for i in range(size)])
+
+
+def added(left, right):
+    return (left.astype(jnp.float32) + right.astype(jnp.float32)).astype(jnp.bfloat16)
+
+
+def start_scatter(codes, rows, own, slots, group):
+    blocks = codes.shape[0]
+    if group != ("ctx", "expert") or lax.axis_size("ctx") != 4 or lax.axis_size("expert") != 2:
+        every = jnp.arange(blocks, dtype=jnp.int32)
+        return lax.psum_scatter(
+            combine(every, codes, rows, own, slots), group, scatter_dimension=0
+        )
+    here = lax.axis_index(group).astype(jnp.int32)
+    far = here ^ jnp.array([2, 3, 6, 7], jnp.int32)
+    near = here ^ jnp.array([0, 1, 4, 5], jnp.int32)
+    sent = swap(combine(far, codes, rows, own, slots), "ctx", 1)
+    return added(combine(near, codes, rows, own, slots), sent)
+
+
+def finish_scatter(part, middle=None, later=None, work=None):
+    if part.ndim == 2:
+        return part.astype(jnp.float32), None if work is None else work(later)
+    half = part.shape[-1] // 2
+    left, right = part[:, :, :half], part[:, :, half:]
+    left_sent = swap(left[2:], "ctx", 2)
+    right_sent = swap(jnp.stack([right[1], right[3]]), "expert", 1)
+    if work is not None:
+        left_sent, right_sent, _, later = lax.optimization_barrier(
+            (left_sent, right_sent, middle, later)
+        )
+    left_on = swap(added(left[1], left_sent[1]), "expert", 1)
+    right_on = swap(added(right[2], right_sent[1]), "ctx", 2)
+    made = None
+    if work is not None:
+        left_on, right_on, made = lax.optimization_barrier((left_on, right_on, work(later)))
+    wide = lambda *pieces: sum(piece.astype(jnp.float32) for piece in pieces)
+    whole = jnp.concatenate(
+        [wide(left[0], left_sent[0], left_on), wide(right[0], right_sent[0], right_on)], axis=1
+    )
+    return whole, made
+
+
+def lane_half(shape):
+    return lax.broadcasted_iota(jnp.int32, shape, 1) // HEAD_SIZE
+
+
+def turn(values, cosine, sine):
+    half_dim = HEAD_SIZE // 2
+    width = values.shape[1]
+    lane = lax.broadcasted_iota(jnp.int32, values.shape, 1) % HEAD_SIZE
+    partner = jnp.where(
+        lane < half_dim,
+        pltpu.roll(values, width - half_dim, 1),
+        pltpu.roll(values, half_dim, 1),
+    )
+    return values * cosine + partner * sine
+
+
+def to_key_half(values, swap, key_half):
+    moved = jnp.where(swap, pltpu.roll(values, HEAD_SIZE, 1), values)
+    return jnp.where(lane_half(values.shape) == key_half, moved, 0.0)
+
+
+def head_place(group):
+    head = pl.program_id(0)
+    key_half = (head // group) % 2
+    return head, key_half, (head % 2) != key_half
+
+
+def attend_forward_body(
+    group, prompt_rows, cont_len, pos_ref, q_ref, cos_ref, sin_ref, kp_ref, vp_ref, kc_ref, vc_ref,
+    qr_ref, out_ref, log_ref,
+):
+    head, key_half, swap = head_place(group)
+    rotated = turn(q_ref[...], cos_ref[...], sin_ref[...]).astype(jnp.bfloat16)
+    qr_ref[...] = rotated
+    query = to_key_half(rotated.astype(jnp.float32), swap, key_half) * ATT_SCALE
+    query = query.astype(jnp.bfloat16)
+    nt = (((1,), (1,)), ((), ()))
+
+    def finish(parts, rows):
+        highest = parts[0][0].max(axis=1, keepdims=True)
+        for scores, _ in parts[1:]:
+            highest = jnp.maximum(highest, scores.max(axis=1, keepdims=True))
+        lifted = [jnp.exp(scores - highest) for scores, _ in parts]
+        total = lifted[0].sum(axis=1, keepdims=True)
+        for piece in lifted[1:]:
+            total = total + piece.sum(axis=1, keepdims=True)
+        inverse = 1.0 / total
+        result = None
+        for piece, (_, value) in zip(lifted, parts):
+            term = jnp.dot(
+                (piece * inverse).astype(jnp.bfloat16), value, preferred_element_type=jnp.float32
+            )
+            result = term if result is None else result + term
+        log_total = jnp.broadcast_to(highest + jnp.log(total), (total.shape[0], 128))
+        log_ref[0, :, rows] = jnp.transpose(log_total)[:8]
+        keep = jnp.where(lane_half(result.shape) == key_half, result, 0.0)
+        keep = jnp.where(swap, pltpu.roll(keep, HEAD_SIZE, 1), keep).astype(jnp.bfloat16)
+
+        @pl.when(head % 2 == 0)
+        def _():
+            out_ref[rows, :] = keep
+
+        @pl.when(head % 2 == 1)
+        def _():
+            out_ref[rows, :] = out_ref[rows, :] + keep
+
+    total_rows = q_ref.shape[0]
+    first = lax.dot_general(
+        query[:prompt_rows], kp_ref[...], nt, preferred_element_type=jnp.float32
+    )
+    row = lax.broadcasted_iota(jnp.int32, first.shape, 0) + pos_ref[0]
+    first = jnp.where(lax.broadcasted_iota(jnp.int32, first.shape, 1) <= row, first, NEG)
+    finish([(first, vp_ref[...])], pl.ds(0, prompt_rows))
+    lower = query[prompt_rows:]
+    wide = lax.dot_general(lower, kp_ref[...], nt, preferred_element_type=jnp.float32)
+    near = lax.dot_general(lower, kc_ref[...], nt, preferred_element_type=jnp.float32)
+    row = lax.broadcasted_iota(jnp.int32, near.shape, 0)
+    col = lax.broadcasted_iota(jnp.int32, near.shape, 1)
+    near = jnp.where((col <= row) & (col // cont_len == row // cont_len), near, NEG)
+    finish([(wide, vp_ref[...]), (near, vc_ref[...])], pl.ds(prompt_rows, total_rows - prompt_rows))
+
+
+def attend_forward(q_lin, key_prompt, value_prompt, key_cont, value_cont, cosine, sine, start, rows, cont_len):
+    tokens, width = q_lin.shape
+    heads = width // HEAD_SIZE
+    group = heads // (key_prompt.shape[1] // HEAD_SIZE)
+    keys, near = key_prompt.shape[0], key_cont.shape[0]
+    tile = lambda h, *_: (0, h // 2)
+    key_tile = lambda h, *_: (0, h // (2 * group))
+    same = lambda h, *_: (0, 0)
+    return pl.pallas_call(
+        partial(attend_forward_body, group, rows, cont_len),
+        grid_spec=pltpu.PrefetchScalarGridSpec(
+            num_scalar_prefetch=1,
+            grid=(heads,),
+            in_specs=[
+                pl.BlockSpec((tokens, 128), tile),
+                pl.BlockSpec((tokens, 128), same),
+                pl.BlockSpec((tokens, 128), same),
+                pl.BlockSpec((keys, 128), key_tile),
+                pl.BlockSpec((keys, 128), key_tile),
+                pl.BlockSpec((near, 128), key_tile),
+                pl.BlockSpec((near, 128), key_tile),
+            ],
+            out_specs=[
+                pl.BlockSpec((tokens, 128), tile),
+                pl.BlockSpec((tokens, 128), tile),
+                pl.BlockSpec((1, 8, tokens), lambda h, *_: (h, 0, 0)),
+            ],
+        ),
+        out_shape=[
+            jax.ShapeDtypeStruct((tokens, width), jnp.bfloat16),
+            jax.ShapeDtypeStruct((tokens, width), jnp.bfloat16),
+            jax.ShapeDtypeStruct((heads, 8, tokens), jnp.float32),
         ],
-        out_specs=pl.BlockSpec((1, tokens, width), lambda b: (b, 0, 0)),
-        out_shape=jax.ShapeDtypeStruct((blocks, tokens, width), jnp.bfloat16),
         cost_estimate=pl.CostEstimate(
-            flops=2 * blocks * own * slots * tokens * width,
-            transcendentals=0,
-            bytes_accessed=2 * blocks * (tokens + own * slots) * width,
-        ),
-        name="combine",
-    )(codes, rows)
-
-
-def attend_forward(allowed, pieces):
-    query_row_block, key_row_block, value_row_block = pieces
-    scores = (
-        jnp.einsum(
-            "trd,kd->trk", query_row_block, key_row_block, preferred_element_type=jnp.float32
+            flops=4 * heads * tokens * (keys + near) * 128,
+            transcendentals=heads * tokens * (keys + near),
+            bytes_accessed=8 * tokens * width,
+        ),
+        name="attend_forward",
+    )(start, q_lin, cosine, sine, key_prompt, value_prompt, key_cont, value_cont)
+
+
+def attend_backward_body(
+    group, prompt_rows, cont_len, chunk, pos_ref, q_ref, do_ref, out_ref, log_ref, cos_ref, sin_ref,
+    kcos_ref, ksin_ref, kp_ref, vp_ref, kc_ref, vc_ref,
+    dq_ref, dkp_ref, dvp_ref, dkc_ref, dvc_ref, dk_acc, dv_acc,
+):
+    head, key_half, swap = head_place(group)
+    tokens = q_ref.shape[0]
+    keys = kp_ref.shape[0]
+    near = kc_ref.shape[0]
+    nt = (((1,), (1,)), ((), ()))
+    tn = (((0,), (0,)), ((), ()))
+
+    @pl.when(head % (2 * group) == 0)
+    def _():
+        dk_acc[...] = jnp.zeros_like(dk_acc)
+        dv_acc[...] = jnp.zeros_like(dv_acc)
+
+    query = to_key_half(q_ref[...].astype(jnp.float32), swap, key_half) * ATT_SCALE
+    query = query.astype(jnp.bfloat16)
+    d_out = to_key_half(do_ref[...].astype(jnp.float32), swap, key_half)
+    result = to_key_half(out_ref[...].astype(jnp.float32), swap, key_half)
+    centre = jnp.transpose(
+        jnp.broadcast_to(jnp.sum(d_out * result, axis=1, keepdims=True), (tokens, 128))
+    )[:1]
+    d_out = d_out.astype(jnp.bfloat16)
+    log_total = log_ref[0][:1]
+    row = lax.broadcasted_iota(jnp.int32, (1, tokens), 1)
+    limit = jnp.where(row < prompt_rows, row + pos_ref[0], keys)
+
+    def step(key, value, query, d_out, log_total, centre, allowed, at, count):
+        scores = lax.dot_general(key, query, nt, preferred_element_type=jnp.float32)
+        scores = jnp.where(allowed(scores.shape), scores, NEG)
+        weights = jnp.exp(scores - log_total)
+        d_weights = lax.dot_general(value, d_out, nt, preferred_element_type=jnp.float32)
+        d_scores = (weights * (d_weights - centre)).astype(jnp.bfloat16)
+        dv_acc[at : at + count] += jnp.dot(
+            weights.astype(jnp.bfloat16), d_out, preferred_element_type=jnp.float32
         )
-        * ATT_SCALE
-    )
-    scores = jnp.where(allowed[:, None, :], scores, NEG)
-    highest = jnp.max(scores, axis=-1, keepdims=True)
-    lifted = jnp.exp(scores - highest)
-    summed = jnp.sum(lifted, axis=-1, keepdims=True)
-    weights = (lifted / summed).astype(jnp.bfloat16)
-    result = jnp.einsum("trk,kd->trd", weights, value_row_block, preferred_element_type=jnp.float32)
-    return (result, highest[..., 0] + jnp.log(summed[..., 0]))
-
-
-def attend_backward(allowed, pieces):
-    query_row_block, key_row_block, value_row_block, d_out, out_rows, log_total = pieces
-    scores = (
-        jnp.einsum(
-            "trd,kd->trk", query_row_block, key_row_block, preferred_element_type=jnp.float32
+        dk_acc[at : at + count] += jnp.dot(d_scores, query, preferred_element_type=jnp.float32)
+        return lax.dot_general(d_scores, key, tn, preferred_element_type=jnp.float32)
+
+    d_query = jnp.zeros((tokens, 128), jnp.float32)
+    for at in range(0, keys, chunk):
+
+        def seen(shape, at=at):
+            return lax.broadcasted_iota(jnp.int32, shape, 0) + at <= limit
+
+        d_query = d_query + step(
+            kp_ref[at : at + chunk], vp_ref[at : at + chunk], query, d_out, log_total, centre, seen,
+            at, chunk,
         )
-        * ATT_SCALE
-    )
-    scores = jnp.where(allowed[:, None, :], scores, NEG)
-    weights = jnp.exp(scores - log_total[..., None])
-    d_weights = jnp.einsum(
-        "trd,kd->trk", d_out, value_row_block, preferred_element_type=jnp.float32
-    )
-    centre = jnp.sum(d_out.astype(jnp.float32) * out_rows, axis=-1, keepdims=True)
-    d_scores = (weights * (d_weights - centre)).astype(jnp.bfloat16)
-    d_query = (
-        jnp.einsum("trk,kd->trd", d_scores, key_row_block, preferred_element_type=jnp.float32)
-        * ATT_SCALE
-    )
-    d_key = (
-        jnp.einsum("trk,trd->kd", d_scores, query_row_block, preferred_element_type=jnp.float32)
-        * ATT_SCALE
-    )
-    d_value = jnp.einsum(
-        "trk,trd->kd", weights.astype(jnp.bfloat16), d_out, preferred_element_type=jnp.float32
-    )
-    return (d_query, d_key, d_value)
+
+    def nearby(shape):
+        key_at = lax.broadcasted_iota(jnp.int32, shape, 0)
+        query_at = lax.broadcasted_iota(jnp.int32, shape, 1)
+        return (key_at <= query_at) & (key_at // cont_len == query_at // cont_len)
+
+    tail = step(
+        kc_ref[...], vc_ref[...], query[prompt_rows:], d_out[prompt_rows:],
+        log_total[:, prompt_rows:], centre[:, prompt_rows:], nearby, keys, near,
+    )
+    d_query = jnp.concatenate([d_query[:prompt_rows], d_query[prompt_rows:] + tail], axis=0)
+    d_query = jnp.where(lane_half(d_query.shape) == key_half, d_query * ATT_SCALE, 0.0)
+    d_query = jnp.where(swap, pltpu.roll(d_query, HEAD_SIZE, 1), d_query)
+    d_query = turn(d_query, cos_ref[...], -sin_ref[...]).astype(jnp.bfloat16)
+
+    @pl.when(head % 2 == 0)
+    def _():
+        dq_ref[...] = d_query
+
+    @pl.when(head % 2 == 1)
+    def _():
+        dq_ref[...] = dq_ref[...] + d_query
+
+    @pl.when(head % (2 * group) == 2 * group - 1)
+    def _():
+        dk = turn(dk_acc[...], kcos_ref[...], -ksin_ref[...]).astype(jnp.bfloat16)
+        dv = dv_acc[...].astype(jnp.bfloat16)
+        dkp_ref[...] = dk[:keys]
+        dkc_ref[...] = dk[keys:]
+        dvp_ref[...] = dv[:keys]
+        dvc_ref[...] = dv[keys:]
+
+
+def attend_backward(
+    query, d_out, result, log_total, key_prompt, value_prompt, key_cont, value_cont, cosine, sine,
+    key_cosine, key_sine, start, rows, cont_len,
+):
+    tokens, width = query.shape
+    heads = width // HEAD_SIZE
+    key_width = key_prompt.shape[1]
+    group = heads // (key_width // HEAD_SIZE)
+    keys, near = key_prompt.shape[0], key_cont.shape[0]
+    chunk = min(256, keys)
+    tile = lambda h, *_: (0, h // 2)
+    key_tile = lambda h, *_: (0, h // (2 * group))
+    same = lambda h, *_: (0, 0)
+    return pl.pallas_call(
+        partial(attend_backward_body, group, rows, cont_len, chunk),
+        grid_spec=pltpu.PrefetchScalarGridSpec(
+            num_scalar_prefetch=1,
+            grid=(heads,),
+            in_specs=[
+                pl.BlockSpec((tokens, 128), tile),
+                pl.BlockSpec((tokens, 128), tile),
+                pl.BlockSpec((tokens, 128), tile),
+                pl.BlockSpec((1, 8, tokens), lambda h, *_: (h, 0, 0)),
+                pl.BlockSpec((tokens, 128), same),
+                pl.BlockSpec((tokens, 128), same),
+                pl.BlockSpec((keys + near, 128), same),
+                pl.BlockSpec((keys + near, 128), same),
+                pl.BlockSpec((keys, 128), key_tile),
+                pl.BlockSpec((keys, 128), key_tile),
+                pl.BlockSpec((near, 128), key_tile),
+                pl.BlockSpec((near, 128), key_tile),
+            ],
+            out_specs=[
+                pl.BlockSpec((tokens, 128), tile),
+                pl.BlockSpec((keys, 128), key_tile),
+                pl.BlockSpec((keys, 128), key_tile),
+                pl.BlockSpec((near, 128), key_tile),
+                pl.BlockSpec((near, 128), key_tile),
+            ],
+            scratch_shapes=[
+                pltpu.VMEM((keys + near, 128), jnp.float32),
+                pltpu.VMEM((keys + near, 128), jnp.float32),
+            ],
+        ),
+        out_shape=[
+            jax.ShapeDtypeStruct((tokens, width), jnp.bfloat16),
+            jax.ShapeDtypeStruct((keys, key_width), jnp.bfloat16),
+            jax.ShapeDtypeStruct((keys, key_width), jnp.bfloat16),
+            jax.ShapeDtypeStruct((near, key_width), jnp.bfloat16),
+            jax.ShapeDtypeStruct((near, key_width), jnp.bfloat16),
+        ],
+        cost_estimate=pl.CostEstimate(
+            flops=10 * heads * tokens * (keys + near) * 128,
+            transcendentals=heads * tokens * (keys + near),
+            bytes_accessed=8 * tokens * width,
+        ),
+        name="attend_backward",
+    )(
+        start, query, d_out, result, log_total, cosine, sine, key_cosine, key_sine, key_prompt,
+        value_prompt, key_cont, value_cont,
+    )
 
 
 def reduce_experts(grad, split):
@@ -180,6 +456,29 @@
         ).astype(jnp.float32)
     part = lax.psum_scatter(grad, "dp", scatter_dimension=1, tiled=True)
     return lax.all_to_all(part, "ctx", split_axis=1, concat_axis=0, tiled=True).astype(jnp.float32)
+
+
+def scatter_keys(d_key, d_value, rows):
+    size = lax.axis_size("ctx")
+    here = lax.axis_index("ctx")
+
+    def share(owner):
+        return jnp.concatenate(
+            [
+                lax.dynamic_slice_in_dim(d_key, owner * rows, rows, axis=0),
+                lax.dynamic_slice_in_dim(d_value, owner * rows, rows, axis=0),
+            ],
+            axis=1,
+        )
+
+    total = share(here).astype(jnp.float32)
+    for hop in range(1, size):
+        moved = lax.ppermute(
+            share((here + hop) % size), "ctx", [(i, (i + hop) % size) for i in range(size)]
+        )
+        total = total + moved.astype(jnp.float32)
+    total = total.astype(jnp.bfloat16)
+    return (total[:, : d_key.shape[1]], total[:, d_key.shape[1] :])
 
 
 def per_device(
@@ -206,7 +505,6 @@
     cont_len = x_cont.shape[2]
     cont_rows = cont_count * cont_len
     count_of_tokens = prompt_rows + cont_rows
-    queries_per_group = QUERY_HEADS // KEY_VALUE_HEADS
     key_value_width = KEY_VALUE_HEADS * HEAD_SIZE
     local_experts = w_gate_up.shape[0]
     expert_groups = lax.axis_size("expert")
@@ -253,27 +551,25 @@
     key_linear = jnp.dot(h1_low, key_weight, preferred_element_type=jnp.float32)
     value_linear = jnp.dot(h1_low, value_weight, preferred_element_type=jnp.float32)
     row_index = jnp.arange(count_of_tokens, dtype=jnp.int32)
-    in_cont = row_index >= prompt_rows
     cont_offset = row_index - prompt_rows
-    ctx_index = lax.axis_index("ctx")
+    start = lax.axis_index("ctx") * prompt_rows
     query_pos = jnp.where(
-        in_cont, prompt_total + cont_offset % cont_len, ctx_index * prompt_rows + row_index
-    )
-    query_cont = jnp.where(in_cont, cont_offset // cont_len, -1)
-    cosine_lookup, sine_lookup = rope_tables(query_pos.astype(jnp.float32), HEAD_SIZE)
-    query_row_block = apply_rotary(
-        q_lin.reshape(count_of_tokens, QUERY_HEADS, HEAD_SIZE), cosine_lookup, sine_lookup, 1.0
-    ).astype(jnp.bfloat16)
-    key_row_block = (
-        apply_rotary(
-            key_linear.reshape(count_of_tokens, KEY_VALUE_HEADS, HEAD_SIZE),
-            cosine_lookup,
-            sine_lookup,
-            1.0,
-        )
-        .astype(jnp.bfloat16)
-        .reshape(count_of_tokens, key_value_width)
-    )
+        cont_offset >= 0, prompt_total + cont_offset % cont_len, start + row_index
+    )
+    key_index = jnp.arange(count_of_keys, dtype=jnp.int32)
+    key_pos = jnp.where(
+        key_index >= prompt_total, prompt_total + (key_index - prompt_total) % cont_len, key_index
+    )
+    start = start.astype(jnp.int32)[None]
+    cosine, sine = signed_tables(query_pos.astype(jnp.float32), 128)
+    key_cosine, key_sine = signed_tables(key_pos.astype(jnp.float32), 128)
+    wide_cosine, wide_sine = signed_tables(query_pos.astype(jnp.float32), key_value_width)
+    half_dim = HEAD_SIZE // 2
+    lane = jnp.arange(key_value_width, dtype=jnp.int32) % HEAD_SIZE
+    partner = jnp.where(
+        lane < half_dim, jnp.roll(key_linear, -half_dim, axis=1), jnp.roll(key_linear, half_dim, axis=1)
+    )
+    key_row_block = (key_linear * wide_cosine + partner * wide_sine).astype(jnp.bfloat16)
     value_row_block = value_linear.astype(jnp.bfloat16)
     prompt_kv = lax.all_gather(
         jnp.stack([key_row_block[:prompt_rows], value_row_block[:prompt_rows]]),
@@ -281,39 +577,18 @@
         axis=1,
         tiled=True,
     )
-    every_key_row = jnp.concatenate([prompt_kv[0], key_row_block[prompt_rows:]], axis=0)
-    every_value_row = jnp.concatenate([prompt_kv[1], value_row_block[prompt_rows:]], axis=0)
-    key_index = jnp.arange(count_of_keys, dtype=jnp.int32)
-    key_in_cont = key_index >= prompt_total
-    key_offset = key_index - prompt_total
-    key_pos = jnp.where(key_in_cont, prompt_total + key_offset % cont_len, key_index)
-    key_cont = jnp.where(key_in_cont, key_offset // cont_len, -1)
-    seen = key_pos[None, :] <= query_pos[:, None]
-    allowed = (key_cont[None, :] < 0) & ((query_cont[:, None] >= 0) | seen) | (
-        key_cont[None, :] >= 0
-    ) & (key_cont[None, :] == query_cont[:, None]) & seen
-    grouped_query = query_row_block.reshape(
-        count_of_tokens, KEY_VALUE_HEADS, queries_per_group, HEAD_SIZE
-    ).transpose(1, 0, 2, 3)
-    grouped_key = every_key_row.reshape(count_of_keys, KEY_VALUE_HEADS, HEAD_SIZE).transpose(
-        1, 0, 2
-    )
-    grouped_value = every_value_row.reshape(count_of_keys, KEY_VALUE_HEADS, HEAD_SIZE).transpose(
-        1, 0, 2
-    )
-    attended, log_total = lax.map(
-        partial(attend_forward, allowed), (grouped_query, grouped_key, grouped_value)
-    )
-    merged_low = (
-        attended.transpose(1, 0, 2, 3)
-        .reshape(count_of_tokens, QUERY_HEADS * HEAD_SIZE)
-        .astype(jnp.bfloat16)
+    keys_values = (
+        prompt_kv[0], prompt_kv[1], key_row_block[prompt_rows:], value_row_block[prompt_rows:]
+    )
+    query_row_block, merged_low, log_total = attend_forward(
+        q_lin, *keys_values, cosine, sine, start, prompt_rows, cont_len
     )
     branch = jnp.dot(merged_low, w_out, preferred_element_type=jnp.float32)
     resid = tokens + RESID * branch
     normed_two, scale_two = rms_forward(resid, gain_two)
     h2_low = normed_two.astype(jnp.bfloat16)
     rows_all = lax.all_gather(h2_low, group, axis=0, tiled=False)
+    rows_all, d_plain = lax.optimization_barrier((rows_all, d_plain))
     slot_rows = dispatch(own_codes, rows_all, own, slots)
     logits = jnp.einsum("btd,de->bet", rows_all, w_router, preferred_element_type=jnp.float32)
     named = codes_all > -1.5
@@ -338,10 +613,28 @@
     d_hidden = weight * d_plain
     d_gate = d_hidden * up_part * logistic * (1.0 + gate_part * (1.0 - logistic))
     d_both = jnp.concatenate([d_gate, d_hidden * silu], axis=-1).astype(jnp.bfloat16)
+    grad_down = jnp.einsum(
+        "ecf,ecd->efd", weighted, d_slot_rows, preferred_element_type=jnp.float32
+    ).astype(jnp.bfloat16)
+    d_both, grad_down = lax.optimization_barrier((d_both, grad_down))
+    grad_down = reduce_experts(grad_down, split)
     d_slots = jnp.einsum(
         "ecf,edf->ecd", d_both, gate_up_own, preferred_element_type=jnp.float32
     ).astype(jnp.bfloat16)
-    d_rows = lax.psum_scatter(combine(own_codes, d_slots, own, slots), group, scatter_dimension=0)
+    d_rows_parts, weighted, slot_rows = lax.optimization_barrier(
+        (start_scatter(own_codes, d_slots, own, slots, group), weighted, slot_rows)
+    )
+    grad_gate_up = jnp.einsum(
+        "ecd,ecf->edf", slot_rows, d_both, preferred_element_type=jnp.float32
+    ).astype(jnp.bfloat16)
+
+    def forward_rows(weighted):
+        expert_out = jnp.einsum(
+            "ecf,efd->ecd", weighted, down_own, preferred_element_type=jnp.float32
+        ).astype(jnp.bfloat16)
+        return start_scatter(own_codes, expert_out, own, slots, group)
+
+    d_rows, mixed_part = finish_scatter(d_rows_parts, grad_gate_up, weighted, forward_rows)
     d_gates_own = jnp.sum(
         jnp.where(
             picked,
@@ -360,30 +653,14 @@
         group,
         scatter_dimension=0,
     )
+    grad_gate_up = reduce_experts(grad_gate_up, split)
     d_logits = (
         gates * (d_gates - jnp.sum(gates * d_gates, axis=0, keepdims=True))
     ).astype(jnp.bfloat16)
     grad_router = jnp.einsum("td,et->de", h2_low, d_logits, preferred_element_type=jnp.float32)
-    d_normed_two = d_rows.astype(jnp.float32) + jnp.einsum(
+    d_normed_two = d_rows + jnp.einsum(
         "et,de->td", d_logits, w_router, preferred_element_type=jnp.float32
     )
-    grad_down = jnp.einsum(
-        "ecf,ecd->efd", weighted, d_slot_rows, preferred_element_type=jnp.float32
-    ).astype(jnp.bfloat16)
-    grad_gate_up = jnp.einsum(
-        "ecd,ecf->edf", slot_rows, d_both, preferred_element_type=jnp.float32
-    ).astype(jnp.bfloat16)
-    grad_down = reduce_experts(grad_down, split)
-    grad_gate_up = reduce_experts(grad_gate_up, split)
-    expert_out = jnp.einsum(
-        "ecf,efd->ecd", weighted, down_own, preferred_element_type=jnp.float32
-    ).astype(jnp.bfloat16)
-    mixed = lax.psum_scatter(
-        combine(own_codes, expert_out, own, slots), group, scatter_dimension=0
-    ).astype(jnp.float32)
-    output = resid + mixed
-    y_prompt = output[:prompt_rows].astype(jnp.bfloat16)[None]
-    y_cont = output[prompt_rows:].reshape(1, cont_count, cont_len, model_width).astype(jnp.bfloat16)
     d_resid_norm, grad_norm2 = rms_backward(resid, scale_two, gain_two, d_normed_two)
     d_resid = upstream + d_resid_norm
     d_branch = (RESID * d_resid).astype(jnp.bfloat16)
@@ -391,38 +668,18 @@
     merged_gradient = jnp.einsum(
         "td,qd->tq", d_branch, w_out, preferred_element_type=jnp.float32
     ).astype(jnp.bfloat16)
-    grouped_output_gradient = merged_gradient.reshape(
-        count_of_tokens, KEY_VALUE_HEADS, queries_per_group, HEAD_SIZE
-    ).transpose(1, 0, 2, 3)
-    d_q, d_k, d_v = lax.map(
-        partial(attend_backward, allowed),
-        (grouped_query, grouped_key, grouped_value, grouped_output_gradient, attended, log_total),
-    )
-    d_query = d_q.transpose(1, 0, 2, 3).reshape(count_of_tokens, QUERY_HEADS, HEAD_SIZE)
-    d_key_all = d_k.transpose(1, 0, 2).reshape(count_of_keys, key_value_width)
-    d_value_all = d_v.transpose(1, 0, 2).reshape(count_of_keys, key_value_width)
-    summed = lax.psum_scatter(
-        jnp.stack([d_key_all[:prompt_total], d_value_all[:prompt_total]]).astype(jnp.bfloat16),
-        "ctx",
-        scatter_dimension=1,
-        tiled=True,
-    ).astype(jnp.float32)
-    d_key = jnp.concatenate([summed[0], d_key_all[prompt_total:]], axis=0).reshape(
-        count_of_tokens, KEY_VALUE_HEADS, HEAD_SIZE
-    )
-    d_value_low = jnp.concatenate([summed[1], d_value_all[prompt_total:]], axis=0).astype(
-        jnp.bfloat16
-    )
-    d_query_low = (
-        apply_rotary(d_query, cosine_lookup, sine_lookup, -1.0)
-        .reshape(count_of_tokens, QUERY_HEADS * HEAD_SIZE)
-        .astype(jnp.bfloat16)
-    )
-    d_key_low = (
-        apply_rotary(d_key, cosine_lookup, sine_lookup, -1.0)
-        .reshape(count_of_tokens, key_value_width)
-        .astype(jnp.bfloat16)
-    )
+    mixed_part, merged_gradient = lax.optimization_barrier((mixed_part, merged_gradient))
+    d_query_low, d_key_prompt, d_value_prompt, d_key_cont, d_value_cont = attend_backward(
+        query_row_block, merged_gradient, merged_low, log_total, *keys_values, cosine, sine,
+        key_cosine, key_sine, start, prompt_rows, cont_len,
+    )
+    mixed, d_key_prompt = finish_scatter(mixed_part, d_key_prompt, d_key_prompt, lambda v: v)
+    output = resid + mixed
+    y_prompt = output[:prompt_rows].astype(jnp.bfloat16)[None]
+    y_cont = output[prompt_rows:].reshape(1, cont_count, cont_len, model_width).astype(jnp.bfloat16)
+    d_key_prompt, d_value_prompt = scatter_keys(d_key_prompt, d_value_prompt, prompt_rows)
+    d_key_low = jnp.concatenate([d_key_prompt, d_key_cont], axis=0)
+    d_value_low = jnp.concatenate([d_value_prompt, d_value_cont], axis=0)
     grad_query = jnp.einsum("td,tq->dq", h1_low, d_query_low, preferred_element_type=jnp.float32)
     grad_key = jnp.einsum("td,tq->dq", h1_low, d_key_low, preferred_element_type=jnp.float32)
     grad_value = jnp.einsum("td,tq->dq", h1_low, d_value_low, preferred_element_type=jnp.float32)

time: 1370 us -> 951 us (0.69)
  waiting for transfers between devices: 686 us -> 329 us
  matrix products: 355 us -> 175 us
  Pallas kernels: 61 us -> 185 us
  other arithmetic: 117 us -> 97.8 us
    reduce_scatter x2, waiting for transfers between devices: 334 us -> 47.2 us  [reduce_experts(): part = lax.psum_scatter(grad, 'dp', scatter_dimension=1, tiled=True)]
    dot_general x57 -> x1, matrix products: 185 us -> 13.8 us  [forward_rows(): jnp.einsum('ecf,efd->ecd', weighted, down_own, preferred_element_type=jnp...]
    reduce_scatter x3 -> x0, waiting for transfers between devices: 148 us -> none  [the longest x1 90.5 us: per_device(): lax.psum_scatter(combine(own_codes, expert_out, own, slots), group, scatt...]
    pallas_call x2 -> x6, Pallas kernels: 32.7 us -> 157 us  [the longest x1 63.8 us: attend_backward(): pl.pallas_call(partial(attend_backward_body, group, rows, cont_len, chunk...]
    ppermute x0 -> x13, waiting for transfers between devices: none -> 65.9 us  [the longest x10 46.8 us: swap(): return lax.ppermute(values, axis, [(i, i ^ bit) for i in range(size)])]
    convert_element_type x5 -> x8, other arithmetic: 5.35 us -> 26.2 us  [the longest x4 22.9 us: added(): (left.astype(jnp.float32) + right.astype(jnp.float32)).astype(jnp.bfloat16)]
    or x16 -> x0, other arithmetic: 18.9 us -> none  [per_device(): (key_cont[None, :] < 0) & ((query_cont[:, None] >= 0) | seen)]
    reduce_sum x16 -> x1, other arithmetic: 26.9 us -> 9.73 us  [per_device(): d_slot_gate = RESID * jnp.sum(hidden * d_plain, axis=-1)]
  transfers between devices with their start and end apart: 13 -> 23, of which waited for: 8 -> 12; matrix products, arithmetic and copies ran while one was open for 23% -> 30% of each run, Pallas kernels for 3% -> 18%
where the time goes in v2:
time: 951 us; the launch traced here: 939 us
  waiting for transfers between devices  329 us (35%)
  Pallas kernels  185 us (19%)
  matrix products  175 us (18%)
  other arithmetic  97.8 us (10%)
  local copies, waits for them, and re-layouts  95.4 us (10%)
  starting transfers between devices  22.2 us (2%)
  blocking collectives  18.9 us (2%)
  between operations  15.4 us (2%)
    unnamed x9, waiting for transfers between devices  139 us
    pallas_call x1, Pallas kernels, attend_backward(): pl.pallas_call(partial(attend_backward_body, group, rows, cont_len, chunk...  63.8 us
    pallas_call x1, Pallas kernels, attend_forward(): pl.pallas_call(partial(attend_forward_body, group, rows, cont_len), grid_...  53.7 us
    reduce_scatter x2, waiting for transfers between devices, reduce_experts(): part = lax.psum_scatter(grad, 'dp', scatter_dimension=1, tiled=True)  47.2 us
    ppermute x10, waiting for transfers between devices, swap(): return lax.ppermute(values, axis, [(i, i ^ bit) for i in range(size)])  46.8 us
    pallas_call x4, Pallas kernels, combine(): pl.pallas_call(partial(combine_body, own, slots), grid_spec=pltpu.Prefetc...  39.1 us
    all_gather x1, waiting for transfers between devices, per_device(): rows_all = lax.all_gather(h2_low, group, axis=0, tiled=False)  35 us
    unnamed x110, local copies, waits for them, and re-layouts  32.9 us
  transfers between devices with their start and end apart: 23, of which 12 were waited for; matrix products, arithmetic and copies ran while one was open for 30% of the time, Pallas kernels for 18%

profile of v2, /device:TPU:9, one launch (start us, length us, event | category | flops | bytes accessed | tf_op | source)
XLA Modules:
  0.0 938.8 jit_solution(4121525448148367869)
XLA Ops:
  45.2 11.2 %all-gather.7.cloned.1.call-done = bf16[2,1024,512]{2,1,0:T(8,128)(2,1)} async-done(((bf16[2,256,512]{2,1,0:T(8,128)(2,1)}), bf16[2,1024,512]{2,1,0:T(8,128)(2,1)}) %all-gather.7.cloned.1.call-update) | async-done | bytes 2097168 | tf_op jit(solution)/shard_map/all_gather | solution.py:574
  59.4 53.7 %attend_forward.1 = (bf16[512,1536]{1,0:T(8,128)(2,1)}, bf16[512,1536]{1,0:T(8,128)(2,1)}, f32[24,8,512]{2,1,0:T(8,128)}) custom-call(s32[1]{0:T(128)} %bitcast.2.pos_ref, f32[512,1536]{1,0:T(8,128)} %fusion.92.q_ref, f32[512,128]{1,0:T(8,128)} %copy.115.cos_ref, f32[512,128]{1,0:T(8,128)} %copy.116.sin_ref, bf16[1024,512]{1,0:T(8,128)(2,1)} %get-tuple-element.164.kp_ref, ...), custom_call_target="tpu_custom_call" | custom-call | flops 8053063680 | bytes 6291456 | tf_op jit(solution)/shard_map/attend_forward/pallas_call | solution.py:271
  122.5 18.9 %all-gather = f32[320,512]{1,0:T(8,128)S(1)} all-gather(f32[40,512]{1,0:T(8,128)S(1)} %fusion.54), channel_id=2, replica_groups=mesh['dp'=4,'ctx'=4,'expert'=2] {'ctx','expert'}, dimensions={0}, use_global_device_ids=true | all-gather | bytes 737280 | tf_op jit(solution)/shard_map/all_gather | solution.py:533
  142.2 14.5 %dispatch.2 = bf16[5,832,1536]{2,1,0:T(8,128)(2,1)} custom-call(f32[8,8,512]{2,1,0:T(8,128)} %pad.9.codes_ref, bf16[8,512,1536]{2,1,0:T(8,128)(2,1)} %bitcast.122), custom_call_target="tpu_custom_call" | custom-call | flops 6543114240 | bytes 25362432 | tf_op jit(solution)/shard_map/dispatch/pallas_call | solution.py:85
  156.7 14.1 %fusion.14 = f32[5,832,512]{2,1,0:T(8,128)} fusion(bf16[5,832,1536]{2,1,0:T(8,128)(2,1)} %dispatch.2, bf16[20,512,1536]{2,1,0:T(8,128)(2,1)} %param.30, s32[]{:T(128)S(6)} %select_n.129), kind=kOutput, calls=%fused_computation.28 | convolution fusion | flops 6543114240 | bytes 29163524 | tf_op jit(solution)/shard_map/ecd,efd->ecf/dot_general | solution.py:542
  170.8 35.0 %all-gather.9.cloned.1.call-done = bf16[4096,1536]{1,0:T(8,128)(2,1)} async-done(((bf16[512,1536]{1,0:T(8,128)(2,1)}), bf16[4096,1536]{1,0:T(8,128)(2,1)}) %all-gather.9.cloned.1.call-update) | async-done | bytes 12582928 | tf_op jit(solution)/shard_map/all_gather | solution.py:590
  205.7 14.2 %dispatch.3 = bf16[5,832,1536]{2,1,0:T(8,128)(2,1)} custom-call(f32[8,8,512]{2,1,0:T(8,128)} %pad.9.codes_ref, bf16[8,512,1536]{2,1,0:T(8,128)(2,1)} %bitcast.118), custom_call_target="tpu_custom_call" | custom-call | flops 6543114240 | bytes 25362432 | tf_op jit(solution)/shard_map/dispatch/pallas_call | solution.py:85
  219.9 8.4 fusion.103
  229.2 23.1 %fusion.3 = f32[5,832,1024]{2,1,0:T(8,128)} fusion(bf16[5,832,1536]{2,1,0:T(8,128)(2,1)} %dispatch.3, bf16[20,1536,1024]{2,1,0:T(8,128)(2,1)} %param.29, s32[]{:T(128)S(6)} %select_n.129), kind=kOutput, calls=%fused_computation.3 | convolution fusion | flops 13086228480 | bytes 45547524 | tf_op jit(solution)/shard_map/ecd,edf->ecf/dot_general | solution.py:604
  252.3 9.7 %multiply_reduce_fusion = f32[5,832]{1,0:T(8,128)S(1)} fusion(f32[5,832,512]{2,1,0:T(8,128)} %fusion.14, f32[5,832,1024]{2,1,0:T(8,128)} %fusion.3), kind=kLoop, calls=%fused_computation.16 | loop fusion | flops 14905280 | bytes 25575680 | tf_op jit(solution)/shard_map/reduce_sum | solution.py:611
  266.7 14.3 %multiply_convert_fusion.2 = (bf16[5,832,512]{2,1,0:T(8,128)(2,1)}, bf16[5,832,512]{2,1,0:T(8,128)(2,1)}, bf16[5,832,512]{2,1,0:T(8,128)(2,1)S(1)}) fusion(f32[5,832,1024]{2,1,0:T(8,128)} %fusion.3, f32[5,832,512]{2,1,0:T(8,128)} %fusion.14, f32[5,832]{1,0:T(8,128)S(1)} %mul.307), kind=kLoop, calls=%fused_computation.19 | loop fusion | flops 36208640 | bytes 38355200 | tf_op jit(solution)/shard_map/convert.20
  282.9 15.2 %convolution_convert_fusion.4 = bf16[5,512,1536]{2,1,0:T(8,128)(2,1)} fusion(bf16[5,832,512]{2,1,0:T(8,128)(2,1)S(1)} %get-tuple-element.51, bf16[5,832,1536]{2,1,0:T(8,128)(2,1)} %dispatch.2), kind=kOutput, calls=%fused_computation.31 | convolution fusion | flops 6547046400 | bytes 24903680 | tf_op jit(solution)/shard_map/ecf,ecd->efd/dot_general | solution.py:616
  298.2 8.4 pad_maximum_fusion
  307.7 21.0 %fusion.5.rows_ref = bf16[5,832,1536]{2,1,0:T(8,128)(2,1)} fusion(bf16[5,832,1024]{2,1,0:T(8,128)(2,1)} %pad_maximum_fusion, bf16[20,1536,1024]{2,1,0:T(8,128)(2,1)} %param.29, s32[]{:T(128)S(6)} %select_n.129), kind=kOutput, calls=%fused_computation.10 | convolution fusion | flops 13092618240 | bytes 37027844 | tf_op jit(solution)/shard_map/ecf,edf->ecd/dot_general | solution.py:621
  328.7 9.8 %combine.5 = bf16[4,512,1536]{2,1,0:T(8,128)(2,1)} custom-call(s32[4]{0:T(128)} %broadcast_xor_fusion.at_ref, f32[8,8,512]{2,1,0:T(8,128)} %pad.9.codes_ref, bf16[5,832,1536]{2,1,0:T(8,128)(2,1)} %fusion.5.rows_ref), custom_call_target="tpu_custom_call" | custom-call | flops 3271557120 | bytes 12681216 | tf_op jit(solution)/shard_map/combine/pallas_call | solution.py:114
  339.3 9.7 %combine.4 = bf16[4,512,1536]{2,1,0:T(8,128)(2,1)} custom-call(s32[4]{0:T(128)} %broadcast_xor_fusion.1.at_ref, f32[8,8,512]{2,1,0:T(8,128)} %pad.9.codes_ref, bf16[5,832,1536]{2,1,0:T(8,128)(2,1)} %fusion.5.rows_ref), custom_call_target="tpu_custom_call" | custom-call | flops 3271557120 | bytes 12681216 | tf_op jit(solution)/shard_map/combine/pallas_call | solution.py:114
  349.0 9.0 add_convert_fusion.1
  358.1 24.1 %convolution_convert_fusion = bf16[5,1536,1024]{2,1,0:T(8,128)(2,1)} fusion(bf16[5,832,1536]{2,1,0:T(8,128)(2,1)} %dispatch.3, bf16[5,832,1024]{2,1,0:T(8,128)(2,1)} %pad_maximum_fusion), kind=kOutput, calls=%fused_computation.5 | convolution fusion | flops 13094092800 | bytes 37027840 | tf_op jit(solution)/shard_map/ecd,ecf->edf/dot_general | solution.py:627
  386.7 34.5 %collective-permute-done.2 = bf16[2,512,768]{2,1,0:T(8,128)(2,1)S(1)} collective-permute-done((bf16[2,512,768]{2,1,0:T(8,128)(2,1)S(1)}, bf16[2,512,768]{2,1,0:T(8,128)(2,1)S(1)}, u32[]{:S(2)}, u32[]{:S(2)}) %collective-permute-start.2) | collective-permute-done | bytes 1572896 | tf_op jit(solution)/shard_map/ppermute | solution.py:137
  422.4 13.8 %convolution_convert_fusion.1.rows_ref = bf16[5,832,1536]{2,1,0:T(8,128)(2,1)} fusion(bf16[5,832,512]{2,1,0:T(8,128)(2,1)} %copy-done.8, bf16[20,512,1536]{2,1,0:T(8,128)(2,1)} %param.30, s32[]{:T(128)S(6)} %select_n.129), kind=kOutput, calls=%fused_computation.9 | convolution fusion | flops 6549504000 | bytes 24903684 | tf_op jit(solution)/shard_map/ecf,efd->ecd/dot_general | solution.py:632
  436.2 9.9 %combine.7 = bf16[4,512,1536]{2,1,0:T(8,128)(2,1)} custom-call(s32[4]{0:T(128)} %broadcast_xor_fusion.at_ref, f32[8,8,512]{2,1,0:T(8,128)} %pad.9.codes_ref, bf16[5,832,1536]{2,1,0:T(8,128)(2,1)} %convolution_convert_fusion.1.rows_ref), custom_call_target="tpu_custom_call" | custom-call | flops 3271557120 | bytes 12681216 | tf_op jit(solution)/shard_map/combine/pallas_call | solution.py:114
  460.5 9.7 %combine.6 = bf16[4,512,1536]{2,1,0:T(8,128)(2,1)} custom-call(s32[4]{0:T(128)} %broadcast_xor_fusion.1.at_ref, f32[8,8,512]{2,1,0:T(8,128)} %pad.9.codes_ref, bf16[5,832,1536]{2,1,0:T(8,128)(2,1)} %convolution_convert_fusion.1.rows_ref), custom_call_target="tpu_custom_call" | custom-call | flops 3271557120 | bytes 12681216 | tf_op jit(solution)/shard_map/combine/pallas_call | solution.py:114
  470.2 9.3 add_convert_fusion
  485.5 13.8 %convolution_convert_fusion.7.do_ref = bf16[512,1536]{1,0:T(8,128)(2,1)} fusion(bf16[1536,1536]{1,0:T(8,128)(2,1)S(1)} %bitcast.162, f32[512,1536]{1,0:T(8,128)S(1)} %multiply_add_fusion), kind=kOutput, calls=%fused_computation.62 | convolution fusion | flops 2418278400 | bytes 9437184 | tf_op jit(solution)/shard_map/td,qd->tq/dot_general | solution.py:668
  502.1 63.8 %attend_backward.1 = (bf16[512,1536]{1,0:T(8,128)(2,1)}, bf16[1024,512]{1,0:T(8,128)(2,1)}, bf16[1024,512]{1,0:T(8,128)(2,1)}, bf16[256,512]{1,0:T(8,128)(2,1)}, bf16[256,512]{1,0:T(8,128)(2,1)}) custom-call(s32[1]{0:T(128)} %bitcast.2.pos_ref, bf16[512,1536]{1,0:T(8,128)(2,1)} %get-tuple-element.56.q_ref, ...), custom_call_target="tpu_custom_call" | custom-call | flops 20132659200 | bytes 6291456 | tf_op jit(solution)/shard_map/attend_backward/pallas_call | solution.py:402
  575.0 11.4 %collective-permute-done.9 = bf16[512,768]{1,0:T(8,128)(2,1)S(1)} collective-permute-done((bf16[512,768]{1,0:T(8,128)(2,1)S(1)}, bf16[512,768]{1,0:T(8,128)(2,1)S(1)}, u32[]{:S(2)}, u32[]{:S(2)}) %collective-permute-start.9) | collective-permute-done | bytes 786464 | tf_op jit(solution)/shard_map/ppermute | solution.py:137
  600.9 13.2 %collective-permute-done.11 = bf16[256,1024]{1,0:T(8,128)(2,1)S(1)} collective-permute-done((bf16[256,1024]{1,0:T(8,128)(2,1)S(1)}, bf16[256,1024]{1,0:T(8,128)(2,1)S(1)}, u32[]{:S(2)}, u32[]{:S(2)}) %collective-permute-start.11) | collective-permute-done | bytes 524320 | tf_op jit(solution)/shard_map/ppermute | solution.py:476
  629.8 16.5 %copy.132 = bf16[1536,4224]{1,0:T(8,128)(2,1)} copy(bf16[1536,4224]{0,1:T(8,128)(2,1)} %fusion.51) | data formatting | bytes 25952256
  660.7 47.2 %reduce-scatter.9.cloned.1.call-done = bf16[5,384,1024]{2,1,0:T(8,128)(2,1)} async-done(((bf16[5,1536,1024]{2,1,0:T(8,128)(2,1)}), bf16[5,384,1024]{2,1,0:T(8,128)(2,1)}) %reduce-scatter.9.cloned.1.call-update) | async-done | bytes 3932176 | tf_op jit(solution)/shard_map/reduce_scatter | solution.py:457
  727.4 139.2 %reduce-scatter.13.cloned.1.call-done = bf16[96,4224]{1,0:T(8,128)(2,1)} async-done(((bf16[1536,4224]{1,0:T(8,128)(2,1)}), bf16[96,4224]{1,0:T(8,128)(2,1)}) %reduce-scatter.13.cloned.1.call-update) | async-done | bytes 811024
  879.7 30.3 %all-reduce.4.cloned.1.call-done = bf16[96,4224]{0,1:T(8,128)(2,1)} async-done(((bf16[96,4224]{0,1:T(8,128)(2,1)}), bf16[96,4224]{0,1:T(8,128)(2,1)}) %all-reduce.4.cloned.1.call-update) | async-done | bytes 811024 | tf_op jit(solution)/shard_map/psum | solution.py:702
  923.8 7.8 copy.124
  (263 shorter events, 188.7 us)
Async XLA Ops:
  7.2 49.2 %all-gather.7.cloned.1.call-start = ((), (), s32[]{:S(2)}) async-start(), calls=%async_computation.6 | async-start | bytes 2621440 | tf_op jit(solution)/shard_map/all_gather | solution.py:574
  9.8 28.5 %copy-start.33 = (f32[1536]{0:T(1024)}, f32[1536]{0:T(1024)S(1)}, u32[]{:S(2)}) copy-start(f32[1536]{0:T(1024)S(1)} %convert_element_type.250) | copy-start | bytes 18436
  32.1 110.0 %all-gather.11.cloned.1.call-start = ((), (), s32[]{:S(2)}) async-start(), calls=%async_computation.12 | async-start | bytes 14155776 | tf_op jit(solution)/shard_map/all_gather | solution.py:540
  34.9 170.8 %all-gather.9.cloned.1.call-start = ((), (), s32[]{:S(2)}) async-start(), calls=%async_computation.11 | async-start | bytes 14155776 | tf_op jit(solution)/shard_map/all_gather | solution.py:590
  35.0 83.3 %copy-start.29 = (f32[1536]{0:T(1024)}, f32[1536]{0:T(1024)S(1)}, u32[]{:S(2)}) copy-start(f32[1536]{0:T(1024)S(1)} %convert_element_type.256) | copy-start | bytes 18436
  121.5 332.7 %reduce-scatter.7.cloned.1.call-start = ((), (), s32[]{:S(2)}) async-start(), calls=%async_computation.7 | async-start | bytes 737280 | tf_op jit(solution)/shard_map/reduce_scatter | solution.py:646
  266.5 379.8 %reduce-scatter.11.cloned.1.call-start = ((), (), s32[]{:S(2)}) async-start(), calls=%async_computation.10 | async-start | bytes 9830400 | tf_op jit(solution)/shard_map/reduce_scatter | solution.py:457
  306.6 401.3 %reduce-scatter.9.cloned.1.call-start = ((), (), s32[]{:S(2)}) async-start(), calls=%async_computation.9 | async-start | bytes 19660800 | tf_op jit(solution)/shard_map/reduce_scatter | solution.py:457
  338.5 10.5 %collective-permute-start = (bf16[4,512,1536]{2,1,0:T(8,128)(2,1)}, bf16[4,512,1536]{2,1,0:T(8,128)(2,1)}, u32[]{:S(2)}, u32[]{:S(2)}) collective-permute-start(bf16[4,512,1536]{2,1,0:T(8,128)(2,1)} %combine.5), channel_id=1, source_target_pairs={{0,2},{2,0},{4,6},{6,4},{1,3},{3,1},{5,7},{7,5},{8,10},{10,8},{12,... | collective-permute-start | bytes 18874376 | tf_op jit(solution)/shard_map/ppermute | solution.py:137
  382.2 484.5 %reduce-scatter.13.cloned.1.call-start = ((), (), s32[]{:S(2)}) async-start(), calls=%async_computation.13 | async-start | bytes 13787136
  385.4 35.9 %collective-permute-start.2 = (bf16[2,512,768]{2,1,0:T(8,128)(2,1)S(1)}, bf16[2,512,768]{2,1,0:T(8,128)(2,1)S(1)}, u32[]{:S(2)}, u32[]{:S(2)}) collective-permute-start(bf16[2,512,768]{2,1,0:T(8,128)(2,1)S(1)} %pad_maximum_fusion.3), channel_id=1, source_target_pairs={{0,1},{1,0},{2,3},{3,2},{4,5},{5,4},{6,7},{7,6},{8,9},{9,8},{10,11... | collective-permute-start | bytes 4718600 | tf_op jit(solution)/shard_map/ppermute | solution.py:137
  385.9 36.5 %collective-permute-start.1 = (bf16[2,512,768]{2,1,0:T(8,128)(2,1)S(1)}, bf16[2,512,768]{2,1,0:T(8,128)(2,1)}, u32[]{:S(2)}, u32[]{:S(2)}) collective-permute-start(bf16[2,512,768]{2,1,0:T(8,128)(2,1)S(1)} %slice.179), channel_id=1, source_target_pairs={{0,4},{2,6},{4,0},{6,2},{1,5},{3,7},{5,1},{7,3},{8,12},{10,14},{12... | collective-permute-start | bytes 4718600 | tf_op jit(solution)/shard_map/ppermute | solution.py:137
  446.1 24.0 %collective-permute-start.5 = (bf16[4,512,1536]{2,1,0:T(8,128)(2,1)}, bf16[4,512,1536]{2,1,0:T(8,128)(2,1)}, u32[]{:S(2)}, u32[]{:S(2)}) collective-permute-start(bf16[4,512,1536]{2,1,0:T(8,128)(2,1)} %combine.7), channel_id=1, source_target_pairs={{0,2},{2,0},{4,6},{6,4},{1,3},{3,1},{5,7},{7,5},{8,10},{10,8},{12,... | collective-permute-start | bytes 18874376 | tf_op jit(solution)/shard_map/ppermute | solution.py:137
  458.7 20.8 %collective-permute-start.4 = (bf16[512,768]{1,0:T(8,128)(2,1)S(1)}, bf16[512,768]{1,0:T(8,128)(2,1)}, u32[]{:S(2)}, u32[]{:S(2)}) collective-permute-start(bf16[512,768]{1,0:T(8,128)(2,1)S(1)} %get-tuple-element.155), channel_id=1, source_target_pairs={{0,4},{2,6},{4,0},{6,2},{1,5},{3,7},{5,1},{7,3},{8,12},{10,14},{12... | collective-permute-start | bytes 2359304 | tf_op jit(solution)/shard_map/ppermute | solution.py:137
  460.0 19.5 %collective-permute-start.3 = (bf16[512,768]{1,0:T(8,128)(2,1)S(1)}, bf16[512,768]{1,0:T(8,128)(2,1)}, u32[]{:S(2)}, u32[]{:S(2)}) collective-permute-start(bf16[512,768]{1,0:T(8,128)(2,1)S(1)} %get-tuple-element.156), channel_id=1, source_target_pairs={{0,1},{1,0},{2,3},{3,2},{4,5},{5,4},{6,7},{7,6},{8,9},{9,8},{10,11... | collective-permute-start | bytes 2359304 | tf_op jit(solution)/shard_map/ppermute | solution.py:137
  500.8 65.1 %collective-permute-start.7 = (bf16[2,512,768]{2,1,0:T(8,128)(2,1)}, bf16[2,512,768]{2,1,0:T(8,128)(2,1)}, u32[]{:S(2)}, u32[]{:S(2)}) collective-permute-start(bf16[2,512,768]{2,1,0:T(8,128)(2,1)} %pad_maximum_fusion.4), channel_id=1, source_target_pairs={{0,1},{1,0},{2,3},{3,2},{4,5},{5,4},{6,7},{7,6},{8,9},{9,8},{10,11... | collective-permute-start | bytes 4718600 | tf_op jit(solution)/shard_map/ppermute | solution.py:137
  501.8 64.1 %collective-permute-start.6 = (bf16[2,512,768]{2,1,0:T(8,128)(2,1)S(1)}, bf16[2,512,768]{2,1,0:T(8,128)(2,1)}, u32[]{:S(2)}, u32[]{:S(2)}) collective-permute-start(bf16[2,512,768]{2,1,0:T(8,128)(2,1)S(1)} %slice.190), channel_id=1, source_target_pairs={{0,4},{2,6},{4,0},{6,2},{1,5},{3,7},{5,1},{7,3},{8,12},{10,14},{12... | collective-permute-start | bytes 4718600 | tf_op jit(solution)/shard_map/ppermute | solution.py:137
  568.3 18.2 %collective-permute-start.9 = (bf16[512,768]{1,0:T(8,128)(2,1)S(1)}, bf16[512,768]{1,0:T(8,128)(2,1)S(1)}, u32[]{:S(2)}, u32[]{:S(2)}) collective-permute-start(bf16[512,768]{1,0:T(8,128)(2,1)S(1)} %get-tuple-element.149), channel_id=1, source_target_pairs={{0,4},{2,6},{4,0},{6,2},{1,5},{3,7},{5,1},{7,3},{8,12},{10,14},{12... | collective-permute-start | bytes 2359304 | tf_op jit(solution)/shard_map/ppermute | solution.py:137
  569.5 17.7 %collective-permute-start.8 = (bf16[512,768]{1,0:T(8,128)(2,1)S(1)}, bf16[512,768]{1,0:T(8,128)(2,1)S(1)}, u32[]{:S(2)}, u32[]{:S(2)}) collective-permute-start(bf16[512,768]{1,0:T(8,128)(2,1)S(1)} %get-tuple-element.150), channel_id=1, source_target_pairs={{0,1},{1,0},{2,3},{3,2},{4,5},{5,4},{6,7},{7,6},{8,9},{9,8},{10,11... | collective-permute-start | bytes 2359304 | tf_op jit(solution)/shard_map/ppermute | solution.py:137
  570.1 17.2 %copy-start.21 = (bf16[1024,512]{1,0:T(8,128)(2,1)S(1)}, bf16[1024,512]{1,0:T(8,128)(2,1)}, u32[]{:S(2)}) copy-start(bf16[1024,512]{1,0:T(8,128)(2,1)} %get-tuple-element.66) | copy-start | bytes 3145732
  575.0 16.3 %copy-start.10 = (bf16[1,1,256,1536]{3,2,1,0:T(8,128)(2,1)S(1)}, bf16[1,1,256,1536]{3,2,1,0:T(8,128)(2,1)}, u32[]{:S(2)}) copy-start(bf16[1,1,256,1536]{3,2,1,0:T(8,128)(2,1)} %param.21) | copy-start | bytes 2359300
  575.0 16.3 %copy-start.12 = (bf16[1,256,1536]{2,1,0:T(8,128)(2,1)S(1)}, bf16[1,256,1536]{2,1,0:T(8,128)(2,1)}, u32[]{:S(2)}) copy-start(bf16[1,256,1536]{2,1,0:T(8,128)(2,1)} %param.20) | copy-start | bytes 2359300
  575.0 16.3 %copy-start.34 = (f32[1536]{0:T(1024)S(1)}, f32[1536]{0:T(1024)}, u32[]{:S(2)}) copy-start(f32[1536]{0:T(1024)} %copy-done.33) | copy-start | bytes 18436
  575.0 16.3 %copy-start.36 = (f32[512]{0:T(512)S(1)}, f32[512]{0:T(512)}, u32[]{:S(2)}) copy-start(f32[512]{0:T(512)} %copy-done.35) | copy-start | bytes 6148
  587.4 13.5 %collective-permute-start.10 = (bf16[256,1024]{1,0:T(8,128)(2,1)S(1)}, bf16[256,1024]{1,0:T(8,128)(2,1)S(1)}, u32[]{:S(2)}, u32[]{:S(2)}) collective-permute-start(bf16[256,1024]{1,0:T(8,128)(2,1)S(1)} %pad_maximum_fusion.6), channel_id=1, source_target_pairs={{0,2},{2,4},{4,6},{6,0},{1,3},{3,5},{5,7},{7,1},{8,10},{10,12},{12... | collective-permute-start | bytes 1572872 | tf_op jit(solution)/shard_map/ppermute | solution.py:476
  590.0 24.2 %collective-permute-start.11 = (bf16[256,1024]{1,0:T(8,128)(2,1)S(1)}, bf16[256,1024]{1,0:T(8,128)(2,1)S(1)}, u32[]{:S(2)}, u32[]{:S(2)}) collective-permute-start(bf16[256,1024]{1,0:T(8,128)(2,1)S(1)} %pad_maximum_fusion.7), channel_id=1, source_target_pairs={{0,4},{2,6},{4,0},{6,2},{1,5},{3,7},{5,1},{7,3},{8,12},{10,14},{12... | collective-permute-start | bytes 1572872 | tf_op jit(solution)/shard_map/ppermute | solution.py:476
  591.2 23.6 %collective-permute-start.12 = (bf16[256,1024]{1,0:T(8,128)(2,1)S(1)}, bf16[256,1024]{1,0:T(8,128)(2,1)S(1)}, u32[]{:S(2)}, u32[]{:S(2)}) collective-permute-start(bf16[256,1024]{1,0:T(8,128)(2,1)S(1)} %pad_maximum_fusion.8), channel_id=1, source_target_pairs={{0,6},{2,0},{4,2},{6,4},{1,7},{3,1},{5,3},{7,5},{8,14},{10,8},{12,... | collective-permute-start | bytes 1572872 | tf_op jit(solution)/shard_map/ppermute | solution.py:476
  595.8 19.4 %copy-start.16 = (bf16[1536,512]{1,0:T(8,128)(2,1)S(1)}, bf16[1536,512]{1,0:T(8,128)(2,1)}, u32[]{:S(2)}) copy-start(bf16[1536,512]{1,0:T(8,128)(2,1)} %param.24) | copy-start | bytes 4718596
  595.8 19.4 %copy-start.28 = (bf16[256,512]{1,0:T(8,128)(2,1)S(1)}, bf16[256,512]{1,0:T(8,128)(2,1)}, u32[]{:S(2)}) copy-start(bf16[256,512]{1,0:T(8,128)(2,1)} %get-tuple-element.68) | copy-start | bytes 786436
  650.7 64.4 %all-to-all-start.1 = ((bf16[5,128,1536]{2,0,1:T(8,128)(2,1)}), bf16[5,128,1536]{2,0,1:T(8,128)(2,1)}, u32[]{:S(2)}, u32[]{:S(2)}) async-start(bf16[5,128,1536]{2,0,1:T(8,128)(2,1)} %copy.125), calls=%async_computation.4 | async-start | bytes 6291456 | tf_op jit(solution)/shard_map/all_to_all | solution.py:458
  715.2 204.2 %all-to-all-start = ((bf16[5,384,1024]{2,0,1:T(8,128)(2,1)}), bf16[5,384,1024]{2,0,1:T(8,128)(2,1)}, u32[]{:S(2)}, u32[]{:S(2)}) async-start(bf16[5,384,1024]{2,0,1:T(8,128)(2,1)} %copy.123), calls=%async_computation.2 | async-start | bytes 12582912 | tf_op jit(solution)/shard_map/all_to_all | solution.py:458
  721.1 188.9 %all-reduce.4.cloned.1.call-start = ((), (), s32[]{:S(2)}) async-start(), calls=%async_computation.8 | async-start | bytes 2162688 | tf_op jit(solution)/shard_map/psum | solution.py:702
  (43 other events, 216.1 us)
Sparse Core Ops, SparseCore 0:
  32.3 24.1 all-gather.6
  58.9 72.9 all-gather.10
  133.8 71.8 all-gather.8
  266.7 33.5 reduce-scatter.6
  306.7 135.7 reduce-scatter.10
  444.7 263.1 reduce-scatter.8
  712.0 154.6 reduce-scatter.12
  869.1 40.8 all-reduce.3

commit v3 on v2

--- a/solution.py
+++ b/solution.py
@@ -479,6 +479,49 @@
         total = total + moved.astype(jnp.float32)
     total = total.astype(jnp.bfloat16)
     return (total[:, : d_key.shape[1]], total[:, d_key.shape[1] :])
+
+
+def fold_dense(grad, cut):
+    rows, width = grad.shape
+    parts = lax.axis_size("dp")
+    core = lax.axis_index("ctx") % 2
+    pair = lax.axis_index("ctx") // 2
+    side = lax.axis_index("expert")
+    take = partial(lax.dynamic_index_in_dim, keepdims=False)
+    grad = grad.reshape(parts, 2, 2, 2, rows // (8 * parts), width)
+    one = added(take(grad, core, 2), swap(take(grad, 1 - core, 2), "ctx", 1))
+    left, right = one[..., :cut], one[..., cut:]
+    left_sent = swap(take(left, 1 - pair, 1), "ctx", 2)
+    right_sent = swap(take(right, 1 - side, 2), "expert", 1)
+    left = added(take(left, pair, 1), left_sent)
+    right = added(take(right, side, 2), right_sent)
+    left_sent = swap(take(left, 1 - side, 1), "expert", 1)
+    right_sent = swap(take(right, 1 - pair, 1), "ctx", 2)
+    return jnp.concatenate(
+        [added(take(left, side, 1), left_sent), added(take(right, pair, 1), right_sent)], axis=-1
+    )
+
+
+def finish_dense(grad, folded):
+    if not folded:
+        return lax.psum(grad, "expert").astype(jnp.float32)
+    other = swap(grad, "expert", 1)
+    first = lax.axis_index("expert") == 0
+    return jnp.concatenate(
+        [jnp.where(first, grad, other), jnp.where(first, other, grad)], axis=0
+    ).astype(jnp.float32)
+
+
+def start_dense(grad, cut):
+    parts = lax.axis_size("dp")
+    folded = (
+        lax.axis_size("ctx") == 4
+        and lax.axis_size("expert") == 2
+        and grad.shape[0] % (64 * parts) == 0
+    )
+    if not folded:
+        return lax.psum_scatter(grad, ("dp", "ctx"), scatter_dimension=0, tiled=True), False
+    return lax.psum_scatter(fold_dense(grad, cut), "dp", scatter_dimension=0), True
 
 
 def per_device(
@@ -664,7 +707,10 @@
     d_resid_norm, grad_norm2 = rms_backward(resid, scale_two, gain_two, d_normed_two)
     d_resid = upstream + d_resid_norm
     d_branch = (RESID * d_resid).astype(jnp.bfloat16)
-    grad_out = jnp.einsum("tq,td->qd", merged_low, d_branch, preferred_element_type=jnp.float32)
+    grad_out = jnp.einsum(
+        "tq,td->qd", merged_low, d_branch, preferred_element_type=jnp.float32
+    ).astype(jnp.bfloat16)
+    grad_out = start_dense(grad_out, grad_out.shape[1] // 256 * 128)
     merged_gradient = jnp.einsum(
         "td,qd->tq", d_branch, w_out, preferred_element_type=jnp.float32
     ).astype(jnp.bfloat16)
@@ -694,27 +740,25 @@
     d_tokens = d_resid + d_tokens_norm
     dx_prompt = d_tokens[:prompt_rows][None]
     dx_cont = d_tokens[prompt_rows:].reshape(1, cont_count, cont_len, model_width)
-    wide = jnp.concatenate([grad_query, grad_key, grad_value, grad_out], axis=1)
     small = jnp.concatenate([grad_router, grad_norm1[:, None], grad_norm2[:, None]], axis=1)
     small = jnp.pad(small, ((0, 0), (0, -small.shape[1] % 128)))
-    dense = jnp.concatenate([wide, small], axis=1).astype(jnp.bfloat16)
-    dense = lax.psum_scatter(dense, ("dp", "ctx"), scatter_dimension=0, tiled=True)
-    dense = lax.psum(dense, "expert").astype(jnp.float32)
+    dense = jnp.concatenate([grad_query, grad_key, grad_value, small], axis=1).astype(jnp.bfloat16)
     heads_width = QUERY_HEADS * HEAD_SIZE
     edge = heads_width + 2 * key_value_width
-    tail = edge + w_out.shape[1]
+    dense = finish_dense(*start_dense(dense, edge // 256 * 128))
+    grad_out = finish_dense(*grad_out)
     return (
         y_prompt,
         y_cont,
         dx_prompt,
         dx_cont,
-        dense[:, tail + expert_total],
+        dense[:, edge + expert_total],
         dense[:, :heads_width],
         dense[:, heads_width : heads_width + key_value_width],
         dense[:, heads_width + key_value_width : edge],
-        dense[:, edge:tail],
-        dense[:, tail + expert_total + 1],
-        dense[:, tail : tail + expert_total],
+        grad_out,
+        dense[:, edge + expert_total + 1],
+        dense[:, edge : edge + expert_total],
         grad_gate_up,
         grad_down,
     )

time: 951 us -> 853 us (0.90)
  waiting for transfers between devices: 329 us -> 228 us
  other arithmetic: 97.8 us -> 112 us
  local copies, waits for them, and re-layouts: 95.4 us -> 82 us
  starting transfers between devices: 22.2 us -> 34.8 us
  matrix products: 175 us -> 164 us
    unnamed x9 -> x8, waiting for transfers between devices: 139 us -> 0.13 us
    ppermute x10 -> x22, waiting for transfers between devices: 46.8 us -> 120 us  [swap(): return lax.ppermute(values, axis, [(i, i ^ bit) for i in range(size)])]
    reduce_scatter x2, waiting for transfers between devices: 47.2 us -> 0.01 us  [reduce_experts(): part = lax.psum_scatter(grad, 'dp', scatter_dimension=1, tiled=True)]
    all_to_all x2, waiting for transfers between devices: 0.01 us -> 41.9 us  [reduce_experts(): lax.all_to_all(part, 'ctx', split_axis=1, concat_axis=0, tiled=True)]
    psum x1 -> x0, waiting for transfers between devices: 30.3 us -> none  [per_device(): dense = lax.psum(dense, 'expert').astype(jnp.float32)]
    unnamed x110 -> x132, local copies, waits for them, and re-layouts: 32.9 us -> 13.3 us
    dot_general x1, matrix products: 13.8 us -> 3.85 us  [per_device(): jnp.einsum('td,qd->tq', d_branch, w_out, preferred_element_type=jnp.float32)]
    convert_element_type x4 -> x14, other arithmetic: 22.9 us -> 32.7 us  [added(): (left.astype(jnp.float32) + right.astype(jnp.float32)).astype(jnp.bfloat16)]
  transfers between devices with their start and end apart: 23 -> 35, of which waited for: 12 -> 18; matrix products, arithmetic and copies ran while one was open for 30% -> 32% of each run, Pallas kernels for 18% -> 20%
where the time goes in v3:
time: 853 us; the launch traced here: 841 us
  waiting for transfers between devices  228 us (27%)
  Pallas kernels  186 us (22%)
  matrix products  164 us (19%)
  other arithmetic  112 us (13%)
  local copies, waits for them, and re-layouts  82 us (10%)
  starting transfers between devices  34.8 us (4%)
  blocking collectives  18.9 us (2%)
  between operations  15.5 us (2%)
    ppermute x22, waiting for transfers between devices, swap(): return lax.ppermute(values, axis, [(i, i ^ bit) for i in range(size)])  120 us
    pallas_call x1, Pallas kernels, attend_backward(): pl.pallas_call(partial(attend_backward_body, group, rows, cont_len, chunk...  63.8 us
    pallas_call x1, Pallas kernels, attend_forward(): pl.pallas_call(partial(attend_forward_body, group, rows, cont_len), grid_...  53.7 us
    all_to_all x2, waiting for transfers between devices, reduce_experts(): lax.all_to_all(part, 'ctx', split_axis=1, concat_axis=0, tiled=True)  41.9 us
    pallas_call x4, Pallas kernels, combine(): pl.pallas_call(partial(combine_body, own, slots), grid_spec=pltpu.Prefetc...  39.5 us
    all_gather x1, waiting for transfers between devices, per_device(): rows_all = lax.all_gather(h2_low, group, axis=0, tiled=False)  34.7 us
    convert_element_type x14, other arithmetic, added(): (left.astype(jnp.float32) + right.astype(jnp.float32)).astype(jnp.bfloat16)  32.7 us
    pallas_call x2, Pallas kernels, dispatch(): pl.pallas_call(partial(dispatch_body, own, slots), grid=(blocks,), in_spe...  28.8 us
  transfers between devices with their start and end apart: 35, of which 18 were waited for; matrix products, arithmetic and copies ran while one was open for 32% of the time, Pallas kernels for 20%

profile of v3, /device:TPU:9, one launch (start us, length us, event | category | flops | bytes accessed | tf_op | source)
XLA Modules:
  0.0 841.2 jit_solution(14074637170407586003)
XLA Ops:
  45.1 11.2 %all-gather.7.cloned.1.call-done = bf16[2,1024,512]{2,1,0:T(8,128)(2,1)} async-done(((bf16[2,256,512]{2,1,0:T(8,128)(2,1)}), bf16[2,1024,512]{2,1,0:T(8,128)(2,1)}) %all-gather.7.cloned.1.call-update) | async-done | bytes 2097168 | tf_op jit(solution)/shard_map/all_gather | solution.py:617
  59.4 53.7 %attend_forward.1 = (bf16[512,1536]{1,0:T(8,128)(2,1)}, bf16[512,1536]{1,0:T(8,128)(2,1)}, f32[24,8,512]{2,1,0:T(8,128)}) custom-call(s32[1]{0:T(128)} %bitcast.2.pos_ref, f32[512,1536]{1,0:T(8,128)} %fusion.92.q_ref, f32[512,128]{1,0:T(8,128)} %copy.151.cos_ref, f32[512,128]{1,0:T(8,128)} %copy.152.sin_ref, bf16[1024,512]{1,0:T(8,128)(2,1)} %get-tuple-element.181.kp_ref, ...), custom_call_target="tpu_custom_call" | custom-call | flops 8053063680 | bytes 6291456 | tf_op jit(solution)/shard_map/attend_forward/pallas_call | solution.py:271
  122.6 18.9 %all-gather = f32[320,512]{1,0:T(8,128)S(1)} all-gather(f32[40,512]{1,0:T(8,128)S(1)} %fusion.54), channel_id=2, replica_groups=mesh['dp'=4,'ctx'=4,'expert'=2] {'ctx','expert'}, dimensions={0}, use_global_device_ids=true | all-gather | bytes 737280 | tf_op jit(solution)/shard_map/all_gather | solution.py:576
  142.2 14.7 %dispatch.2 = bf16[5,832,1536]{2,1,0:T(8,128)(2,1)} custom-call(f32[8,8,512]{2,1,0:T(8,128)} %pad.9.codes_ref, bf16[8,512,1536]{2,1,0:T(8,128)(2,1)} %bitcast.185), custom_call_target="tpu_custom_call" | custom-call | flops 6543114240 | bytes 25362432 | tf_op jit(solution)/shard_map/dispatch/pallas_call | solution.py:85
  156.9 14.1 %fusion.13 = f32[5,832,512]{2,1,0:T(8,128)} fusion(bf16[5,832,1536]{2,1,0:T(8,128)(2,1)} %dispatch.2, bf16[20,512,1536]{2,1,0:T(8,128)(2,1)} %param.30, s32[]{:T(128)S(6)} %select_n.205), kind=kOutput, calls=%fused_computation.29 | convolution fusion | flops 6543114240 | bytes 29163524 | tf_op jit(solution)/shard_map/ecd,efd->ecf/dot_general | solution.py:585
  171.0 34.7 %all-gather.9.cloned.1.call-done = bf16[4096,1536]{1,0:T(8,128)(2,1)} async-done(((bf16[512,1536]{1,0:T(8,128)(2,1)}), bf16[4096,1536]{1,0:T(8,128)(2,1)}) %all-gather.9.cloned.1.call-update) | async-done | bytes 12582928 | tf_op jit(solution)/shard_map/all_gather | solution.py:633
  205.7 14.2 %dispatch.3 = bf16[5,832,1536]{2,1,0:T(8,128)(2,1)} custom-call(f32[8,8,512]{2,1,0:T(8,128)} %pad.9.codes_ref, bf16[8,512,1536]{2,1,0:T(8,128)(2,1)} %bitcast.179), custom_call_target="tpu_custom_call" | custom-call | flops 6543114240 | bytes 25362432 | tf_op jit(solution)/shard_map/dispatch/pallas_call | solution.py:85
  219.8 8.4 fusion.102
  229.2 23.1 %fusion.3 = f32[5,832,1024]{2,1,0:T(8,128)} fusion(bf16[5,832,1536]{2,1,0:T(8,128)(2,1)} %dispatch.3, bf16[20,1536,1024]{2,1,0:T(8,128)(2,1)} %param.29, s32[]{:T(128)S(6)} %select_n.205), kind=kOutput, calls=%fused_computation.3 | convolution fusion | flops 13086228480 | bytes 45547524 | tf_op jit(solution)/shard_map/ecd,edf->ecf/dot_general | solution.py:647
  252.3 9.7 %multiply_reduce_fusion = f32[5,832]{1,0:T(8,128)S(1)} fusion(f32[5,832,512]{2,1,0:T(8,128)} %fusion.13, f32[5,832,1024]{2,1,0:T(8,128)} %fusion.3), kind=kLoop, calls=%fused_computation.16 | loop fusion | flops 14905280 | bytes 25575680 | tf_op jit(solution)/shard_map/reduce_sum | solution.py:654
  266.4 14.3 %multiply_convert_fusion.2 = (bf16[5,832,512]{2,1,0:T(8,128)(2,1)}, bf16[5,832,512]{2,1,0:T(8,128)(2,1)}, bf16[5,832,512]{2,1,0:T(8,128)(2,1)S(1)}) fusion(f32[5,832,1024]{2,1,0:T(8,128)} %fusion.3, f32[5,832,512]{2,1,0:T(8,128)} %fusion.13, f32[5,832]{1,0:T(8,128)S(1)} %mul.307), kind=kLoop, calls=%fused_computation.19 | loop fusion | flops 36208640 | bytes 38355200 | tf_op jit(solution)/shard_map/convert.33
  282.7 15.2 %convolution_convert_fusion.4 = bf16[5,512,1536]{2,1,0:T(8,128)(2,1)} fusion(bf16[5,832,512]{2,1,0:T(8,128)(2,1)S(1)} %get-tuple-element.51, bf16[5,832,1536]{2,1,0:T(8,128)(2,1)} %dispatch.2), kind=kOutput, calls=%fused_computation.32 | convolution fusion | flops 6547046400 | bytes 24903680 | tf_op jit(solution)/shard_map/ecf,ecd->efd/dot_general | solution.py:659
  297.9 8.3 pad_maximum_fusion
  307.4 20.9 %fusion.5.rows_ref = bf16[5,832,1536]{2,1,0:T(8,128)(2,1)} fusion(bf16[5,832,1024]{2,1,0:T(8,128)(2,1)} %pad_maximum_fusion, bf16[20,1536,1024]{2,1,0:T(8,128)(2,1)} %param.29, s32[]{:T(128)S(6)} %select_n.205), kind=kOutput, calls=%fused_computation.10 | convolution fusion | flops 13092618240 | bytes 37027844 | tf_op jit(solution)/shard_map/ecf,edf->ecd/dot_general | solution.py:664
  328.3 9.9 %combine.5 = bf16[4,512,1536]{2,1,0:T(8,128)(2,1)} custom-call(s32[4]{0:T(128)} %broadcast_xor_fusion.at_ref, f32[8,8,512]{2,1,0:T(8,128)} %pad.9.codes_ref, bf16[5,832,1536]{2,1,0:T(8,128)(2,1)} %fusion.5.rows_ref), custom_call_target="tpu_custom_call" | custom-call | flops 3271557120 | bytes 12681216 | tf_op jit(solution)/shard_map/combine/pallas_call | solution.py:114
  339.0 9.7 %combine.4 = bf16[4,512,1536]{2,1,0:T(8,128)(2,1)} custom-call(s32[4]{0:T(128)} %broadcast_xor_fusion.1.at_ref, f32[8,8,512]{2,1,0:T(8,128)} %pad.9.codes_ref, bf16[5,832,1536]{2,1,0:T(8,128)(2,1)} %fusion.5.rows_ref), custom_call_target="tpu_custom_call" | custom-call | flops 3271557120 | bytes 12681216 | tf_op jit(solution)/shard_map/combine/pallas_call | solution.py:114
  348.8 9.0 %add_convert_fusion.1 = bf16[4,512,1536]{2,1,0:T(8,128)(2,1)} fusion(bf16[4,512,1536]{2,1,0:T(8,128)(2,1)} %collective-permute-done, bf16[4,512,1536]{2,1,0:T(8,128)(2,1)} %combine.4), kind=kLoop, calls=%fused_computation.8 | loop fusion | flops 12582912 | bytes 18874368 | tf_op jit(solution)/shard_map/convert_element_type | solution.py:141
  357.8 24.3 %convolution_convert_fusion = bf16[5,1536,1024]{2,1,0:T(8,128)(2,1)} fusion(bf16[5,832,1536]{2,1,0:T(8,128)(2,1)} %dispatch.3, bf16[5,832,1024]{2,1,0:T(8,128)(2,1)} %pad_maximum_fusion), kind=kOutput, calls=%fused_computation.5 | convolution fusion | flops 13094092800 | bytes 37027840 | tf_op jit(solution)/shard_map/ecd,ecf->edf/dot_general | solution.py:670
  386.6 34.5 %collective-permute-done.2 = bf16[2,512,768]{2,1,0:T(8,128)(2,1)S(1)} collective-permute-done((bf16[2,512,768]{2,1,0:T(8,128)(2,1)S(1)}, bf16[2,512,768]{2,1,0:T(8,128)(2,1)S(1)}, u32[]{:S(2)}, u32[]{:S(2)}) %collective-permute-start.2) | collective-permute-done | bytes 1572896 | tf_op jit(solution)/shard_map/ppermute | solution.py:137
  422.2 13.5 %convolution_convert_fusion.1.rows_ref = bf16[5,832,1536]{2,1,0:T(8,128)(2,1)} fusion(bf16[5,832,512]{2,1,0:T(8,128)(2,1)} %copy-done.7, bf16[20,512,1536]{2,1,0:T(8,128)(2,1)} %param.30, s32[]{:T(128)S(6)} %select_n.205), kind=kOutput, calls=%fused_computation.9 | convolution fusion | flops 6549504000 | bytes 24903684 | tf_op jit(solution)/shard_map/ecf,efd->ecd/dot_general | solution.py:675
  435.7 10.0 %combine.7 = bf16[4,512,1536]{2,1,0:T(8,128)(2,1)} custom-call(s32[4]{0:T(128)} %broadcast_xor_fusion.at_ref, f32[8,8,512]{2,1,0:T(8,128)} %pad.9.codes_ref, bf16[5,832,1536]{2,1,0:T(8,128)(2,1)} %convolution_convert_fusion.1.rows_ref), custom_call_target="tpu_custom_call" | custom-call | flops 3271557120 | bytes 12681216 | tf_op jit(solution)/shard_map/combine/pallas_call | solution.py:114
  460.7 9.9 %combine.6 = bf16[4,512,1536]{2,1,0:T(8,128)(2,1)} custom-call(s32[4]{0:T(128)} %broadcast_xor_fusion.1.at_ref, f32[8,8,512]{2,1,0:T(8,128)} %pad.9.codes_ref, bf16[5,832,1536]{2,1,0:T(8,128)(2,1)} %convolution_convert_fusion.1.rows_ref), custom_call_target="tpu_custom_call" | custom-call | flops 3271557120 | bytes 12681216 | tf_op jit(solution)/shard_map/combine/pallas_call | solution.py:114
  470.6 9.3 %add_convert_fusion = bf16[4,512,1536]{2,1,0:T(8,128)(2,1)} fusion(bf16[4,512,1536]{2,1,0:T(8,128)(2,1)} %collective-permute-done.5, bf16[4,512,1536]{2,1,0:T(8,128)(2,1)} %combine.6), kind=kLoop, calls=%fused_computation.7 | loop fusion | flops 12582912 | bytes 18874368 | tf_op jit(solution)/shard_map/convert_element_type | solution.py:141
  497.1 63.8 %attend_backward.1 = (bf16[512,1536]{1,0:T(8,128)(2,1)}, bf16[1024,512]{1,0:T(8,128)(2,1)}, bf16[1024,512]{1,0:T(8,128)(2,1)}, bf16[256,512]{1,0:T(8,128)(2,1)}, bf16[256,512]{1,0:T(8,128)(2,1)}) custom-call(s32[1]{0:T(128)} %bitcast.2.pos_ref, bf16[512,1536]{1,0:T(8,128)(2,1)} %get-tuple-element.56.q_ref, ...), custom_call_target="tpu_custom_call" | custom-call | flops 20132659200 | bytes 6291456 | tf_op jit(solution)/shard_map/attend_backward/pallas_call | solution.py:402
  570.1 11.3 %collective-permute-done.9 = bf16[512,768]{1,0:T(8,128)(2,1)S(1)} collective-permute-done((bf16[512,768]{1,0:T(8,128)(2,1)S(1)}, bf16[512,768]{1,0:T(8,128)(2,1)S(1)}, u32[]{:S(2)}, u32[]{:S(2)}) %collective-permute-start.9) | collective-permute-done | bytes 786464 | tf_op jit(solution)/shard_map/ppermute | solution.py:137
  595.9 13.2 %collective-permute-done.11 = bf16[256,1024]{1,0:T(8,128)(2,1)S(1)} collective-permute-done((bf16[256,1024]{1,0:T(8,128)(2,1)S(1)}, bf16[256,1024]{1,0:T(8,128)(2,1)S(1)}, u32[]{:S(2)}, u32[]{:S(2)}) %collective-permute-start.11) | collective-permute-done | bytes 524320 | tf_op jit(solution)/shard_map/ppermute | solution.py:476
  646.4 8.6 %collective-permute-done.22 = bf16[4,2,48,768]{3,2,0,1:T(8,128)(2,1)S(1)} collective-permute-done((bf16[4,2,48,768]{3,2,0,1:T(8,128)(2,1)S(1)}, bf16[4,2,48,768]{3,2,0,1:T(8,128)(2,1)S(1)}, u32[]{:S(2)}, u32[]{:S(2)}) %collective-permute-start.22) | collective-permute-done | bytes 589856 | tf_op jit(solution)/shard_map/ppermute | solution.py:137
  660.2 24.7 %collective-permute-done.20 = bf16[4,2,48,768]{3,2,0,1:T(8,128)(2,1)S(1)} collective-permute-done((bf16[4,2,48,768]{3,2,0,1:T(8,128)(2,1)S(1)}, bf16[4,2,48,768]{3,2,0,1:T(8,128)(2,1)S(1)}, u32[]{:S(2)}, u32[]{:S(2)}) %collective-permute-start.20) | collective-permute-done | bytes 589856 | tf_op jit(solution)/shard_map/ppermute | solution.py:137
  692.4 19.7 %collective-permute-done.14 = bf16[4,2,48,1280]{3,2,1,0:T(8,128)(2,1)S(1)} collective-permute-done((bf16[4,2,48,1280]{3,2,1,0:T(8,128)(2,1)S(1)}, bf16[4,2,48,1280]{3,2,1,0:T(8,128)(2,1)S(1)}, u32[]{:S(2)}, u32[]{:S(2)}) %collective-permute-start.14) | collective-permute-done | bytes 983072 | tf_op jit(solution)/shard_map/ppermute | solution.py:137
  718.7 8.2 collective-permute-done.15
  743.5 8.7 %all-to-all-start = ((bf16[5,384,1024]{2,0,1:T(8,128)(2,1)}), bf16[5,384,1024]{2,0,1:T(8,128)(2,1)}, u32[]{:S(2)}, u32[]{:S(2)}) async-start(bf16[5,384,1024]{2,0,1:T(8,128)(2,1)} %copy.163), calls=%async_computation.4 | async-start | bytes 12582912 | tf_op jit(solution)/shard_map/all_to_all | solution.py:458
  780.1 41.9 %all-to-all-done = bf16[5,384,1024]{2,0,1:T(8,128)(2,1)} async-done(((bf16[5,384,1024]{2,0,1:T(8,128)(2,1)}), bf16[5,384,1024]{2,0,1:T(8,128)(2,1)}, u32[]{:S(2)}, u32[]{:S(2)}) %all-to-all-start) | async-done | bytes 3932192 | tf_op jit(solution)/shard_map/all_to_all | solution.py:458
  (343 shorter events, 234.2 us)
Async XLA Ops:
  7.2 49.2 %all-gather.7.cloned.1.call-start = ((), (), s32[]{:S(2)}) async-start(), calls=%async_computation.7 | async-start | bytes 2621440 | tf_op jit(solution)/shard_map/all_gather | solution.py:617
  32.1 110.1 %all-gather.11.cloned.1.call-start = ((), (), s32[]{:S(2)}) async-start(), calls=%async_computation.14 | async-start | bytes 14155776 | tf_op jit(solution)/shard_map/all_gather | solution.py:583
  34.9 170.8 %all-gather.9.cloned.1.call-start = ((), (), s32[]{:S(2)}) async-start(), calls=%async_computation.13 | async-start | bytes 14155776 | tf_op jit(solution)/shard_map/all_gather | solution.py:633
  121.5 332.3 %reduce-scatter.6.cloned.1.call-start = ((), (), s32[]{:S(2)}) async-start(), calls=%async_computation.8 | async-start | bytes 737280 | tf_op jit(solution)/shard_map/reduce_scatter | solution.py:689
  266.3 360.4 %reduce-scatter.14.cloned.1.call-start = ((), (), s32[]{:S(2)}) async-start(), calls=%async_computation.12 | async-start | bytes 9830400 | tf_op jit(solution)/shard_map/reduce_scatter | solution.py:457
  306.3 429.9 %reduce-scatter.12.cloned.1.call-start = ((), (), s32[]{:S(2)}) async-start(), calls=%async_computation.11 | async-start | bytes 19660800 | tf_op jit(solution)/shard_map/reduce_scatter | solution.py:457
  385.2 35.9 %collective-permute-start.2 = (bf16[2,512,768]{2,1,0:T(8,128)(2,1)S(1)}, bf16[2,512,768]{2,1,0:T(8,128)(2,1)S(1)}, u32[]{:S(2)}, u32[]{:S(2)}) collective-permute-start(bf16[2,512,768]{2,1,0:T(8,128)(2,1)S(1)} %pad_maximum_fusion.4), channel_id=1, source_target_pairs={{0,1},{1,0},{2,3},{3,2},{4,5},{5,4},{6,7},{7,6},{8,9},{9,8},{10,11... | collective-permute-start | bytes 4718600 | tf_op jit(solution)/shard_map/ppermute | solution.py:137
  385.8 36.4 %collective-permute-start.1 = (bf16[2,512,768]{2,1,0:T(8,128)(2,1)S(1)}, bf16[2,512,768]{2,1,0:T(8,128)(2,1)}, u32[]{:S(2)}, u32[]{:S(2)}) collective-permute-start(bf16[2,512,768]{2,1,0:T(8,128)(2,1)S(1)} %slice.188), channel_id=1, source_target_pairs={{0,4},{2,6},{4,0},{6,2},{1,5},{3,7},{5,1},{7,3},{8,12},{10,14},{12... | collective-permute-start | bytes 4718600 | tf_op jit(solution)/shard_map/ppermute | solution.py:137
  445.7 24.9 %collective-permute-start.5 = (bf16[4,512,1536]{2,1,0:T(8,128)(2,1)}, bf16[4,512,1536]{2,1,0:T(8,128)(2,1)}, u32[]{:S(2)}, u32[]{:S(2)}) collective-permute-start(bf16[4,512,1536]{2,1,0:T(8,128)(2,1)} %combine.7), channel_id=1, source_target_pairs={{0,2},{2,0},{4,6},{6,4},{1,3},{3,1},{5,7},{7,5},{8,10},{10,8},{12,... | collective-permute-start | bytes 18874376 | tf_op jit(solution)/shard_map/ppermute | solution.py:137
  458.9 20.9 %collective-permute-start.4 = (bf16[512,768]{1,0:T(8,128)(2,1)S(1)}, bf16[512,768]{1,0:T(8,128)(2,1)}, u32[]{:S(2)}, u32[]{:S(2)}) collective-permute-start(bf16[512,768]{1,0:T(8,128)(2,1)S(1)} %get-tuple-element.170), channel_id=1, source_target_pairs={{0,4},{2,6},{4,0},{6,2},{1,5},{3,7},{5,1},{7,3},{8,12},{10,14},{12... | collective-permute-start | bytes 2359304 | tf_op jit(solution)/shard_map/ppermute | solution.py:137
  460.2 19.7 %collective-permute-start.3 = (bf16[512,768]{1,0:T(8,128)(2,1)S(1)}, bf16[512,768]{1,0:T(8,128)(2,1)}, u32[]{:S(2)}, u32[]{:S(2)}) collective-permute-start(bf16[512,768]{1,0:T(8,128)(2,1)S(1)} %get-tuple-element.171), channel_id=1, source_target_pairs={{0,1},{1,0},{2,3},{3,2},{4,5},{5,4},{6,7},{7,6},{8,9},{9,8},{10,11... | collective-permute-start | bytes 2359304 | tf_op jit(solution)/shard_map/ppermute | solution.py:137
  491.3 69.5 %collective-permute-start.7 = (bf16[2,512,768]{2,1,0:T(8,128)(2,1)}, bf16[2,512,768]{2,1,0:T(8,128)(2,1)}, u32[]{:S(2)}, u32[]{:S(2)}) collective-permute-start(bf16[2,512,768]{2,1,0:T(8,128)(2,1)} %pad_maximum_fusion.5), channel_id=1, source_target_pairs={{0,1},{1,0},{2,3},{3,2},{4,5},{5,4},{6,7},{7,6},{8,9},{9,8},{10,11... | collective-permute-start | bytes 4718600 | tf_op jit(solution)/shard_map/ppermute | solution.py:137
  492.3 68.6 %collective-permute-start.6 = (bf16[2,512,768]{2,1,0:T(8,128)(2,1)S(1)}, bf16[2,512,768]{2,1,0:T(8,128)(2,1)}, u32[]{:S(2)}, u32[]{:S(2)}) collective-permute-start(bf16[2,512,768]{2,1,0:T(8,128)(2,1)S(1)} %slice.199), channel_id=1, source_target_pairs={{0,4},{2,6},{4,0},{6,2},{1,5},{3,7},{5,1},{7,3},{8,12},{10,14},{12... | collective-permute-start | bytes 4718600 | tf_op jit(solution)/shard_map/ppermute | solution.py:137
  563.3 18.1 %collective-permute-start.9 = (bf16[512,768]{1,0:T(8,128)(2,1)S(1)}, bf16[512,768]{1,0:T(8,128)(2,1)S(1)}, u32[]{:S(2)}, u32[]{:S(2)}) collective-permute-start(bf16[512,768]{1,0:T(8,128)(2,1)S(1)} %get-tuple-element.164), channel_id=1, source_target_pairs={{0,4},{2,6},{4,0},{6,2},{1,5},{3,7},{5,1},{7,3},{8,12},{10,14},{12... | collective-permute-start | bytes 2359304 | tf_op jit(solution)/shard_map/ppermute | solution.py:137
  564.5 17.8 %collective-permute-start.8 = (bf16[512,768]{1,0:T(8,128)(2,1)S(1)}, bf16[512,768]{1,0:T(8,128)(2,1)S(1)}, u32[]{:S(2)}, u32[]{:S(2)}) collective-permute-start(bf16[512,768]{1,0:T(8,128)(2,1)S(1)} %get-tuple-element.165), channel_id=1, source_target_pairs={{0,1},{1,0},{2,3},{3,2},{4,5},{5,4},{6,7},{7,6},{8,9},{9,8},{10,11... | collective-permute-start | bytes 2359304 | tf_op jit(solution)/shard_map/ppermute | solution.py:137
  582.4 13.5 %collective-permute-start.10 = (bf16[256,1024]{1,0:T(8,128)(2,1)S(1)}, bf16[256,1024]{1,0:T(8,128)(2,1)S(1)}, u32[]{:S(2)}, u32[]{:S(2)}) collective-permute-start(bf16[256,1024]{1,0:T(8,128)(2,1)S(1)} %pad_maximum_fusion.9), channel_id=1, source_target_pairs={{0,2},{2,4},{4,6},{6,0},{1,3},{3,5},{5,7},{7,1},{8,10},{10,12},{12... | collective-permute-start | bytes 1572872 | tf_op jit(solution)/shard_map/ppermute | solution.py:476
  584.9 24.2 %collective-permute-start.11 = (bf16[256,1024]{1,0:T(8,128)(2,1)S(1)}, bf16[256,1024]{1,0:T(8,128)(2,1)S(1)}, u32[]{:S(2)}, u32[]{:S(2)}) collective-permute-start(bf16[256,1024]{1,0:T(8,128)(2,1)S(1)} %pad_maximum_fusion.10), channel_id=1, source_target_pairs={{0,4},{2,6},{4,0},{6,2},{1,5},{3,7},{5,1},{7,3},{8,12},{10,14},{12... | collective-permute-start | bytes 1572872 | tf_op jit(solution)/shard_map/ppermute | solution.py:476
  586.2 23.6 %collective-permute-start.12 = (bf16[256,1024]{1,0:T(8,128)(2,1)S(1)}, bf16[256,1024]{1,0:T(8,128)(2,1)S(1)}, u32[]{:S(2)}, u32[]{:S(2)}) collective-permute-start(bf16[256,1024]{1,0:T(8,128)(2,1)S(1)} %pad_maximum_fusion.11), channel_id=1, source_target_pairs={{0,6},{2,0},{4,2},{6,4},{1,7},{3,1},{5,3},{7,5},{8,14},{10,8},{12,... | collective-permute-start | bytes 1572872 | tf_op jit(solution)/shard_map/ppermute | solution.py:476
  589.9 46.7 %collective-permute-start.19 = (bf16[4,2,2,48,1536]{4,3,0,1,2:T(8,128)(2,1)}, bf16[4,2,2,48,1536]{4,3,0,1,2:T(8,128)(2,1)}, u32[]{:S(2)}, u32[]{:S(2)}) collective-permute-start(bf16[4,2,2,48,1536]{4,3,0,1,2:T(8,128)(2,1)} %bitcast.178), channel_id=1, source_target_pairs={{0,2},{2,0},{4,6},{6,4},{1,3},{3,1},{5,7},{7,5},{8,10},{10,8},{12,... | collective-permute-start | bytes 7077896 | tf_op jit(solution)/shard_map/ppermute | solution.py:137
  626.7 29.5 %collective-permute-start.13 = (bf16[4,2,2,48,2688]{4,3,2,1,0:T(8,128)(2,1)}, bf16[4,2,2,48,2688]{4,3,2,1,0:T(8,128)(2,1)}, u32[]{:S(2)}, u32[]{:S(2)}) collective-permute-start(bf16[4,2,2,48,2688]{4,3,2,1,0:T(8,128)(2,1)} %dynamic-slice_bitcast_fusion), channel_id=1, source_target_pairs={{0,2},{2,0},{4,6},{6,4},{1,3},{3,1},{5,7},{7,5},{8,10},{10,8},{12,... | collective-permute-start | bytes 12386312 | tf_op jit(solution)/shard_map/ppermute | solution.py:137
  631.1 112.4 %all-to-all-start.1 = ((bf16[5,128,1536]{2,0,1:T(8,128)(2,1)}), bf16[5,128,1536]{2,0,1:T(8,128)(2,1)}, u32[]{:S(2)}, u32[]{:S(2)}) async-start(bf16[5,128,1536]{2,0,1:T(8,128)(2,1)} %copy.165), calls=%async_computation.6 | async-start | bytes 6291456 | tf_op jit(solution)/shard_map/all_to_all | solution.py:458
  636.2 119.8 %reduce-scatter.10.cloned.1.call-start = ((), (), s32[]{:S(2)}) async-start(), calls=%async_computation.10 | async-start | bytes 737280 | tf_op jit(solution)/shard_map/reduce_scatter | solution.py:524
  640.0 15.0 %collective-permute-start.22 = (bf16[4,2,48,768]{3,2,0,1:T(8,128)(2,1)S(1)}, bf16[4,2,48,768]{3,2,0,1:T(8,128)(2,1)S(1)}, u32[]{:S(2)}, u32[]{:S(2)}) collective-permute-start(bf16[4,2,48,768]{3,2,0,1:T(8,128)(2,1)S(1)} %dynamic-slice_bitcast_fusion.3), channel_id=1, source_target_pairs={{0,1},{1,0},{2,3},{3,2},{4,5},{5,4},{6,7},{7,6},{8,9},{9,8},{10,11... | collective-permute-start | bytes 1769480 | tf_op jit(solution)/shard_map/ppermute | solution.py:137
  640.6 44.3 %collective-permute-start.20 = (bf16[4,2,48,768]{3,2,0,1:T(8,128)(2,1)S(1)}, bf16[4,2,48,768]{3,2,0,1:T(8,128)(2,1)S(1)}, u32[]{:S(2)}, u32[]{:S(2)}) collective-permute-start(bf16[4,2,48,768]{3,2,0,1:T(8,128)(2,1)S(1)} %dynamic-slice_bitcast_fusion.4), channel_id=1, source_target_pairs={{0,4},{2,6},{4,0},{6,2},{1,5},{3,7},{5,1},{7,3},{8,12},{10,14},{12... | collective-permute-start | bytes 1769480 | tf_op jit(solution)/shard_map/ppermute | solution.py:137
  655.1 36.1 %collective-permute-start.23 = (bf16[4,48,768]{2,1,0:T(8,128)(2,1)S(1)}, bf16[4,48,768]{2,1,0:T(8,128)(2,1)S(1)}, u32[]{:S(2)}, u32[]{:S(2)}) collective-permute-start(bf16[4,48,768]{2,1,0:T(8,128)(2,1)S(1)} %dynamic-slice_bitcast_fusion.7), channel_id=1, source_target_pairs={{0,4},{2,6},{4,0},{6,2},{1,5},{3,7},{5,1},{7,3},{8,12},{10,14},{12... | collective-permute-start | bytes 884744 | tf_op jit(solution)/shard_map/ppermute | solution.py:137
  659.7 52.5 %collective-permute-start.14 = (bf16[4,2,48,1280]{3,2,1,0:T(8,128)(2,1)S(1)}, bf16[4,2,48,1280]{3,2,1,0:T(8,128)(2,1)S(1)}, u32[]{:S(2)}, u32[]{:S(2)}) collective-permute-start(bf16[4,2,48,1280]{3,2,1,0:T(8,128)(2,1)S(1)} %dynamic-slice_bitcast_fusion.2), channel_id=1, source_target_pairs={{0,4},{2,6},{4,0},{6,2},{1,5},{3,7},{5,1},{7,3},{8,12},{10,14},{12... | collective-permute-start | bytes 2949128 | tf_op jit(solution)/shard_map/ppermute | solution.py:137
  685.9 29.5 %collective-permute-start.16 = (bf16[4,2,48,1408]{3,2,1,0:T(8,128)(2,1)S(1)}, bf16[4,2,48,1408]{3,2,1,0:T(8,128)(2,1)S(1)}, u32[]{:S(2)}, u32[]{:S(2)}) collective-permute-start(bf16[4,2,48,1408]{3,2,1,0:T(8,128)(2,1)S(1)} %dynamic-slice_bitcast_fusion.1), channel_id=1, source_target_pairs={{0,1},{1,0},{2,3},{3,2},{4,5},{5,4},{6,7},{7,6},{8,9},{9,8},{10,11... | collective-permute-start | bytes 3244040 | tf_op jit(solution)/shard_map/ppermute | solution.py:137
  713.3 13.6 %collective-permute-start.15 = (bf16[4,48,1280]{2,1,0:T(8,128)(2,1)}, bf16[4,48,1280]{2,1,0:T(8,128)(2,1)}, u32[]{:S(2)}, u32[]{:S(2)}) collective-permute-start(bf16[4,48,1280]{2,1,0:T(8,128)(2,1)} %dynamic-slice_bitcast_fusion.6), channel_id=1, source_target_pairs={{0,1},{1,0},{2,3},{3,2},{4,5},{5,4},{6,7},{7,6},{8,9},{9,8},{10,11... | collective-permute-start | bytes 1474568 | tf_op jit(solution)/shard_map/ppermute | solution.py:137
  716.6 11.7 %collective-permute-start.17 = (bf16[4,48,1408]{2,1,0:T(8,128)(2,1)}, bf16[4,48,1408]{2,1,0:T(8,128)(2,1)}, u32[]{:S(2)}, u32[]{:S(2)}) collective-permute-start(bf16[4,48,1408]{2,1,0:T(8,128)(2,1)} %dynamic-slice_bitcast_fusion.5), channel_id=1, source_target_pairs={{0,4},{2,6},{4,0},{6,2},{1,5},{3,7},{5,1},{7,3},{8,12},{10,14},{12... | collective-permute-start | bytes 1622024 | tf_op jit(solution)/shard_map/ppermute | solution.py:137
  718.6 50.2 %reduce-scatter.8.cloned.1.call-start = ((), (), s32[]{:S(2)}) async-start(), calls=%async_computation.9 | async-start | bytes 1290240 | tf_op jit(solution)/shard_map/reduce_scatter | solution.py:524
  743.5 78.5 %all-to-all-start = ((bf16[5,384,1024]{2,0,1:T(8,128)(2,1)}), bf16[5,384,1024]{2,0,1:T(8,128)(2,1)}, u32[]{:S(2)}, u32[]{:S(2)}) async-start(bf16[5,384,1024]{2,0,1:T(8,128)(2,1)} %copy.163), calls=%async_computation.4 | async-start | bytes 12582912 | tf_op jit(solution)/shard_map/all_to_all | solution.py:458
  756.0 14.0 %collective-permute-start.24 = (bf16[48,1536]{1,0:T(8,128)(2,1)}, bf16[48,1536]{1,0:T(8,128)(2,1)S(1)}, u32[]{:S(2)}, u32[]{:S(2)}) collective-permute-start(bf16[48,1536]{1,0:T(8,128)(2,1)} %bitcast.230), channel_id=1, source_target_pairs={{0,1},{1,0},{2,3},{3,2},{4,5},{5,4},{6,7},{7,6},{8,9},{9,8},{10,11... | collective-permute-start | bytes 442376 | tf_op jit(solution)/shard_map/ppermute | solution.py:137
  (68 other events, 467.8 us)
Sparse Core Ops, SparseCore 0:
  32.2 24.1 all-gather.6
  58.8 72.9 all-gather.10
  133.7 71.8 all-gather.8
  266.4 33.5 reduce-scatter.5
  306.4 135.7 reduce-scatter.13
  444.4 263.1 reduce-scatter.11
  718.8 20.9 reduce-scatter.9
  742.1 26.7 reduce-scatter.7

commit v4 on v3

--- a/solution.py
+++ b/solution.py
@@ -17,23 +17,15 @@
 ATT_SCALE = 0.015625
 THETA = 10000.0
 NEG = -1e30
-
-
-def rope_tables(positions, head_dim):
-    half_dim = head_dim // 2
-    frequency = THETA ** (-(jnp.arange(half_dim, dtype=jnp.float32) * 2.0 / head_dim))
+LOG2E = 1.4426950408889634
+
+
+def signed_tables(positions):
+    lane = jnp.arange(2 * HEAD_SIZE, dtype=jnp.int32) % HEAD_SIZE
+    half_dim = HEAD_SIZE // 2
+    frequency = THETA ** (-((lane % half_dim).astype(jnp.float32) * 2.0 / HEAD_SIZE))
     angles = positions[:, None] * frequency[None, :]
-    cosine_lookup = jnp.concatenate([jnp.cos(angles), jnp.cos(angles)], axis=-1)
-    sine_lookup = jnp.concatenate([jnp.sin(angles), jnp.sin(angles)], axis=-1)
-    return (cosine_lookup, sine_lookup)
-
-
-def signed_tables(positions, width):
-    cosine_lookup, sine_lookup = rope_tables(positions, HEAD_SIZE)
-    half_dim = HEAD_SIZE // 2
-    sine_lookup = jnp.concatenate([-sine_lookup[:, :half_dim], sine_lookup[:, half_dim:]], axis=-1)
-    copies = width // HEAD_SIZE
-    return (jnp.tile(cosine_lookup, (1, copies)), jnp.tile(sine_lookup, (1, copies)))
+    return (jnp.cos(angles), jnp.where(lane < half_dim, -1.0, 1.0) * jnp.sin(angles))
 
 
 def rms_forward(values, norm_gain):
@@ -81,7 +73,8 @@
 
 
 def dispatch(codes, rows, own, slots):
-    blocks, tokens, width = rows.shape
+    blocks, _, width = rows.shape
+    tokens = codes.shape[2]
     return pl.pallas_call(
         partial(dispatch_body, own, slots),
         grid=(blocks,),
@@ -100,6 +93,62 @@
     )(codes, rows)
 
 
+def experts_body(at_ref, rows_ref, gate_up_ref, plain_ref, weight_ref, out_ref, both_ref, d_weight_ref):
+    total = rows_ref.shape[1]
+    hidden_units = plain_ref.shape[2]
+    chunk = total // 2 if total % 16 == 0 else total
+    for at in range(0, total, chunk):
+        rows = pl.ds(at, chunk)
+        both = jnp.dot(rows_ref[0, rows], gate_up_ref[0], preferred_element_type=jnp.float32)
+        gate, up = both[:, :hidden_units], both[:, hidden_units:]
+        plain, weight = plain_ref[0, rows], weight_ref[0, rows]
+        logistic = jax.nn.sigmoid(gate)
+        silu = gate * logistic
+        hidden = silu * up
+        d_weight_ref[0, rows] = jnp.sum(hidden * plain, axis=1, keepdims=True)
+        out_ref[0, rows] = (weight * hidden).astype(jnp.bfloat16)
+        d_hidden = weight * plain
+        d_gate = d_hidden * up * (logistic + silu * (1.0 - logistic))
+        both_ref[0, rows, :hidden_units] = d_gate.astype(jnp.bfloat16)
+        both_ref[0, rows, hidden_units:] = (d_hidden * silu).astype(jnp.bfloat16)
+
+
+def experts(offset, rows, gate_up, plain, weight):
+    own, total, width = rows.shape
+    hidden_units = plain.shape[2]
+    part = total // 2 if total % 32 == 0 else total
+    tile = lambda e, r, at: (e, r, 0)
+    return pl.pallas_call(
+        experts_body,
+        grid_spec=pltpu.PrefetchScalarGridSpec(
+            num_scalar_prefetch=1,
+            grid=(own, total // part),
+            in_specs=[
+                pl.BlockSpec((1, part, width), tile),
+                pl.BlockSpec((1, width, 2 * hidden_units), lambda e, r, at: (at[0] + e, 0, 0)),
+                pl.BlockSpec((1, part, hidden_units), tile),
+                pl.BlockSpec((1, part, 1), tile),
+            ],
+            out_specs=[
+                pl.BlockSpec((1, part, hidden_units), tile),
+                pl.BlockSpec((1, part, 2 * hidden_units), tile),
+                pl.BlockSpec((1, part, 1), tile),
+            ],
+        ),
+        out_shape=[
+            jax.ShapeDtypeStruct((own, total, hidden_units), jnp.bfloat16),
+            jax.ShapeDtypeStruct((own, total, 2 * hidden_units), jnp.bfloat16),
+            jax.ShapeDtypeStruct((own, total, 1), jnp.float32),
+        ],
+        cost_estimate=pl.CostEstimate(
+            flops=4 * own * total * width * hidden_units,
+            transcendentals=own * total * hidden_units,
+            bytes_accessed=2 * own * (total * (width + 4 * hidden_units) + 2 * width * hidden_units),
+        ),
+        name="experts",
+    )(jnp.asarray(offset, jnp.int32).reshape(1), rows, gate_up, plain, weight)
+
+
 def combine_body(own, slots, at_ref, codes_ref, rows_ref, out_ref):
     pick = selection(codes_ref[0], own, slots)
     rows = rows_ref[...].reshape(own * slots, rows_ref.shape[-1])
@@ -135,6 +184,44 @@
 def swap(values, axis, bit):
     size = lax.axis_size(axis)
     return lax.ppermute(values, axis, [(i, i ^ bit) for i in range(size)])
+
+
+def exchange(values, bit, axis, stride, dim):
+    take = partial(lax.dynamic_index_in_dim, axis=dim, keepdims=False)
+    away = swap(take(values, 1 - bit), axis, stride)
+    stay = take(values, bit)
+    first = bit == 0
+    return jnp.stack([jnp.where(first, stay, away), jnp.where(first, away, stay)])
+
+
+def paired(group):
+    return group == ("ctx", "expert") and lax.axis_size("ctx") == 4 and lax.axis_size("expert") == 2
+
+
+def gather_gates(gates, group, first_expert, own):
+    if not paired(group):
+        whole = lax.all_gather(gates, group, axis=0, tiled=False)
+        return lax.dynamic_slice_in_dim(whole, first_expert, own, axis=1)
+    ctx, side = lax.axis_index("ctx"), lax.axis_index("expert")
+    parts = gates.reshape(2, 2, 2, own, gates.shape[1])
+    parts = exchange(parts, side, "expert", 1, 0)
+    parts = exchange(parts, ctx % 2, "ctx", 1, 2)
+    parts = exchange(parts, ctx // 2, "ctx", 2, 2)
+    return parts.reshape(8, own, gates.shape[1])
+
+
+def return_gates(values, group, first_expert, experts):
+    blocks, own, tokens = values.shape
+    if not paired(group):
+        whole = jnp.zeros((blocks, experts, tokens), values.dtype)
+        whole = lax.dynamic_update_slice_in_dim(whole, values, first_expert, axis=1)
+        return lax.psum_scatter(whole, group, scatter_dimension=0)
+    ctx, side = lax.axis_index("ctx"), lax.axis_index("expert")
+    parts = values.reshape(2, 2, 2, own, tokens)
+    parts = exchange(parts, ctx // 2, "ctx", 2, 0)
+    parts = exchange(parts, ctx % 2, "ctx", 1, 1)
+    parts = exchange(parts, side, "expert", 1, 2)
+    return parts.transpose(0, 2, 1, 3, 4).reshape(experts, tokens)
 
 
 def added(left, right):
@@ -199,6 +286,62 @@
     return jnp.where(lane_half(values.shape) == key_half, moved, 0.0)
 
 
+def project_keys_body(rows, h_ref, kw_ref, vw_ref, cos_ref, sin_ref, prompt_ref, cont_ref):
+    key = jnp.dot(h_ref[...], kw_ref[...], preferred_element_type=jnp.float32)
+    key = turn(key, cos_ref[...], sin_ref[...]).astype(jnp.bfloat16)
+    value = jnp.dot(h_ref[...], vw_ref[...], preferred_element_type=jnp.float32)
+    value = value.astype(jnp.bfloat16)
+    prompt_ref[0] = key[:rows]
+    prompt_ref[1] = value[:rows]
+    cont_ref[0] = key[rows:]
+    cont_ref[1] = value[rows:]
+
+
+def project_keys(hidden, key_weight, value_weight, cosine, sine, rows):
+    tokens, depth = hidden.shape
+    width = key_weight.shape[1]
+    whole = lambda j: (0, 0)
+    column = lambda j: (0, j)
+    return pl.pallas_call(
+        partial(project_keys_body, rows),
+        grid=(width // 128,),
+        in_specs=[
+            pl.BlockSpec((tokens, depth), whole),
+            pl.BlockSpec((depth, 128), column),
+            pl.BlockSpec((depth, 128), column),
+            pl.BlockSpec((tokens, 128), whole),
+            pl.BlockSpec((tokens, 128), whole),
+        ],
+        out_specs=[
+            pl.BlockSpec((2, rows, 128), lambda j: (0, 0, j)),
+            pl.BlockSpec((2, tokens - rows, 128), lambda j: (0, 0, j)),
+        ],
+        out_shape=[
+            jax.ShapeDtypeStruct((2, rows, width), jnp.bfloat16),
+            jax.ShapeDtypeStruct((2, tokens - rows, width), jnp.bfloat16),
+        ],
+        cost_estimate=pl.CostEstimate(
+            flops=4 * tokens * depth * width,
+            transcendentals=0,
+            bytes_accessed=2 * (tokens * depth + 2 * depth * width + 2 * tokens * width),
+        ),
+        name="project_keys",
+    )(hidden, key_weight, value_weight, cosine, sine)
+
+
+def gather_keys(near_kv):
+    if lax.axis_size("ctx") != 4:
+        return lax.all_gather(near_kv, "ctx", axis=1, tiled=True)
+    rows = near_kv.shape[1]
+    here = lax.axis_index("ctx")
+    pair = swap(near_kv, "ctx", 2)
+    whole = jnp.zeros((2, 4 * rows, near_kv.shape[2]), near_kv.dtype)
+    pieces = ((0, near_kv), (2, pair), (1, swap(near_kv, "ctx", 1)), (3, swap(pair, "ctx", 1)))
+    for step, piece in pieces:
+        whole = lax.dynamic_update_slice_in_dim(whole, piece, (here ^ step) * rows, axis=1)
+    return whole
+
+
 def head_place(group):
     head = pl.program_id(0)
     key_half = (head // group) % 2
@@ -220,7 +363,7 @@
         highest = parts[0][0].max(axis=1, keepdims=True)
         for scores, _ in parts[1:]:
             highest = jnp.maximum(highest, scores.max(axis=1, keepdims=True))
-        lifted = [jnp.exp(scores - highest) for scores, _ in parts]
+        lifted = [jnp.exp2(scores * LOG2E - highest * LOG2E) for scores, _ in parts]
         total = lifted[0].sum(axis=1, keepdims=True)
         for piece in lifted[1:]:
             total = total + piece.sum(axis=1, keepdims=True)
@@ -228,12 +371,12 @@
         result = None
         for piece, (_, value) in zip(lifted, parts):
             term = jnp.dot(
-                (piece * inverse).astype(jnp.bfloat16), value, preferred_element_type=jnp.float32
+                piece.astype(jnp.bfloat16), value, preferred_element_type=jnp.float32
             )
             result = term if result is None else result + term
         log_total = jnp.broadcast_to(highest + jnp.log(total), (total.shape[0], 128))
         log_ref[0, :, rows] = jnp.transpose(log_total)[:8]
-        keep = jnp.where(lane_half(result.shape) == key_half, result, 0.0)
+        keep = jnp.where(lane_half(result.shape) == key_half, result * inverse, 0.0)
         keep = jnp.where(swap, pltpu.roll(keep, HEAD_SIZE, 1), keep).astype(jnp.bfloat16)
 
         @pl.when(head % 2 == 0)
@@ -334,7 +477,7 @@
     def step(key, value, query, d_out, log_total, centre, allowed, at, count):
         scores = lax.dot_general(key, query, nt, preferred_element_type=jnp.float32)
         scores = jnp.where(allowed(scores.shape), scores, NEG)
-        weights = jnp.exp(scores - log_total)
+        weights = jnp.exp2(scores * LOG2E - log_total * LOG2E)
         d_weights = lax.dot_general(value, d_out, nt, preferred_element_type=jnp.float32)
         d_scores = (weights * (d_weights - centre)).astype(jnp.bfloat16)
         dv_acc[at : at + count] += jnp.dot(
@@ -455,7 +598,23 @@
             grad, ("dp", "ctx"), scatter_dimension=1, tiled=True
         ).astype(jnp.float32)
     part = lax.psum_scatter(grad, "dp", scatter_dimension=1, tiled=True)
-    return lax.all_to_all(part, "ctx", split_axis=1, concat_axis=0, tiled=True).astype(jnp.float32)
+    size = lax.axis_size("ctx")
+    if size & (size - 1):
+        return lax.all_to_all(part, "ctx", split_axis=1, concat_axis=0, tiled=True).astype(
+            jnp.float32
+        )
+    own, rows, width = part.shape
+    here = lax.axis_index("ctx")
+    part = part.reshape(own, size, rows // size, width)
+    whole = jnp.zeros((own * size, rows // size, width), jnp.float32)
+    for step in range(size):
+        piece = lax.dynamic_index_in_dim(part, here ^ step, 1, keepdims=False)
+        if step:
+            piece = swap(piece, "ctx", step)
+        whole = lax.dynamic_update_slice_in_dim(
+            whole, piece.astype(jnp.float32), (here ^ step) * own, axis=0
+        )
+    return whole
 
 
 def scatter_keys(d_key, d_value, rows):
@@ -502,6 +661,19 @@
     )
 
 
+def scatter_parts(parts):
+    size = lax.axis_size("dp")
+    here = lax.axis_index("dp")
+    take = partial(lax.dynamic_index_in_dim, axis=0, keepdims=False)
+    total = take(parts, here).astype(jnp.float32)
+    for hop in range(1, size):
+        moved = lax.ppermute(
+            take(parts, (here + hop) % size), "dp", [(i, (i + hop) % size) for i in range(size)]
+        )
+        total = total + moved.astype(jnp.float32)
+    return total.astype(jnp.bfloat16)
+
+
 def finish_dense(grad, folded):
     if not folded:
         return lax.psum(grad, "expert").astype(jnp.float32)
@@ -521,7 +693,7 @@
     )
     if not folded:
         return lax.psum_scatter(grad, ("dp", "ctx"), scatter_dimension=0, tiled=True), False
-    return lax.psum_scatter(fold_dense(grad, cut), "dp", scatter_dimension=0), True
+    return scatter_parts(fold_dense(grad, cut)), True
 
 
 def per_device(
@@ -573,14 +745,32 @@
     routes = jnp.concatenate(
         [routes_prompt[0], routes_cont[0].reshape(cont_rows, top_count)], axis=0
     )
-    codes_all = lax.all_gather(
-        slot_codes(routes, slot_order[0, 0], expert_total, capacity), group, axis=0, tiled=False
-    )
+    codes = slot_codes(routes, slot_order[0, 0], expert_total, capacity)
+    upstream_low = jnp.concatenate([dy_prompt[0], dy_cont[0].reshape(cont_rows, model_width)], axis=0)
+    upstream = upstream_low.astype(jnp.float32)
+    assert capacity <= 256
+    fold = model_width // count_of_tokens
+    code_rows = -(-expert_total // (8 * fold)) * 8
+    code_table = jnp.pad(
+        codes.astype(jnp.bfloat16),
+        ((0, code_rows * fold - expert_total), (0, 0)),
+        constant_values=-2.0,
+    )
+    code_table = jnp.concatenate(
+        [code_table[i * code_rows : (i + 1) * code_rows] for i in range(fold)], axis=1
+    )
+    upstream_all = lax.all_gather(
+        jnp.concatenate([upstream_low, code_table], axis=0), group, axis=0, tiled=False
+    )
+    codes_all = upstream_all[:, count_of_tokens:]
+    codes_all = jnp.concatenate(
+        [
+            codes_all[:, :, i * count_of_tokens : (i + 1) * count_of_tokens] for i in range(fold)
+        ],
+        axis=1,
+    ).astype(jnp.float32)
     own_codes = lax.dynamic_slice_in_dim(codes_all, first_expert, own, axis=1)
     own_codes = jnp.pad(own_codes, ((0, 0), (0, -own % 8), (0, 0)), constant_values=-2.0)
-    upstream_low = jnp.concatenate([dy_prompt[0], dy_cont[0].reshape(cont_rows, model_width)], axis=0)
-    upstream = upstream_low.astype(jnp.float32)
-    upstream_all = lax.all_gather(upstream_low, group, axis=0, tiled=False)
     d_slot_rows = dispatch(own_codes, upstream_all, own, slots)
     d_plain = jnp.einsum("ecd,efd->ecf", d_slot_rows, down_own, preferred_element_type=jnp.float32)
     gain_one = norm1_gain.astype(jnp.float32)
@@ -590,9 +780,6 @@
     ).astype(jnp.float32)
     normed_one, scale_one = rms_forward(tokens, gain_one)
     h1_low = normed_one.astype(jnp.bfloat16)
-    q_lin = jnp.dot(h1_low, w_query, preferred_element_type=jnp.float32)
-    key_linear = jnp.dot(h1_low, key_weight, preferred_element_type=jnp.float32)
-    value_linear = jnp.dot(h1_low, value_weight, preferred_element_type=jnp.float32)
     row_index = jnp.arange(count_of_tokens, dtype=jnp.int32)
     cont_offset = row_index - prompt_rows
     start = lax.axis_index("ctx") * prompt_rows
@@ -604,25 +791,14 @@
         key_index >= prompt_total, prompt_total + (key_index - prompt_total) % cont_len, key_index
     )
     start = start.astype(jnp.int32)[None]
-    cosine, sine = signed_tables(query_pos.astype(jnp.float32), 128)
-    key_cosine, key_sine = signed_tables(key_pos.astype(jnp.float32), 128)
-    wide_cosine, wide_sine = signed_tables(query_pos.astype(jnp.float32), key_value_width)
-    half_dim = HEAD_SIZE // 2
-    lane = jnp.arange(key_value_width, dtype=jnp.int32) % HEAD_SIZE
-    partner = jnp.where(
-        lane < half_dim, jnp.roll(key_linear, -half_dim, axis=1), jnp.roll(key_linear, half_dim, axis=1)
-    )
-    key_row_block = (key_linear * wide_cosine + partner * wide_sine).astype(jnp.bfloat16)
-    value_row_block = value_linear.astype(jnp.bfloat16)
-    prompt_kv = lax.all_gather(
-        jnp.stack([key_row_block[:prompt_rows], value_row_block[:prompt_rows]]),
-        "ctx",
-        axis=1,
-        tiled=True,
-    )
-    keys_values = (
-        prompt_kv[0], prompt_kv[1], key_row_block[prompt_rows:], value_row_block[prompt_rows:]
-    )
+    cosine, sine = signed_tables(query_pos.astype(jnp.float32))
+    key_cosine, key_sine = signed_tables(key_pos.astype(jnp.float32))
+    near_kv, cont_kv = project_keys(
+        h1_low, key_weight, value_weight, cosine, sine, prompt_rows
+    )
+    prompt_kv = gather_keys(near_kv)
+    keys_values = (prompt_kv[0], prompt_kv[1], cont_kv[0], cont_kv[1])
+    q_lin = jnp.dot(h1_low, w_query, preferred_element_type=jnp.float32)
     query_row_block, merged_low, log_total = attend_forward(
         q_lin, *keys_values, cosine, sine, start, prompt_rows, cont_len
     )
@@ -631,31 +807,23 @@
     normed_two, scale_two = rms_forward(resid, gain_two)
     h2_low = normed_two.astype(jnp.bfloat16)
     rows_all = lax.all_gather(h2_low, group, axis=0, tiled=False)
-    rows_all, d_plain = lax.optimization_barrier((rows_all, d_plain))
+    named = codes > -1.5
+    logits = jnp.einsum("td,de->et", h2_low, w_router, preferred_element_type=jnp.float32)
+    logits = jnp.where(named, logits, NEG)
+    lifted = jnp.where(named, jnp.exp(logits - jnp.max(logits, axis=0, keepdims=True)), 0.0)
+    gates = lifted / jnp.sum(lifted, axis=0, keepdims=True)
+    own_gates, rows_all, d_plain = lax.optimization_barrier(
+        (gather_gates(gates, group, first_expert, own), rows_all, d_plain)
+    )
     slot_rows = dispatch(own_codes, rows_all, own, slots)
-    logits = jnp.einsum("btd,de->bet", rows_all, w_router, preferred_element_type=jnp.float32)
-    named = codes_all > -1.5
-    logits = jnp.where(named, logits, NEG)
-    lifted = jnp.where(named, jnp.exp(logits - jnp.max(logits, axis=1, keepdims=True)), 0.0)
-    gates_all = lifted / jnp.sum(lifted, axis=1, keepdims=True)
-    own_gates = lax.dynamic_slice_in_dim(gates_all, first_expert, own, axis=1)
-    gates = lax.dynamic_index_in_dim(gates_all, block_index, 0, keepdims=False)
     slot_index = jnp.arange(slots, dtype=jnp.int32).astype(jnp.float32)
     picked = own_codes[:, :own, None, :] == slot_index[None, None, :, None]
     slot_gate = jnp.sum(jnp.where(picked, own_gates[:, :, None, :], 0.0), axis=-1)
     slot_gate = slot_gate.transpose(1, 0, 2).reshape(own, blocks * slots)
-    both = jnp.einsum("ecd,edf->ecf", slot_rows, gate_up_own, preferred_element_type=jnp.float32)
-    gate_part = both[..., :hidden_units]
-    up_part = both[..., hidden_units:]
-    weight = RESID * slot_gate[:, :, None]
-    logistic = jax.nn.sigmoid(gate_part)
-    silu = gate_part * logistic
-    hidden = silu * up_part
-    d_slot_gate = RESID * jnp.sum(hidden * d_plain, axis=-1)
-    weighted = (weight * hidden).astype(jnp.bfloat16)
-    d_hidden = weight * d_plain
-    d_gate = d_hidden * up_part * logistic * (1.0 + gate_part * (1.0 - logistic))
-    d_both = jnp.concatenate([d_gate, d_hidden * silu], axis=-1).astype(jnp.bfloat16)
+    weighted, d_both, d_slot_gate = experts(
+        own_offset, slot_rows, w_gate_up, d_plain, RESID * slot_gate[:, :, None]
+    )
+    d_slot_gate = RESID * d_slot_gate[:, :, 0]
     grad_down = jnp.einsum(
         "ecf,ecd->efd", weighted, d_slot_rows, preferred_element_type=jnp.float32
     ).astype(jnp.bfloat16)
@@ -672,12 +840,11 @@
     ).astype(jnp.bfloat16)
 
     def forward_rows(weighted):
-        expert_out = jnp.einsum(
+        return jnp.einsum(
             "ecf,efd->ecd", weighted, down_own, preferred_element_type=jnp.float32
         ).astype(jnp.bfloat16)
-        return start_scatter(own_codes, expert_out, own, slots, group)
-
-    d_rows, mixed_part = finish_scatter(d_rows_parts, grad_gate_up, weighted, forward_rows)
+
+    d_rows, expert_out = finish_scatter(d_rows_parts, grad_gate_up, weighted, forward_rows)
     d_gates_own = jnp.sum(
         jnp.where(
             picked,
@@ -686,17 +853,15 @@
         ),
         axis=2,
     )
-    d_gates = lax.psum_scatter(
-        lax.dynamic_update_slice_in_dim(
-            jnp.zeros((blocks, expert_total, count_of_tokens), jnp.float32),
-            d_gates_own,
-            first_expert,
-            axis=1,
-        ),
-        group,
-        scatter_dimension=0,
-    )
-    grad_gate_up = reduce_experts(grad_gate_up, split)
+    d_gates = return_gates(d_gates_own, group, first_expert, expert_total)
+    cut = hidden_units
+    grad_gate_up = jnp.concatenate(
+        [
+            reduce_experts(grad_gate_up[..., :cut], split),
+            reduce_experts(grad_gate_up[..., cut:], split),
+        ],
+        axis=-1,
+    )
     d_logits = (
         gates * (d_gates - jnp.sum(gates * d_gates, axis=0, keepdims=True))
     ).astype(jnp.bfloat16)
@@ -714,12 +879,12 @@
     merged_gradient = jnp.einsum(
         "td,qd->tq", d_branch, w_out, preferred_element_type=jnp.float32
     ).astype(jnp.bfloat16)
-    mixed_part, merged_gradient = lax.optimization_barrier((mixed_part, merged_gradient))
     d_query_low, d_key_prompt, d_value_prompt, d_key_cont, d_value_cont = attend_backward(
         query_row_block, merged_gradient, merged_low, log_total, *keys_values, cosine, sine,
         key_cosine, key_sine, start, prompt_rows, cont_len,
     )
-    mixed, d_key_prompt = finish_scatter(mixed_part, d_key_prompt, d_key_prompt, lambda v: v)
+    expert_out, d_key_prompt = lax.optimization_barrier((expert_out, d_key_prompt))
+    mixed, _ = finish_scatter(start_scatter(own_codes, expert_out, own, slots, group))
     output = resid + mixed
     y_prompt = output[:prompt_rows].astype(jnp.bfloat16)[None]
     y_cont = output[prompt_rows:].reshape(1, cont_count, cont_len, model_width).astype(jnp.bfloat16)

time: 853 us -> 853 us (level)
  waiting for transfers between devices: 228 us -> 281 us
  other arithmetic: 112 us -> 76.2 us
  matrix products: 164 us -> 131 us
  Pallas kernels: 186 us -> 218 us
  starting transfers between devices: 34.8 us -> 54.2 us
  blocking collectives: 18.9 us -> 0 us
  local copies, waits for them, and re-layouts: 82 us -> 66.6 us
    ppermute x22 -> x40, waiting for transfers between devices: 120 us -> 183 us  [swap(): return lax.ppermute(values, axis, [(i, i ^ bit) for i in range(size)])]
    ppermute x0 -> x6, waiting for transfers between devices: none -> 55.5 us  [scatter_parts(): lax.ppermute(take(parts, (here + hop) % size), 'dp', [(i, (i + hop) % siz...]
    all_to_all x2 -> x0, waiting for transfers between devices: 41.9 us -> none  [reduce_experts(): lax.all_to_all(part, 'ctx', split_axis=1, concat_axis=0, tiled=True)]
    pallas_call x0 -> x2, Pallas kernels: none -> 36.1 us  [the longest x1 29 us: experts(): pl.pallas_call(experts_body, grid_spec=pltpu.PrefetchScalarGridSpec(num_s...]
    dot_general x3 -> x1, matrix products: 28.2 us -> 1.99 us  [per_device(): jnp.einsum('td,de->et', h2_low, w_router, preferred_element_type=jnp.floa...]
    ppermute x22 -> x40, starting transfers between devices: 16.6 us -> 38 us  [swap(): return lax.ppermute(values, axis, [(i, i ^ bit) for i in range(size)])]
    all_gather x1 -> x0, blocking collectives: 18.9 us -> none  [per_device(): lax.all_gather(slot_codes(routes, slot_order[0, 0], expert_total, capacit...]
    another operation x12 -> x3, local copies, waits for them, and re-layouts: 17.9 us -> 0.98 us  [the longest x6 10.1 us: signed_tables(): jnp.tile(cosine_lookup, (1, copies))]
  transfers between devices with their start and end apart: 35 -> 54, of which waited for: 18 -> 30; matrix products, arithmetic and copies ran while one was open for 32% -> 28% of each run, Pallas kernels for 20% -> 21%
where the time goes in v4:
time: 853 us; the launch traced here: 843 us
  waiting for transfers between devices  281 us (33%)
  Pallas kernels  218 us (26%)
  matrix products  131 us (15%)
  other arithmetic  76.2 us (9%)
  local copies, waits for them, and re-layouts  66.6 us (8%)
  starting transfers between devices  54.2 us (6%)
  between operations  15.5 us (2%)
    ppermute x40, waiting for transfers between devices, swap(): return lax.ppermute(values, axis, [(i, i ^ bit) for i in range(size)])  183 us
    pallas_call x1, Pallas kernels, attend_backward(): pl.pallas_call(partial(attend_backward_body, group, rows, cont_len, chunk...  64.2 us
    ppermute x6, waiting for transfers between devices, scatter_parts(): lax.ppermute(take(parts, (here + hop) % size), 'dp', [(i, (i + hop) % siz...  55.5 us
    pallas_call x1, Pallas kernels, attend_forward(): pl.pallas_call(partial(attend_forward_body, group, rows, cont_len), grid_...  50.5 us
    pallas_call x4, Pallas kernels, combine(): pl.pallas_call(partial(combine_body, own, slots), grid_spec=pltpu.Prefetc...  39.1 us
    ppermute x40, starting transfers between devices, swap(): return lax.ppermute(values, axis, [(i, i ^ bit) for i in range(size)])  38 us
    all_gather x1, waiting for transfers between devices, per_device(): rows_all = lax.all_gather(h2_low, group, axis=0, tiled=False)  32.2 us
    pallas_call x1, Pallas kernels, experts(): pl.pallas_call(experts_body, grid_spec=pltpu.PrefetchScalarGridSpec(num_s...  29 us
  transfers between devices with their start and end apart: 54, of which 30 were waited for; matrix products, arithmetic and copies ran while one was open for 28% of the time, Pallas kernels for 21%

profile of v4, /device:TPU:9, one launch (start us, length us, event | category | flops | bytes accessed | tf_op | source)
XLA Modules:
  0.0 843.2 jit_solution(10418970917081302046)
XLA Ops:
  32.3 16.2 %collective-permute-done = bf16[2,256,512]{2,1,0:T(8,128)(2,1)} collective-permute-done((bf16[2,256,512]{2,1,0:T(8,128)(2,1)}, bf16[2,256,512]{2,1,0:T(8,128)(2,1)}, u32[]{:S(2)}, u32[]{:S(2)}) %collective-permute-start) | collective-permute-done | bytes 524320 | tf_op jit(solution)/shard_map/ppermute | solution.py:186
  58.1 50.5 %attend_forward.1 = (bf16[512,1536]{1,0:T(8,128)(2,1)}, bf16[512,1536]{1,0:T(8,128)(2,1)}, f32[24,8,512]{2,1,0:T(8,128)}) custom-call(s32[1]{0:T(128)} %bitcast.2.pos_ref, f32[512,1536]{1,0:T(8,128)} %fusion.126.q_ref, f32[512,128]{1,0:T(8,128)} %get-tuple-element.258.cos_ref, f32[512,128]{1,0:T(8,128)} %get-tuple-element.257.sin_ref, ...), custom_call_target="tpu_custom_call" | custom-call | flops 8053063680 | bytes 6291456 | tf_op jit(solution)/shard_map/attend_forward/pallas_call | solution.py:414
  129.5 14.4 %dispatch.2 = bf16[5,832,1536]{2,1,0:T(8,128)(2,1)} custom-call(f32[8,8,512]{2,1,0:T(8,128)} %pad.14.codes_ref, bf16[8,528,1536]{2,1,0:T(8,128)(2,1)} %bitcast.285), custom_call_target="tpu_custom_call" | custom-call | flops 6543114240 | bytes 25362432 | tf_op jit(solution)/shard_map/dispatch/pallas_call | solution.py:78
  143.9 14.1 %fusion.9.plain_ref = f32[5,832,512]{2,1,0:T(8,128)} fusion(bf16[5,832,1536]{2,1,0:T(8,128)(2,1)} %dispatch.2, bf16[20,512,1536]{2,1,0:T(8,128)(2,1)} %param.30, s32[]{:T(128)S(6)} %select_n.415), kind=kOutput, calls=%fused_computation.18 | convolution fusion | flops 6543114240 | bytes 29163524 | tf_op jit(solution)/shard_map/ecd,efd->ecf/dot_general | solution.py:775
  158.0 32.2 %all-gather.7.cloned.1.call-done = bf16[4096,1536]{1,0:T(8,128)(2,1)} async-done(((bf16[512,1536]{1,0:T(8,128)(2,1)}), bf16[4096,1536]{1,0:T(8,128)(2,1)}) %all-gather.7.cloned.1.call-update) | async-done | bytes 12582928 | tf_op jit(solution)/shard_map/all_gather | solution.py:809
  190.2 14.2 %dispatch.3.rows_ref = bf16[5,832,1536]{2,1,0:T(8,128)(2,1)} custom-call(f32[8,8,512]{2,1,0:T(8,128)} %pad.14.codes_ref, bf16[8,512,1536]{2,1,0:T(8,128)(2,1)} %bitcast.286), custom_call_target="tpu_custom_call" | custom-call | flops 6543114240 | bytes 25362432 | tf_op jit(solution)/shard_map/dispatch/pallas_call | solution.py:78
  207.5 29.0 %experts.1 = (bf16[5,832,512]{2,1,0:T(8,128)(2,1)}, bf16[5,832,1024]{2,1,0:T(8,128)(2,1)}, f32[5,832,1]{2,1,0:T(8,128)}) custom-call(s32[1]{0:T(128)} %bitcast.14.at_ref, bf16[5,832,1536]{2,1,0:T(8,128)(2,1)} %dispatch.3.rows_ref, bf16[20,1536,1024]{2,1,0:T(8,128)(2,1)} %gate_up_ref.1, f32[5,832,512]{2,1,0:T(8,128)} %fusion.9.plain_ref, ...), custom_call_target="tpu_custom_call" | custom-call | flops 13086228480 | bytes 45547520 | tf_op jit(solution)/shard_map/experts/pallas_call | solution.py:121
  236.6 15.8 %convolution_convert_fusion.4 = bf16[5,512,1536]{2,1,0:T(8,128)(2,1)} fusion(bf16[5,832,512]{2,1,0:T(8,128)(2,1)} %get-tuple-element.56, bf16[5,832,1536]{2,1,0:T(8,128)(2,1)} %dispatch.2), kind=kOutput, calls=%fused_computation.20 | convolution fusion | flops 6547046400 | bytes 24903680 | tf_op jit(solution)/shard_map/ecf,ecd->efd/dot_general | solution.py:827
  253.5 21.4 %fusion.2.rows_ref = bf16[5,832,1536]{2,1,0:T(8,128)(2,1)} fusion(bf16[5,832,1024]{2,1,0:T(8,128)(2,1)} %get-tuple-element.50, bf16[20,1536,1024]{2,1,0:T(8,128)(2,1)} %gate_up_ref.1, s32[]{:T(128)S(6)} %select_n.415), kind=kOutput, calls=%fused_computation.6 | convolution fusion | flops 13092618240 | bytes 37027844 | tf_op jit(solution)/shard_map/ecf,edf->ecd/dot_general | solution.py:832
  274.9 9.8 %combine.5 = bf16[4,512,1536]{2,1,0:T(8,128)(2,1)} custom-call(s32[4]{0:T(128)} %broadcast_xor_fusion.at_ref, f32[8,8,512]{2,1,0:T(8,128)} %pad.14.codes_ref, bf16[5,832,1536]{2,1,0:T(8,128)(2,1)} %fusion.2.rows_ref), custom_call_target="tpu_custom_call" | custom-call | flops 3271557120 | bytes 12681216 | tf_op jit(solution)/shard_map/combine/pallas_call | solution.py:163
  285.6 9.7 %combine.4 = bf16[4,512,1536]{2,1,0:T(8,128)(2,1)} custom-call(s32[4]{0:T(128)} %broadcast_xor_fusion.1.at_ref, f32[8,8,512]{2,1,0:T(8,128)} %pad.14.codes_ref, bf16[5,832,1536]{2,1,0:T(8,128)(2,1)} %fusion.2.rows_ref), custom_call_target="tpu_custom_call" | custom-call | flops 3271557120 | bytes 12681216 | tf_op jit(solution)/shard_map/combine/pallas_call | solution.py:163
  295.3 9.1 %add_convert_fusion.1 = bf16[4,512,1536]{2,1,0:T(8,128)(2,1)} fusion(bf16[4,512,1536]{2,1,0:T(8,128)(2,1)} %collective-permute-done.6, bf16[4,512,1536]{2,1,0:T(8,128)(2,1)} %combine.4), kind=kLoop, calls=%fused_computation.4 | loop fusion | flops 12582912 | bytes 18874368 | tf_op jit(solution)/shard_map/convert_element_type | solution.py:228
  304.4 23.9 %convolution_convert_fusion = bf16[5,1536,1024]{2,1,0:T(8,128)(2,1)} fusion(bf16[5,832,1536]{2,1,0:T(8,128)(2,1)} %dispatch.3.rows_ref, bf16[5,832,1024]{2,1,0:T(8,128)(2,1)} %get-tuple-element.50), kind=kOutput, calls=%fused_computation.2 | convolution fusion | flops 13094092800 | bytes 37027840 | tf_op jit(solution)/shard_map/ecd,ecf->edf/dot_general | solution.py:838
  328.2 11.2 %fusion.117 = (bf16[5,1536,512]{2,1,0:T(8,128)(2,1)}, bf16[5,1536,512]{2,1,0:T(8,128)(2,1)}) fusion(bf16[5,1536,1024]{2,1,0:T(8,128)(2,1)} %convolution_convert_fusion), kind=kLoop, calls=%fused_computation.335 | loop fusion | bytes 31457280 | tf_op jit(solution)/shard_map/slice | solution.py:860
  360.1 30.3 %collective-permute-done.13 = f32[2,2,5,512]{3,1,2,0:T(2,128)S(1)} collective-permute-done((f32[2,2,5,512]{3,1,2,0:T(2,128)S(1)}, f32[2,2,5,512]{3,1,2,0:T(2,128)S(1)}, u32[]{:S(2)}, u32[]{:S(2)}) %collective-permute-start.13) | collective-permute-done | bytes 40992 | tf_op jit(solution)/shard_map/ppermute | solution.py:186
  396.8 14.9 %convolution_convert_fusion.1.rows_ref = bf16[5,832,1536]{2,1,0:T(8,128)(2,1)} fusion(bf16[5,832,512]{2,1,0:T(8,128)(2,1)} %get-tuple-element.56, bf16[20,512,1536]{2,1,0:T(8,128)(2,1)} %param.30, s32[]{:T(128)S(6)} %select_n.415), kind=kOutput, calls=%fused_computation.5 | convolution fusion | flops 6549504000 | bytes 24903684 | tf_op jit(solution)/shard_map/ecf,efd->ecd/dot_general | solution.py:843
  427.9 64.2 %attend_backward.1 = (bf16[512,1536]{1,0:T(8,128)(2,1)}, bf16[1024,512]{1,0:T(8,128)(2,1)}, bf16[1024,512]{1,0:T(8,128)(2,1)}, bf16[256,512]{1,0:T(8,128)(2,1)}, bf16[256,512]{1,0:T(8,128)(2,1)}) custom-call(s32[1]{0:T(128)} %bitcast.2.pos_ref, bf16[512,1536]{1,0:T(8,128)(2,1)} %get-tuple-element.58.q_ref, ...), custom_call_target="tpu_custom_call" | custom-call | flops 20132659200 | bytes 6291456 | tf_op jit(solution)/shard_map/attend_backward/pallas_call | solution.py:545
  492.1 9.7 %combine.6 = bf16[4,512,1536]{2,1,0:T(8,128)(2,1)} custom-call(s32[4]{0:T(128)} %broadcast_xor_fusion.1.at_ref, f32[8,8,512]{2,1,0:T(8,128)} %pad.14.codes_ref, bf16[5,832,1536]{2,1,0:T(8,128)(2,1)} %convolution_convert_fusion.1.rows_ref), custom_call_target="tpu_custom_call" | custom-call | flops 3271557120 | bytes 12681216 | tf_op jit(solution)/shard_map/combine/pallas_call | solution.py:163
  501.8 9.8 %combine.7 = bf16[4,512,1536]{2,1,0:T(8,128)(2,1)} custom-call(s32[4]{0:T(128)} %broadcast_xor_fusion.at_ref, f32[8,8,512]{2,1,0:T(8,128)} %pad.14.codes_ref, bf16[5,832,1536]{2,1,0:T(8,128)(2,1)} %convolution_convert_fusion.1.rows_ref), custom_call_target="tpu_custom_call" | custom-call | flops 3271557120 | bytes 12681216 | tf_op jit(solution)/shard_map/combine/pallas_call | solution.py:163
  531.4 9.5 %collective-permute-done.20 = bf16[256,1024]{1,0:T(8,128)(2,1)S(1)} collective-permute-done((bf16[256,1024]{1,0:T(8,128)(2,1)S(1)}, bf16[256,1024]{1,0:T(8,128)(2,1)S(1)}, u32[]{:S(2)}, u32[]{:S(2)}) %collective-permute-start.20) | collective-permute-done | bytes 524320 | tf_op jit(solution)/shard_map/ppermute | solution.py:635
  563.7 11.7 %collective-permute-done.34 = bf16[4,2,48,768]{3,2,0,1:T(8,128)(2,1)S(1)} collective-permute-done((bf16[4,2,48,768]{3,2,0,1:T(8,128)(2,1)S(1)}, bf16[4,2,48,768]{3,2,0,1:T(8,128)(2,1)S(1)}, u32[]{:S(2)}, u32[]{:S(2)}) %collective-permute-start.34) | collective-permute-done | bytes 589856 | tf_op jit(solution)/shard_map/ppermute | solution.py:186
  597.6 16.1 %collective-permute-done.37 = bf16[48,1536]{1,0:T(8,128)(2,1)S(1)} collective-permute-done((bf16[48,1536]{1,0:T(8,128)(2,1)S(1)}, bf16[48,1536]{1,0:T(8,128)(2,1)S(1)}, u32[]{:S(2)}, u32[]{:S(2)}) %collective-permute-start.37) | collective-permute-done | bytes 147488 | tf_op jit(solution)/shard_map/ppermute | solution.py:670
  620.1 18.1 %collective-permute-done.25 = bf16[4,2,48,1408]{3,2,1,0:T(8,128)(2,1)S(1)} collective-permute-done((bf16[4,2,48,1408]{3,2,1,0:T(8,128)(2,1)S(1)}, bf16[4,2,48,1408]{3,2,1,0:T(8,128)(2,1)S(1)}, u32[]{:S(2)}, u32[]{:S(2)}) %collective-permute-start.25) | collective-permute-done | bytes 1081376 | tf_op jit(solution)/shard_map/ppermute | solution.py:186
  640.5 8.2 collective-permute-done.24
  657.7 9.1 %add_convert_fusion = bf16[4,512,1536]{2,1,0:T(8,128)(2,1)} fusion(bf16[4,512,1536]{2,1,0:T(8,128)(2,1)} %collective-permute-done.14, bf16[4,512,1536]{2,1,0:T(8,128)(2,1)} %combine.6), kind=kLoop, calls=%fused_computation.3 | loop fusion | flops 12582912 | bytes 18874368 | tf_op jit(solution)/shard_map/convert_element_type | solution.py:228
  666.8 26.4 %collective-permute-done.28 = bf16[48,2688]{1,0:T(8,128)(2,1)S(1)} collective-permute-done((bf16[48,2688]{1,0:T(8,128)(2,1)S(1)}, bf16[48,2688]{1,0:T(8,128)(2,1)S(1)}, u32[]{:S(2)}, u32[]{:S(2)}) %collective-permute-start.28) | collective-permute-done | bytes 258080 | tf_op jit(solution)/shard_map/ppermute | solution.py:670
  724.0 17.3 %collective-permute-done.17 = bf16[2,512,768]{2,1,0:T(8,128)(2,1)} collective-permute-done((bf16[2,512,768]{2,1,0:T(8,128)(2,1)}, bf16[2,512,768]{2,1,0:T(8,128)(2,1)}, u32[]{:S(2)}, u32[]{:S(2)}) %collective-permute-start.17) | collective-permute-done | bytes 1572896 | tf_op jit(solution)/shard_map/ppermute | solution.py:186
  751.2 14.1 %collective-permute-done.48 = bf16[5,32,1536]{2,1,0:T(8,128)(2,1)S(1)} collective-permute-done((bf16[5,32,1536]{2,1,0:T(8,128)(2,1)}, bf16[5,32,1536]{2,1,0:T(8,128)(2,1)S(1)}, u32[]{:S(2)}, u32[]{:S(2)}) %collective-permute-start.48) | collective-permute-done | bytes 491552 | tf_op jit(solution)/shard_map/ppermute | solution.py:186
  767.3 11.2 %collective-permute-done.18 = bf16[512,768]{1,0:T(8,128)(2,1)S(1)} collective-permute-done((bf16[512,768]{1,0:T(8,128)(2,1)S(1)}, bf16[512,768]{1,0:T(8,128)(2,1)S(1)}, u32[]{:S(2)}, u32[]{:S(2)}) %collective-permute-start.18) | collective-permute-done | bytes 786464 | tf_op jit(solution)/shard_map/ppermute | solution.py:186
  800.4 11.4 %collective-permute-done.42 = bf16[5,96,512]{2,1,0:T(8,128)(2,1)S(1)} collective-permute-done((bf16[5,96,512]{2,1,0:T(8,128)(2,1)S(1)}, bf16[5,96,512]{2,1,0:T(8,128)(2,1)S(1)}, u32[]{:S(2)}, u32[]{:S(2)}) %collective-permute-start.42) | collective-permute-done | bytes 491552 | tf_op jit(solution)/shard_map/ppermute | solution.py:186
  812.0 9.3 %collective-permute-done.44 = bf16[5,96,512]{2,1,0:T(8,128)(2,1)S(1)} collective-permute-done((bf16[5,96,512]{2,1,0:T(8,128)(2,1)S(1)}, bf16[5,96,512]{2,1,0:T(8,128)(2,1)S(1)}, u32[]{:S(2)}, u32[]{:S(2)}) %collective-permute-start.44) | collective-permute-done | bytes 491552 | tf_op jit(solution)/shard_map/ppermute | solution.py:186
  821.4 10.8 %collective-permute-done.45 = bf16[5,96,512]{2,1,0:T(8,128)(2,1)S(1)} collective-permute-done((bf16[5,96,512]{2,1,0:T(8,128)(2,1)S(1)}, bf16[5,96,512]{2,1,0:T(8,128)(2,1)S(1)}, u32[]{:S(2)}, u32[]{:S(2)}) %collective-permute-start.45) | collective-permute-done | bytes 491552 | tf_op jit(solution)/shard_map/ppermute | solution.py:186
  (383 shorter events, 254.2 us)
Async XLA Ops:
  7.2 120.4 %all-gather.5.cloned.1.call-start = ((), (), s32[]{:S(2)}) async-start(), calls=%async_computation.6 | async-start | bytes 14598144 | tf_op jit(solution)/shard_map/all_gather | solution.py:762
  12.4 177.8 %all-gather.7.cloned.1.call-start = ((), (), s32[]{:S(2)}) async-start(), calls=%async_computation.7 | async-start | bytes 14155776 | tf_op jit(solution)/shard_map/all_gather | solution.py:809
  23.5 25.0 %collective-permute-start = (bf16[2,256,512]{2,1,0:T(8,128)(2,1)}, bf16[2,256,512]{2,1,0:T(8,128)(2,1)}, u32[]{:S(2)}, u32[]{:S(2)}) collective-permute-start(bf16[2,256,512]{2,1,0:T(8,128)(2,1)} %get-tuple-element.42), channel_id=1, source_target_pairs={{0,4},{2,6},{4,0},{6,2},{1,5},{3,7},{5,1},{7,3},{8,12},{10,14},{12... | collective-permute-start | bytes 1572872 | tf_op jit(solution)/shard_map/ppermute | solution.py:186
  24.7 29.7 %collective-permute-start.1 = (bf16[2,256,512]{2,1,0:T(8,128)(2,1)}, bf16[2,256,512]{2,1,0:T(8,128)(2,1)}, u32[]{:S(2)}, u32[]{:S(2)}) collective-permute-start(bf16[2,256,512]{2,1,0:T(8,128)(2,1)} %get-tuple-element.42), channel_id=1, source_target_pairs={{0,2},{2,0},{4,6},{6,4},{1,3},{3,1},{5,7},{7,5},{8,10},{10,8},{12,... | collective-permute-start | bytes 1572872 | tf_op jit(solution)/shard_map/ppermute | solution.py:186
  116.9 592.0 %reduce-scatter.8.cloned.1.call-start = ((), (), s32[]{:S(2)}) async-start(), calls=%async_computation.5 | async-start | bytes 9830400 | tf_op jit(solution)/shard_map/reduce_scatter | solution.py:600
  252.3 530.1 %reduce-scatter.4.cloned.1.call-start = ((), (), s32[]{:S(2)}) async-start(), calls=%async_computation.3 | async-start | bytes 9830400 | tf_op jit(solution)/shard_map/reduce_scatter | solution.py:600
  339.4 450.1 %reduce-scatter.6.cloned.1.call-start = ((), (), s32[]{:S(2)}) async-start(), calls=%async_computation.4 | async-start | bytes 9830400 | tf_op jit(solution)/shard_map/reduce_scatter | solution.py:600
  353.6 39.6 %collective-permute-start.8 = (bf16[2,512,768]{2,1,0:T(8,128)(2,1)}, bf16[2,512,768]{2,1,0:T(8,128)(2,1)}, u32[]{:S(2)}, u32[]{:S(2)}) collective-permute-start(bf16[2,512,768]{2,1,0:T(8,128)(2,1)} %pad_maximum_fusion.3), channel_id=1, source_target_pairs={{0,1},{1,0},{2,3},{3,2},{4,5},{5,4},{6,7},{7,6},{8,9},{9,8},{10,11... | collective-permute-start | bytes 4718600 | tf_op jit(solution)/shard_map/ppermute | solution.py:186
  354.2 39.0 %collective-permute-start.7 = (bf16[2,512,768]{2,1,0:T(8,128)(2,1)S(1)}, bf16[2,512,768]{2,1,0:T(8,128)(2,1)}, u32[]{:S(2)}, u32[]{:S(2)}) collective-permute-start(bf16[2,512,768]{2,1,0:T(8,128)(2,1)S(1)} %slice.188), channel_id=1, source_target_pairs={{0,4},{2,6},{4,0},{6,2},{1,5},{3,7},{5,1},{7,3},{8,12},{10,14},{12... | collective-permute-start | bytes 4718600 | tf_op jit(solution)/shard_map/ppermute | solution.py:186
  355.0 35.3 %collective-permute-start.13 = (f32[2,2,5,512]{3,1,2,0:T(2,128)S(1)}, f32[2,2,5,512]{3,1,2,0:T(2,128)S(1)}, u32[]{:S(2)}, u32[]{:S(2)}) collective-permute-start(f32[2,2,5,512]{3,1,2,0:T(2,128)S(1)} %bitcast.318), channel_id=1, source_target_pairs={{0,1},{1,0},{2,3},{3,2},{4,5},{5,4},{6,7},{7,6},{8,9},{9,8},{10,11... | collective-permute-start | bytes 122888 | tf_op jit(solution)/shard_map/ppermute | solution.py:186
  516.7 24.2 %collective-permute-start.20 = (bf16[256,1024]{1,0:T(8,128)(2,1)S(1)}, bf16[256,1024]{1,0:T(8,128)(2,1)S(1)}, u32[]{:S(2)}, u32[]{:S(2)}) collective-permute-start(bf16[256,1024]{1,0:T(8,128)(2,1)S(1)} %pad_maximum_fusion.6), channel_id=1, source_target_pairs={{0,4},{2,6},{4,0},{6,2},{1,5},{3,7},{5,1},{7,3},{8,12},{10,14},{12... | collective-permute-start | bytes 1572872 | tf_op jit(solution)/shard_map/ppermute | solution.py:635
  518.0 23.6 %collective-permute-start.21 = (bf16[256,1024]{1,0:T(8,128)(2,1)S(1)}, bf16[256,1024]{1,0:T(8,128)(2,1)S(1)}, u32[]{:S(2)}, u32[]{:S(2)}) collective-permute-start(bf16[256,1024]{1,0:T(8,128)(2,1)S(1)} %pad_maximum_fusion.7), channel_id=1, source_target_pairs={{0,6},{2,0},{4,2},{6,4},{1,7},{3,1},{5,3},{7,5},{8,14},{10,8},{12,... | collective-permute-start | bytes 1572872 | tf_op jit(solution)/shard_map/ppermute | solution.py:635
  526.4 31.4 %collective-permute-start.31 = (bf16[4,2,2,48,1536]{4,3,0,1,2:T(8,128)(2,1)}, bf16[4,2,2,48,1536]{4,3,0,1,2:T(8,128)(2,1)}, u32[]{:S(2)}, u32[]{:S(2)}) collective-permute-start(bf16[4,2,2,48,1536]{4,3,0,1,2:T(8,128)(2,1)} %bitcast.278), channel_id=1, source_target_pairs={{0,2},{2,0},{4,6},{6,4},{1,3},{3,1},{5,7},{7,5},{8,10},{10,8},{12,... | collective-permute-start | bytes 7077896 | tf_op jit(solution)/shard_map/ppermute | solution.py:186
  527.0 130.7 %collective-permute-start.14 = (bf16[4,512,1536]{2,1,0:T(8,128)(2,1)}, bf16[4,512,1536]{2,1,0:T(8,128)(2,1)}, u32[]{:S(2)}, u32[]{:S(2)}) collective-permute-start(bf16[4,512,1536]{2,1,0:T(8,128)(2,1)} %combine.7), channel_id=1, source_target_pairs={{0,2},{2,0},{4,6},{6,4},{1,3},{3,1},{5,7},{7,5},{8,10},{10,8},{12,... | collective-permute-start | bytes 18874376 | tf_op jit(solution)/shard_map/ppermute | solution.py:186
  557.7 29.8 %collective-permute-start.22 = (bf16[4,2,2,48,2688]{4,3,2,1,0:T(8,128)(2,1)}, bf16[4,2,2,48,2688]{4,3,2,1,0:T(8,128)(2,1)S(1)}, u32[]{:S(2)}, u32[]{:S(2)}) collective-permute-start(bf16[4,2,2,48,2688]{4,3,2,1,0:T(8,128)(2,1)} %dynamic-slice_bitcast_fusion), channel_id=1, source_target_pairs={{0,2},{2,0},{4,6},{6,4},{1,3},{3,1},{5,7},{7,5},{8,10},{10,8},{12,... | collective-permute-start | bytes 12386312 | tf_op jit(solution)/shard_map/ppermute | solution.py:186
  585.0 28.7 %collective-permute-start.37 = (bf16[48,1536]{1,0:T(8,128)(2,1)S(1)}, bf16[48,1536]{1,0:T(8,128)(2,1)S(1)}, u32[]{:S(2)}, u32[]{:S(2)}) collective-permute-start(bf16[48,1536]{1,0:T(8,128)(2,1)S(1)} %get-tuple-element.218), channel_id=1, source_target_pairs={{0,16},{8,24},{16,0},{24,8},{1,17},{9,25},{17,1},{25,9},{2,18},{10... | collective-permute-start | bytes 442376 | tf_op jit(solution)/shard_map/ppermute | solution.py:670
  586.4 27.3 %collective-permute-start.38 = (bf16[48,1536]{1,0:T(8,128)(2,1)S(1)}, bf16[48,1536]{1,0:T(8,128)(2,1)S(1)}, u32[]{:S(2)}, u32[]{:S(2)}) collective-permute-start(bf16[48,1536]{1,0:T(8,128)(2,1)S(1)} %get-tuple-element.219), channel_id=1, source_target_pairs={{0,24},{8,0},{16,8},{24,16},{1,25},{9,1},{17,9},{25,17},{2,26},{10... | collective-permute-start | bytes 442376 | tf_op jit(solution)/shard_map/ppermute | solution.py:670
  588.9 29.4 %collective-permute-start.23 = (bf16[4,2,48,1280]{3,2,1,0:T(8,128)(2,1)S(1)}, bf16[4,2,48,1280]{3,2,1,0:T(8,128)(2,1)S(1)}, u32[]{:S(2)}, u32[]{:S(2)}) collective-permute-start(bf16[4,2,48,1280]{3,2,1,0:T(8,128)(2,1)S(1)} %dynamic-slice_bitcast_fusion.2), channel_id=1, source_target_pairs={{0,4},{2,6},{4,0},{6,2},{1,5},{3,7},{5,1},{7,3},{8,12},{10,14},{12... | collective-permute-start | bytes 2949128 | tf_op jit(solution)/shard_map/ppermute | solution.py:186
  615.5 22.6 %collective-permute-start.25 = (bf16[4,2,48,1408]{3,2,1,0:T(8,128)(2,1)S(1)}, bf16[4,2,48,1408]{3,2,1,0:T(8,128)(2,1)S(1)}, u32[]{:S(2)}, u32[]{:S(2)}) collective-permute-start(bf16[4,2,48,1408]{3,2,1,0:T(8,128)(2,1)S(1)} %dynamic-slice_bitcast_fusion.1), channel_id=1, source_target_pairs={{0,1},{1,0},{2,3},{3,2},{4,5},{5,4},{6,7},{7,6},{8,9},{9,8},{10,11... | collective-permute-start | bytes 3244040 | tf_op jit(solution)/shard_map/ppermute | solution.py:186
  618.6 30.1 %collective-permute-start.24 = (bf16[4,48,1280]{2,1,0:T(8,128)(2,1)S(1)}, bf16[4,48,1280]{2,1,0:T(8,128)(2,1)S(1)}, u32[]{:S(2)}, u32[]{:S(2)}) collective-permute-start(bf16[4,48,1280]{2,1,0:T(8,128)(2,1)S(1)} %dynamic-slice_bitcast_fusion.15), channel_id=1, source_target_pairs={{0,1},{1,0},{2,3},{3,2},{4,5},{5,4},{6,7},{7,6},{8,9},{9,8},{10,11... | collective-permute-start | bytes 1474568 | tf_op jit(solution)/shard_map/ppermute | solution.py:186
  649.2 44.1 %collective-permute-start.28 = (bf16[48,2688]{1,0:T(8,128)(2,1)S(1)}, bf16[48,2688]{1,0:T(8,128)(2,1)S(1)}, u32[]{:S(2)}, u32[]{:S(2)}) collective-permute-start(bf16[48,2688]{1,0:T(8,128)(2,1)S(1)} %get-tuple-element.215), channel_id=1, source_target_pairs={{0,16},{8,24},{16,0},{24,8},{1,17},{9,25},{17,1},{25,9},{2,18},{10... | collective-permute-start | bytes 774152 | tf_op jit(solution)/shard_map/ppermute | solution.py:670
  656.3 42.4 %collective-permute-start.29 = (bf16[48,2688]{1,0:T(8,128)(2,1)S(1)}, bf16[48,2688]{1,0:T(8,128)(2,1)S(1)}, u32[]{:S(2)}, u32[]{:S(2)}) collective-permute-start(bf16[48,2688]{1,0:T(8,128)(2,1)S(1)} %get-tuple-element.216), channel_id=1, source_target_pairs={{0,24},{8,0},{16,8},{24,16},{1,25},{9,1},{17,9},{25,17},{2,26},{10... | collective-permute-start | bytes 774152 | tf_op jit(solution)/shard_map/ppermute | solution.py:670
  705.8 35.5 %collective-permute-start.17 = (bf16[2,512,768]{2,1,0:T(8,128)(2,1)}, bf16[2,512,768]{2,1,0:T(8,128)(2,1)}, u32[]{:S(2)}, u32[]{:S(2)}) collective-permute-start(bf16[2,512,768]{2,1,0:T(8,128)(2,1)} %pad_maximum_fusion.4), channel_id=1, source_target_pairs={{0,1},{1,0},{2,3},{3,2},{4,5},{5,4},{6,7},{7,6},{8,9},{9,8},{10,11... | collective-permute-start | bytes 4718600 | tf_op jit(solution)/shard_map/ppermute | solution.py:186
  705.9 35.4 %collective-permute-start.15 = (bf16[2,512,768]{2,1,0:T(8,128)(2,1)}, bf16[2,512,768]{2,1,0:T(8,128)(2,1)}, u32[]{:S(2)}, u32[]{:S(2)}) collective-permute-start(bf16[2,512,768]{2,1,0:T(8,128)(2,1)} %slice.235), channel_id=1, source_target_pairs={{0,4},{2,6},{4,0},{6,2},{1,5},{3,7},{5,1},{7,3},{8,12},{10,14},{12... | collective-permute-start | bytes 4718600 | tf_op jit(solution)/shard_map/ppermute | solution.py:186
  719.6 31.5 %collective-permute-start.47 = (bf16[5,32,1536]{2,1,0:T(8,128)(2,1)}, bf16[5,32,1536]{2,1,0:T(8,128)(2,1)S(1)}, u32[]{:S(2)}, u32[]{:S(2)}) collective-permute-start(bf16[5,32,1536]{2,1,0:T(8,128)(2,1)} %get-tuple-element.196), channel_id=1, source_target_pairs={{0,4},{2,6},{4,0},{6,2},{1,5},{3,7},{5,1},{7,3},{8,12},{10,14},{12... | collective-permute-start | bytes 1474568 | tf_op jit(solution)/shard_map/ppermute | solution.py:186
  719.9 45.4 %collective-permute-start.48 = (bf16[5,32,1536]{2,1,0:T(8,128)(2,1)}, bf16[5,32,1536]{2,1,0:T(8,128)(2,1)S(1)}, u32[]{:S(2)}, u32[]{:S(2)}) collective-permute-start(bf16[5,32,1536]{2,1,0:T(8,128)(2,1)} %get-tuple-element.195), channel_id=1, source_target_pairs={{0,6},{2,4},{4,2},{6,0},{1,7},{3,5},{5,3},{7,1},{8,14},{10,12},{12... | collective-permute-start | bytes 1474568 | tf_op jit(solution)/shard_map/ppermute | solution.py:186
  743.5 21.9 %collective-permute-start.16 = (bf16[512,768]{1,0:T(8,128)(2,1)S(1)}, bf16[512,768]{1,0:T(8,128)(2,1)S(1)}, u32[]{:S(2)}, u32[]{:S(2)}) collective-permute-start(bf16[512,768]{1,0:T(8,128)(2,1)S(1)} %get-tuple-element.177), channel_id=1, source_target_pairs={{0,1},{1,0},{2,3},{3,2},{4,5},{5,4},{6,7},{7,6},{8,9},{9,8},{10,11... | collective-permute-start | bytes 2359304 | tf_op jit(solution)/shard_map/ppermute | solution.py:186
  744.8 33.7 %collective-permute-start.18 = (bf16[512,768]{1,0:T(8,128)(2,1)S(1)}, bf16[512,768]{1,0:T(8,128)(2,1)S(1)}, u32[]{:S(2)}, u32[]{:S(2)}) collective-permute-start(bf16[512,768]{1,0:T(8,128)(2,1)S(1)} %get-tuple-element.178), channel_id=1, source_target_pairs={{0,4},{2,6},{4,0},{6,2},{1,5},{3,7},{5,1},{7,3},{8,12},{10,14},{12... | collective-permute-start | bytes 2359304 | tf_op jit(solution)/shard_map/ppermute | solution.py:186
  788.8 23.0 %collective-permute-start.42 = (bf16[5,96,512]{2,1,0:T(8,128)(2,1)S(1)}, bf16[5,96,512]{2,1,0:T(8,128)(2,1)S(1)}, u32[]{:S(2)}, u32[]{:S(2)}) collective-permute-start(bf16[5,96,512]{2,1,0:T(8,128)(2,1)S(1)} %get-tuple-element.198), channel_id=1, source_target_pairs={{0,6},{2,4},{4,2},{6,0},{1,7},{3,5},{5,3},{7,1},{8,14},{10,12},{12... | collective-permute-start | bytes 1474568 | tf_op jit(solution)/shard_map/ppermute | solution.py:186
  790.9 21.0 %collective-permute-start.43 = (bf16[5,96,512]{2,1,0:T(8,128)(2,1)S(1)}, bf16[5,96,512]{2,1,0:T(8,128)(2,1)S(1)}, u32[]{:S(2)}, u32[]{:S(2)}) collective-permute-start(bf16[5,96,512]{2,1,0:T(8,128)(2,1)S(1)} %get-tuple-element.203), channel_id=1, source_target_pairs={{0,2},{2,0},{4,6},{6,4},{1,3},{3,1},{5,7},{7,5},{8,10},{10,8},{12,... | collective-permute-start | bytes 1474568 | tf_op jit(solution)/shard_map/ppermute | solution.py:186
  791.0 30.3 %collective-permute-start.44 = (bf16[5,96,512]{2,1,0:T(8,128)(2,1)S(1)}, bf16[5,96,512]{2,1,0:T(8,128)(2,1)S(1)}, u32[]{:S(2)}, u32[]{:S(2)}) collective-permute-start(bf16[5,96,512]{2,1,0:T(8,128)(2,1)S(1)} %get-tuple-element.202), channel_id=1, source_target_pairs={{0,4},{2,6},{4,0},{6,2},{1,5},{3,7},{5,1},{7,3},{8,12},{10,14},{12... | collective-permute-start | bytes 1474568 | tf_op jit(solution)/shard_map/ppermute | solution.py:186
  795.6 36.7 %collective-permute-start.45 = (bf16[5,96,512]{2,1,0:T(8,128)(2,1)S(1)}, bf16[5,96,512]{2,1,0:T(8,128)(2,1)S(1)}, u32[]{:S(2)}, u32[]{:S(2)}) collective-permute-start(bf16[5,96,512]{2,1,0:T(8,128)(2,1)S(1)} %get-tuple-element.201), channel_id=1, source_target_pairs={{0,6},{2,4},{4,2},{6,0},{1,7},{3,5},{5,3},{7,1},{8,14},{10,12},{12... | collective-permute-start | bytes 1474568 | tf_op jit(solution)/shard_map/ppermute | solution.py:186
  (79 other events, 678.9 us)
Sparse Core Ops, SparseCore 0:
  12.6 85.9 all-gather.4
  117.0 73.1 all-gather.6
  252.5 135.7 reduce-scatter.7
  391.0 136.7 reduce-scatter.3
  530.0 171.5 reduce-scatter.5

commit v5 on v4

--- a/solution.py
+++ b/solution.py
@@ -172,11 +172,7 @@
             out_specs=pl.BlockSpec((1, tokens, width), lambda b, at: (b, 0, 0)),
         ),
         out_shape=jax.ShapeDtypeStruct((count, tokens, width), jnp.bfloat16),
-        cost_estimate=pl.CostEstimate(
-            flops=2 * count * own * slots * tokens * width,
-            transcendentals=0,
-            bytes_accessed=2 * count * (tokens + own * slots) * width,
-        ),
+        cost_estimate=pl.CostEstimate(flops=1, transcendentals=0, bytes_accessed=1),
         name="combine",
     )(at, codes, rows)
 
@@ -228,41 +224,50 @@
     return (left.astype(jnp.float32) + right.astype(jnp.float32)).astype(jnp.bfloat16)
 
 
-def start_scatter(codes, rows, own, slots, group):
-    blocks = codes.shape[0]
-    if group != ("ctx", "expert") or lax.axis_size("ctx") != 4 or lax.axis_size("expert") != 2:
-        every = jnp.arange(blocks, dtype=jnp.int32)
+def pair_sums(codes, rows, own, slots, group):
+    if not paired(group):
+        every = jnp.arange(codes.shape[0], dtype=jnp.int32)
         return lax.psum_scatter(
             combine(every, codes, rows, own, slots), group, scatter_dimension=0
-        )
+        ), None
     here = lax.axis_index(group).astype(jnp.int32)
     far = here ^ jnp.array([2, 3, 6, 7], jnp.int32)
     near = here ^ jnp.array([0, 1, 4, 5], jnp.int32)
-    sent = swap(combine(far, codes, rows, own, slots), "ctx", 1)
-    return added(combine(near, codes, rows, own, slots), sent)
-
-
-def finish_scatter(part, middle=None, later=None, work=None):
+    return combine(far, codes, rows, own, slots), combine(near, codes, rows, own, slots)
+
+
+def scatter_one(far, near):
+    return far if near is None else added(near, swap(far, "ctx", 1))
+
+
+def scatter_two(part):
     if part.ndim == 2:
-        return part.astype(jnp.float32), None if work is None else work(later)
+        return part, ()
     half = part.shape[-1] // 2
     left, right = part[:, :, :half], part[:, :, half:]
-    left_sent = swap(left[2:], "ctx", 2)
-    right_sent = swap(jnp.stack([right[1], right[3]]), "expert", 1)
-    if work is not None:
-        left_sent, right_sent, _, later = lax.optimization_barrier(
-            (left_sent, right_sent, middle, later)
-        )
-    left_on = swap(added(left[1], left_sent[1]), "expert", 1)
-    right_on = swap(added(right[2], right_sent[1]), "ctx", 2)
-    made = None
-    if work is not None:
-        left_on, right_on, made = lax.optimization_barrier((left_on, right_on, work(later)))
+    moved = swap(left[2:], "ctx", 2), swap(jnp.stack([right[1], right[3]]), "expert", 1)
+    return (left[0], left[1], right[0], right[2]), moved
+
+
+def scatter_three(kept, moved):
+    if not moved:
+        return kept, ()
+    left, left_other, right, right_other = kept
+    left_sent, right_sent = moved
+    onward = (
+        swap(added(left_other, left_sent[1]), "expert", 1),
+        swap(added(right_other, right_sent[1]), "ctx", 2),
+    )
+    return (left, left_sent[0], right, right_sent[0]), onward
+
+
+def scatter_end(kept, moved):
+    if not moved:
+        return kept.astype(jnp.float32)
     wide = lambda *pieces: sum(piece.astype(jnp.float32) for piece in pieces)
-    whole = jnp.concatenate(
-        [wide(left[0], left_sent[0], left_on), wide(right[0], right_sent[0], right_on)], axis=1
-    )
-    return whole, made
+    return jnp.concatenate(
+        [wide(kept[0], kept[1], moved[0]), wide(kept[2], kept[3], moved[1])], axis=1
+    )
 
 
 def lane_half(shape):
@@ -403,13 +408,12 @@
     finish([(wide, vp_ref[...]), (near, vc_ref[...])], pl.ds(prompt_rows, total_rows - prompt_rows))
 
 
-def attend_forward(q_lin, key_prompt, value_prompt, key_cont, value_cont, cosine, sine, start, rows, cont_len):
+def attend_forward(q_lin, prompt_kv, cont_kv, cosine, sine, start, rows, cont_len):
     tokens, width = q_lin.shape
     heads = width // HEAD_SIZE
-    group = heads // (key_prompt.shape[1] // HEAD_SIZE)
-    keys, near = key_prompt.shape[0], key_cont.shape[0]
+    group = heads // (prompt_kv.shape[2] // HEAD_SIZE)
+    keys, near = prompt_kv.shape[1], cont_kv.shape[1]
     tile = lambda h, *_: (0, h // 2)
-    key_tile = lambda h, *_: (0, h // (2 * group))
     same = lambda h, *_: (0, 0)
     return pl.pallas_call(
         partial(attend_forward_body, group, rows, cont_len),
@@ -420,10 +424,10 @@
                 pl.BlockSpec((tokens, 128), tile),
                 pl.BlockSpec((tokens, 128), same),
                 pl.BlockSpec((tokens, 128), same),
-                pl.BlockSpec((keys, 128), key_tile),
-                pl.BlockSpec((keys, 128), key_tile),
-                pl.BlockSpec((near, 128), key_tile),
-                pl.BlockSpec((near, 128), key_tile),
+                pl.BlockSpec((None, keys, 128), lambda h, *_: (0, 0, h // (2 * group))),
+                pl.BlockSpec((None, keys, 128), lambda h, *_: (1, 0, h // (2 * group))),
+                pl.BlockSpec((None, near, 128), lambda h, *_: (0, 0, h // (2 * group))),
+                pl.BlockSpec((None, near, 128), lambda h, *_: (1, 0, h // (2 * group))),
             ],
             out_specs=[
                 pl.BlockSpec((tokens, 128), tile),
@@ -442,7 +446,7 @@
             bytes_accessed=8 * tokens * width,
         ),
         name="attend_forward",
-    )(start, q_lin, cosine, sine, key_prompt, value_prompt, key_cont, value_cont)
+    )(start, q_lin, cosine, sine, prompt_kv, prompt_kv, cont_kv, cont_kv)
 
 
 def attend_backward_body(
@@ -530,14 +534,14 @@
 
 
 def attend_backward(
-    query, d_out, result, log_total, key_prompt, value_prompt, key_cont, value_cont, cosine, sine,
+    query, d_out, result, log_total, prompt_kv, cont_kv, cosine, sine,
     key_cosine, key_sine, start, rows, cont_len,
 ):
     tokens, width = query.shape
     heads = width // HEAD_SIZE
-    key_width = key_prompt.shape[1]
+    key_width = prompt_kv.shape[2]
     group = heads // (key_width // HEAD_SIZE)
-    keys, near = key_prompt.shape[0], key_cont.shape[0]
+    keys, near = prompt_kv.shape[1], cont_kv.shape[1]
     chunk = min(256, keys)
     tile = lambda h, *_: (0, h // 2)
     key_tile = lambda h, *_: (0, h // (2 * group))
@@ -556,10 +560,10 @@
                 pl.BlockSpec((tokens, 128), same),
                 pl.BlockSpec((keys + near, 128), same),
                 pl.BlockSpec((keys + near, 128), same),
-                pl.BlockSpec((keys, 128), key_tile),
-                pl.BlockSpec((keys, 128), key_tile),
-                pl.BlockSpec((near, 128), key_tile),
-                pl.BlockSpec((near, 128), key_tile),
+                pl.BlockSpec((None, keys, 128), lambda h, *_: (0, 0, h // (2 * group))),
+                pl.BlockSpec((None, keys, 128), lambda h, *_: (1, 0, h // (2 * group))),
+                pl.BlockSpec((None, near, 128), lambda h, *_: (0, 0, h // (2 * group))),
+                pl.BlockSpec((None, near, 128), lambda h, *_: (1, 0, h // (2 * group))),
             ],
             out_specs=[
                 pl.BlockSpec((tokens, 128), tile),
@@ -587,30 +591,36 @@
         ),
         name="attend_backward",
     )(
-        start, query, d_out, result, log_total, cosine, sine, key_cosine, key_sine, key_prompt,
-        value_prompt, key_cont, value_cont,
+        start, query, d_out, result, log_total, cosine, sine, key_cosine, key_sine, prompt_kv,
+        prompt_kv, cont_kv, cont_kv,
     )
 
 
 def reduce_experts(grad, split):
+    axes = ("dp", "ctx") if split == 1 else "dp"
+    return lax.psum_scatter(grad, axes, scatter_dimension=1, tiled=True)
+
+
+def send_experts(part, split):
+    size = lax.axis_size("ctx")
     if split == 1:
-        return lax.psum_scatter(
-            grad, ("dp", "ctx"), scatter_dimension=1, tiled=True
-        ).astype(jnp.float32)
-    part = lax.psum_scatter(grad, "dp", scatter_dimension=1, tiled=True)
-    size = lax.axis_size("ctx")
+        return (part,)
     if size & (size - 1):
-        return lax.all_to_all(part, "ctx", split_axis=1, concat_axis=0, tiled=True).astype(
-            jnp.float32
-        )
+        return (lax.all_to_all(part, "ctx", split_axis=1, concat_axis=0, tiled=True),)
     own, rows, width = part.shape
     here = lax.axis_index("ctx")
     part = part.reshape(own, size, rows // size, width)
-    whole = jnp.zeros((own * size, rows // size, width), jnp.float32)
-    for step in range(size):
-        piece = lax.dynamic_index_in_dim(part, here ^ step, 1, keepdims=False)
-        if step:
-            piece = swap(piece, "ctx", step)
+    pieces = [lax.dynamic_index_in_dim(part, here ^ step, 1, keepdims=False) for step in range(size)]
+    return tuple(swap(piece, "ctx", step) if step else piece for step, piece in enumerate(pieces))
+
+
+def place_experts(pieces):
+    if len(pieces) == 1:
+        return pieces[0].astype(jnp.float32)
+    here = lax.axis_index("ctx")
+    own, rows, width = pieces[0].shape
+    whole = jnp.zeros((own * len(pieces), rows, width), jnp.float32)
+    for step, piece in enumerate(pieces):
         whole = lax.dynamic_update_slice_in_dim(
             whole, piece.astype(jnp.float32), (here ^ step) * own, axis=0
         )
@@ -640,25 +650,45 @@
     return (total[:, : d_key.shape[1]], total[:, d_key.shape[1] :])
 
 
-def fold_dense(grad, cut):
+def folds(grad):
+    return paired(("ctx", "expert")) and grad.shape[0] % (64 * lax.axis_size("dp")) == 0
+
+
+def fold_one(grad):
+    if not folds(grad):
+        return lax.psum_scatter(grad, ("dp", "ctx"), scatter_dimension=0, tiled=True)
     rows, width = grad.shape
     parts = lax.axis_size("dp")
     core = lax.axis_index("ctx") % 2
+    take = partial(lax.dynamic_index_in_dim, axis=2, keepdims=False)
+    grad = grad.reshape(parts, 2, 2, 2, rows // (8 * parts), width)
+    return added(take(grad, core), swap(take(grad, 1 - core), "ctx", 1))
+
+
+def fold_two(one, cut):
+    if one.ndim == 2:
+        return one, ()
     pair = lax.axis_index("ctx") // 2
     side = lax.axis_index("expert")
     take = partial(lax.dynamic_index_in_dim, keepdims=False)
-    grad = grad.reshape(parts, 2, 2, 2, rows // (8 * parts), width)
-    one = added(take(grad, core, 2), swap(take(grad, 1 - core, 2), "ctx", 1))
     left, right = one[..., :cut], one[..., cut:]
-    left_sent = swap(take(left, 1 - pair, 1), "ctx", 2)
-    right_sent = swap(take(right, 1 - side, 2), "expert", 1)
-    left = added(take(left, pair, 1), left_sent)
-    right = added(take(right, side, 2), right_sent)
+    moved = swap(take(left, 1 - pair, 1), "ctx", 2), swap(take(right, 1 - side, 2), "expert", 1)
+    return (take(left, pair, 1), take(right, side, 2)), moved
+
+
+def fold_three(kept, moved):
+    if not moved:
+        return kept
+    pair = lax.axis_index("ctx") // 2
+    side = lax.axis_index("expert")
+    take = partial(lax.dynamic_index_in_dim, keepdims=False)
+    left, right = added(kept[0], moved[0]), added(kept[1], moved[1])
     left_sent = swap(take(left, 1 - side, 1), "expert", 1)
     right_sent = swap(take(right, 1 - pair, 1), "ctx", 2)
-    return jnp.concatenate(
+    whole = jnp.concatenate(
         [added(take(left, side, 1), left_sent), added(take(right, pair, 1), right_sent)], axis=-1
     )
+    return scatter_parts(whole)
 
 
 def scatter_parts(parts):
@@ -674,26 +704,14 @@
     return total.astype(jnp.bfloat16)
 
 
-def finish_dense(grad, folded):
-    if not folded:
+def finish_dense(grad, rows):
+    if grad.shape[0] == rows:
         return lax.psum(grad, "expert").astype(jnp.float32)
     other = swap(grad, "expert", 1)
     first = lax.axis_index("expert") == 0
     return jnp.concatenate(
         [jnp.where(first, grad, other), jnp.where(first, other, grad)], axis=0
     ).astype(jnp.float32)
-
-
-def start_dense(grad, cut):
-    parts = lax.axis_size("dp")
-    folded = (
-        lax.axis_size("ctx") == 4
-        and lax.axis_size("expert") == 2
-        and grad.shape[0] % (64 * parts) == 0
-    )
-    if not folded:
-        return lax.psum_scatter(grad, ("dp", "ctx"), scatter_dimension=0, tiled=True), False
-    return scatter_parts(fold_dense(grad, cut)), True
 
 
 def per_device(
@@ -797,10 +815,9 @@
         h1_low, key_weight, value_weight, cosine, sine, prompt_rows
     )
     prompt_kv = gather_keys(near_kv)
-    keys_values = (prompt_kv[0], prompt_kv[1], cont_kv[0], cont_kv[1])
     q_lin = jnp.dot(h1_low, w_query, preferred_element_type=jnp.float32)
     query_row_block, merged_low, log_total = attend_forward(
-        q_lin, *keys_values, cosine, sine, start, prompt_rows, cont_len
+        q_lin, prompt_kv, cont_kv, cosine, sine, start, prompt_rows, cont_len
     )
     branch = jnp.dot(merged_low, w_out, preferred_element_type=jnp.float32)
     resid = tokens + RESID * branch
@@ -827,24 +844,6 @@
     grad_down = jnp.einsum(
         "ecf,ecd->efd", weighted, d_slot_rows, preferred_element_type=jnp.float32
     ).astype(jnp.bfloat16)
-    d_both, grad_down = lax.optimization_barrier((d_both, grad_down))
-    grad_down = reduce_experts(grad_down, split)
-    d_slots = jnp.einsum(
-        "ecf,edf->ecd", d_both, gate_up_own, preferred_element_type=jnp.float32
-    ).astype(jnp.bfloat16)
-    d_rows_parts, weighted, slot_rows = lax.optimization_barrier(
-        (start_scatter(own_codes, d_slots, own, slots, group), weighted, slot_rows)
-    )
-    grad_gate_up = jnp.einsum(
-        "ecd,ecf->edf", slot_rows, d_both, preferred_element_type=jnp.float32
-    ).astype(jnp.bfloat16)
-
-    def forward_rows(weighted):
-        return jnp.einsum(
-            "ecf,efd->ecd", weighted, down_own, preferred_element_type=jnp.float32
-        ).astype(jnp.bfloat16)
-
-    d_rows, expert_out = finish_scatter(d_rows_parts, grad_gate_up, weighted, forward_rows)
     d_gates_own = jnp.sum(
         jnp.where(
             picked,
@@ -853,15 +852,36 @@
         ),
         axis=2,
     )
-    d_gates = return_gates(d_gates_own, group, first_expert, expert_total)
-    cut = hidden_units
-    grad_gate_up = jnp.concatenate(
-        [
-            reduce_experts(grad_gate_up[..., :cut], split),
-            reduce_experts(grad_gate_up[..., cut:], split),
-        ],
-        axis=-1,
-    )
+    d_both, _, d_gates = lax.optimization_barrier(
+        (d_both, grad_down, return_gates(d_gates_own, group, first_expert, expert_total))
+    )
+    down_part = reduce_experts(grad_down, split)
+    d_slots = jnp.einsum(
+        "ecf,edf->ecd", d_both, gate_up_own, preferred_element_type=jnp.float32
+    ).astype(jnp.bfloat16)
+    part, weighted, slot_rows = lax.optimization_barrier(
+        (scatter_one(*pair_sums(own_codes, d_slots, own, slots, group)), weighted, slot_rows)
+    )
+    kept, moved = scatter_two(part)
+    grad_gate, grad_up = (
+        jnp.einsum(
+            "ecd,ecf->edf", slot_rows, d_part, preferred_element_type=jnp.float32
+        ).astype(jnp.bfloat16)
+        for d_part in (d_both[..., :hidden_units], d_both[..., hidden_units:])
+    )
+    expert_out = jnp.einsum(
+        "ecf,efd->ecd", weighted, down_own, preferred_element_type=jnp.float32
+    ).astype(jnp.bfloat16)
+    moved, grad_gate, grad_up, expert_out = lax.optimization_barrier(
+        (moved, grad_gate, grad_up, expert_out)
+    )
+    gate_part, up_part = reduce_experts(grad_gate, split), reduce_experts(grad_up, split)
+    kept, moved = scatter_three(kept, moved)
+    moved, sums = lax.optimization_barrier(
+        (moved, pair_sums(own_codes, expert_out, own, slots, group))
+    )
+    d_rows = scatter_end(kept, moved)
+    mixed_part = scatter_one(*sums)
     d_logits = (
         gates * (d_gates - jnp.sum(gates * d_gates, axis=0, keepdims=True))
     ).astype(jnp.bfloat16)
@@ -875,16 +895,27 @@
     grad_out = jnp.einsum(
         "tq,td->qd", merged_low, d_branch, preferred_element_type=jnp.float32
     ).astype(jnp.bfloat16)
-    grad_out = start_dense(grad_out, grad_out.shape[1] // 256 * 128)
+    out_cut = grad_out.shape[1] // 256 * 128
+    grad_out = fold_one(grad_out)
     merged_gradient = jnp.einsum(
         "td,qd->tq", d_branch, w_out, preferred_element_type=jnp.float32
     ).astype(jnp.bfloat16)
+    grad_out, mixed_part, down_part, merged_gradient = lax.optimization_barrier(
+        (grad_out, mixed_part, down_part, merged_gradient)
+    )
+    mixed_kept, mixed_moved = scatter_two(mixed_part)
+    out_kept, out_moved = fold_two(grad_out, out_cut)
+    down_sent = send_experts(down_part, split)
     d_query_low, d_key_prompt, d_value_prompt, d_key_cont, d_value_cont = attend_backward(
-        query_row_block, merged_gradient, merged_low, log_total, *keys_values, cosine, sine,
+        query_row_block, merged_gradient, merged_low, log_total, prompt_kv, cont_kv, cosine, sine,
         key_cosine, key_sine, start, prompt_rows, cont_len,
     )
-    expert_out, d_key_prompt = lax.optimization_barrier((expert_out, d_key_prompt))
-    mixed, _ = finish_scatter(start_scatter(own_codes, expert_out, own, slots, group))
+    mixed_moved, out_moved, down_sent, d_key_prompt = lax.optimization_barrier(
+        (mixed_moved, out_moved, down_sent, d_key_prompt)
+    )
+    mixed_kept, mixed_moved = scatter_three(mixed_kept, mixed_moved)
+    grad_out = fold_three(out_kept, out_moved)
+    mixed = scatter_end(mixed_kept, mixed_moved)
     output = resid + mixed
     y_prompt = output[:prompt_rows].astype(jnp.bfloat16)[None]
     y_cont = output[prompt_rows:].reshape(1, cont_count, cont_len, model_width).astype(jnp.bfloat16)
@@ -910,8 +941,18 @@
     dense = jnp.concatenate([grad_query, grad_key, grad_value, small], axis=1).astype(jnp.bfloat16)
     heads_width = QUERY_HEADS * HEAD_SIZE
     edge = heads_width + 2 * key_value_width
-    dense = finish_dense(*start_dense(dense, edge // 256 * 128))
-    grad_out = finish_dense(*grad_out)
+    dense, gate_part = lax.optimization_barrier((fold_one(dense), gate_part))
+    gate_sent = send_experts(gate_part, split)
+    dense_kept, dense_moved = fold_two(dense, edge // 256 * 128)
+    dense_moved, gate_sent = lax.optimization_barrier((dense_moved, gate_sent))
+    dense_rows = w_query.shape[0] // (lax.axis_size("dp") * lax.axis_size("ctx"))
+    dense = finish_dense(fold_three(dense_kept, dense_moved), dense_rows)
+    grad_out = finish_dense(grad_out, dense_rows)
+    grad_down = place_experts(down_sent)
+    grad_gate = place_experts(gate_sent)
+    dense, up_part = lax.optimization_barrier((dense, up_part))
+    grad_up = place_experts(send_experts(up_part, split))
+    grad_gate_up = jnp.concatenate([grad_gate, grad_up], axis=-1)
     return (
         y_prompt,
         y_cont,

time: 853 us -> 774 us (0.907)
  waiting for transfers between devices: 281 us -> 198 us
  other arithmetic: 76.2 us -> 88.5 us
  local copies, waits for them, and re-layouts: 66.6 us -> 55.2 us
  matrix products: 131 us -> 140 us
    ppermute x40, waiting for transfers between devices: 183 us -> 107 us  [swap(): return lax.ppermute(values, axis, [(i, i ^ bit) for i in range(size)])]
    slice x8 -> x10, local copies, waits for them, and re-layouts: 18.9 us -> 12.1 us  [the longest x3 4.77 us: fold_two(): left, right = (one[..., :cut], one[..., cut:])]
    dot_general x2 -> x3, matrix products: 38.8 us -> 42.9 us  [the longest x2 29.3 us: per_device(): jnp.einsum('ecd,ecf->edf', slot_rows, d_part, preferred_element_type=jnp....]
  transfers between devices with their start and end apart: 54 -> 54, of which waited for: 30 -> 23; matrix products, arithmetic and copies ran while one was open for 28% -> 34% of each run, Pallas kernels for 21% -> 23%
where the time goes in v5:
time: 774 us; the launch traced here: 765 us
  Pallas kernels  218 us (28%)
  waiting for transfers between devices  198 us (26%)
  matrix products  140 us (18%)
  other arithmetic  88.5 us (11%)
  local copies, waits for them, and re-layouts  55.2 us (7%)
  starting transfers between devices  50.1 us (6%)
  between operations  15.5 us (2%)
    ppermute x40, waiting for transfers between devices, swap(): return lax.ppermute(values, axis, [(i, i ^ bit) for i in range(size)])  107 us
    pallas_call x1, Pallas kernels, attend_backward(): pl.pallas_call(partial(attend_backward_body, group, rows, cont_len, chunk...  63.9 us
    pallas_call x1, Pallas kernels, attend_forward(): pl.pallas_call(partial(attend_forward_body, group, rows, cont_len), grid_...  50.4 us
    ppermute x6, waiting for transfers between devices, scatter_parts(): lax.ppermute(take(parts, (here + hop) % size), 'dp', [(i, (i + hop) % siz...  47.1 us
    pallas_call x4, Pallas kernels, combine(): pl.pallas_call(partial(combine_body, own, slots), grid_spec=pltpu.Prefetc...  39.1 us
    ppermute x40, starting transfers between devices, swap(): return lax.ppermute(values, axis, [(i, i ^ bit) for i in range(size)])  39 us
    convert_element_type x14, other arithmetic, added(): (left.astype(jnp.float32) + right.astype(jnp.float32)).astype(jnp.bfloat16)  33.4 us
    all_gather x1, waiting for transfers between devices, per_device(): rows_all = lax.all_gather(h2_low, group, axis=0, tiled=False)  32 us
  transfers between devices with their start and end apart: 54, of which 23 were waited for; matrix products, arithmetic and copies ran while one was open for 34% of the time, Pallas kernels for 23%

profile of v5, /device:TPU:9, one launch (start us, length us, event | category | flops | bytes accessed | tf_op | source)
XLA Modules:
  0.0 765.4 jit_solution(7165154254188469885)
XLA Ops:
  16.4 7.1 project_keys.1
  25.7 22.8 %collective-permute-done = bf16[2,256,512]{2,1,0:T(8,128)(2,1)} collective-permute-done((bf16[2,256,512]{2,1,0:T(8,128)(2,1)}, bf16[2,256,512]{2,1,0:T(8,128)(2,1)}, u32[]{:S(2)}, u32[]{:S(2)}) %collective-permute-start) | collective-permute-done | bytes 524320 | tf_op jit(solution)/shard_map/ppermute | solution.py:182
  50.2 6.6 fusion.131.q_ref
  65.9 50.4 %attend_forward.1 = (bf16[512,1536]{1,0:T(8,128)(2,1)}, bf16[512,1536]{1,0:T(8,128)(2,1)}, f32[24,8,512]{2,1,0:T(8,128)}) custom-call(s32[1]{0:T(128)} %bitcast.2.pos_ref, f32[512,1536]{1,0:T(8,128)} %fusion.131.q_ref, f32[512,128]{1,0:T(8,128)} %get-tuple-element.302.cos_ref, f32[512,128]{1,0:T(8,128)} %get-tuple-element.301.sin_ref, ...), custom_call_target="tpu_custom_call" | custom-call | flops 8053063680 | bytes 6291456 | tf_op jit(solution)/shard_map/attend_forward/pallas_call | solution.py:418
  137.7 14.3 %dispatch.2 = bf16[5,832,1536]{2,1,0:T(8,128)(2,1)} custom-call(f32[8,8,512]{2,1,0:T(8,128)} %pad.14.codes_ref, bf16[8,528,1536]{2,1,0:T(8,128)(2,1)} %bitcast.271), custom_call_target="tpu_custom_call" | custom-call | flops 6543114240 | bytes 25362432 | tf_op jit(solution)/shard_map/dispatch/pallas_call | solution.py:78
  151.9 14.1 %fusion.9.plain_ref = f32[5,832,512]{2,1,0:T(8,128)} fusion(bf16[5,832,1536]{2,1,0:T(8,128)(2,1)} %dispatch.2, bf16[20,512,1536]{2,1,0:T(8,128)(2,1)} %param.30, s32[]{:T(128)S(6)} %select_n.417), kind=kOutput, calls=%fused_computation.17 | convolution fusion | flops 6543114240 | bytes 29163524 | tf_op jit(solution)/shard_map/ecd,efd->ecf/dot_general | solution.py:793
  166.0 32.0 %all-gather.7.cloned.1.call-done = bf16[4096,1536]{1,0:T(8,128)(2,1)} async-done(((bf16[512,1536]{1,0:T(8,128)(2,1)}), bf16[4096,1536]{1,0:T(8,128)(2,1)}) %all-gather.7.cloned.1.call-update) | async-done | bytes 12582928 | tf_op jit(solution)/shard_map/all_gather | solution.py:826
  198.0 14.1 %dispatch.3.rows_ref = bf16[5,832,1536]{2,1,0:T(8,128)(2,1)} custom-call(f32[8,8,512]{2,1,0:T(8,128)} %pad.14.codes_ref, bf16[8,512,1536]{2,1,0:T(8,128)(2,1)} %bitcast.272), custom_call_target="tpu_custom_call" | custom-call | flops 6543114240 | bytes 25362432 | tf_op jit(solution)/shard_map/dispatch/pallas_call | solution.py:78
  215.2 29.0 %experts.1 = (bf16[5,832,512]{2,1,0:T(8,128)(2,1)}, bf16[5,832,1024]{2,1,0:T(8,128)(2,1)}, f32[5,832,1]{2,1,0:T(8,128)}) custom-call(s32[1]{0:T(128)} %bitcast.10.at_ref, bf16[5,832,1536]{2,1,0:T(8,128)(2,1)} %dispatch.3.rows_ref, bf16[20,1536,1024]{2,1,0:T(8,128)(2,1)} %gate_up_ref.1, f32[5,832,512]{2,1,0:T(8,128)} %fusion.9.plain_ref, ...), custom_call_target="tpu_custom_call" | custom-call | flops 13086228480 | bytes 45547520 | tf_op jit(solution)/shard_map/experts/pallas_call | solution.py:121
  253.0 15.7 %convolution_convert_fusion.5 = bf16[5,512,1536]{2,1,0:T(8,128)(2,1)} fusion(bf16[5,832,512]{2,1,0:T(8,128)(2,1)} %get-tuple-element.78, bf16[5,832,1536]{2,1,0:T(8,128)(2,1)} %dispatch.2), kind=kOutput, calls=%fused_computation.21 | convolution fusion | flops 6547046400 | bytes 24903680 | tf_op jit(solution)/shard_map/ecf,ecd->efd/dot_general | solution.py:844
  272.1 22.8 %fusion.2.rows_ref = bf16[5,832,1536]{2,1,0:T(8,128)(2,1)} fusion(bf16[5,832,1024]{2,1,0:T(8,128)(2,1)} %get-tuple-element.75, bf16[20,1536,1024]{2,1,0:T(8,128)(2,1)} %gate_up_ref.1, s32[]{:T(128)S(6)} %select_n.417), kind=kOutput, calls=%fused_computation.5 | convolution fusion | flops 13092618240 | bytes 37027844 | tf_op jit(solution)/shard_map/ecf,edf->ecd/dot_general | solution.py:859
  294.8 9.8 %combine.5 = bf16[4,512,1536]{2,1,0:T(8,128)(2,1)} custom-call(s32[4]{0:T(128)} %broadcast_xor_fusion.at_ref, f32[8,8,512]{2,1,0:T(8,128)} %pad.14.codes_ref, bf16[5,832,1536]{2,1,0:T(8,128)(2,1)} %fusion.2.rows_ref), custom_call_target="tpu_custom_call" | custom-call | flops 1 | bytes 1 | tf_op jit(solution)/shard_map/combine/pallas_call | solution.py:163
  306.4 9.7 %combine.4 = bf16[4,512,1536]{2,1,0:T(8,128)(2,1)} custom-call(s32[4]{0:T(128)} %broadcast_xor_fusion.1.at_ref, f32[8,8,512]{2,1,0:T(8,128)} %pad.14.codes_ref, bf16[5,832,1536]{2,1,0:T(8,128)(2,1)} %fusion.2.rows_ref), custom_call_target="tpu_custom_call" | custom-call | flops 1 | bytes 1 | tf_op jit(solution)/shard_map/combine/pallas_call | solution.py:163
  316.1 6.5 add_convert_fusion.1
  327.4 13.6 %convolution_convert_fusion.rows_ref = bf16[5,832,1536]{2,1,0:T(8,128)(2,1)} fusion(bf16[5,832,512]{2,1,0:T(8,128)(2,1)} %get-tuple-element.78, bf16[20,512,1536]{2,1,0:T(8,128)(2,1)} %param.30, s32[]{:T(128)S(6)} %select_n.417), kind=kOutput, calls=%fused_computation.4 | convolution fusion | flops 6549504000 | bytes 24903684 | tf_op jit(solution)/shard_map/ecf,efd->ecd/dot_general | solution.py:872
  341.0 14.7 %convolution_convert_fusion.3 = bf16[5,1536,512]{2,1,0:T(8,128)(2,1)} fusion(bf16[5,832,1536]{2,1,0:T(8,128)(2,1)} %dispatch.3.rows_ref, bf16[5,832,1024]{2,1,0:T(8,128)(2,1)} %get-tuple-element.75), kind=kOutput, calls=%fused_computation.19 | convolution fusion | flops 6547046400 | bytes 24903680 | tf_op jit(solution)/shard_map/ecd,ecf->edf/dot_general | solution.py:867
  355.7 14.6 %convolution_convert_fusion.4 = bf16[5,1536,512]{2,1,0:T(8,128)(2,1)} fusion(bf16[5,832,1536]{2,1,0:T(8,128)(2,1)} %dispatch.3.rows_ref, bf16[5,832,1024]{2,1,0:T(8,128)(2,1)} %get-tuple-element.75), kind=kOutput, calls=%fused_computation.20 | convolution fusion | flops 6547046400 | bytes 24903680 | tf_op jit(solution)/shard_map/ecd,ecf->edf/dot_general | solution.py:867
  374.2 9.7 %combine.7 = bf16[4,512,1536]{2,1,0:T(8,128)(2,1)} custom-call(s32[4]{0:T(128)} %broadcast_xor_fusion.1.at_ref, f32[8,8,512]{2,1,0:T(8,128)} %pad.14.codes_ref, bf16[5,832,1536]{2,1,0:T(8,128)(2,1)} %convolution_convert_fusion.rows_ref), custom_call_target="tpu_custom_call" | custom-call | flops 1 | bytes 1 | tf_op jit(solution)/shard_map/combine/pallas_call | solution.py:163
  383.9 9.9 %combine.6 = bf16[4,512,1536]{2,1,0:T(8,128)(2,1)} custom-call(s32[4]{0:T(128)} %broadcast_xor_fusion.at_ref, f32[8,8,512]{2,1,0:T(8,128)} %pad.14.codes_ref, bf16[5,832,1536]{2,1,0:T(8,128)(2,1)} %convolution_convert_fusion.rows_ref), custom_call_target="tpu_custom_call" | custom-call | flops 1 | bytes 1 | tf_op jit(solution)/shard_map/combine/pallas_call | solution.py:163
  415.4 7.4 convolution_convert_fusion.8.do_ref
  426.5 9.2 %add_convert_fusion = bf16[4,512,1536]{2,1,0:T(8,128)(2,1)} fusion(bf16[4,512,1536]{2,1,0:T(8,128)(2,1)} %collective-permute-done.15, bf16[4,512,1536]{2,1,0:T(8,128)(2,1)} %combine.7), kind=kLoop, calls=%fused_computation.2 | loop fusion | flops 12582912 | bytes 18874368 | tf_op jit(solution)/shard_map/convert_element_type | solution.py:224
  450.0 63.9 %attend_backward.1 = (bf16[512,1536]{1,0:T(8,128)(2,1)}, bf16[1024,512]{1,0:T(8,128)(2,1)}, bf16[1024,512]{1,0:T(8,128)(2,1)}, bf16[256,512]{1,0:T(8,128)(2,1)}, bf16[256,512]{1,0:T(8,128)(2,1)}) custom-call(s32[1]{0:T(128)} %bitcast.2.pos_ref, bf16[512,1536]{1,0:T(8,128)(2,1)} %get-tuple-element.90.q_ref, ...), custom_call_target="tpu_custom_call" | custom-call | flops 20132659200 | bytes 6291456 | tf_op jit(solution)/shard_map/attend_backward/pallas_call | solution.py:549
  524.0 7.1 collective-permute-done.22
  545.6 10.2 %collective-permute-done.26 = bf16[256,1024]{1,0:T(8,128)(2,1)S(1)} collective-permute-done((bf16[256,1024]{1,0:T(8,128)(2,1)S(1)}, bf16[256,1024]{1,0:T(8,128)(2,1)S(1)}, u32[]{:S(2)}, u32[]{:S(2)}) %collective-permute-start.26) | collective-permute-done | bytes 524320 | tf_op jit(solution)/shard_map/ppermute | solution.py:645
  583.5 11.9 %collective-permute-done.42 = bf16[48,1536]{1,0:T(8,128)(2,1)S(1)} collective-permute-done((bf16[48,1536]{1,0:T(8,128)(2,1)S(1)}, bf16[48,1536]{1,0:T(8,128)(2,1)S(1)}, u32[]{:S(2)}, u32[]{:S(2)}) %collective-permute-start.42) | collective-permute-done | bytes 147488 | tf_op jit(solution)/shard_map/ppermute | solution.py:700
  596.1 13.0 %collective-permute-done.43 = bf16[48,1536]{1,0:T(8,128)(2,1)S(1)} collective-permute-done((bf16[48,1536]{1,0:T(8,128)(2,1)S(1)}, bf16[48,1536]{1,0:T(8,128)(2,1)S(1)}, u32[]{:S(2)}, u32[]{:S(2)}) %collective-permute-start.43) | collective-permute-done | bytes 147488 | tf_op jit(solution)/shard_map/ppermute | solution.py:700
  635.1 25.4 %collective-permute-done.32 = bf16[5,96,512]{2,1,0:T(8,128)(2,1)S(1)} collective-permute-done((bf16[5,96,512]{2,1,0:T(8,128)(2,1)S(1)}, bf16[5,96,512]{2,1,0:T(8,128)(2,1)S(1)}, u32[]{:S(2)}, u32[]{:S(2)}) %collective-permute-start.32) | collective-permute-done | bytes 491552 | tf_op jit(solution)/shard_map/ppermute | solution.py:182
  660.6 12.4 %collective-permute-done.33 = bf16[5,96,512]{2,1,0:T(8,128)(2,1)S(1)} collective-permute-done((bf16[5,96,512]{2,1,0:T(8,128)(2,1)S(1)}, bf16[5,96,512]{2,1,0:T(8,128)(2,1)S(1)}, u32[]{:S(2)}, u32[]{:S(2)}) %collective-permute-start.33) | collective-permute-done | bytes 491552 | tf_op jit(solution)/shard_map/ppermute | solution.py:182
  678.4 7.2 collective-permute-done.34
  694.1 14.5 %collective-permute-done.36 = bf16[48,2688]{1,0:T(8,128)(2,1)S(1)} collective-permute-done((bf16[48,2688]{1,0:T(8,128)(2,1)S(1)}, bf16[48,2688]{1,0:T(8,128)(2,1)S(1)}, u32[]{:S(2)}, u32[]{:S(2)}) %collective-permute-start.36) | collective-permute-done | bytes 258080 | tf_op jit(solution)/shard_map/ppermute | solution.py:700
  742.8 9.5 %collective-permute-done.48 = bf16[5,96,512]{2,1,0:T(8,128)(2,1)S(1)} collective-permute-done((bf16[5,96,512]{2,1,0:T(8,128)(2,1)S(1)}, bf16[5,96,512]{2,1,0:T(8,128)(2,1)S(1)}, u32[]{:S(2)}, u32[]{:S(2)}) %collective-permute-start.48) | collective-permute-done | bytes 491552 | tf_op jit(solution)/shard_map/ppermute | solution.py:182
  752.4 6.3 pad_maximum_fusion.1
  (406 shorter events, 234.5 us)
Async XLA Ops:
  7.2 128.4 %all-gather.5.cloned.1.call-start = ((), (), s32[]{:S(2)}) async-start(), calls=%async_computation.6 | async-start | bytes 14598144 | tf_op jit(solution)/shard_map/all_gather | solution.py:780
  12.4 185.5 %all-gather.7.cloned.1.call-start = ((), (), s32[]{:S(2)}) async-start(), calls=%async_computation.7 | async-start | bytes 14155776 | tf_op jit(solution)/shard_map/all_gather | solution.py:826
  23.5 25.1 %collective-permute-start = (bf16[2,256,512]{2,1,0:T(8,128)(2,1)}, bf16[2,256,512]{2,1,0:T(8,128)(2,1)}, u32[]{:S(2)}, u32[]{:S(2)}) collective-permute-start(bf16[2,256,512]{2,1,0:T(8,128)(2,1)} %get-tuple-element.66), channel_id=1, source_target_pairs={{0,4},{2,6},{4,0},{6,2},{1,5},{3,7},{5,1},{7,3},{8,12},{10,14},{12... | collective-permute-start | bytes 1572872 | tf_op jit(solution)/shard_map/ppermute | solution.py:182
  24.7 37.4 %collective-permute-start.1 = (bf16[2,256,512]{2,1,0:T(8,128)(2,1)}, bf16[2,256,512]{2,1,0:T(8,128)(2,1)}, u32[]{:S(2)}, u32[]{:S(2)}) collective-permute-start(bf16[2,256,512]{2,1,0:T(8,128)(2,1)} %get-tuple-element.66), channel_id=1, source_target_pairs={{0,2},{2,0},{4,6},{6,4},{1,3},{3,1},{5,7},{7,5},{8,10},{10,8},{12,... | collective-permute-start | bytes 1572872 | tf_op jit(solution)/shard_map/ppermute | solution.py:182
  124.7 311.0 %reduce-scatter.4.cloned.1.call-start = ((), (), s32[]{:S(2)}) async-start(), calls=%async_computation.3 | async-start | bytes 9830400 | tf_op jit(solution)/shard_map/reduce_scatter | solution.py:601
  268.7 354.2 %reduce-scatter.6.cloned.1.call-start = ((), (), s32[]{:S(2)}) async-start(), calls=%async_computation.4 | async-start | bytes 9830400 | tf_op jit(solution)/shard_map/reduce_scatter | solution.py:601
  325.8 44.5 %collective-permute-start.11 = (bf16[2,512,768]{2,1,0:T(8,128)(2,1)}, bf16[2,512,768]{2,1,0:T(8,128)(2,1)}, u32[]{:S(2)}, u32[]{:S(2)}) collective-permute-start(bf16[2,512,768]{2,1,0:T(8,128)(2,1)} %pad_maximum_fusion.3), channel_id=1, source_target_pairs={{0,1},{1,0},{2,3},{3,2},{4,5},{5,4},{6,7},{7,6},{8,9},{9,8},{10,11... | collective-permute-start | bytes 4718600 | tf_op jit(solution)/shard_map/ppermute | solution.py:182
  326.5 43.8 %collective-permute-start.10 = (bf16[2,512,768]{2,1,0:T(8,128)(2,1)}, bf16[2,512,768]{2,1,0:T(8,128)(2,1)}, u32[]{:S(2)}, u32[]{:S(2)}) collective-permute-start(bf16[2,512,768]{2,1,0:T(8,128)(2,1)} %slice.172), channel_id=1, source_target_pairs={{0,4},{2,6},{4,0},{6,2},{1,5},{3,7},{5,1},{7,3},{8,12},{10,14},{12... | collective-permute-start | bytes 4718600 | tf_op jit(solution)/shard_map/ppermute | solution.py:182
  370.4 353.7 %reduce-scatter.8.cloned.1.call-start = ((), (), s32[]{:S(2)}) async-start(), calls=%async_computation.5 | async-start | bytes 9830400 | tf_op jit(solution)/shard_map/reduce_scatter | solution.py:601
  372.6 21.1 %collective-permute-start.12 = (bf16[512,768]{1,0:T(8,128)(2,1)S(1)}, bf16[512,768]{1,0:T(8,128)(2,1)S(1)}, u32[]{:S(2)}, u32[]{:S(2)}) collective-permute-start(bf16[512,768]{1,0:T(8,128)(2,1)S(1)} %get-tuple-element.230), channel_id=1, source_target_pairs={{0,1},{1,0},{2,3},{3,2},{4,5},{5,4},{6,7},{7,6},{8,9},{9,8},{10,11... | collective-permute-start | bytes 2359304 | tf_op jit(solution)/shard_map/ppermute | solution.py:182
  393.7 32.8 %collective-permute-start.15 = (bf16[4,512,1536]{2,1,0:T(8,128)(2,1)}, bf16[4,512,1536]{2,1,0:T(8,128)(2,1)}, u32[]{:S(2)}, u32[]{:S(2)}) collective-permute-start(bf16[4,512,1536]{2,1,0:T(8,128)(2,1)} %combine.6), channel_id=1, source_target_pairs={{0,2},{2,0},{4,6},{6,4},{1,3},{3,1},{5,7},{7,5},{8,10},{10,8},{12,... | collective-permute-start | bytes 18874376 | tf_op jit(solution)/shard_map/ppermute | solution.py:182
  441.4 89.8 %collective-permute-start.17 = (bf16[2,512,768]{2,1,0:T(8,128)(2,1)}, bf16[2,512,768]{2,1,0:T(8,128)(2,1)}, u32[]{:S(2)}, u32[]{:S(2)}) collective-permute-start(bf16[2,512,768]{2,1,0:T(8,128)(2,1)} %pad_maximum_fusion.4), channel_id=1, source_target_pairs={{0,1},{1,0},{2,3},{3,2},{4,5},{5,4},{6,7},{7,6},{8,9},{9,8},{10,11... | collective-permute-start | bytes 4718600 | tf_op jit(solution)/shard_map/ppermute | solution.py:182
  445.3 85.9 %collective-permute-start.18 = (bf16[4,2,48,768]{3,2,0,1:T(8,128)(2,1)}, bf16[4,2,48,768]{3,2,0,1:T(8,128)(2,1)}, u32[]{:S(2)}, u32[]{:S(2)}) collective-permute-start(bf16[4,2,48,768]{3,2,0,1:T(8,128)(2,1)} %dynamic-slice_bitcast_fusion.4), channel_id=1, source_target_pairs={{0,4},{2,6},{4,0},{6,2},{1,5},{3,7},{5,1},{7,3},{8,12},{10,14},{12... | collective-permute-start | bytes 1769480 | tf_op jit(solution)/shard_map/ppermute | solution.py:182
  446.2 85.0 %collective-permute-start.16 = (bf16[2,512,768]{2,1,0:T(8,128)(2,1)}, bf16[2,512,768]{2,1,0:T(8,128)(2,1)}, u32[]{:S(2)}, u32[]{:S(2)}) collective-permute-start(bf16[2,512,768]{2,1,0:T(8,128)(2,1)} %slice.185), channel_id=1, source_target_pairs={{0,4},{2,6},{4,0},{6,2},{1,5},{3,7},{5,1},{7,3},{8,12},{10,14},{12... | collective-permute-start | bytes 4718600 | tf_op jit(solution)/shard_map/ppermute | solution.py:182
  448.1 67.2 %collective-permute-start.20 = (bf16[5,32,1536]{2,1,0:T(8,128)(2,1)}, bf16[5,32,1536]{2,1,0:T(8,128)(2,1)}, u32[]{:S(2)}, u32[]{:S(2)}) collective-permute-start(bf16[5,32,1536]{2,1,0:T(8,128)(2,1)} %get-tuple-element.248), channel_id=1, source_target_pairs={{0,2},{2,0},{4,6},{6,4},{1,3},{3,1},{5,7},{7,5},{8,10},{10,8},{12,... | collective-permute-start | bytes 1474568 | tf_op jit(solution)/shard_map/ppermute | solution.py:182
  449.0 68.3 %collective-permute-start.21 = (bf16[5,32,1536]{2,1,0:T(8,128)(2,1)}, bf16[5,32,1536]{2,1,0:T(8,128)(2,1)}, u32[]{:S(2)}, u32[]{:S(2)}) collective-permute-start(bf16[5,32,1536]{2,1,0:T(8,128)(2,1)} %get-tuple-element.247), channel_id=1, source_target_pairs={{0,4},{2,6},{4,0},{6,2},{1,5},{3,7},{5,1},{7,3},{8,12},{10,14},{12... | collective-permute-start | bytes 1474568 | tf_op jit(solution)/shard_map/ppermute | solution.py:182
  532.1 23.7 %collective-permute-start.26 = (bf16[256,1024]{1,0:T(8,128)(2,1)S(1)}, bf16[256,1024]{1,0:T(8,128)(2,1)S(1)}, u32[]{:S(2)}, u32[]{:S(2)}) collective-permute-start(bf16[256,1024]{1,0:T(8,128)(2,1)S(1)} %pad_maximum_fusion.6), channel_id=1, source_target_pairs={{0,4},{2,6},{4,0},{6,2},{1,5},{3,7},{5,1},{7,3},{8,12},{10,14},{12... | collective-permute-start | bytes 1572872 | tf_op jit(solution)/shard_map/ppermute | solution.py:645
  533.2 24.7 %collective-permute-start.27 = (bf16[256,1024]{1,0:T(8,128)(2,1)S(1)}, bf16[256,1024]{1,0:T(8,128)(2,1)S(1)}, u32[]{:S(2)}, u32[]{:S(2)}) collective-permute-start(bf16[256,1024]{1,0:T(8,128)(2,1)S(1)} %pad_maximum_fusion.7), channel_id=1, source_target_pairs={{0,6},{2,0},{4,2},{6,4},{1,7},{3,1},{5,3},{7,5},{8,14},{10,8},{12,... | collective-permute-start | bytes 1572872 | tf_op jit(solution)/shard_map/ppermute | solution.py:645
  534.6 40.2 %collective-permute-start.41 = (bf16[4,48,768]{2,1,0:T(8,128)(2,1)}, bf16[4,48,768]{2,1,0:T(8,128)(2,1)}, u32[]{:S(2)}, u32[]{:S(2)}) collective-permute-start(bf16[4,48,768]{2,1,0:T(8,128)(2,1)} %dynamic-slice_bitcast_fusion.18), channel_id=1, source_target_pairs={{0,4},{2,6},{4,0},{6,2},{1,5},{3,7},{5,1},{7,3},{8,12},{10,14},{12... | collective-permute-start | bytes 884744 | tf_op jit(solution)/shard_map/ppermute | solution.py:182
  537.5 39.5 %collective-permute-start.40 = (bf16[4,48,768]{2,1,0:T(8,128)(2,1)}, bf16[4,48,768]{2,1,0:T(8,128)(2,1)}, u32[]{:S(2)}, u32[]{:S(2)}) collective-permute-start(bf16[4,48,768]{2,1,0:T(8,128)(2,1)} %dynamic-slice_bitcast_fusion.19), channel_id=1, source_target_pairs={{0,1},{1,0},{2,3},{3,2},{4,5},{5,4},{6,7},{7,6},{8,9},{9,8},{10,11... | collective-permute-start | bytes 884744 | tf_op jit(solution)/shard_map/ppermute | solution.py:182
  544.8 70.5 %collective-permute-start.23 = (bf16[512,768]{1,0:T(8,128)(2,1)}, bf16[512,768]{1,0:T(8,128)(2,1)}, u32[]{:S(2)}, u32[]{:S(2)}) collective-permute-start(bf16[512,768]{1,0:T(8,128)(2,1)} %get-tuple-element.223), channel_id=1, source_target_pairs={{0,1},{1,0},{2,3},{3,2},{4,5},{5,4},{6,7},{7,6},{8,9},{9,8},{10,11... | collective-permute-start | bytes 2359304 | tf_op jit(solution)/shard_map/ppermute | solution.py:182
  574.8 45.0 %collective-permute-start.28 = (bf16[4,2,2,48,2688]{4,3,2,1,0:T(8,128)(2,1)S(1)}, bf16[4,2,2,48,2688]{4,3,2,1,0:T(8,128)(2,1)S(1)}, u32[]{:S(2)}, u32[]{:S(2)}) collective-permute-start(bf16[4,2,2,48,2688]{4,3,2,1,0:T(8,128)(2,1)S(1)} %dynamic-slice_bitcast_fusion), channel_id=1, source_target_pairs={{0,2},{2,0},{4,6},{6,4},{1,3},{3,1},{5,7},{7,5},{8,10},{10,8},{12,... | collective-permute-start | bytes 12386312 | tf_op jit(solution)/shard_map/ppermute | solution.py:182
  579.7 29.3 %collective-permute-start.43 = (bf16[48,1536]{1,0:T(8,128)(2,1)S(1)}, bf16[48,1536]{1,0:T(8,128)(2,1)S(1)}, u32[]{:S(2)}, u32[]{:S(2)}) collective-permute-start(bf16[48,1536]{1,0:T(8,128)(2,1)S(1)} %get-tuple-element.266), channel_id=1, source_target_pairs={{0,16},{8,24},{16,0},{24,8},{1,17},{9,25},{17,1},{25,9},{2,18},{10... | collective-permute-start | bytes 442376 | tf_op jit(solution)/shard_map/ppermute | solution.py:700
  580.9 28.2 %collective-permute-start.44 = (bf16[48,1536]{1,0:T(8,128)(2,1)S(1)}, bf16[48,1536]{1,0:T(8,128)(2,1)S(1)}, u32[]{:S(2)}, u32[]{:S(2)}) collective-permute-start(bf16[48,1536]{1,0:T(8,128)(2,1)S(1)} %get-tuple-element.267), channel_id=1, source_target_pairs={{0,24},{8,0},{16,8},{24,16},{1,25},{9,1},{17,9},{25,17},{2,26},{10... | collective-permute-start | bytes 442376 | tf_op jit(solution)/shard_map/ppermute | solution.py:700
  626.6 46.3 %collective-permute-start.30 = (bf16[4,2,48,1408]{3,2,1,0:T(8,128)(2,1)S(1)}, bf16[4,2,48,1408]{3,2,1,0:T(8,128)(2,1)S(1)}, u32[]{:S(2)}, u32[]{:S(2)}) collective-permute-start(bf16[4,2,48,1408]{3,2,1,0:T(8,128)(2,1)S(1)} %dynamic-slice_bitcast_fusion.1), channel_id=1, source_target_pairs={{0,1},{1,0},{2,3},{3,2},{4,5},{5,4},{6,7},{7,6},{8,9},{9,8},{10,11... | collective-permute-start | bytes 3244040 | tf_op jit(solution)/shard_map/ppermute | solution.py:182
  628.0 45.0 %collective-permute-start.29 = (bf16[4,2,48,1280]{3,2,1,0:T(8,128)(2,1)S(1)}, bf16[4,2,48,1280]{3,2,1,0:T(8,128)(2,1)S(1)}, u32[]{:S(2)}, u32[]{:S(2)}) collective-permute-start(bf16[4,2,48,1280]{3,2,1,0:T(8,128)(2,1)S(1)} %dynamic-slice_bitcast_fusion.2), channel_id=1, source_target_pairs={{0,4},{2,6},{4,0},{6,2},{1,5},{3,7},{5,1},{7,3},{8,12},{10,14},{12... | collective-permute-start | bytes 2949128 | tf_op jit(solution)/shard_map/ppermute | solution.py:182
  632.2 28.4 %collective-permute-start.32 = (bf16[5,96,512]{2,1,0:T(8,128)(2,1)S(1)}, bf16[5,96,512]{2,1,0:T(8,128)(2,1)S(1)}, u32[]{:S(2)}, u32[]{:S(2)}) collective-permute-start(bf16[5,96,512]{2,1,0:T(8,128)(2,1)S(1)} %get-tuple-element.243), channel_id=1, source_target_pairs={{0,4},{2,6},{4,0},{6,2},{1,5},{3,7},{5,1},{7,3},{8,12},{10,14},{12... | collective-permute-start | bytes 1474568 | tf_op jit(solution)/shard_map/ppermute | solution.py:182
  633.1 39.9 %collective-permute-start.33 = (bf16[5,96,512]{2,1,0:T(8,128)(2,1)S(1)}, bf16[5,96,512]{2,1,0:T(8,128)(2,1)S(1)}, u32[]{:S(2)}, u32[]{:S(2)}) collective-permute-start(bf16[5,96,512]{2,1,0:T(8,128)(2,1)S(1)} %get-tuple-element.242), channel_id=1, source_target_pairs={{0,6},{2,4},{4,2},{6,0},{1,7},{3,5},{5,3},{7,1},{8,14},{10,12},{12... | collective-permute-start | bytes 1474568 | tf_op jit(solution)/shard_map/ppermute | solution.py:182
  688.3 20.3 %collective-permute-start.36 = (bf16[48,2688]{1,0:T(8,128)(2,1)S(1)}, bf16[48,2688]{1,0:T(8,128)(2,1)S(1)}, u32[]{:S(2)}, u32[]{:S(2)}) collective-permute-start(bf16[48,2688]{1,0:T(8,128)(2,1)S(1)} %get-tuple-element.262), channel_id=1, source_target_pairs={{0,8},{8,16},{16,24},{24,0},{1,9},{9,17},{17,25},{25,1},{2,10},{10... | collective-permute-start | bytes 774152 | tf_op jit(solution)/shard_map/ppermute | solution.py:700
  690.7 23.5 %collective-permute-start.37 = (bf16[48,2688]{1,0:T(8,128)(2,1)S(1)}, bf16[48,2688]{1,0:T(8,128)(2,1)S(1)}, u32[]{:S(2)}, u32[]{:S(2)}) collective-permute-start(bf16[48,2688]{1,0:T(8,128)(2,1)S(1)} %get-tuple-element.263), channel_id=1, source_target_pairs={{0,16},{8,24},{16,0},{24,8},{1,17},{9,25},{17,1},{25,9},{2,18},{10... | collective-permute-start | bytes 774152 | tf_op jit(solution)/shard_map/ppermute | solution.py:700
  691.6 24.6 %collective-permute-start.38 = (bf16[48,2688]{1,0:T(8,128)(2,1)S(1)}, bf16[48,2688]{1,0:T(8,128)(2,1)S(1)}, u32[]{:S(2)}, u32[]{:S(2)}) collective-permute-start(bf16[48,2688]{1,0:T(8,128)(2,1)S(1)} %get-tuple-element.264), channel_id=1, source_target_pairs={{0,24},{8,0},{16,8},{24,16},{1,25},{9,1},{17,9},{25,17},{2,26},{10... | collective-permute-start | bytes 774152 | tf_op jit(solution)/shard_map/ppermute | solution.py:700
  730.0 22.3 %collective-permute-start.48 = (bf16[5,96,512]{2,1,0:T(8,128)(2,1)S(1)}, bf16[5,96,512]{2,1,0:T(8,128)(2,1)S(1)}, u32[]{:S(2)}, u32[]{:S(2)}) collective-permute-start(bf16[5,96,512]{2,1,0:T(8,128)(2,1)S(1)} %get-tuple-element.239), channel_id=1, source_target_pairs={{0,6},{2,4},{4,2},{6,0},{1,7},{3,5},{5,3},{7,1},{8,14},{10,12},{12... | collective-permute-start | bytes 1474568 | tf_op jit(solution)/shard_map/ppermute | solution.py:182
  (92 other events, 915.3 us)
Sparse Core Ops, SparseCore 0:
  12.6 86.0 all-gather.4
  124.8 73.0 all-gather.6
  268.9 135.7 reduce-scatter.3
  406.8 136.7 reduce-scatter.5
  546.3 161.2 reduce-scatter.7

commit v6 on v5

--- a/solution.py
+++ b/solution.py
@@ -149,15 +149,19 @@
     )(jnp.asarray(offset, jnp.int32).reshape(1), rows, gate_up, plain, weight)
 
 
-def combine_body(own, slots, at_ref, codes_ref, rows_ref, out_ref):
+def combine_body(own, slots, at_ref, codes_ref, rows_ref, *refs):
+    out_ref = refs[-1]
     pick = selection(codes_ref[0], own, slots)
     rows = rows_ref[...].reshape(own * slots, rows_ref.shape[-1])
-    out_ref[0] = lax.dot_general(
+    total = lax.dot_general(
         pick, rows, (((0,), (0,)), ((), ())), preferred_element_type=jnp.float32
-    ).astype(out_ref.dtype)
-
-
-def combine(at, codes, rows, own, slots):
+    )
+    for ref in refs[:-1]:
+        total = total + ref[0].astype(jnp.float32)
+    out_ref[0] = total.astype(out_ref.dtype)
+
+
+def combine(at, codes, rows, own, slots, *more):
     count, tokens = at.shape[0], codes.shape[2]
     width = rows.shape[-1]
     return pl.pallas_call(
@@ -168,13 +172,14 @@
             in_specs=[
                 pl.BlockSpec((1, codes.shape[1], tokens), lambda b, at: (at[b], 0, 0)),
                 pl.BlockSpec((own, slots, width), lambda b, at: (0, at[b], 0)),
-            ],
+            ]
+            + [pl.BlockSpec((1, tokens, width), lambda b, at: (b, 0, 0)) for _ in more],
             out_specs=pl.BlockSpec((1, tokens, width), lambda b, at: (b, 0, 0)),
         ),
         out_shape=jax.ShapeDtypeStruct((count, tokens, width), jnp.bfloat16),
         cost_estimate=pl.CostEstimate(flops=1, transcendentals=0, bytes_accessed=1),
         name="combine",
-    )(at, codes, rows)
+    )(at, codes, rows, *more)
 
 
 def swap(values, axis, bit):
@@ -224,20 +229,25 @@
     return (left.astype(jnp.float32) + right.astype(jnp.float32)).astype(jnp.bfloat16)
 
 
-def pair_sums(codes, rows, own, slots, group):
+def far_sum(codes, rows, own, slots, group):
+    if not paired(group):
+        return jnp.zeros((), jnp.bfloat16)
+    far = lax.axis_index(group).astype(jnp.int32) ^ jnp.array([2, 3, 6, 7], jnp.int32)
+    return combine(far, codes, rows, own, slots)
+
+
+def cross(far):
+    return swap(far, "ctx", 1) if far.ndim else far
+
+
+def scatter_one(codes, rows, own, slots, group, sent):
     if not paired(group):
         every = jnp.arange(codes.shape[0], dtype=jnp.int32)
         return lax.psum_scatter(
             combine(every, codes, rows, own, slots), group, scatter_dimension=0
-        ), None
-    here = lax.axis_index(group).astype(jnp.int32)
-    far = here ^ jnp.array([2, 3, 6, 7], jnp.int32)
-    near = here ^ jnp.array([0, 1, 4, 5], jnp.int32)
-    return combine(far, codes, rows, own, slots), combine(near, codes, rows, own, slots)
-
-
-def scatter_one(far, near):
-    return far if near is None else added(near, swap(far, "ctx", 1))
+        )
+    near = lax.axis_index(group).astype(jnp.int32) ^ jnp.array([0, 1, 4, 5], jnp.int32)
+    return combine(near, codes, rows, own, slots, sent)
 
 
 def scatter_two(part):
@@ -334,17 +344,19 @@
     )(hidden, key_weight, value_weight, cosine, sine)
 
 
-def gather_keys(near_kv):
+def gather_keys(near_kv, work):
     if lax.axis_size("ctx") != 4:
-        return lax.all_gather(near_kv, "ctx", axis=1, tiled=True)
+        return lax.all_gather(near_kv, "ctx", axis=1, tiled=True), work
     rows = near_kv.shape[1]
     here = lax.axis_index("ctx")
-    pair = swap(near_kv, "ctx", 2)
+    pair, side, work = lax.optimization_barrier(
+        (swap(near_kv, "ctx", 2), swap(near_kv, "ctx", 1), work)
+    )
     whole = jnp.zeros((2, 4 * rows, near_kv.shape[2]), near_kv.dtype)
-    pieces = ((0, near_kv), (2, pair), (1, swap(near_kv, "ctx", 1)), (3, swap(pair, "ctx", 1)))
+    pieces = ((0, near_kv), (2, pair), (1, side), (3, swap(pair, "ctx", 1)))
     for step, piece in pieces:
         whole = lax.dynamic_update_slice_in_dim(whole, piece, (here ^ step) * rows, axis=1)
-    return whole
+    return whole, work
 
 
 def head_place(group):
@@ -614,16 +626,31 @@
     return tuple(swap(piece, "ctx", step) if step else piece for step, piece in enumerate(pieces))
 
 
-def place_experts(pieces):
-    if len(pieces) == 1:
-        return pieces[0].astype(jnp.float32)
+def pairs_experts(part, split):
+    if split != 4:
+        return part, ()
+    own, rows, width = part.shape
+    part = part.reshape(own, 2, 2, rows // 4, width)
+    pair = lax.axis_index("ctx") // 2
+    take = partial(lax.dynamic_index_in_dim, axis=1, keepdims=False)
+    return take(part, pair), swap(take(part, 1 - pair), "ctx", 2)
+
+
+def cores_experts(kept, moved, split):
+    if split != 4:
+        return send_experts(kept, split)
+    core = lax.axis_index("ctx") % 2
+    take = partial(lax.dynamic_index_in_dim, axis=1, keepdims=False)
+    crossed = swap(jnp.stack([take(kept, 1 - core), take(moved, 1 - core)]), "ctx", 1)
+    return take(kept, core), crossed[0], take(moved, core), crossed[1]
+
+
+def place_experts(whole, pieces, column):
     here = lax.axis_index("ctx")
-    own, rows, width = pieces[0].shape
-    whole = jnp.zeros((own * len(pieces), rows, width), jnp.float32)
+    own = pieces[0].shape[0]
     for step, piece in enumerate(pieces):
-        whole = lax.dynamic_update_slice_in_dim(
-            whole, piece.astype(jnp.float32), (here ^ step) * own, axis=0
-        )
+        first = (here ^ step) * own if len(pieces) > 1 else 0
+        whole = lax.dynamic_update_slice(whole, piece.astype(jnp.float32), (first, 0, column))
     return whole
 
 
@@ -688,7 +715,7 @@
     whole = jnp.concatenate(
         [added(take(left, side, 1), left_sent), added(take(right, pair, 1), right_sent)], axis=-1
     )
-    return scatter_parts(whole)
+    return whole
 
 
 def scatter_parts(parts):
@@ -704,9 +731,10 @@
     return total.astype(jnp.bfloat16)
 
 
-def finish_dense(grad, rows):
-    if grad.shape[0] == rows:
+def finish_dense(grad):
+    if grad.ndim == 2:
         return lax.psum(grad, "expert").astype(jnp.float32)
+    grad = scatter_parts(grad)
     other = swap(grad, "expert", 1)
     first = lax.axis_index("expert") == 0
     return jnp.concatenate(
@@ -814,8 +842,10 @@
     near_kv, cont_kv = project_keys(
         h1_low, key_weight, value_weight, cosine, sine, prompt_rows
     )
-    prompt_kv = gather_keys(near_kv)
-    q_lin = jnp.dot(h1_low, w_query, preferred_element_type=jnp.float32)
+    near_kv, h1_late = lax.optimization_barrier((near_kv, h1_low))
+    prompt_kv, q_lin = gather_keys(
+        near_kv, jnp.dot(h1_late, w_query, preferred_element_type=jnp.float32)
+    )
     query_row_block, merged_low, log_total = attend_forward(
         q_lin, prompt_kv, cont_kv, cosine, sine, start, prompt_rows, cont_len
     )
@@ -844,6 +874,10 @@
     grad_down = jnp.einsum(
         "ecf,ecd->efd", weighted, d_slot_rows, preferred_element_type=jnp.float32
     ).astype(jnp.bfloat16)
+    d_both, _, d_slot_gate = lax.optimization_barrier(
+        (d_both, grad_down, d_slot_gate)
+    )
+    down_part = reduce_experts(grad_down, split)
     d_gates_own = jnp.sum(
         jnp.where(
             picked,
@@ -852,36 +886,43 @@
         ),
         axis=2,
     )
-    d_both, _, d_gates = lax.optimization_barrier(
-        (d_both, grad_down, return_gates(d_gates_own, group, first_expert, expert_total))
-    )
-    down_part = reduce_experts(grad_down, split)
+    d_gates = return_gates(d_gates_own, group, first_expert, expert_total)
     d_slots = jnp.einsum(
         "ecf,edf->ecd", d_both, gate_up_own, preferred_element_type=jnp.float32
     ).astype(jnp.bfloat16)
-    part, weighted, slot_rows = lax.optimization_barrier(
-        (scatter_one(*pair_sums(own_codes, d_slots, own, slots, group)), weighted, slot_rows)
-    )
-    kept, moved = scatter_two(part)
-    grad_gate, grad_up = (
-        jnp.einsum(
+    far, d_gates, slot_rows = lax.optimization_barrier(
+        (far_sum(own_codes, d_slots, own, slots, group), d_gates, slot_rows)
+    )
+    sent = cross(far)
+
+    def expert_gradient(slot_rows, d_part):
+        return jnp.einsum(
             "ecd,ecf->edf", slot_rows, d_part, preferred_element_type=jnp.float32
         ).astype(jnp.bfloat16)
-        for d_part in (d_both[..., :hidden_units], d_both[..., hidden_units:])
-    )
+
+    sent, grad_gate = lax.optimization_barrier(
+        (sent, expert_gradient(slot_rows, d_both[..., :hidden_units]))
+    )
+    gate_part = reduce_experts(grad_gate, split)
+    part, weighted, slot_rows = lax.optimization_barrier(
+        (scatter_one(own_codes, d_slots, own, slots, group, sent), weighted, slot_rows)
+    )
+    kept, moved = scatter_two(part)
     expert_out = jnp.einsum(
         "ecf,efd->ecd", weighted, down_own, preferred_element_type=jnp.float32
     ).astype(jnp.bfloat16)
-    moved, grad_gate, grad_up, expert_out = lax.optimization_barrier(
-        (moved, grad_gate, grad_up, expert_out)
-    )
-    gate_part, up_part = reduce_experts(grad_gate, split), reduce_experts(grad_up, split)
+    far, slot_rows = lax.optimization_barrier(
+        (far_sum(own_codes, expert_out, own, slots, group), slot_rows)
+    )
+    moved, sent, grad_up, expert_out = lax.optimization_barrier(
+        (moved, cross(far), expert_gradient(slot_rows, d_both[..., hidden_units:]), expert_out)
+    )
+    up_part = reduce_experts(grad_up, split)
     kept, moved = scatter_three(kept, moved)
-    moved, sums = lax.optimization_barrier(
-        (moved, pair_sums(own_codes, expert_out, own, slots, group))
+    moved, mixed_part = lax.optimization_barrier(
+        (moved, scatter_one(own_codes, expert_out, own, slots, group, sent))
     )
     d_rows = scatter_end(kept, moved)
-    mixed_part = scatter_one(*sums)
     d_logits = (
         gates * (d_gates - jnp.sum(gates * d_gates, axis=0, keepdims=True))
     ).astype(jnp.bfloat16)
@@ -905,13 +946,13 @@
     )
     mixed_kept, mixed_moved = scatter_two(mixed_part)
     out_kept, out_moved = fold_two(grad_out, out_cut)
-    down_sent = send_experts(down_part, split)
+    down_kept, down_moved = pairs_experts(down_part, split)
     d_query_low, d_key_prompt, d_value_prompt, d_key_cont, d_value_cont = attend_backward(
         query_row_block, merged_gradient, merged_low, log_total, prompt_kv, cont_kv, cosine, sine,
         key_cosine, key_sine, start, prompt_rows, cont_len,
     )
-    mixed_moved, out_moved, down_sent, d_key_prompt = lax.optimization_barrier(
-        (mixed_moved, out_moved, down_sent, d_key_prompt)
+    mixed_moved, out_moved, down_moved, d_key_prompt = lax.optimization_barrier(
+        (mixed_moved, out_moved, down_moved, d_key_prompt)
     )
     mixed_kept, mixed_moved = scatter_three(mixed_kept, mixed_moved)
     grad_out = fold_three(out_kept, out_moved)
@@ -941,18 +982,25 @@
     dense = jnp.concatenate([grad_query, grad_key, grad_value, small], axis=1).astype(jnp.bfloat16)
     heads_width = QUERY_HEADS * HEAD_SIZE
     edge = heads_width + 2 * key_value_width
-    dense, gate_part = lax.optimization_barrier((fold_one(dense), gate_part))
-    gate_sent = send_experts(gate_part, split)
-    dense_kept, dense_moved = fold_two(dense, edge // 256 * 128)
-    dense_moved, gate_sent = lax.optimization_barrier((dense_moved, gate_sent))
-    dense_rows = w_query.shape[0] // (lax.axis_size("dp") * lax.axis_size("ctx"))
-    dense = finish_dense(fold_three(dense_kept, dense_moved), dense_rows)
-    grad_out = finish_dense(grad_out, dense_rows)
-    grad_down = place_experts(down_sent)
-    grad_gate = place_experts(gate_sent)
-    dense, up_part = lax.optimization_barrier((dense, up_part))
-    grad_up = place_experts(send_experts(up_part, split))
-    grad_gate_up = jnp.concatenate([grad_gate, grad_up], axis=-1)
+    gate_part, dense = lax.optimization_barrier((gate_part, dense))
+    gate_kept, gate_moved = pairs_experts(gate_part, split)
+    dense = fold_three(*fold_two(fold_one(dense), edge // 256 * 128))
+    dense, gate_moved = lax.optimization_barrier((dense, gate_moved))
+    shares = lax.axis_size("dp") * lax.axis_size("ctx")
+    grad_down = place_experts(
+        jnp.zeros((local_experts, hidden_units // shares, model_width), jnp.float32),
+        cores_experts(down_kept, down_moved, split),
+        0,
+    )
+    grad_gate_up = place_experts(
+        jnp.zeros((local_experts, model_width // shares, 2 * hidden_units), jnp.float32),
+        cores_experts(gate_kept, gate_moved, split),
+        0,
+    )
+    dense = finish_dense(jnp.concatenate([dense, grad_out], axis=-1))
+    tail = edge + small.shape[1]
+    dense, up_part, grad_gate_up = lax.optimization_barrier((dense, up_part, grad_gate_up))
+    grad_gate_up = place_experts(grad_gate_up, send_experts(up_part, split), hidden_units)
     return (
         y_prompt,
         y_cont,
@@ -962,7 +1010,7 @@
         dense[:, :heads_width],
         dense[:, heads_width : heads_width + key_value_width],
         dense[:, heads_width + key_value_width : edge],
-        grad_out,
+        dense[:, tail:],
         dense[:, edge + expert_total + 1],
         dense[:, edge : edge + expert_total],
         grad_gate_up,

time: 774 us -> 766 us (0.990)
  other arithmetic: 88.5 us -> 67.2 us
  waiting for transfers between devices: 198 us -> 213 us
  local copies, waits for them, and re-layouts: 55.2 us -> 66.1 us
    ppermute x40 -> x37, waiting for transfers between devices: 107 us -> 129 us  [swap(): return lax.ppermute(values, axis, [(i, i ^ bit) for i in range(size)])]
    convert_element_type x14 -> x12, other arithmetic: 33.4 us -> 15.2 us  [added(): (left.astype(jnp.float32) + right.astype(jnp.float32)).astype(jnp.bfloat16)]
    ppermute x6 -> x3, waiting for transfers between devices: 47.1 us -> 33.6 us  [scatter_parts(): lax.ppermute(take(parts, (here + hop) % size), 'dp', [(i, (i + hop) % siz...]
    optimization_barrier x0 -> x1, local copies, waits for them, and re-layouts: none -> 11.7 us  [per_device(): gate_part, dense = lax.optimization_barrier((gate_part, dense))]
    ppermute x40 -> x37, starting transfers between devices: 39 us -> 35.6 us  [swap(): return lax.ppermute(values, axis, [(i, i ^ bit) for i in range(size)])]
  transfers between devices with their start and end apart: 54 -> 48, of which waited for: 23 -> 27; matrix products, arithmetic and copies ran while one was open for 34% -> 30% of each run, Pallas kernels for 23% -> 23%
where the time goes in v6:
time: 766 us; the launch traced here: 757 us
  Pallas kernels  221 us (29%)
  waiting for transfers between devices  213 us (28%)
  matrix products  133 us (17%)
  other arithmetic  67.2 us (9%)
  local copies, waits for them, and re-layouts  66.1 us (9%)
  starting transfers between devices  42.4 us (6%)
  between operations  15.6 us (2%)
    ppermute x37, waiting for transfers between devices, swap(): return lax.ppermute(values, axis, [(i, i ^ bit) for i in range(size)])  129 us
    pallas_call x1, Pallas kernels, attend_backward(): pl.pallas_call(partial(attend_backward_body, group, rows, cont_len, chunk...  64.1 us
    pallas_call x1, Pallas kernels, attend_forward(): pl.pallas_call(partial(attend_forward_body, group, rows, cont_len), grid_...  50.4 us
    pallas_call x4, Pallas kernels, combine(): pl.pallas_call(partial(combine_body, own, slots), grid_spec=pltpu.Prefetc...  41.8 us
    ppermute x37, starting transfers between devices, swap(): return lax.ppermute(values, axis, [(i, i ^ bit) for i in range(size)])  35.6 us
    ppermute x3, waiting for transfers between devices, scatter_parts(): lax.ppermute(take(parts, (here + hop) % size), 'dp', [(i, (i + hop) % siz...  33.6 us
    all_gather x1, waiting for transfers between devices, per_device(): rows_all = lax.all_gather(h2_low, group, axis=0, tiled=False)  32.2 us
    dot_general x2, matrix products, expert_gradient(): jnp.einsum('ecd,ecf->edf', slot_rows, d_part, preferred_element_type=jnp....  29.4 us
  transfers between devices with their start and end apart: 48, of which 27 were waited for; matrix products, arithmetic and copies ran while one was open for 30% of the time, Pallas kernels for 23%

profile of v6, /device:TPU:9, one launch (start us, length us, event | category | flops | bytes accessed | tf_op | source)
XLA Modules:
  0.0 757.4 jit_solution(4932164468194425658)
XLA Ops:
  16.4 7.1 project_keys.1
  25.7 6.6 fusion.118.q_ref
  32.3 16.2 %collective-permute-done = bf16[2,256,512]{2,1,0:T(8,128)(2,1)} collective-permute-done((bf16[2,256,512]{2,1,0:T(8,128)(2,1)}, bf16[2,256,512]{2,1,0:T(8,128)(2,1)}, u32[]{:S(2)}, u32[]{:S(2)}) %collective-permute-start) | collective-permute-done | bytes 524320 | tf_op jit(solution)/shard_map/ppermute | solution.py:187
  58.2 50.4 %attend_forward.1 = (bf16[512,1536]{1,0:T(8,128)(2,1)}, bf16[512,1536]{1,0:T(8,128)(2,1)}, f32[24,8,512]{2,1,0:T(8,128)}) custom-call(s32[1]{0:T(128)} %bitcast.2.pos_ref, f32[512,1536]{1,0:T(8,128)} %fusion.118.q_ref, f32[512,128]{1,0:T(8,128)} %get-tuple-element.277.cos_ref, f32[512,128]{1,0:T(8,128)} %get-tuple-element.276.sin_ref, ...), custom_call_target="tpu_custom_call" | custom-call | flops 8053063680 | bytes 6291456 | tf_op jit(solution)/shard_map/attend_forward/pallas_call | solution.py:430
  108.5 5.2 multiply_reduce_fusion.2
  129.6 14.3 %dispatch.2 = bf16[5,832,1536]{2,1,0:T(8,128)(2,1)} custom-call(f32[8,8,512]{2,1,0:T(8,128)} %pad.14.codes_ref, bf16[8,528,1536]{2,1,0:T(8,128)(2,1)} %bitcast.292), custom_call_target="tpu_custom_call" | custom-call | flops 6543114240 | bytes 25362432 | tf_op jit(solution)/shard_map/dispatch/pallas_call | solution.py:78
  144.0 14.1 %fusion.9.plain_ref = f32[5,832,512]{2,1,0:T(8,128)} fusion(bf16[5,832,1536]{2,1,0:T(8,128)(2,1)} %dispatch.2, bf16[20,512,1536]{2,1,0:T(8,128)(2,1)} %param.30, s32[]{:T(128)S(6)} %select_n.413), kind=kOutput, calls=%fused_computation.14 | convolution fusion | flops 6543114240 | bytes 29163524 | tf_op jit(solution)/shard_map/ecd,efd->ecf/dot_general | solution.py:821
  158.1 32.2 %all-gather.7.cloned.1.call-done = bf16[4096,1536]{1,0:T(8,128)(2,1)} async-done(((bf16[512,1536]{1,0:T(8,128)(2,1)}), bf16[4096,1536]{1,0:T(8,128)(2,1)}) %all-gather.7.cloned.1.call-update) | async-done | bytes 12582928 | tf_op jit(solution)/shard_map/all_gather | solution.py:856
  190.2 14.1 %dispatch.3.rows_ref = bf16[5,832,1536]{2,1,0:T(8,128)(2,1)} custom-call(f32[8,8,512]{2,1,0:T(8,128)} %pad.14.codes_ref, bf16[8,512,1536]{2,1,0:T(8,128)(2,1)} %bitcast.293), custom_call_target="tpu_custom_call" | custom-call | flops 6543114240 | bytes 25362432 | tf_op jit(solution)/shard_map/dispatch/pallas_call | solution.py:78
  207.4 29.0 %experts.1 = (bf16[5,832,512]{2,1,0:T(8,128)(2,1)}, bf16[5,832,1024]{2,1,0:T(8,128)(2,1)}, f32[5,832,1]{2,1,0:T(8,128)}) custom-call(s32[1]{0:T(128)} %bitcast.10.at_ref, bf16[5,832,1536]{2,1,0:T(8,128)(2,1)} %dispatch.3.rows_ref, bf16[20,1536,1024]{2,1,0:T(8,128)(2,1)} %gate_up_ref.1, f32[5,832,512]{2,1,0:T(8,128)} %fusion.9.plain_ref, ...), custom_call_target="tpu_custom_call" | custom-call | flops 13086228480 | bytes 45547520 | tf_op jit(solution)/shard_map/experts/pallas_call | solution.py:121
  236.4 15.8 %convolution_convert_fusion.5 = bf16[5,512,1536]{2,1,0:T(8,128)(2,1)} fusion(bf16[5,832,512]{2,1,0:T(8,128)(2,1)} %get-tuple-element.91, bf16[5,832,1536]{2,1,0:T(8,128)(2,1)} %dispatch.2), kind=kOutput, calls=%fused_computation.18 | convolution fusion | flops 6547046400 | bytes 24903680 | tf_op jit(solution)/shard_map/ecf,ecd->efd/dot_general | solution.py:874
  262.9 20.9 %fusion.2.rows_ref = bf16[5,832,1536]{2,1,0:T(8,128)(2,1)} fusion(bf16[5,832,1024]{2,1,0:T(8,128)(2,1)} %get-tuple-element.85, bf16[20,1536,1024]{2,1,0:T(8,128)(2,1)} %gate_up_ref.1, s32[]{:T(128)S(6)} %select_n.413), kind=kOutput, calls=%fused_computation.3 | convolution fusion | flops 13092618240 | bytes 37027844 | tf_op jit(solution)/shard_map/ecf,edf->ecd/dot_general | solution.py:890
  283.9 9.7 %combine.4 = bf16[4,512,1536]{2,1,0:T(8,128)(2,1)} custom-call(s32[4]{0:T(128)} %get-tuple-element.286.at_ref, f32[8,8,512]{2,1,0:T(8,128)} %pad.14.codes_ref, bf16[5,832,1536]{2,1,0:T(8,128)(2,1)} %fusion.2.rows_ref), custom_call_target="tpu_custom_call" | custom-call | flops 1 | bytes 1 | tf_op jit(solution)/shard_map/combine/pallas_call | solution.py:167
  294.5 14.7 %convolution_convert_fusion.4 = bf16[5,1536,512]{2,1,0:T(8,128)(2,1)} fusion(bf16[5,832,1536]{2,1,0:T(8,128)(2,1)} %dispatch.3.rows_ref, bf16[5,832,1024]{2,1,0:T(8,128)(2,1)} %get-tuple-element.85), kind=kOutput, calls=%fused_computation.17 | convolution fusion | flops 6547046400 | bytes 24903680 | tf_op jit(solution)/shard_map/ecd,ecf->edf/dot_general | solution.py:899
  309.3 11.4 %combine.5 = bf16[4,512,1536]{2,1,0:T(8,128)(2,1)} custom-call(s32[4]{0:T(128)} %get-tuple-element.287.at_ref, f32[8,8,512]{2,1,0:T(8,128)} %pad.14.codes_ref, bf16[5,832,1536]{2,1,0:T(8,128)(2,1)} %fusion.2.rows_ref, bf16[4,512,1536]{2,1,0:T(8,128)(2,1)} %collective-permute-done.9.refs_0_), custom_call_target="tpu_custom_call" | custom-call | flops 1 | bytes 1 | tf_op jit(solution)/shard_map/combine/pallas_call | solution.py:167
  320.6 13.6 %convolution_convert_fusion.rows_ref = bf16[5,832,1536]{2,1,0:T(8,128)(2,1)} fusion(bf16[5,832,512]{2,1,0:T(8,128)(2,1)} %get-tuple-element.91, bf16[20,512,1536]{2,1,0:T(8,128)(2,1)} %param.30, s32[]{:T(128)S(6)} %select_n.413), kind=kOutput, calls=%fused_computation.2 | convolution fusion | flops 6549504000 | bytes 24903684 | tf_op jit(solution)/shard_map/ecf,efd->ecd/dot_general | solution.py:911
  334.3 9.7 %combine.6 = bf16[4,512,1536]{2,1,0:T(8,128)(2,1)} custom-call(s32[4]{0:T(128)} %get-tuple-element.286.at_ref, f32[8,8,512]{2,1,0:T(8,128)} %pad.14.codes_ref, bf16[5,832,1536]{2,1,0:T(8,128)(2,1)} %convolution_convert_fusion.rows_ref), custom_call_target="tpu_custom_call" | custom-call | flops 1 | bytes 1 | tf_op jit(solution)/shard_map/combine/pallas_call | solution.py:167
  349.0 14.7 %convolution_convert_fusion.3 = bf16[5,1536,512]{2,1,0:T(8,128)(2,1)} fusion(bf16[5,832,1536]{2,1,0:T(8,128)(2,1)} %dispatch.3.rows_ref, bf16[5,832,1024]{2,1,0:T(8,128)(2,1)} %get-tuple-element.85), kind=kOutput, calls=%fused_computation.16 | convolution fusion | flops 6547046400 | bytes 24903680 | tf_op jit(solution)/shard_map/ecd,ecf->edf/dot_general | solution.py:899
  363.7 19.1 %collective-permute-done.11 = bf16[2,512,768]{2,1,0:T(8,128)(2,1)} collective-permute-done((bf16[2,512,768]{2,1,0:T(8,128)(2,1)S(1)}, bf16[2,512,768]{2,1,0:T(8,128)(2,1)}, u32[]{:S(2)}, u32[]{:S(2)}) %collective-permute-start.11) | collective-permute-done | bytes 1572896 | tf_op jit(solution)/shard_map/ppermute | solution.py:187
  387.9 11.0 %combine.7 = bf16[4,512,1536]{2,1,0:T(8,128)(2,1)} custom-call(s32[4]{0:T(128)} %get-tuple-element.287.at_ref, f32[8,8,512]{2,1,0:T(8,128)} %pad.14.codes_ref, bf16[5,832,1536]{2,1,0:T(8,128)(2,1)} %convolution_convert_fusion.rows_ref, bf16[4,512,1536]{2,1,0:T(8,128)(2,1)} %collective-permute-done.12.refs_0_), custom_call_target="tpu_custom_call" | custom-call | flops 1 | bytes 1 | tf_op jit(solution)/shard_map/combine/pallas_call | solution.py:167
  398.9 5.4 collective-permute-done.13
  425.3 7.2 convolution_convert_fusion.8.do_ref
  448.4 64.1 %attend_backward.1 = (bf16[512,1536]{1,0:T(8,128)(2,1)}, bf16[1024,512]{1,0:T(8,128)(2,1)}, bf16[1024,512]{1,0:T(8,128)(2,1)}, bf16[256,512]{1,0:T(8,128)(2,1)}, bf16[256,512]{1,0:T(8,128)(2,1)}) custom-call(s32[1]{0:T(128)} %bitcast.2.pos_ref, bf16[512,1536]{1,0:T(8,128)(2,1)} %get-tuple-element.106.q_ref, ...), custom_call_target="tpu_custom_call" | custom-call | flops 20132659200 | bytes 6291456 | tf_op jit(solution)/shard_map/attend_backward/pallas_call | solution.py:561
  535.2 12.5 %collective-permute-done.24 = bf16[256,1024]{1,0:T(8,128)(2,1)S(1)} collective-permute-done((bf16[256,1024]{1,0:T(8,128)(2,1)S(1)}, bf16[256,1024]{1,0:T(8,128)(2,1)S(1)}, u32[]{:S(2)}, u32[]{:S(2)}) %collective-permute-start.24) | collective-permute-done | bytes 524320 | tf_op jit(solution)/shard_map/ppermute | solution.py:672
  563.4 11.7 %copy.133 = bf16[1536,2688]{1,0:T(8,128)(2,1)} copy(bf16[1536,2688]{0,1:T(8,128)(2,1)} %pad_maximum_fusion) | data formatting | bytes 16515072 | tf_op jit(solution)/shard_map/optimization_barrier | solution.py:985
  590.3 11.1 %collective-permute-done.21 = bf16[512,768]{1,0:T(8,128)(2,1)S(1)} collective-permute-done((bf16[512,768]{1,0:T(8,128)(2,1)S(1)}, bf16[512,768]{1,0:T(8,128)(2,1)S(1)}, u32[]{:S(2)}, u32[]{:S(2)}) %collective-permute-start.21) | collective-permute-done | bytes 786464 | tf_op jit(solution)/shard_map/ppermute | solution.py:187
  615.5 18.1 %collective-permute-done.27 = bf16[4,2,48,1280]{3,2,0,1:T(8,128)(2,1)S(1)} collective-permute-done((bf16[4,2,48,1280]{3,2,0,1:T(8,128)(2,1)S(1)}, bf16[4,2,48,1280]{3,2,0,1:T(8,128)(2,1)S(1)}, u32[]{:S(2)}, u32[]{:S(2)}) %collective-permute-start.27) | collective-permute-done | bytes 983072 | tf_op jit(solution)/shard_map/ppermute | solution.py:187
  638.8 8.6 %collective-permute-done.28 = bf16[4,48,1280]{2,1,0:T(8,128)(2,1)S(1)} collective-permute-done((bf16[4,48,1280]{2,1,0:T(8,128)(2,1)S(1)}, bf16[4,48,1280]{2,1,0:T(8,128)(2,1)S(1)}, u32[]{:S(2)}, u32[]{:S(2)}) %collective-permute-start.28) | collective-permute-done | bytes 491552 | tf_op jit(solution)/shard_map/ppermute | solution.py:187
  647.7 20.2 %collective-permute-done.31 = bf16[5,2,96,512]{3,2,0,1:T(8,128)(2,1)S(1)} collective-permute-done((bf16[5,2,96,512]{3,2,0,1:T(8,128)(2,1)S(1)}, bf16[5,2,96,512]{3,2,0,1:T(8,128)(2,1)S(1)}, u32[]{:S(2)}, u32[]{:S(2)}) %collective-permute-start.31) | collective-permute-done | bytes 983072 | tf_op jit(solution)/shard_map/ppermute | solution.py:187
  675.0 25.3 %collective-permute-done.35 = bf16[48,4224]{1,0:T(8,128)(2,1)S(1)} collective-permute-done((bf16[48,4224]{1,0:T(8,128)(2,1)S(1)}, bf16[48,4224]{1,0:T(8,128)(2,1)S(1)}, u32[]{:S(2)}, u32[]{:S(2)}) %collective-permute-start.35) | collective-permute-done | bytes 405536 | tf_op jit(solution)/shard_map/ppermute | solution.py:727
  700.3 6.3 collective-permute-done.36
  739.7 8.6 %collective-permute-done.41 = bf16[5,96,512]{2,1,0:T(8,128)(2,1)} collective-permute-done((bf16[5,96,512]{2,1,0:T(8,128)(2,1)S(1)}, bf16[5,96,512]{2,1,0:T(8,128)(2,1)}, u32[]{:S(2)}, u32[]{:S(2)}) %collective-permute-start.41) | collective-permute-done | bytes 491552 | tf_op jit(solution)/shard_map/ppermute | solution.py:187
  (373 shorter events, 212.9 us)
Async XLA Ops:
  7.2 120.5 %all-gather.5.cloned.1.call-start = ((), (), s32[]{:S(2)}) async-start(), calls=%async_computation.6 | async-start | bytes 14598144 | tf_op jit(solution)/shard_map/all_gather | solution.py:808
  12.4 177.8 %all-gather.7.cloned.1.call-start = ((), (), s32[]{:S(2)}) async-start(), calls=%async_computation.7 | async-start | bytes 14155776 | tf_op jit(solution)/shard_map/all_gather | solution.py:856
  23.5 25.1 %collective-permute-start = (bf16[2,256,512]{2,1,0:T(8,128)(2,1)}, bf16[2,256,512]{2,1,0:T(8,128)(2,1)}, u32[]{:S(2)}, u32[]{:S(2)}) collective-permute-start(bf16[2,256,512]{2,1,0:T(8,128)(2,1)} %get-tuple-element.72), channel_id=1, source_target_pairs={{0,4},{2,6},{4,0},{6,2},{1,5},{3,7},{5,1},{7,3},{8,12},{10,14},{12... | collective-permute-start | bytes 1572872 | tf_op jit(solution)/shard_map/ppermute | solution.py:187
  24.7 23.8 %collective-permute-start.1 = (bf16[2,256,512]{2,1,0:T(8,128)(2,1)}, bf16[2,256,512]{2,1,0:T(8,128)(2,1)}, u32[]{:S(2)}, u32[]{:S(2)}) collective-permute-start(bf16[2,256,512]{2,1,0:T(8,128)(2,1)} %get-tuple-element.72), channel_id=1, source_target_pairs={{0,2},{2,0},{4,6},{6,4},{1,3},{3,1},{5,7},{7,5},{8,10},{10,8},{12,... | collective-permute-start | bytes 1572872 | tf_op jit(solution)/shard_map/ppermute | solution.py:187
  117.0 319.3 %reduce-scatter.4.cloned.1.call-start = ((), (), s32[]{:S(2)}) async-start(), calls=%async_computation.3 | async-start | bytes 9830400 | tf_op jit(solution)/shard_map/reduce_scatter | solution.py:613
  252.2 311.2 %reduce-scatter.6.cloned.1.call-start = ((), (), s32[]{:S(2)}) async-start(), calls=%async_computation.4 | async-start | bytes 9830400 | tf_op jit(solution)/shard_map/reduce_scatter | solution.py:613
  262.2 31.4 %collective-permute-start.8 = (f32[2,2,5,512]{3,1,2,0:T(2,128)S(1)}, f32[2,2,5,512]{3,1,2,0:T(2,128)S(1)}, u32[]{:S(2)}, u32[]{:S(2)}) collective-permute-start(f32[2,2,5,512]{3,1,2,0:T(2,128)S(1)} %bitcast.324), channel_id=1, source_target_pairs={{0,1},{1,0},{2,3},{3,2},{4,5},{5,4},{6,7},{7,6},{8,9},{9,8},{10,11... | collective-permute-start | bytes 122888 | tf_op jit(solution)/shard_map/ppermute | solution.py:187
  309.2 411.5 %reduce-scatter.8.cloned.1.call-start = ((), (), s32[]{:S(2)}) async-start(), calls=%async_computation.5 | async-start | bytes 9830400 | tf_op jit(solution)/shard_map/reduce_scatter | solution.py:613
  344.0 39.2 %collective-permute-start.12 = (bf16[4,512,1536]{2,1,0:T(8,128)(2,1)}, bf16[4,512,1536]{2,1,0:T(8,128)(2,1)}, u32[]{:S(2)}, u32[]{:S(2)}) collective-permute-start(bf16[4,512,1536]{2,1,0:T(8,128)(2,1)} %combine.6), channel_id=1, source_target_pairs={{0,2},{2,0},{4,6},{6,4},{1,3},{3,1},{5,7},{7,5},{8,10},{10,8},{12,... | collective-permute-start | bytes 18874376 | tf_op jit(solution)/shard_map/ppermute | solution.py:187
  347.2 35.6 %collective-permute-start.11 = (bf16[2,512,768]{2,1,0:T(8,128)(2,1)S(1)}, bf16[2,512,768]{2,1,0:T(8,128)(2,1)}, u32[]{:S(2)}, u32[]{:S(2)}) collective-permute-start(bf16[2,512,768]{2,1,0:T(8,128)(2,1)S(1)} %pad_maximum_fusion.3), channel_id=1, source_target_pairs={{0,1},{1,0},{2,3},{3,2},{4,5},{5,4},{6,7},{7,6},{8,9},{9,8},{10,11... | collective-permute-start | bytes 4718600 | tf_op jit(solution)/shard_map/ppermute | solution.py:187
  348.0 35.2 %collective-permute-start.10 = (bf16[2,512,768]{2,1,0:T(8,128)(2,1)S(1)}, bf16[2,512,768]{2,1,0:T(8,128)(2,1)}, u32[]{:S(2)}, u32[]{:S(2)}) collective-permute-start(bf16[2,512,768]{2,1,0:T(8,128)(2,1)S(1)} %slice.188), channel_id=1, source_target_pairs={{0,4},{2,6},{4,0},{6,2},{1,5},{3,7},{5,1},{7,3},{8,12},{10,14},{12... | collective-permute-start | bytes 4718600 | tf_op jit(solution)/shard_map/ppermute | solution.py:187
  386.6 17.7 %collective-permute-start.13 = (bf16[512,768]{1,0:T(8,128)(2,1)}, bf16[512,768]{1,0:T(8,128)(2,1)}, u32[]{:S(2)}, u32[]{:S(2)}) collective-permute-start(bf16[512,768]{1,0:T(8,128)(2,1)} %get-tuple-element.214), channel_id=1, source_target_pairs={{0,1},{1,0},{2,3},{3,2},{4,5},{5,4},{6,7},{7,6},{8,9},{9,8},{10,11... | collective-permute-start | bytes 2359304 | tf_op jit(solution)/shard_map/ppermute | solution.py:187
  387.3 17.5 %collective-permute-start.14 = (bf16[512,768]{1,0:T(8,128)(2,1)}, bf16[512,768]{1,0:T(8,128)(2,1)}, u32[]{:S(2)}, u32[]{:S(2)}) collective-permute-start(bf16[512,768]{1,0:T(8,128)(2,1)} %get-tuple-element.213), channel_id=1, source_target_pairs={{0,4},{2,6},{4,0},{6,2},{1,5},{3,7},{5,1},{7,3},{8,12},{10,14},{12... | collective-permute-start | bytes 2359304 | tf_op jit(solution)/shard_map/ppermute | solution.py:187
  416.8 15.7 %collective-permute-start.15 = (bf16[4,2,2,48,1536]{4,3,0,1,2:T(8,128)(2,1)}, bf16[4,2,2,48,1536]{4,3,0,1,2:T(8,128)(2,1)}, u32[]{:S(2)}, u32[]{:S(2)}) collective-permute-start(bf16[4,2,2,48,1536]{4,3,0,1,2:T(8,128)(2,1)} %bitcast.280), channel_id=1, source_target_pairs={{0,2},{2,0},{4,6},{6,4},{1,3},{3,1},{5,7},{7,5},{8,10},{10,8},{12,... | collective-permute-start | bytes 7077896 | tf_op jit(solution)/shard_map/ppermute | solution.py:187
  441.9 78.6 %collective-permute-start.17 = (bf16[2,512,768]{2,1,0:T(8,128)(2,1)}, bf16[2,512,768]{2,1,0:T(8,128)(2,1)}, u32[]{:S(2)}, u32[]{:S(2)}) collective-permute-start(bf16[2,512,768]{2,1,0:T(8,128)(2,1)} %pad_maximum_fusion.4), channel_id=1, source_target_pairs={{0,1},{1,0},{2,3},{3,2},{4,5},{5,4},{6,7},{7,6},{8,9},{9,8},{10,11... | collective-permute-start | bytes 4718600 | tf_op jit(solution)/shard_map/ppermute | solution.py:187
  443.8 76.7 %collective-permute-start.18 = (bf16[4,2,48,768]{3,2,0,1:T(8,128)(2,1)}, bf16[4,2,48,768]{3,2,0,1:T(8,128)(2,1)}, u32[]{:S(2)}, u32[]{:S(2)}) collective-permute-start(bf16[4,2,48,768]{3,2,0,1:T(8,128)(2,1)} %dynamic-slice_bitcast_fusion.3), channel_id=1, source_target_pairs={{0,4},{2,6},{4,0},{6,2},{1,5},{3,7},{5,1},{7,3},{8,12},{10,14},{12... | collective-permute-start | bytes 1769480 | tf_op jit(solution)/shard_map/ppermute | solution.py:187
  445.6 74.8 %collective-permute-start.19 = (bf16[4,2,48,768]{3,2,0,1:T(8,128)(2,1)}, bf16[4,2,48,768]{3,2,0,1:T(8,128)(2,1)}, u32[]{:S(2)}, u32[]{:S(2)}) collective-permute-start(bf16[4,2,48,768]{3,2,0,1:T(8,128)(2,1)} %dynamic-slice_bitcast_fusion.2), channel_id=1, source_target_pairs={{0,1},{1,0},{2,3},{3,2},{4,5},{5,4},{6,7},{7,6},{8,9},{9,8},{10,11... | collective-permute-start | bytes 1769480 | tf_op jit(solution)/shard_map/ppermute | solution.py:187
  445.8 74.7 %collective-permute-start.16 = (bf16[2,512,768]{2,1,0:T(8,128)(2,1)}, bf16[2,512,768]{2,1,0:T(8,128)(2,1)}, u32[]{:S(2)}, u32[]{:S(2)}) collective-permute-start(bf16[2,512,768]{2,1,0:T(8,128)(2,1)} %slice.200), channel_id=1, source_target_pairs={{0,4},{2,6},{4,0},{6,2},{1,5},{3,7},{5,1},{7,3},{8,12},{10,14},{12... | collective-permute-start | bytes 4718600 | tf_op jit(solution)/shard_map/ppermute | solution.py:187
  448.0 72.5 %collective-permute-start.20 = (bf16[5,2,32,1536]{3,2,0,1:T(8,128)(2,1)}, bf16[5,2,32,1536]{3,2,0,1:T(8,128)(2,1)}, u32[]{:S(2)}, u32[]{:S(2)}) collective-permute-start(bf16[5,2,32,1536]{3,2,0,1:T(8,128)(2,1)} %copy_bitcast_fusion.5), channel_id=1, source_target_pairs={{0,4},{2,6},{4,0},{6,2},{1,5},{3,7},{5,1},{7,3},{8,12},{10,14},{12... | collective-permute-start | bytes 2949128 | tf_op jit(solution)/shard_map/ppermute | solution.py:187
  524.2 23.5 %collective-permute-start.24 = (bf16[256,1024]{1,0:T(8,128)(2,1)S(1)}, bf16[256,1024]{1,0:T(8,128)(2,1)S(1)}, u32[]{:S(2)}, u32[]{:S(2)}) collective-permute-start(bf16[256,1024]{1,0:T(8,128)(2,1)S(1)} %pad_maximum_fusion.9), channel_id=1, source_target_pairs={{0,4},{2,6},{4,0},{6,2},{1,5},{3,7},{5,1},{7,3},{8,12},{10,14},{12... | collective-permute-start | bytes 1572872 | tf_op jit(solution)/shard_map/ppermute | solution.py:672
  524.8 23.6 %collective-permute-start.25 = (bf16[256,1024]{1,0:T(8,128)(2,1)S(1)}, bf16[256,1024]{1,0:T(8,128)(2,1)S(1)}, u32[]{:S(2)}, u32[]{:S(2)}) collective-permute-start(bf16[256,1024]{1,0:T(8,128)(2,1)S(1)} %pad_maximum_fusion.10), channel_id=1, source_target_pairs={{0,6},{2,0},{4,2},{6,4},{1,7},{3,1},{5,3},{7,5},{8,14},{10,8},{12,... | collective-permute-start | bytes 1572872 | tf_op jit(solution)/shard_map/ppermute | solution.py:672
  525.9 87.4 %collective-permute-start.42 = (bf16[2,5,32,1536]{3,2,1,0:T(8,128)(2,1)}, bf16[2,5,32,1536]{3,2,1,0:T(8,128)(2,1)}, u32[]{:S(2)}, u32[]{:S(2)}) collective-permute-start(bf16[2,5,32,1536]{3,2,1,0:T(8,128)(2,1)} %pad_maximum_fusion.7), channel_id=1, source_target_pairs={{0,2},{2,0},{4,6},{6,4},{1,3},{3,1},{5,7},{7,5},{8,10},{10,8},{12,... | collective-permute-start | bytes 2949128 | tf_op jit(solution)/shard_map/ppermute | solution.py:187
  530.1 53.4 %collective-permute-start.32 = (bf16[4,48,768]{2,1,0:T(8,128)(2,1)}, bf16[4,48,768]{2,1,0:T(8,128)(2,1)}, u32[]{:S(2)}, u32[]{:S(2)}) collective-permute-start(bf16[4,48,768]{2,1,0:T(8,128)(2,1)} %dynamic-slice_bitcast_fusion.17), channel_id=1, source_target_pairs={{0,1},{1,0},{2,3},{3,2},{4,5},{5,4},{6,7},{7,6},{8,9},{9,8},{10,11... | collective-permute-start | bytes 884744 | tf_op jit(solution)/shard_map/ppermute | solution.py:187
  577.7 31.0 %collective-permute-start.26 = (bf16[4,2,2,48,2688]{4,3,2,1,0:T(8,128)(2,1)S(1)}, bf16[4,2,2,48,2688]{4,3,2,1,0:T(8,128)(2,1)S(1)}, u32[]{:S(2)}, u32[]{:S(2)}) collective-permute-start(bf16[4,2,2,48,2688]{4,3,2,1,0:T(8,128)(2,1)S(1)} %dynamic-slice_bitcast_fusion), channel_id=1, source_target_pairs={{0,2},{2,0},{4,6},{6,4},{1,3},{3,1},{5,7},{7,5},{8,10},{10,8},{12,... | collective-permute-start | bytes 12386312 | tf_op jit(solution)/shard_map/ppermute | solution.py:187
  582.7 18.7 %collective-permute-start.21 = (bf16[512,768]{1,0:T(8,128)(2,1)S(1)}, bf16[512,768]{1,0:T(8,128)(2,1)S(1)}, u32[]{:S(2)}, u32[]{:S(2)}) collective-permute-start(bf16[512,768]{1,0:T(8,128)(2,1)S(1)} %get-tuple-element.207), channel_id=1, source_target_pairs={{0,1},{1,0},{2,3},{3,2},{4,5},{5,4},{6,7},{7,6},{8,9},{9,8},{10,11... | collective-permute-start | bytes 2359304 | tf_op jit(solution)/shard_map/ppermute | solution.py:187
  583.5 20.9 %collective-permute-start.22 = (bf16[512,768]{1,0:T(8,128)(2,1)S(1)}, bf16[512,768]{1,0:T(8,128)(2,1)S(1)}, u32[]{:S(2)}, u32[]{:S(2)}) collective-permute-start(bf16[512,768]{1,0:T(8,128)(2,1)S(1)} %get-tuple-element.208), channel_id=1, source_target_pairs={{0,4},{2,6},{4,0},{6,2},{1,5},{3,7},{5,1},{7,3},{8,12},{10,14},{12... | collective-permute-start | bytes 2359304 | tf_op jit(solution)/shard_map/ppermute | solution.py:187
  611.4 22.3 %collective-permute-start.27 = (bf16[4,2,48,1280]{3,2,0,1:T(8,128)(2,1)S(1)}, bf16[4,2,48,1280]{3,2,0,1:T(8,128)(2,1)S(1)}, u32[]{:S(2)}, u32[]{:S(2)}) collective-permute-start(bf16[4,2,48,1280]{3,2,0,1:T(8,128)(2,1)S(1)} %bitcast.317), channel_id=1, source_target_pairs={{0,4},{2,6},{4,0},{6,2},{1,5},{3,7},{5,1},{7,3},{8,12},{10,14},{12... | collective-permute-start | bytes 2949128 | tf_op jit(solution)/shard_map/ppermute | solution.py:187
  612.6 24.1 %collective-permute-start.29 = (bf16[4,2,48,1408]{3,2,1,0:T(8,128)(2,1)S(1)}, bf16[4,2,48,1408]{3,2,1,0:T(8,128)(2,1)S(1)}, u32[]{:S(2)}, u32[]{:S(2)}) collective-permute-start(bf16[4,2,48,1408]{3,2,1,0:T(8,128)(2,1)S(1)} %dynamic-slice_bitcast_fusion.1), channel_id=1, source_target_pairs={{0,1},{1,0},{2,3},{3,2},{4,5},{5,4},{6,7},{7,6},{8,9},{9,8},{10,11... | collective-permute-start | bytes 3244040 | tf_op jit(solution)/shard_map/ppermute | solution.py:187
  637.6 30.3 %collective-permute-start.31 = (bf16[5,2,96,512]{3,2,0,1:T(8,128)(2,1)S(1)}, bf16[5,2,96,512]{3,2,0,1:T(8,128)(2,1)S(1)}, u32[]{:S(2)}, u32[]{:S(2)}) collective-permute-start(bf16[5,2,96,512]{3,2,0,1:T(8,128)(2,1)S(1)} %copy_bitcast_fusion.4), channel_id=1, source_target_pairs={{0,4},{2,6},{4,0},{6,2},{1,5},{3,7},{5,1},{7,3},{8,12},{10,14},{12... | collective-permute-start | bytes 2949128 | tf_op jit(solution)/shard_map/ppermute | solution.py:187
  669.4 30.9 %collective-permute-start.35 = (bf16[48,4224]{1,0:T(8,128)(2,1)S(1)}, bf16[48,4224]{1,0:T(8,128)(2,1)S(1)}, u32[]{:S(2)}, u32[]{:S(2)}) collective-permute-start(bf16[48,4224]{1,0:T(8,128)(2,1)S(1)} %get-tuple-element.234), channel_id=1, source_target_pairs={{0,16},{8,24},{16,0},{24,8},{1,17},{9,25},{17,1},{25,9},{2,18},{10... | collective-permute-start | bytes 1216520 | tf_op jit(solution)/shard_map/ppermute | solution.py:727
  670.6 36.0 %collective-permute-start.36 = (bf16[48,4224]{1,0:T(8,128)(2,1)S(1)}, bf16[48,4224]{1,0:T(8,128)(2,1)S(1)}, u32[]{:S(2)}, u32[]{:S(2)}) collective-permute-start(bf16[48,4224]{1,0:T(8,128)(2,1)S(1)} %get-tuple-element.233), channel_id=1, source_target_pairs={{0,24},{8,0},{16,8},{24,16},{1,25},{9,1},{17,9},{25,17},{2,26},{10... | collective-permute-start | bytes 1216520 | tf_op jit(solution)/shard_map/ppermute | solution.py:727
  725.7 22.6 %collective-permute-start.41 = (bf16[5,96,512]{2,1,0:T(8,128)(2,1)S(1)}, bf16[5,96,512]{2,1,0:T(8,128)(2,1)}, u32[]{:S(2)}, u32[]{:S(2)}) collective-permute-start(bf16[5,96,512]{2,1,0:T(8,128)(2,1)S(1)} %get-tuple-element.223), channel_id=1, source_target_pairs={{0,6},{2,4},{4,2},{6,0},{1,7},{3,5},{5,3},{7,1},{8,14},{10,12},{12... | collective-permute-start | bytes 1474568 | tf_op jit(solution)/shard_map/ppermute | solution.py:187
  (76 other events, 660.8 us)
Sparse Core Ops, SparseCore 0:
  12.6 85.9 all-gather.4
  117.1 73.1 all-gather.6
  252.3 135.7 reduce-scatter.3
  390.9 136.7 reduce-scatter.5
  529.8 136.7 reduce-scatter.7

commit v7 on v6

--- a/solution.py
+++ b/solution.py
@@ -731,10 +731,13 @@
     return total.astype(jnp.bfloat16)
 
 
-def finish_dense(grad):
-    if grad.ndim == 2:
-        return lax.psum(grad, "expert").astype(jnp.float32)
-    grad = scatter_parts(grad)
+def sum_dense(grad):
+    return lax.psum(grad, "expert") if grad.ndim == 2 else scatter_parts(grad)
+
+
+def finish_dense(grad, halves):
+    if not halves:
+        return grad.astype(jnp.float32)
     other = swap(grad, "expert", 1)
     first = lax.axis_index("expert") == 0
     return jnp.concatenate(
@@ -805,20 +808,6 @@
     code_table = jnp.concatenate(
         [code_table[i * code_rows : (i + 1) * code_rows] for i in range(fold)], axis=1
     )
-    upstream_all = lax.all_gather(
-        jnp.concatenate([upstream_low, code_table], axis=0), group, axis=0, tiled=False
-    )
-    codes_all = upstream_all[:, count_of_tokens:]
-    codes_all = jnp.concatenate(
-        [
-            codes_all[:, :, i * count_of_tokens : (i + 1) * count_of_tokens] for i in range(fold)
-        ],
-        axis=1,
-    ).astype(jnp.float32)
-    own_codes = lax.dynamic_slice_in_dim(codes_all, first_expert, own, axis=1)
-    own_codes = jnp.pad(own_codes, ((0, 0), (0, -own % 8), (0, 0)), constant_values=-2.0)
-    d_slot_rows = dispatch(own_codes, upstream_all, own, slots)
-    d_plain = jnp.einsum("ecd,efd->ecf", d_slot_rows, down_own, preferred_element_type=jnp.float32)
     gain_one = norm1_gain.astype(jnp.float32)
     gain_two = norm2_gain.astype(jnp.float32)
     tokens = jnp.concatenate(
@@ -846,6 +835,20 @@
     prompt_kv, q_lin = gather_keys(
         near_kv, jnp.dot(h1_late, w_query, preferred_element_type=jnp.float32)
     )
+    travel = jnp.concatenate([upstream_low, code_table], axis=0)
+    prompt_kv, travel = lax.optimization_barrier((prompt_kv, travel))
+    upstream_all = lax.all_gather(travel, group, axis=0, tiled=False)
+    codes_all = upstream_all[:, count_of_tokens:]
+    codes_all = jnp.concatenate(
+        [
+            codes_all[:, :, i * count_of_tokens : (i + 1) * count_of_tokens] for i in range(fold)
+        ],
+        axis=1,
+    ).astype(jnp.float32)
+    own_codes = lax.dynamic_slice_in_dim(codes_all, first_expert, own, axis=1)
+    own_codes = jnp.pad(own_codes, ((0, 0), (0, -own % 8), (0, 0)), constant_values=-2.0)
+    d_slot_rows = dispatch(own_codes, upstream_all, own, slots)
+    d_plain = jnp.einsum("ecd,efd->ecf", d_slot_rows, down_own, preferred_element_type=jnp.float32)
     query_row_block, merged_low, log_total = attend_forward(
         q_lin, prompt_kv, cont_kv, cosine, sine, start, prompt_rows, cont_len
     )
@@ -982,10 +985,13 @@
     dense = jnp.concatenate([grad_query, grad_key, grad_value, small], axis=1).astype(jnp.bfloat16)
     heads_width = QUERY_HEADS * HEAD_SIZE
     edge = heads_width + 2 * key_value_width
-    gate_part, dense = lax.optimization_barrier((gate_part, dense))
+    dense, gate_part = lax.optimization_barrier((fold_one(dense), gate_part))
     gate_kept, gate_moved = pairs_experts(gate_part, split)
-    dense = fold_three(*fold_two(fold_one(dense), edge // 256 * 128))
-    dense, gate_moved = lax.optimization_barrier((dense, gate_moved))
+    dense = fold_three(*fold_two(dense, edge // 256 * 128))
+    dense = jnp.concatenate([dense, grad_out], axis=-1)
+    dense, gate_moved, up_part = lax.optimization_barrier((dense, gate_moved, up_part))
+    up_kept, up_moved = pairs_experts(up_part, split)
+    dense = sum_dense(dense)
     shares = lax.axis_size("dp") * lax.axis_size("ctx")
     grad_down = place_experts(
         jnp.zeros((local_experts, hidden_units // shares, model_width), jnp.float32),
@@ -997,10 +1003,12 @@
         cores_experts(gate_kept, gate_moved, split),
         0,
     )
-    dense = finish_dense(jnp.concatenate([dense, grad_out], axis=-1))
+    dense, up_moved, grad_gate_up = lax.optimization_barrier((dense, up_moved, grad_gate_up))
+    grad_gate_up = place_experts(
+        grad_gate_up, cores_experts(up_kept, up_moved, split), hidden_units
+    )
+    dense = finish_dense(dense, dense.shape[0] < w_query.shape[0] // shares)
     tail = edge + small.shape[1]
-    dense, up_part, grad_gate_up = lax.optimization_barrier((dense, up_part, grad_gate_up))
-    grad_gate_up = place_experts(grad_gate_up, send_experts(up_part, split), hidden_units)
     return (
         y_prompt,
         y_cont,

time: 766 us -> 741 us (0.967)
  waiting for transfers between devices: 213 us -> 192 us
  local copies, waits for them, and re-layouts: 66.1 us -> 51.3 us
    ppermute x37 -> x36, waiting for transfers between devices: 129 us -> 94.1 us  [swap(): return lax.ppermute(values, axis, [(i, i ^ bit) for i in range(size)])]
    optimization_barrier x1 -> x0, local copies, waits for them, and re-layouts: 11.7 us -> none  [per_device(): gate_part, dense = lax.optimization_barrier((gate_part, dense))]
    all_gather x1, waiting for transfers between devices: 32.2 us -> 43.2 us  [per_device(): rows_all = lax.all_gather(h2_low, group, axis=0, tiled=False)]
    ppermute x37 -> x36, starting transfers between devices: 35.6 us -> 34.4 us  [swap(): return lax.ppermute(values, axis, [(i, i ^ bit) for i in range(size)])]
  transfers between devices with their start and end apart: 48 -> 47, of which waited for: 27 -> 27; matrix products, arithmetic and copies ran while one was open for 30% -> 31% of each run, Pallas kernels for 23% -> 23%
where the time goes in v7:
time: 741 us; the launch traced here: 732 us
  Pallas kernels  221 us (30%)
  waiting for transfers between devices  192 us (26%)
  matrix products  139 us (19%)
  other arithmetic  72.6 us (10%)
  local copies, waits for them, and re-layouts  51.3 us (7%)
  starting transfers between devices  39.6 us (5%)
  between operations  15.7 us (2%)
    ppermute x36, waiting for transfers between devices, swap(): return lax.ppermute(values, axis, [(i, i ^ bit) for i in range(size)])  94.1 us
    pallas_call x1, Pallas kernels, attend_backward(): pl.pallas_call(partial(attend_backward_body, group, rows, cont_len, chunk...  64 us
    pallas_call x1, Pallas kernels, attend_forward(): pl.pallas_call(partial(attend_forward_body, group, rows, cont_len), grid_...  50.5 us
    all_gather x1, waiting for transfers between devices, per_device(): rows_all = lax.all_gather(h2_low, group, axis=0, tiled=False)  43.2 us
    pallas_call x4, Pallas kernels, combine(): pl.pallas_call(partial(combine_body, own, slots), grid_spec=pltpu.Prefetc...  41.7 us
    ppermute x36, starting transfers between devices, swap(): return lax.ppermute(values, axis, [(i, i ^ bit) for i in range(size)])  34.4 us
    ppermute x3, waiting for transfers between devices, scatter_parts(): lax.ppermute(take(parts, (here + hop) % size), 'dp', [(i, (i + hop) % siz...  31 us
    dot_general x2, matrix products, expert_gradient(): jnp.einsum('ecd,ecf->edf', slot_rows, d_part, preferred_element_type=jnp....  29 us
  transfers between devices with their start and end apart: 47, of which 27 were waited for; matrix products, arithmetic and copies ran while one was open for 31% of the time, Pallas kernels for 23%

profile of v7, /device:TPU:9, one launch (start us, length us, event | category | flops | bytes accessed | tf_op | source)
XLA Modules:
  0.0 731.7 jit_solution(46959673509558033)
XLA Ops:
  15.2 6.9 project_keys.1
  26.6 7.2 fusion.109.q_ref
  40.8 50.5 %attend_forward.1 = (bf16[512,1536]{1,0:T(8,128)(2,1)}, bf16[512,1536]{1,0:T(8,128)(2,1)}, f32[24,8,512]{2,1,0:T(8,128)}) custom-call(s32[1]{0:T(128)} %bitcast.2.pos_ref, f32[512,1536]{1,0:T(8,128)} %fusion.109.q_ref, f32[512,128]{1,0:T(8,128)} %get-tuple-element.302.cos_ref, f32[512,128]{1,0:T(8,128)} %get-tuple-element.301.sin_ref, ...), custom_call_target="tpu_custom_call" | custom-call | flops 8053063680 | bytes 6291456 | tf_op jit(solution)/shard_map/attend_forward/pallas_call | solution.py:430
  91.3 5.2 multiply_reduce_fusion.2
  117.3 14.8 %dispatch.2 = bf16[5,832,1536]{2,1,0:T(8,128)(2,1)} custom-call(f32[8,8,512]{2,1,0:T(8,128)} %pad.14.codes_ref, bf16[8,528,1536]{2,1,0:T(8,128)(2,1)} %bitcast.304), custom_call_target="tpu_custom_call" | custom-call | flops 6543114240 | bytes 25362432 | tf_op jit(solution)/shard_map/dispatch/pallas_call | solution.py:78
  132.0 14.1 %fusion.9.plain_ref = f32[5,832,512]{2,1,0:T(8,128)} fusion(bf16[5,832,1536]{2,1,0:T(8,128)(2,1)} %dispatch.2, bf16[20,512,1536]{2,1,0:T(8,128)(2,1)} %param.30, s32[]{:T(128)S(6)} %select_n.409), kind=kOutput, calls=%fused_computation.14 | convolution fusion | flops 6543114240 | bytes 29163524 | tf_op jit(solution)/shard_map/ecd,efd->ecf/dot_general | solution.py:851
  146.1 43.2 %all-gather.7.cloned.1.call-done = bf16[4096,1536]{1,0:T(8,128)(2,1)} async-done(((bf16[512,1536]{1,0:T(8,128)(2,1)}), bf16[4096,1536]{1,0:T(8,128)(2,1)}) %all-gather.7.cloned.1.call-update) | async-done | bytes 12582928 | tf_op jit(solution)/shard_map/all_gather | solution.py:859
  192.4 14.1 %dispatch.3.rows_ref = bf16[5,832,1536]{2,1,0:T(8,128)(2,1)} custom-call(f32[8,8,512]{2,1,0:T(8,128)} %pad.14.codes_ref, bf16[8,512,1536]{2,1,0:T(8,128)(2,1)} %bitcast.305), custom_call_target="tpu_custom_call" | custom-call | flops 6543114240 | bytes 25362432 | tf_op jit(solution)/shard_map/dispatch/pallas_call | solution.py:78
  206.5 29.0 %experts.1 = (bf16[5,832,512]{2,1,0:T(8,128)(2,1)}, bf16[5,832,1024]{2,1,0:T(8,128)(2,1)}, f32[5,832,1]{2,1,0:T(8,128)}) custom-call(s32[1]{0:T(128)} %bitcast.10.at_ref, bf16[5,832,1536]{2,1,0:T(8,128)(2,1)} %dispatch.3.rows_ref, bf16[20,1536,1024]{2,1,0:T(8,128)(2,1)} %gate_up_ref.1, f32[5,832,512]{2,1,0:T(8,128)} %fusion.9.plain_ref, ...), custom_call_target="tpu_custom_call" | custom-call | flops 13086228480 | bytes 45547520 | tf_op jit(solution)/shard_map/experts/pallas_call | solution.py:121
  235.5 15.7 %convolution_convert_fusion.5 = bf16[5,512,1536]{2,1,0:T(8,128)(2,1)} fusion(bf16[5,832,512]{2,1,0:T(8,128)(2,1)} %get-tuple-element.96, bf16[5,832,1536]{2,1,0:T(8,128)(2,1)} %dispatch.2), kind=kOutput, calls=%fused_computation.18 | convolution fusion | flops 6547046400 | bytes 24903680 | tf_op jit(solution)/shard_map/ecf,ecd->efd/dot_general | solution.py:877
  262.0 20.9 %fusion.2.rows_ref = bf16[5,832,1536]{2,1,0:T(8,128)(2,1)} fusion(bf16[5,832,1024]{2,1,0:T(8,128)(2,1)} %get-tuple-element.90, bf16[20,1536,1024]{2,1,0:T(8,128)(2,1)} %gate_up_ref.1, s32[]{:T(128)S(6)} %select_n.409), kind=kOutput, calls=%fused_computation.3 | convolution fusion | flops 13092618240 | bytes 37027844 | tf_op jit(solution)/shard_map/ecf,edf->ecd/dot_general | solution.py:893
  282.9 9.7 %combine.4 = bf16[4,512,1536]{2,1,0:T(8,128)(2,1)} custom-call(s32[4]{0:T(128)} %get-tuple-element.311.at_ref, f32[8,8,512]{2,1,0:T(8,128)} %pad.14.codes_ref, bf16[5,832,1536]{2,1,0:T(8,128)(2,1)} %fusion.2.rows_ref), custom_call_target="tpu_custom_call" | custom-call | flops 1 | bytes 1 | tf_op jit(solution)/shard_map/combine/pallas_call | solution.py:167
  293.6 14.5 %convolution_convert_fusion.4 = bf16[5,1536,512]{2,1,0:T(8,128)(2,1)} fusion(bf16[5,832,1536]{2,1,0:T(8,128)(2,1)} %dispatch.3.rows_ref, bf16[5,832,1024]{2,1,0:T(8,128)(2,1)} %get-tuple-element.90), kind=kOutput, calls=%fused_computation.17 | convolution fusion | flops 6547046400 | bytes 24903680 | tf_op jit(solution)/shard_map/ecd,ecf->edf/dot_general | solution.py:902
  308.2 11.3 %combine.5 = bf16[4,512,1536]{2,1,0:T(8,128)(2,1)} custom-call(s32[4]{0:T(128)} %get-tuple-element.312.at_ref, f32[8,8,512]{2,1,0:T(8,128)} %pad.14.codes_ref, bf16[5,832,1536]{2,1,0:T(8,128)(2,1)} %fusion.2.rows_ref, bf16[4,512,1536]{2,1,0:T(8,128)(2,1)} %collective-permute-done.9.refs_0_), custom_call_target="tpu_custom_call" | custom-call | flops 1 | bytes 1 | tf_op jit(solution)/shard_map/combine/pallas_call | solution.py:167
  319.5 13.7 %convolution_convert_fusion.rows_ref = bf16[5,832,1536]{2,1,0:T(8,128)(2,1)} fusion(bf16[5,832,512]{2,1,0:T(8,128)(2,1)} %get-tuple-element.96, bf16[20,512,1536]{2,1,0:T(8,128)(2,1)} %param.30, s32[]{:T(128)S(6)} %select_n.409), kind=kOutput, calls=%fused_computation.2 | convolution fusion | flops 6549504000 | bytes 24903684 | tf_op jit(solution)/shard_map/ecf,efd->ecd/dot_general | solution.py:914
  333.2 9.7 %combine.6 = bf16[4,512,1536]{2,1,0:T(8,128)(2,1)} custom-call(s32[4]{0:T(128)} %get-tuple-element.311.at_ref, f32[8,8,512]{2,1,0:T(8,128)} %pad.14.codes_ref, bf16[5,832,1536]{2,1,0:T(8,128)(2,1)} %convolution_convert_fusion.rows_ref), custom_call_target="tpu_custom_call" | custom-call | flops 1 | bytes 1 | tf_op jit(solution)/shard_map/combine/pallas_call | solution.py:167
  347.9 14.5 %convolution_convert_fusion.3 = bf16[5,1536,512]{2,1,0:T(8,128)(2,1)} fusion(bf16[5,832,1536]{2,1,0:T(8,128)(2,1)} %dispatch.3.rows_ref, bf16[5,832,1024]{2,1,0:T(8,128)(2,1)} %get-tuple-element.90), kind=kOutput, calls=%fused_computation.16 | convolution fusion | flops 6547046400 | bytes 24903680 | tf_op jit(solution)/shard_map/ecd,ecf->edf/dot_general | solution.py:902
  362.4 19.3 %collective-permute-done.11 = bf16[2,512,768]{2,1,0:T(8,128)(2,1)} collective-permute-done((bf16[2,512,768]{2,1,0:T(8,128)(2,1)S(1)}, bf16[2,512,768]{2,1,0:T(8,128)(2,1)}, u32[]{:S(2)}, u32[]{:S(2)}) %collective-permute-start.11) | collective-permute-done | bytes 1572896 | tf_op jit(solution)/shard_map/ppermute | solution.py:187
  386.8 11.0 %combine.7 = bf16[4,512,1536]{2,1,0:T(8,128)(2,1)} custom-call(s32[4]{0:T(128)} %get-tuple-element.312.at_ref, f32[8,8,512]{2,1,0:T(8,128)} %pad.14.codes_ref, bf16[5,832,1536]{2,1,0:T(8,128)(2,1)} %convolution_convert_fusion.rows_ref, bf16[4,512,1536]{2,1,0:T(8,128)(2,1)} %collective-permute-done.12.refs_0_), custom_call_target="tpu_custom_call" | custom-call | flops 1 | bytes 1 | tf_op jit(solution)/shard_map/combine/pallas_call | solution.py:167
  397.8 5.3 collective-permute-done.13
  425.1 7.1 convolution_convert_fusion.8.do_ref
  432.2 4.5 fusion.15
  448.9 64.0 %attend_backward.1 = (bf16[512,1536]{1,0:T(8,128)(2,1)}, bf16[1024,512]{1,0:T(8,128)(2,1)}, bf16[1024,512]{1,0:T(8,128)(2,1)}, bf16[256,512]{1,0:T(8,128)(2,1)}, bf16[256,512]{1,0:T(8,128)(2,1)}) custom-call(s32[1]{0:T(128)} %bitcast.2.pos_ref, bf16[512,1536]{1,0:T(8,128)(2,1)} %get-tuple-element.111.q_ref, ...), custom_call_target="tpu_custom_call" | custom-call | flops 20132659200 | bytes 6291456 | tf_op jit(solution)/shard_map/attend_backward/pallas_call | solution.py:561
  512.9 5.3 fusion.110
  522.0 4.4 convolution_convert_fusion.1
  542.4 12.1 %collective-permute-done.24 = bf16[256,1024]{1,0:T(8,128)(2,1)S(1)} collective-permute-done((bf16[256,1024]{1,0:T(8,128)(2,1)S(1)}, bf16[256,1024]{1,0:T(8,128)(2,1)S(1)}, u32[]{:S(2)}, u32[]{:S(2)}) %collective-permute-start.24) | collective-permute-done | bytes 524320 | tf_op jit(solution)/shard_map/ppermute | solution.py:672
  586.1 9.4 %collective-permute-done.21 = bf16[512,768]{1,0:T(8,128)(2,1)} collective-permute-done((bf16[512,768]{1,0:T(8,128)(2,1)}, bf16[512,768]{1,0:T(8,128)(2,1)}, u32[]{:S(2)}, u32[]{:S(2)}) %collective-permute-start.21) | collective-permute-done | bytes 786464 | tf_op jit(solution)/shard_map/ppermute | solution.py:187
  614.1 15.6 %collective-permute-done.27 = bf16[4,2,48,1280]{3,2,1,0:T(8,128)(2,1)S(1)} collective-permute-done((bf16[4,2,48,1280]{3,2,1,0:T(8,128)(2,1)S(1)}, bf16[4,2,48,1280]{3,2,1,0:T(8,128)(2,1)S(1)}, u32[]{:S(2)}, u32[]{:S(2)}) %collective-permute-start.27) | collective-permute-done | bytes 983072 | tf_op jit(solution)/shard_map/ppermute | solution.py:187
  635.8 4.2 broadcast_in_dim.115
  644.6 17.8 %collective-permute-done.30 = bf16[4,48,1408]{2,1,0:T(8,128)(2,1)S(1)} collective-permute-done((bf16[4,48,1408]{2,1,0:T(8,128)(2,1)S(1)}, bf16[4,48,1408]{2,1,0:T(8,128)(2,1)S(1)}, u32[]{:S(2)}, u32[]{:S(2)}) %collective-permute-start.30) | collective-permute-done | bytes 540704 | tf_op jit(solution)/shard_map/ppermute | solution.py:187
  676.1 25.6 %collective-permute-done.35 = bf16[48,4224]{1,0:T(8,128)(2,1)S(1)} collective-permute-done((bf16[48,4224]{1,0:T(8,128)(2,1)S(1)}, bf16[48,4224]{1,0:T(8,128)(2,1)S(1)}, u32[]{:S(2)}, u32[]{:S(2)}) %collective-permute-start.35) | collective-permute-done | bytes 405536 | tf_op jit(solution)/shard_map/ppermute | solution.py:727
  710.8 7.2 collective-permute-done.39
  (400 shorter events, 208.5 us)
Async XLA Ops:
  7.2 108.2 %all-gather.5.cloned.1.call-start = ((), (), s32[]{:S(2)}) async-start(), calls=%async_computation.6 | async-start | bytes 14598144 | tf_op jit(solution)/shard_map/all_gather | solution.py:840
  39.4 149.9 %all-gather.7.cloned.1.call-start = ((), (), s32[]{:S(2)}) async-start(), calls=%async_computation.7 | async-start | bytes 14155776 | tf_op jit(solution)/shard_map/all_gather | solution.py:859
  99.7 337.0 %reduce-scatter.4.cloned.1.call-start = ((), (), s32[]{:S(2)}) async-start(), calls=%async_computation.3 | async-start | bytes 9830400 | tf_op jit(solution)/shard_map/reduce_scatter | solution.py:613
  251.3 354.5 %reduce-scatter.6.cloned.1.call-start = ((), (), s32[]{:S(2)}) async-start(), calls=%async_computation.4 | async-start | bytes 9830400 | tf_op jit(solution)/shard_map/reduce_scatter | solution.py:613
  261.3 31.4 %collective-permute-start.8 = (f32[2,2,5,512]{3,1,2,0:T(2,128)S(1)}, f32[2,2,5,512]{3,1,2,0:T(2,128)S(1)}, u32[]{:S(2)}, u32[]{:S(2)}) collective-permute-start(f32[2,2,5,512]{3,1,2,0:T(2,128)S(1)} %bitcast.343), channel_id=1, source_target_pairs={{0,1},{1,0},{2,3},{3,2},{4,5},{5,4},{6,7},{7,6},{8,9},{9,8},{10,11... | collective-permute-start | bytes 122888 | tf_op jit(solution)/shard_map/ppermute | solution.py:187
  308.1 357.6 %reduce-scatter.8.cloned.1.call-start = ((), (), s32[]{:S(2)}) async-start(), calls=%async_computation.5 | async-start | bytes 9830400 | tf_op jit(solution)/shard_map/reduce_scatter | solution.py:613
  342.9 39.2 %collective-permute-start.12 = (bf16[4,512,1536]{2,1,0:T(8,128)(2,1)}, bf16[4,512,1536]{2,1,0:T(8,128)(2,1)}, u32[]{:S(2)}, u32[]{:S(2)}) collective-permute-start(bf16[4,512,1536]{2,1,0:T(8,128)(2,1)} %combine.6), channel_id=1, source_target_pairs={{0,2},{2,0},{4,6},{6,4},{1,3},{3,1},{5,7},{7,5},{8,10},{10,8},{12,... | collective-permute-start | bytes 18874376 | tf_op jit(solution)/shard_map/ppermute | solution.py:187
  346.0 35.6 %collective-permute-start.11 = (bf16[2,512,768]{2,1,0:T(8,128)(2,1)S(1)}, bf16[2,512,768]{2,1,0:T(8,128)(2,1)}, u32[]{:S(2)}, u32[]{:S(2)}) collective-permute-start(bf16[2,512,768]{2,1,0:T(8,128)(2,1)S(1)} %pad_maximum_fusion.3), channel_id=1, source_target_pairs={{0,1},{1,0},{2,3},{3,2},{4,5},{5,4},{6,7},{7,6},{8,9},{9,8},{10,11... | collective-permute-start | bytes 4718600 | tf_op jit(solution)/shard_map/ppermute | solution.py:187
  346.9 35.2 %collective-permute-start.10 = (bf16[2,512,768]{2,1,0:T(8,128)(2,1)S(1)}, bf16[2,512,768]{2,1,0:T(8,128)(2,1)}, u32[]{:S(2)}, u32[]{:S(2)}) collective-permute-start(bf16[2,512,768]{2,1,0:T(8,128)(2,1)S(1)} %slice.194), channel_id=1, source_target_pairs={{0,4},{2,6},{4,0},{6,2},{1,5},{3,7},{5,1},{7,3},{8,12},{10,14},{12... | collective-permute-start | bytes 4718600 | tf_op jit(solution)/shard_map/ppermute | solution.py:187
  385.4 17.7 %collective-permute-start.13 = (bf16[512,768]{1,0:T(8,128)(2,1)}, bf16[512,768]{1,0:T(8,128)(2,1)}, u32[]{:S(2)}, u32[]{:S(2)}) collective-permute-start(bf16[512,768]{1,0:T(8,128)(2,1)} %get-tuple-element.246), channel_id=1, source_target_pairs={{0,1},{1,0},{2,3},{3,2},{4,5},{5,4},{6,7},{7,6},{8,9},{9,8},{10,11... | collective-permute-start | bytes 2359304 | tf_op jit(solution)/shard_map/ppermute | solution.py:187
  386.2 17.5 %collective-permute-start.14 = (bf16[512,768]{1,0:T(8,128)(2,1)}, bf16[512,768]{1,0:T(8,128)(2,1)}, u32[]{:S(2)}, u32[]{:S(2)}) collective-permute-start(bf16[512,768]{1,0:T(8,128)(2,1)} %get-tuple-element.245), channel_id=1, source_target_pairs={{0,4},{2,6},{4,0},{6,2},{1,5},{3,7},{5,1},{7,3},{8,12},{10,14},{12... | collective-permute-start | bytes 2359304 | tf_op jit(solution)/shard_map/ppermute | solution.py:187
  442.3 84.1 %collective-permute-start.17 = (bf16[2,512,768]{2,1,0:T(8,128)(2,1)}, bf16[2,512,768]{2,1,0:T(8,128)(2,1)}, u32[]{:S(2)}, u32[]{:S(2)}) collective-permute-start(bf16[2,512,768]{2,1,0:T(8,128)(2,1)} %pad_maximum_fusion.4), channel_id=1, source_target_pairs={{0,1},{1,0},{2,3},{3,2},{4,5},{5,4},{6,7},{7,6},{8,9},{9,8},{10,11... | collective-permute-start | bytes 4718600 | tf_op jit(solution)/shard_map/ppermute | solution.py:187
  444.2 82.2 %collective-permute-start.18 = (bf16[4,2,48,768]{3,2,1,0:T(8,128)(2,1)}, bf16[4,2,48,768]{3,2,1,0:T(8,128)(2,1)}, u32[]{:S(2)}, u32[]{:S(2)}) collective-permute-start(bf16[4,2,48,768]{3,2,1,0:T(8,128)(2,1)} %dynamic-slice_bitcast_fusion.5), channel_id=1, source_target_pairs={{0,4},{2,6},{4,0},{6,2},{1,5},{3,7},{5,1},{7,3},{8,12},{10,14},{12... | collective-permute-start | bytes 1769480 | tf_op jit(solution)/shard_map/ppermute | solution.py:187
  446.1 80.2 %collective-permute-start.19 = (bf16[4,2,48,768]{3,2,1,0:T(8,128)(2,1)}, bf16[4,2,48,768]{3,2,1,0:T(8,128)(2,1)}, u32[]{:S(2)}, u32[]{:S(2)}) collective-permute-start(bf16[4,2,48,768]{3,2,1,0:T(8,128)(2,1)} %dynamic-slice_bitcast_fusion.4), channel_id=1, source_target_pairs={{0,1},{1,0},{2,3},{3,2},{4,5},{5,4},{6,7},{7,6},{8,9},{9,8},{10,11... | collective-permute-start | bytes 1769480 | tf_op jit(solution)/shard_map/ppermute | solution.py:187
  446.3 80.1 %collective-permute-start.16 = (bf16[2,512,768]{2,1,0:T(8,128)(2,1)}, bf16[2,512,768]{2,1,0:T(8,128)(2,1)}, u32[]{:S(2)}, u32[]{:S(2)}) collective-permute-start(bf16[2,512,768]{2,1,0:T(8,128)(2,1)} %slice.206), channel_id=1, source_target_pairs={{0,4},{2,6},{4,0},{6,2},{1,5},{3,7},{5,1},{7,3},{8,12},{10,14},{12... | collective-permute-start | bytes 4718600 | tf_op jit(solution)/shard_map/ppermute | solution.py:187
  448.4 78.0 %collective-permute-start.20 = (bf16[5,2,32,1536]{3,2,0,1:T(8,128)(2,1)}, bf16[5,2,32,1536]{3,2,0,1:T(8,128)(2,1)}, u32[]{:S(2)}, u32[]{:S(2)}) collective-permute-start(bf16[5,2,32,1536]{3,2,0,1:T(8,128)(2,1)} %copy_bitcast_fusion.2), channel_id=1, source_target_pairs={{0,4},{2,6},{4,0},{6,2},{1,5},{3,7},{5,1},{7,3},{8,12},{10,14},{12... | collective-permute-start | bytes 2949128 | tf_op jit(solution)/shard_map/ppermute | solution.py:187
  528.6 71.9 %collective-permute-start.41 = (bf16[2,5,32,1536]{3,2,1,0:T(8,128)(2,1)}, bf16[2,5,32,1536]{3,2,1,0:T(8,128)(2,1)}, u32[]{:S(2)}, u32[]{:S(2)}) collective-permute-start(bf16[2,5,32,1536]{3,2,1,0:T(8,128)(2,1)} %pad_maximum_fusion.7), channel_id=1, source_target_pairs={{0,2},{2,0},{4,6},{6,4},{1,3},{3,1},{5,7},{7,5},{8,10},{10,8},{12,... | collective-permute-start | bytes 2949128 | tf_op jit(solution)/shard_map/ppermute | solution.py:187
  531.3 23.2 %collective-permute-start.24 = (bf16[256,1024]{1,0:T(8,128)(2,1)S(1)}, bf16[256,1024]{1,0:T(8,128)(2,1)S(1)}, u32[]{:S(2)}, u32[]{:S(2)}) collective-permute-start(bf16[256,1024]{1,0:T(8,128)(2,1)S(1)} %pad_maximum_fusion.9), channel_id=1, source_target_pairs={{0,4},{2,6},{4,0},{6,2},{1,5},{3,7},{5,1},{7,3},{8,12},{10,14},{12... | collective-permute-start | bytes 1572872 | tf_op jit(solution)/shard_map/ppermute | solution.py:672
  532.0 24.8 %collective-permute-start.25 = (bf16[256,1024]{1,0:T(8,128)(2,1)S(1)}, bf16[256,1024]{1,0:T(8,128)(2,1)S(1)}, u32[]{:S(2)}, u32[]{:S(2)}) collective-permute-start(bf16[256,1024]{1,0:T(8,128)(2,1)S(1)} %pad_maximum_fusion.10), channel_id=1, source_target_pairs={{0,6},{2,0},{4,2},{6,4},{1,7},{3,1},{5,3},{7,5},{8,14},{10,8},{12,... | collective-permute-start | bytes 1572872 | tf_op jit(solution)/shard_map/ppermute | solution.py:672
  534.5 43.0 %collective-permute-start.31 = (bf16[4,48,768]{2,1,0:T(8,128)(2,1)}, bf16[4,48,768]{2,1,0:T(8,128)(2,1)}, u32[]{:S(2)}, u32[]{:S(2)}) collective-permute-start(bf16[4,48,768]{2,1,0:T(8,128)(2,1)} %dynamic-slice_bitcast_fusion.18), channel_id=1, source_target_pairs={{0,1},{1,0},{2,3},{3,2},{4,5},{5,4},{6,7},{7,6},{8,9},{9,8},{10,11... | collective-permute-start | bytes 884744 | tf_op jit(solution)/shard_map/ppermute | solution.py:187
  541.8 37.9 %collective-permute-start.32 = (bf16[4,48,768]{2,1,0:T(8,128)(2,1)}, bf16[4,48,768]{2,1,0:T(8,128)(2,1)}, u32[]{:S(2)}, u32[]{:S(2)}) collective-permute-start(bf16[4,48,768]{2,1,0:T(8,128)(2,1)} %dynamic-slice_bitcast_fusion.17), channel_id=1, source_target_pairs={{0,4},{2,6},{4,0},{6,2},{1,5},{3,7},{5,1},{7,3},{8,12},{10,14},{12... | collective-permute-start | bytes 884744 | tf_op jit(solution)/shard_map/ppermute | solution.py:187
  573.2 29.4 %collective-permute-start.26 = (bf16[4,2,2,48,2688]{4,3,2,1,0:T(8,128)(2,1)}, bf16[4,2,2,48,2688]{4,3,2,1,0:T(8,128)(2,1)S(1)}, u32[]{:S(2)}, u32[]{:S(2)}) collective-permute-start(bf16[4,2,2,48,2688]{4,3,2,1,0:T(8,128)(2,1)} %dynamic-slice_bitcast_fusion), channel_id=1, source_target_pairs={{0,2},{2,0},{4,6},{6,4},{1,3},{3,1},{5,7},{7,5},{8,10},{10,8},{12,... | collective-permute-start | bytes 12386312 | tf_op jit(solution)/shard_map/ppermute | solution.py:187
  576.3 19.1 %collective-permute-start.21 = (bf16[512,768]{1,0:T(8,128)(2,1)}, bf16[512,768]{1,0:T(8,128)(2,1)}, u32[]{:S(2)}, u32[]{:S(2)}) collective-permute-start(bf16[512,768]{1,0:T(8,128)(2,1)} %get-tuple-element.239), channel_id=1, source_target_pairs={{0,1},{1,0},{2,3},{3,2},{4,5},{5,4},{6,7},{7,6},{8,9},{9,8},{10,11... | collective-permute-start | bytes 2359304 | tf_op jit(solution)/shard_map/ppermute | solution.py:187
  577.5 18.8 %collective-permute-start.22 = (bf16[512,768]{1,0:T(8,128)(2,1)}, bf16[512,768]{1,0:T(8,128)(2,1)}, u32[]{:S(2)}, u32[]{:S(2)}) collective-permute-start(bf16[512,768]{1,0:T(8,128)(2,1)} %get-tuple-element.240), channel_id=1, source_target_pairs={{0,4},{2,6},{4,0},{6,2},{1,5},{3,7},{5,1},{7,3},{8,12},{10,14},{12... | collective-permute-start | bytes 2359304 | tf_op jit(solution)/shard_map/ppermute | solution.py:187
  607.7 22.0 %collective-permute-start.27 = (bf16[4,2,48,1280]{3,2,1,0:T(8,128)(2,1)S(1)}, bf16[4,2,48,1280]{3,2,1,0:T(8,128)(2,1)S(1)}, u32[]{:S(2)}, u32[]{:S(2)}) collective-permute-start(bf16[4,2,48,1280]{3,2,1,0:T(8,128)(2,1)S(1)} %dynamic-slice_bitcast_fusion.3), channel_id=1, source_target_pairs={{0,4},{2,6},{4,0},{6,2},{1,5},{3,7},{5,1},{7,3},{8,12},{10,14},{12... | collective-permute-start | bytes 2949128 | tf_op jit(solution)/shard_map/ppermute | solution.py:187
  610.3 23.6 %collective-permute-start.29 = (bf16[4,2,48,1408]{3,2,1,0:T(8,128)(2,1)S(1)}, bf16[4,2,48,1408]{3,2,1,0:T(8,128)(2,1)S(1)}, u32[]{:S(2)}, u32[]{:S(2)}) collective-permute-start(bf16[4,2,48,1408]{3,2,1,0:T(8,128)(2,1)S(1)} %dynamic-slice_bitcast_fusion.2), channel_id=1, source_target_pairs={{0,1},{1,0},{2,3},{3,2},{4,5},{5,4},{6,7},{7,6},{8,9},{9,8},{10,11... | collective-permute-start | bytes 3244040 | tf_op jit(solution)/shard_map/ppermute | solution.py:187
  613.5 49.2 %collective-permute-start.33 = (bf16[5,2,96,512]{3,2,0,1:T(8,128)(2,1)S(1)}, bf16[5,2,96,512]{3,2,0,1:T(8,128)(2,1)S(1)}, u32[]{:S(2)}, u32[]{:S(2)}) collective-permute-start(bf16[5,2,96,512]{3,2,0,1:T(8,128)(2,1)S(1)} %copy_bitcast_fusion.1), channel_id=1, source_target_pairs={{0,4},{2,6},{4,0},{6,2},{1,5},{3,7},{5,1},{7,3},{8,12},{10,14},{12... | collective-permute-start | bytes 2949128 | tf_op jit(solution)/shard_map/ppermute | solution.py:187
  634.3 28.1 %collective-permute-start.30 = (bf16[4,48,1408]{2,1,0:T(8,128)(2,1)S(1)}, bf16[4,48,1408]{2,1,0:T(8,128)(2,1)S(1)}, u32[]{:S(2)}, u32[]{:S(2)}) collective-permute-start(bf16[4,48,1408]{2,1,0:T(8,128)(2,1)S(1)} %dynamic-slice_bitcast_fusion.6), channel_id=1, source_target_pairs={{0,4},{2,6},{4,0},{6,2},{1,5},{3,7},{5,1},{7,3},{8,12},{10,14},{12... | collective-permute-start | bytes 1622024 | tf_op jit(solution)/shard_map/ppermute | solution.py:187
  667.6 34.1 %collective-permute-start.35 = (bf16[48,4224]{1,0:T(8,128)(2,1)S(1)}, bf16[48,4224]{1,0:T(8,128)(2,1)S(1)}, u32[]{:S(2)}, u32[]{:S(2)}) collective-permute-start(bf16[48,4224]{1,0:T(8,128)(2,1)S(1)} %get-tuple-element.257), channel_id=1, source_target_pairs={{0,16},{8,24},{16,0},{24,8},{1,17},{9,25},{17,1},{25,9},{2,18},{10... | collective-permute-start | bytes 1216520 | tf_op jit(solution)/shard_map/ppermute | solution.py:727
  668.2 35.9 %collective-permute-start.36 = (bf16[48,4224]{1,0:T(8,128)(2,1)S(1)}, bf16[48,4224]{1,0:T(8,128)(2,1)S(1)}, u32[]{:S(2)}, u32[]{:S(2)}) collective-permute-start(bf16[48,4224]{1,0:T(8,128)(2,1)S(1)} %get-tuple-element.256), channel_id=1, source_target_pairs={{0,24},{8,0},{16,8},{24,16},{1,25},{9,1},{17,9},{25,17},{2,26},{10... | collective-permute-start | bytes 1216520 | tf_op jit(solution)/shard_map/ppermute | solution.py:727
  670.1 34.2 %collective-permute-start.38 = (bf16[2,5,96,512]{3,2,1,0:T(8,128)(2,1)S(1)}, bf16[2,5,96,512]{3,2,1,0:T(8,128)(2,1)S(1)}, u32[]{:S(2)}, u32[]{:S(2)}) collective-permute-start(bf16[2,5,96,512]{3,2,1,0:T(8,128)(2,1)S(1)} %pad_maximum_fusion.5), channel_id=1, source_target_pairs={{0,2},{2,0},{4,6},{6,4},{1,3},{3,1},{5,7},{7,5},{8,10},{10,8},{12,... | collective-permute-start | bytes 2949128 | tf_op jit(solution)/shard_map/ppermute | solution.py:187
  671.7 35.9 %collective-permute-start.37 = (bf16[5,2,96,512]{3,2,0,1:T(8,128)(2,1)S(1)}, bf16[5,2,96,512]{3,2,0,1:T(8,128)(2,1)S(1)}, u32[]{:S(2)}, u32[]{:S(2)}) collective-permute-start(bf16[5,2,96,512]{3,2,0,1:T(8,128)(2,1)S(1)} %copy_bitcast_fusion), channel_id=1, source_target_pairs={{0,4},{2,6},{4,0},{6,2},{1,5},{3,7},{5,1},{7,3},{8,12},{10,14},{12... | collective-permute-start | bytes 2949128 | tf_op jit(solution)/shard_map/ppermute | solution.py:187
  (89 other events, 844.6 us)
Sparse Core Ops, SparseCore 0:
  39.6 75.8 all-gather.4
  117.3 71.9 all-gather.6
  251.4 135.7 reduce-scatter.3
  389.9 136.7 reduce-scatter.5
  528.9 136.7 reduce-scatter.7

commit v8 on v7

--- a/solution.py
+++ b/solution.py
@@ -65,32 +65,36 @@
     return jnp.concatenate(picks, axis=0)
 
 
-def dispatch_body(own, slots, codes_ref, rows_ref, out_ref):
+def dispatch_body(own, slots, codes_ref, *refs):
+    out_ref = refs[-1]
     pick = selection(codes_ref[0], own, slots)
-    moved = jnp.dot(pick, rows_ref[0], preferred_element_type=jnp.float32).astype(jnp.bfloat16)
-    for e in range(own):
-        out_ref[e] = moved[e * slots : (e + 1) * slots]
-
-
-def dispatch(codes, rows, own, slots):
-    blocks, _, width = rows.shape
+    at = 0
+    for rows_ref in refs[:-1]:
+        width = rows_ref.shape[2]
+        moved = jnp.dot(pick, rows_ref[0], preferred_element_type=jnp.float32).astype(jnp.bfloat16)
+        for e in range(own):
+            out_ref[e, :, at : at + width] = moved[e * slots : (e + 1) * slots]
+        at += width
+
+
+def dispatch(codes, parts, own, slots):
+    blocks = parts[0].shape[0]
     tokens = codes.shape[2]
+    widths = [part.shape[2] for part in parts]
     return pl.pallas_call(
         partial(dispatch_body, own, slots),
         grid=(blocks,),
-        in_specs=[
-            pl.BlockSpec((1, codes.shape[1], tokens), lambda b: (b, 0, 0)),
-            pl.BlockSpec((1, tokens, width), lambda b: (b, 0, 0)),
-        ],
-        out_specs=pl.BlockSpec((own, slots, width), lambda b: (0, b, 0)),
-        out_shape=jax.ShapeDtypeStruct((own, blocks * slots, width), jnp.bfloat16),
+        in_specs=[pl.BlockSpec((1, codes.shape[1], tokens), lambda b: (b, 0, 0))]
+        + [pl.BlockSpec((1, tokens, width), lambda b: (b, 0, 0)) for width in widths],
+        out_specs=pl.BlockSpec((own, slots, sum(widths)), lambda b: (0, b, 0)),
+        out_shape=jax.ShapeDtypeStruct((own, blocks * slots, sum(widths)), jnp.bfloat16),
         cost_estimate=pl.CostEstimate(
-            flops=2 * blocks * own * slots * tokens * width,
+            flops=2 * blocks * own * slots * tokens * sum(widths),
             transcendentals=0,
-            bytes_accessed=2 * blocks * (tokens + own * slots) * width,
+            bytes_accessed=2 * blocks * (tokens + own * slots) * sum(widths),
         ),
         name="dispatch",
-    )(codes, rows)
+    )(codes, *parts)
 
 
 def experts_body(at_ref, rows_ref, gate_up_ref, plain_ref, weight_ref, out_ref, both_ref, d_weight_ref):
@@ -797,8 +801,10 @@
     codes = slot_codes(routes, slot_order[0, 0], expert_total, capacity)
     upstream_low = jnp.concatenate([dy_prompt[0], dy_cont[0].reshape(cont_rows, model_width)], axis=0)
     upstream = upstream_low.astype(jnp.float32)
+    first_width = model_width // 384 * 128
+    upstream_first = lax.all_gather(upstream_low[:, :first_width], group, axis=0, tiled=False)
     assert capacity <= 256
-    fold = model_width // count_of_tokens
+    fold = (model_width - first_width) // count_of_tokens
     code_rows = -(-expert_total // (8 * fold)) * 8
     code_table = jnp.pad(
         codes.astype(jnp.bfloat16),
@@ -835,8 +841,10 @@
     prompt_kv, q_lin = gather_keys(
         near_kv, jnp.dot(h1_late, w_query, preferred_element_type=jnp.float32)
     )
-    travel = jnp.concatenate([upstream_low, code_table], axis=0)
-    prompt_kv, travel = lax.optimization_barrier((prompt_kv, travel))
+    travel = jnp.concatenate([upstream_low[:, first_width:], code_table], axis=0)
+    prompt_kv, travel, upstream_first = lax.optimization_barrier(
+        (prompt_kv, travel, upstream_first)
+    )
     upstream_all = lax.all_gather(travel, group, axis=0, tiled=False)
     codes_all = upstream_all[:, count_of_tokens:]
     codes_all = jnp.concatenate(
@@ -847,7 +855,7 @@
     ).astype(jnp.float32)
     own_codes = lax.dynamic_slice_in_dim(codes_all, first_expert, own, axis=1)
     own_codes = jnp.pad(own_codes, ((0, 0), (0, -own % 8), (0, 0)), constant_values=-2.0)
-    d_slot_rows = dispatch(own_codes, upstream_all, own, slots)
+    d_slot_rows = dispatch(own_codes, (upstream_first, upstream_all), own, slots)
     d_plain = jnp.einsum("ecd,efd->ecf", d_slot_rows, down_own, preferred_element_type=jnp.float32)
     query_row_block, merged_low, log_total = attend_forward(
         q_lin, prompt_kv, cont_kv, cosine, sine, start, prompt_rows, cont_len
@@ -865,7 +873,7 @@
     own_gates, rows_all, d_plain = lax.optimization_barrier(
         (gather_gates(gates, group, first_expert, own), rows_all, d_plain)
     )
-    slot_rows = dispatch(own_codes, rows_all, own, slots)
+    slot_rows = dispatch(own_codes, (rows_all,), own, slots)
     slot_index = jnp.arange(slots, dtype=jnp.int32).astype(jnp.float32)
     picked = own_codes[:, :own, None, :] == slot_index[None, None, :, None]
     slot_gate = jnp.sum(jnp.where(picked, own_gates[:, :, None, :], 0.0), axis=-1)

time: 741 us -> 737 us (level)
    all_gather x1, waiting for transfers between devices: 43.2 us -> 32.1 us  [per_device(): rows_all = lax.all_gather(h2_low, group, axis=0, tiled=False)]
  transfers between devices with their start and end apart: 47 -> 48, of which waited for: 27 -> 26; matrix products, arithmetic and copies ran while one was open for 31% -> 32% of each run, Pallas kernels for 23% -> 24%
where the time goes in v8:
time: 737 us; the launch traced here: 727 us
  Pallas kernels  220 us (30%)
  waiting for transfers between devices  186 us (25%)
  matrix products  139 us (19%)
  other arithmetic  71.7 us (10%)
  local copies, waits for them, and re-layouts  54.1 us (7%)
  starting transfers between devices  39.4 us (5%)
  between operations  16 us (2%)
    ppermute x36, waiting for transfers between devices, swap(): return lax.ppermute(values, axis, [(i, i ^ bit) for i in range(size)])  95.8 us
    pallas_call x1, Pallas kernels, attend_backward(): pl.pallas_call(partial(attend_backward_body, group, rows, cont_len, chunk...  64.1 us
    pallas_call x1, Pallas kernels, attend_forward(): pl.pallas_call(partial(attend_forward_body, group, rows, cont_len), grid_...  50.4 us
    pallas_call x4, Pallas kernels, combine(): pl.pallas_call(partial(combine_body, own, slots), grid_spec=pltpu.Prefetc...  41.7 us
    ppermute x36, starting transfers between devices, swap(): return lax.ppermute(values, axis, [(i, i ^ bit) for i in range(size)])  34.2 us
    all_gather x1, waiting for transfers between devices, per_device(): rows_all = lax.all_gather(h2_low, group, axis=0, tiled=False)  32.1 us
    ppermute x3, waiting for transfers between devices, scatter_parts(): lax.ppermute(take(parts, (here + hop) % size), 'dp', [(i, (i + hop) % siz...  31 us
    dot_general x2, matrix products, expert_gradient(): jnp.einsum('ecd,ecf->edf', slot_rows, d_part, preferred_element_type=jnp....  29.3 us
  transfers between devices with their start and end apart: 48, of which 26 were waited for; matrix products, arithmetic and copies ran while one was open for 32% of the time, Pallas kernels for 24%

profile of v8, /device:TPU:9, one launch (start us, length us, event | category | flops | bytes accessed | tf_op | source)
XLA Modules:
  0.0 727.2 jit_solution(818631215076340749)
XLA Ops:
  14.4 6.9 project_keys.1
  26.4 6.7 fusion.110.q_ref
  33.1 5.7 collective-permute-done
  46.0 5.8 all-gather.7.cloned.1.call-done
  52.0 50.4 %attend_forward.1 = (bf16[512,1536]{1,0:T(8,128)(2,1)}, bf16[512,1536]{1,0:T(8,128)(2,1)}, f32[24,8,512]{2,1,0:T(8,128)}) custom-call(s32[1]{0:T(128)} %bitcast.2.pos_ref, f32[512,1536]{1,0:T(8,128)} %fusion.110.q_ref, f32[512,128]{1,0:T(8,128)} %get-tuple-element.302.cos_ref, f32[512,128]{1,0:T(8,128)} %get-tuple-element.301.sin_ref, ...), custom_call_target="tpu_custom_call" | custom-call | flops 8053063680 | bytes 6291456 | tf_op jit(solution)/shard_map/attend_forward/pallas_call | solution.py:434
  102.4 5.2 multiply_reduce_fusion.2
  123.9 14.2 %dispatch.2 = bf16[5,832,1536]{2,1,0:T(8,128)(2,1)} custom-call(f32[8,8,512]{2,1,0:T(8,128)} %pad.14.codes_ref, bf16[8,512,512]{2,1,0:T(8,128)(2,1)} %bitcast.328, bf16[8,536,1024]{2,1,0:T(8,128)(2,1)} %bitcast.306), custom_call_target="tpu_custom_call" | custom-call | flops 6543114240 | bytes 25362432 | tf_op jit(solution)/shard_map/dispatch/pallas_call | solution.py:84
  138.1 14.1 %fusion.9.plain_ref = f32[5,832,512]{2,1,0:T(8,128)} fusion(bf16[5,832,1536]{2,1,0:T(8,128)(2,1)} %dispatch.2, bf16[20,512,1536]{2,1,0:T(8,128)(2,1)} %param.30, s32[]{:T(128)S(6)} %select_n.409), kind=kOutput, calls=%fused_computation.14 | convolution fusion | flops 6543114240 | bytes 29163524 | tf_op jit(solution)/shard_map/ecd,efd->ecf/dot_general | solution.py:859
  152.2 32.1 %all-gather.11.cloned.1.call-done = bf16[4096,1536]{1,0:T(8,128)(2,1)} async-done(((bf16[512,1536]{1,0:T(8,128)(2,1)}), bf16[4096,1536]{1,0:T(8,128)(2,1)}) %all-gather.11.cloned.1.call-update) | async-done | bytes 12582928 | tf_op jit(solution)/shard_map/all_gather | solution.py:867
  187.4 14.1 %dispatch.3.rows_ref = bf16[5,832,1536]{2,1,0:T(8,128)(2,1)} custom-call(f32[8,8,512]{2,1,0:T(8,128)} %pad.14.codes_ref, bf16[8,512,1536]{2,1,0:T(8,128)(2,1)} %bitcast.304), custom_call_target="tpu_custom_call" | custom-call | flops 6543114240 | bytes 25362432 | tf_op jit(solution)/shard_map/dispatch/pallas_call | solution.py:84
  201.5 29.0 %experts.1 = (bf16[5,832,512]{2,1,0:T(8,128)(2,1)}, bf16[5,832,1024]{2,1,0:T(8,128)(2,1)}, f32[5,832,1]{2,1,0:T(8,128)}) custom-call(s32[1]{0:T(128)} %bitcast.11.at_ref, bf16[5,832,1536]{2,1,0:T(8,128)(2,1)} %dispatch.3.rows_ref, bf16[20,1536,1024]{2,1,0:T(8,128)(2,1)} %gate_up_ref.1, f32[5,832,512]{2,1,0:T(8,128)} %fusion.9.plain_ref, ...), custom_call_target="tpu_custom_call" | custom-call | flops 13086228480 | bytes 45547520 | tf_op jit(solution)/shard_map/experts/pallas_call | solution.py:125
  230.5 15.8 %convolution_convert_fusion.5 = bf16[5,512,1536]{2,1,0:T(8,128)(2,1)} fusion(bf16[5,832,512]{2,1,0:T(8,128)(2,1)} %get-tuple-element.98, bf16[5,832,1536]{2,1,0:T(8,128)(2,1)} %dispatch.2), kind=kOutput, calls=%fused_computation.18 | convolution fusion | flops 6547046400 | bytes 24903680 | tf_op jit(solution)/shard_map/ecf,ecd->efd/dot_general | solution.py:885
  257.1 20.9 %fusion.2.rows_ref = bf16[5,832,1536]{2,1,0:T(8,128)(2,1)} fusion(bf16[5,832,1024]{2,1,0:T(8,128)(2,1)} %get-tuple-element.92, bf16[20,1536,1024]{2,1,0:T(8,128)(2,1)} %gate_up_ref.1, s32[]{:T(128)S(6)} %select_n.409), kind=kOutput, calls=%fused_computation.3 | convolution fusion | flops 13092618240 | bytes 37027844 | tf_op jit(solution)/shard_map/ecf,edf->ecd/dot_general | solution.py:901
  278.0 9.7 %combine.4 = bf16[4,512,1536]{2,1,0:T(8,128)(2,1)} custom-call(s32[4]{0:T(128)} %get-tuple-element.311.at_ref, f32[8,8,512]{2,1,0:T(8,128)} %pad.14.codes_ref, bf16[5,832,1536]{2,1,0:T(8,128)(2,1)} %fusion.2.rows_ref), custom_call_target="tpu_custom_call" | custom-call | flops 1 | bytes 1 | tf_op jit(solution)/shard_map/combine/pallas_call | solution.py:171
  288.7 14.7 %convolution_convert_fusion.4 = bf16[5,1536,512]{2,1,0:T(8,128)(2,1)} fusion(bf16[5,832,1536]{2,1,0:T(8,128)(2,1)} %dispatch.3.rows_ref, bf16[5,832,1024]{2,1,0:T(8,128)(2,1)} %get-tuple-element.92), kind=kOutput, calls=%fused_computation.17 | convolution fusion | flops 6547046400 | bytes 24903680 | tf_op jit(solution)/shard_map/ecd,ecf->edf/dot_general | solution.py:910
  303.4 11.4 %combine.5 = bf16[4,512,1536]{2,1,0:T(8,128)(2,1)} custom-call(s32[4]{0:T(128)} %get-tuple-element.312.at_ref, f32[8,8,512]{2,1,0:T(8,128)} %pad.14.codes_ref, bf16[5,832,1536]{2,1,0:T(8,128)(2,1)} %fusion.2.rows_ref, bf16[4,512,1536]{2,1,0:T(8,128)(2,1)} %collective-permute-done.9.refs_0_), custom_call_target="tpu_custom_call" | custom-call | flops 1 | bytes 1 | tf_op jit(solution)/shard_map/combine/pallas_call | solution.py:171
  314.8 13.7 %convolution_convert_fusion.rows_ref = bf16[5,832,1536]{2,1,0:T(8,128)(2,1)} fusion(bf16[5,832,512]{2,1,0:T(8,128)(2,1)} %get-tuple-element.98, bf16[20,512,1536]{2,1,0:T(8,128)(2,1)} %param.30, s32[]{:T(128)S(6)} %select_n.409), kind=kOutput, calls=%fused_computation.2 | convolution fusion | flops 6549504000 | bytes 24903684 | tf_op jit(solution)/shard_map/ecf,efd->ecd/dot_general | solution.py:922
  328.5 9.7 %combine.6 = bf16[4,512,1536]{2,1,0:T(8,128)(2,1)} custom-call(s32[4]{0:T(128)} %get-tuple-element.311.at_ref, f32[8,8,512]{2,1,0:T(8,128)} %pad.14.codes_ref, bf16[5,832,1536]{2,1,0:T(8,128)(2,1)} %convolution_convert_fusion.rows_ref), custom_call_target="tpu_custom_call" | custom-call | flops 1 | bytes 1 | tf_op jit(solution)/shard_map/combine/pallas_call | solution.py:171
  343.2 14.6 %convolution_convert_fusion.3 = bf16[5,1536,512]{2,1,0:T(8,128)(2,1)} fusion(bf16[5,832,1536]{2,1,0:T(8,128)(2,1)} %dispatch.3.rows_ref, bf16[5,832,1024]{2,1,0:T(8,128)(2,1)} %get-tuple-element.92), kind=kOutput, calls=%fused_computation.16 | convolution fusion | flops 6547046400 | bytes 24903680 | tf_op jit(solution)/shard_map/ecd,ecf->edf/dot_general | solution.py:910
  357.7 19.2 %collective-permute-done.11 = bf16[2,512,768]{2,1,0:T(8,128)(2,1)} collective-permute-done((bf16[2,512,768]{2,1,0:T(8,128)(2,1)S(1)}, bf16[2,512,768]{2,1,0:T(8,128)(2,1)}, u32[]{:S(2)}, u32[]{:S(2)}) %collective-permute-start.11) | collective-permute-done | bytes 1572896 | tf_op jit(solution)/shard_map/ppermute | solution.py:191
  382.1 11.0 %combine.7 = bf16[4,512,1536]{2,1,0:T(8,128)(2,1)} custom-call(s32[4]{0:T(128)} %get-tuple-element.312.at_ref, f32[8,8,512]{2,1,0:T(8,128)} %pad.14.codes_ref, bf16[5,832,1536]{2,1,0:T(8,128)(2,1)} %convolution_convert_fusion.rows_ref, bf16[4,512,1536]{2,1,0:T(8,128)(2,1)} %collective-permute-done.12.refs_0_), custom_call_target="tpu_custom_call" | custom-call | flops 1 | bytes 1 | tf_op jit(solution)/shard_map/combine/pallas_call | solution.py:171
  393.1 5.3 collective-permute-done.13
  420.4 7.1 convolution_convert_fusion.8.do_ref
  427.5 4.5 fusion.15
  444.1 64.1 %attend_backward.1 = (bf16[512,1536]{1,0:T(8,128)(2,1)}, bf16[1024,512]{1,0:T(8,128)(2,1)}, bf16[1024,512]{1,0:T(8,128)(2,1)}, bf16[256,512]{1,0:T(8,128)(2,1)}, bf16[256,512]{1,0:T(8,128)(2,1)}) custom-call(s32[1]{0:T(128)} %bitcast.2.pos_ref, bf16[512,1536]{1,0:T(8,128)(2,1)} %get-tuple-element.113.q_ref, ...), custom_call_target="tpu_custom_call" | custom-call | flops 20132659200 | bytes 6291456 | tf_op jit(solution)/shard_map/attend_backward/pallas_call | solution.py:565
  508.2 5.3 fusion.111
  537.7 12.1 %collective-permute-done.24 = bf16[256,1024]{1,0:T(8,128)(2,1)S(1)} collective-permute-done((bf16[256,1024]{1,0:T(8,128)(2,1)S(1)}, bf16[256,1024]{1,0:T(8,128)(2,1)S(1)}, u32[]{:S(2)}, u32[]{:S(2)}) %collective-permute-start.24) | collective-permute-done | bytes 524320 | tf_op jit(solution)/shard_map/ppermute | solution.py:676
  581.3 9.4 %collective-permute-done.21 = bf16[512,768]{1,0:T(8,128)(2,1)} collective-permute-done((bf16[512,768]{1,0:T(8,128)(2,1)}, bf16[512,768]{1,0:T(8,128)(2,1)}, u32[]{:S(2)}, u32[]{:S(2)}) %collective-permute-start.21) | collective-permute-done | bytes 786464 | tf_op jit(solution)/shard_map/ppermute | solution.py:191
  609.4 15.6 %collective-permute-done.27 = bf16[4,2,48,1280]{3,2,1,0:T(8,128)(2,1)S(1)} collective-permute-done((bf16[4,2,48,1280]{3,2,1,0:T(8,128)(2,1)S(1)}, bf16[4,2,48,1280]{3,2,1,0:T(8,128)(2,1)S(1)}, u32[]{:S(2)}, u32[]{:S(2)}) %collective-permute-start.27) | collective-permute-done | bytes 983072 | tf_op jit(solution)/shard_map/ppermute | solution.py:191
  639.8 17.8 %collective-permute-done.30 = bf16[4,48,1408]{2,1,0:T(8,128)(2,1)S(1)} collective-permute-done((bf16[4,48,1408]{2,1,0:T(8,128)(2,1)S(1)}, bf16[4,48,1408]{2,1,0:T(8,128)(2,1)S(1)}, u32[]{:S(2)}, u32[]{:S(2)}) %collective-permute-start.30) | collective-permute-done | bytes 540704 | tf_op jit(solution)/shard_map/ppermute | solution.py:191
  671.2 25.6 %collective-permute-done.35 = bf16[48,4224]{1,0:T(8,128)(2,1)S(1)} collective-permute-done((bf16[48,4224]{1,0:T(8,128)(2,1)S(1)}, bf16[48,4224]{1,0:T(8,128)(2,1)S(1)}, u32[]{:S(2)}, u32[]{:S(2)}) %collective-permute-start.35) | collective-permute-done | bytes 405536 | tf_op jit(solution)/shard_map/ppermute | solution.py:731
  706.0 7.1 collective-permute-done.39
  (407 shorter events, 212.5 us)
Async XLA Ops:
  7.2 44.6 %all-gather.7.cloned.1.call-start = ((), (), s32[]{:S(2)}) async-start(), calls=%async_computation.6 | async-start | bytes 4718592 | tf_op jit(solution)/shard_map/all_gather | solution.py:805
  9.3 112.7 %all-gather.9.cloned.1.call-start = ((), (), s32[]{:S(2)}) async-start(), calls=%async_computation.7 | async-start | bytes 9879552 | tf_op jit(solution)/shard_map/all_gather | solution.py:848
  51.9 132.5 %all-gather.11.cloned.1.call-start = ((), (), s32[]{:S(2)}) async-start(), calls=%async_computation.8 | async-start | bytes 14155776 | tf_op jit(solution)/shard_map/all_gather | solution.py:867
  110.9 321.1 %reduce-scatter.4.cloned.1.call-start = ((), (), s32[]{:S(2)}) async-start(), calls=%async_computation.3 | async-start | bytes 9830400 | tf_op jit(solution)/shard_map/reduce_scatter | solution.py:617
  246.3 354.7 %reduce-scatter.6.cloned.1.call-start = ((), (), s32[]{:S(2)}) async-start(), calls=%async_computation.4 | async-start | bytes 9830400 | tf_op jit(solution)/shard_map/reduce_scatter | solution.py:617
  256.3 31.4 %collective-permute-start.8 = (f32[2,2,5,512]{3,1,2,0:T(2,128)S(1)}, f32[2,2,5,512]{3,1,2,0:T(2,128)S(1)}, u32[]{:S(2)}, u32[]{:S(2)}) collective-permute-start(f32[2,2,5,512]{3,1,2,0:T(2,128)S(1)} %bitcast.347), channel_id=1, source_target_pairs={{0,1},{1,0},{2,3},{3,2},{4,5},{5,4},{6,7},{7,6},{8,9},{9,8},{10,11... | collective-permute-start | bytes 122888 | tf_op jit(solution)/shard_map/ppermute | solution.py:191
  303.4 357.4 %reduce-scatter.8.cloned.1.call-start = ((), (), s32[]{:S(2)}) async-start(), calls=%async_computation.5 | async-start | bytes 9830400 | tf_op jit(solution)/shard_map/reduce_scatter | solution.py:617
  338.2 39.1 %collective-permute-start.12 = (bf16[4,512,1536]{2,1,0:T(8,128)(2,1)}, bf16[4,512,1536]{2,1,0:T(8,128)(2,1)}, u32[]{:S(2)}, u32[]{:S(2)}) collective-permute-start(bf16[4,512,1536]{2,1,0:T(8,128)(2,1)} %combine.6), channel_id=1, source_target_pairs={{0,2},{2,0},{4,6},{6,4},{1,3},{3,1},{5,7},{7,5},{8,10},{10,8},{12,... | collective-permute-start | bytes 18874376 | tf_op jit(solution)/shard_map/ppermute | solution.py:191
  341.3 35.6 %collective-permute-start.11 = (bf16[2,512,768]{2,1,0:T(8,128)(2,1)S(1)}, bf16[2,512,768]{2,1,0:T(8,128)(2,1)}, u32[]{:S(2)}, u32[]{:S(2)}) collective-permute-start(bf16[2,512,768]{2,1,0:T(8,128)(2,1)S(1)} %pad_maximum_fusion.4), channel_id=1, source_target_pairs={{0,1},{1,0},{2,3},{3,2},{4,5},{5,4},{6,7},{7,6},{8,9},{9,8},{10,11... | collective-permute-start | bytes 4718600 | tf_op jit(solution)/shard_map/ppermute | solution.py:191
  342.1 35.2 %collective-permute-start.10 = (bf16[2,512,768]{2,1,0:T(8,128)(2,1)S(1)}, bf16[2,512,768]{2,1,0:T(8,128)(2,1)}, u32[]{:S(2)}, u32[]{:S(2)}) collective-permute-start(bf16[2,512,768]{2,1,0:T(8,128)(2,1)S(1)} %slice.192), channel_id=1, source_target_pairs={{0,4},{2,6},{4,0},{6,2},{1,5},{3,7},{5,1},{7,3},{8,12},{10,14},{12... | collective-permute-start | bytes 4718600 | tf_op jit(solution)/shard_map/ppermute | solution.py:191
  380.7 17.7 %collective-permute-start.13 = (bf16[512,768]{1,0:T(8,128)(2,1)}, bf16[512,768]{1,0:T(8,128)(2,1)}, u32[]{:S(2)}, u32[]{:S(2)}) collective-permute-start(bf16[512,768]{1,0:T(8,128)(2,1)} %get-tuple-element.247), channel_id=1, source_target_pairs={{0,1},{1,0},{2,3},{3,2},{4,5},{5,4},{6,7},{7,6},{8,9},{9,8},{10,11... | collective-permute-start | bytes 2359304 | tf_op jit(solution)/shard_map/ppermute | solution.py:191
  437.6 84.1 %collective-permute-start.17 = (bf16[2,512,768]{2,1,0:T(8,128)(2,1)}, bf16[2,512,768]{2,1,0:T(8,128)(2,1)}, u32[]{:S(2)}, u32[]{:S(2)}) collective-permute-start(bf16[2,512,768]{2,1,0:T(8,128)(2,1)} %pad_maximum_fusion.5), channel_id=1, source_target_pairs={{0,1},{1,0},{2,3},{3,2},{4,5},{5,4},{6,7},{7,6},{8,9},{9,8},{10,11... | collective-permute-start | bytes 4718600 | tf_op jit(solution)/shard_map/ppermute | solution.py:191
  439.4 82.3 %collective-permute-start.18 = (bf16[4,2,48,768]{3,2,1,0:T(8,128)(2,1)}, bf16[4,2,48,768]{3,2,1,0:T(8,128)(2,1)}, u32[]{:S(2)}, u32[]{:S(2)}) collective-permute-start(bf16[4,2,48,768]{3,2,1,0:T(8,128)(2,1)} %dynamic-slice_bitcast_fusion.5), channel_id=1, source_target_pairs={{0,4},{2,6},{4,0},{6,2},{1,5},{3,7},{5,1},{7,3},{8,12},{10,14},{12... | collective-permute-start | bytes 1769480 | tf_op jit(solution)/shard_map/ppermute | solution.py:191
  441.3 80.3 %collective-permute-start.19 = (bf16[4,2,48,768]{3,2,1,0:T(8,128)(2,1)}, bf16[4,2,48,768]{3,2,1,0:T(8,128)(2,1)}, u32[]{:S(2)}, u32[]{:S(2)}) collective-permute-start(bf16[4,2,48,768]{3,2,1,0:T(8,128)(2,1)} %dynamic-slice_bitcast_fusion.4), channel_id=1, source_target_pairs={{0,1},{1,0},{2,3},{3,2},{4,5},{5,4},{6,7},{7,6},{8,9},{9,8},{10,11... | collective-permute-start | bytes 1769480 | tf_op jit(solution)/shard_map/ppermute | solution.py:191
  441.6 80.1 %collective-permute-start.16 = (bf16[2,512,768]{2,1,0:T(8,128)(2,1)}, bf16[2,512,768]{2,1,0:T(8,128)(2,1)}, u32[]{:S(2)}, u32[]{:S(2)}) collective-permute-start(bf16[2,512,768]{2,1,0:T(8,128)(2,1)} %slice.204), channel_id=1, source_target_pairs={{0,4},{2,6},{4,0},{6,2},{1,5},{3,7},{5,1},{7,3},{8,12},{10,14},{12... | collective-permute-start | bytes 4718600 | tf_op jit(solution)/shard_map/ppermute | solution.py:191
  443.7 78.0 %collective-permute-start.20 = (bf16[5,2,32,1536]{3,2,0,1:T(8,128)(2,1)}, bf16[5,2,32,1536]{3,2,0,1:T(8,128)(2,1)}, u32[]{:S(2)}, u32[]{:S(2)}) collective-permute-start(bf16[5,2,32,1536]{3,2,0,1:T(8,128)(2,1)} %copy_bitcast_fusion.2), channel_id=1, source_target_pairs={{0,4},{2,6},{4,0},{6,2},{1,5},{3,7},{5,1},{7,3},{8,12},{10,14},{12... | collective-permute-start | bytes 2949128 | tf_op jit(solution)/shard_map/ppermute | solution.py:191
  523.9 71.9 %collective-permute-start.41 = (bf16[2,5,32,1536]{3,2,1,0:T(8,128)(2,1)}, bf16[2,5,32,1536]{3,2,1,0:T(8,128)(2,1)}, u32[]{:S(2)}, u32[]{:S(2)}) collective-permute-start(bf16[2,5,32,1536]{3,2,1,0:T(8,128)(2,1)} %pad_maximum_fusion.8), channel_id=1, source_target_pairs={{0,2},{2,0},{4,6},{6,4},{1,3},{3,1},{5,7},{7,5},{8,10},{10,8},{12,... | collective-permute-start | bytes 2949128 | tf_op jit(solution)/shard_map/ppermute | solution.py:191
  526.6 23.1 %collective-permute-start.24 = (bf16[256,1024]{1,0:T(8,128)(2,1)S(1)}, bf16[256,1024]{1,0:T(8,128)(2,1)S(1)}, u32[]{:S(2)}, u32[]{:S(2)}) collective-permute-start(bf16[256,1024]{1,0:T(8,128)(2,1)S(1)} %pad_maximum_fusion.10), channel_id=1, source_target_pairs={{0,4},{2,6},{4,0},{6,2},{1,5},{3,7},{5,1},{7,3},{8,12},{10,14},{12... | collective-permute-start | bytes 1572872 | tf_op jit(solution)/shard_map/ppermute | solution.py:676
  527.3 24.8 %collective-permute-start.25 = (bf16[256,1024]{1,0:T(8,128)(2,1)S(1)}, bf16[256,1024]{1,0:T(8,128)(2,1)S(1)}, u32[]{:S(2)}, u32[]{:S(2)}) collective-permute-start(bf16[256,1024]{1,0:T(8,128)(2,1)S(1)} %pad_maximum_fusion.11), channel_id=1, source_target_pairs={{0,6},{2,0},{4,2},{6,4},{1,7},{3,1},{5,3},{7,5},{8,14},{10,8},{12,... | collective-permute-start | bytes 1572872 | tf_op jit(solution)/shard_map/ppermute | solution.py:676
  529.8 43.0 %collective-permute-start.31 = (bf16[4,48,768]{2,1,0:T(8,128)(2,1)}, bf16[4,48,768]{2,1,0:T(8,128)(2,1)}, u32[]{:S(2)}, u32[]{:S(2)}) collective-permute-start(bf16[4,48,768]{2,1,0:T(8,128)(2,1)} %dynamic-slice_bitcast_fusion.18), channel_id=1, source_target_pairs={{0,1},{1,0},{2,3},{3,2},{4,5},{5,4},{6,7},{7,6},{8,9},{9,8},{10,11... | collective-permute-start | bytes 884744 | tf_op jit(solution)/shard_map/ppermute | solution.py:191
  537.1 37.9 %collective-permute-start.32 = (bf16[4,48,768]{2,1,0:T(8,128)(2,1)}, bf16[4,48,768]{2,1,0:T(8,128)(2,1)}, u32[]{:S(2)}, u32[]{:S(2)}) collective-permute-start(bf16[4,48,768]{2,1,0:T(8,128)(2,1)} %dynamic-slice_bitcast_fusion.17), channel_id=1, source_target_pairs={{0,4},{2,6},{4,0},{6,2},{1,5},{3,7},{5,1},{7,3},{8,12},{10,14},{12... | collective-permute-start | bytes 884744 | tf_op jit(solution)/shard_map/ppermute | solution.py:191
  568.5 29.4 %collective-permute-start.26 = (bf16[4,2,2,48,2688]{4,3,2,1,0:T(8,128)(2,1)}, bf16[4,2,2,48,2688]{4,3,2,1,0:T(8,128)(2,1)S(1)}, u32[]{:S(2)}, u32[]{:S(2)}) collective-permute-start(bf16[4,2,2,48,2688]{4,3,2,1,0:T(8,128)(2,1)} %dynamic-slice_bitcast_fusion), channel_id=1, source_target_pairs={{0,2},{2,0},{4,6},{6,4},{1,3},{3,1},{5,7},{7,5},{8,10},{10,8},{12,... | collective-permute-start | bytes 12386312 | tf_op jit(solution)/shard_map/ppermute | solution.py:191
  571.6 19.1 %collective-permute-start.21 = (bf16[512,768]{1,0:T(8,128)(2,1)}, bf16[512,768]{1,0:T(8,128)(2,1)}, u32[]{:S(2)}, u32[]{:S(2)}) collective-permute-start(bf16[512,768]{1,0:T(8,128)(2,1)} %get-tuple-element.240), channel_id=1, source_target_pairs={{0,1},{1,0},{2,3},{3,2},{4,5},{5,4},{6,7},{7,6},{8,9},{9,8},{10,11... | collective-permute-start | bytes 2359304 | tf_op jit(solution)/shard_map/ppermute | solution.py:191
  572.8 18.8 %collective-permute-start.22 = (bf16[512,768]{1,0:T(8,128)(2,1)}, bf16[512,768]{1,0:T(8,128)(2,1)}, u32[]{:S(2)}, u32[]{:S(2)}) collective-permute-start(bf16[512,768]{1,0:T(8,128)(2,1)} %get-tuple-element.241), channel_id=1, source_target_pairs={{0,4},{2,6},{4,0},{6,2},{1,5},{3,7},{5,1},{7,3},{8,12},{10,14},{12... | collective-permute-start | bytes 2359304 | tf_op jit(solution)/shard_map/ppermute | solution.py:191
  602.9 22.0 %collective-permute-start.27 = (bf16[4,2,48,1280]{3,2,1,0:T(8,128)(2,1)S(1)}, bf16[4,2,48,1280]{3,2,1,0:T(8,128)(2,1)S(1)}, u32[]{:S(2)}, u32[]{:S(2)}) collective-permute-start(bf16[4,2,48,1280]{3,2,1,0:T(8,128)(2,1)S(1)} %dynamic-slice_bitcast_fusion.3), channel_id=1, source_target_pairs={{0,4},{2,6},{4,0},{6,2},{1,5},{3,7},{5,1},{7,3},{8,12},{10,14},{12... | collective-permute-start | bytes 2949128 | tf_op jit(solution)/shard_map/ppermute | solution.py:191
  605.5 23.6 %collective-permute-start.29 = (bf16[4,2,48,1408]{3,2,1,0:T(8,128)(2,1)S(1)}, bf16[4,2,48,1408]{3,2,1,0:T(8,128)(2,1)S(1)}, u32[]{:S(2)}, u32[]{:S(2)}) collective-permute-start(bf16[4,2,48,1408]{3,2,1,0:T(8,128)(2,1)S(1)} %dynamic-slice_bitcast_fusion.2), channel_id=1, source_target_pairs={{0,1},{1,0},{2,3},{3,2},{4,5},{5,4},{6,7},{7,6},{8,9},{9,8},{10,11... | collective-permute-start | bytes 3244040 | tf_op jit(solution)/shard_map/ppermute | solution.py:191
  608.8 49.1 %collective-permute-start.33 = (bf16[5,2,96,512]{3,2,0,1:T(8,128)(2,1)S(1)}, bf16[5,2,96,512]{3,2,0,1:T(8,128)(2,1)S(1)}, u32[]{:S(2)}, u32[]{:S(2)}) collective-permute-start(bf16[5,2,96,512]{3,2,0,1:T(8,128)(2,1)S(1)} %copy_bitcast_fusion.1), channel_id=1, source_target_pairs={{0,4},{2,6},{4,0},{6,2},{1,5},{3,7},{5,1},{7,3},{8,12},{10,14},{12... | collective-permute-start | bytes 2949128 | tf_op jit(solution)/shard_map/ppermute | solution.py:191
  629.5 28.1 %collective-permute-start.30 = (bf16[4,48,1408]{2,1,0:T(8,128)(2,1)S(1)}, bf16[4,48,1408]{2,1,0:T(8,128)(2,1)S(1)}, u32[]{:S(2)}, u32[]{:S(2)}) collective-permute-start(bf16[4,48,1408]{2,1,0:T(8,128)(2,1)S(1)} %dynamic-slice_bitcast_fusion.6), channel_id=1, source_target_pairs={{0,4},{2,6},{4,0},{6,2},{1,5},{3,7},{5,1},{7,3},{8,12},{10,14},{12... | collective-permute-start | bytes 1622024 | tf_op jit(solution)/shard_map/ppermute | solution.py:191
  662.7 34.1 %collective-permute-start.35 = (bf16[48,4224]{1,0:T(8,128)(2,1)S(1)}, bf16[48,4224]{1,0:T(8,128)(2,1)S(1)}, u32[]{:S(2)}, u32[]{:S(2)}) collective-permute-start(bf16[48,4224]{1,0:T(8,128)(2,1)S(1)} %get-tuple-element.258), channel_id=1, source_target_pairs={{0,16},{8,24},{16,0},{24,8},{1,17},{9,25},{17,1},{25,9},{2,18},{10... | collective-permute-start | bytes 1216520 | tf_op jit(solution)/shard_map/ppermute | solution.py:731
  663.3 35.9 %collective-permute-start.36 = (bf16[48,4224]{1,0:T(8,128)(2,1)S(1)}, bf16[48,4224]{1,0:T(8,128)(2,1)S(1)}, u32[]{:S(2)}, u32[]{:S(2)}) collective-permute-start(bf16[48,4224]{1,0:T(8,128)(2,1)S(1)} %get-tuple-element.257), channel_id=1, source_target_pairs={{0,24},{8,0},{16,8},{24,16},{1,25},{9,1},{17,9},{25,17},{2,26},{10... | collective-permute-start | bytes 1216520 | tf_op jit(solution)/shard_map/ppermute | solution.py:731
  665.2 34.2 %collective-permute-start.38 = (bf16[2,5,96,512]{3,2,1,0:T(8,128)(2,1)S(1)}, bf16[2,5,96,512]{3,2,1,0:T(8,128)(2,1)S(1)}, u32[]{:S(2)}, u32[]{:S(2)}) collective-permute-start(bf16[2,5,96,512]{3,2,1,0:T(8,128)(2,1)S(1)} %pad_maximum_fusion.6), channel_id=1, source_target_pairs={{0,2},{2,0},{4,6},{6,4},{1,3},{3,1},{5,7},{7,5},{8,10},{10,8},{12,... | collective-permute-start | bytes 2949128 | tf_op jit(solution)/shard_map/ppermute | solution.py:191
  666.8 35.9 %collective-permute-start.37 = (bf16[5,2,96,512]{3,2,0,1:T(8,128)(2,1)S(1)}, bf16[5,2,96,512]{3,2,0,1:T(8,128)(2,1)S(1)}, u32[]{:S(2)}, u32[]{:S(2)}) collective-permute-start(bf16[5,2,96,512]{3,2,0,1:T(8,128)(2,1)S(1)} %copy_bitcast_fusion), channel_id=1, source_target_pairs={{0,4},{2,6},{4,0},{6,2},{1,5},{3,7},{5,1},{7,3},{8,12},{10,14},{12... | collective-permute-start | bytes 2949128 | tf_op jit(solution)/shard_map/ppermute | solution.py:191
  (91 other events, 774.0 us)
Sparse Core Ops, SparseCore 0:
  10.5 41.3 all-gather.6
  54.3 56.0 all-gather.8
  112.3 72.0 all-gather.10
  246.4 135.8 reduce-scatter.3
  385.0 136.7 reduce-scatter.5
  524.0 136.7 reduce-scatter.7
